TPU v7x, 256 devices: a whole 4x4x8 slice. The times are simulated.
256 devices in a mesh: dp: 16 (over y, x_lo, core), tensor: 16 (over x_hi, z).
Axes of the slice: x: 4 (x_hi: 2, x_lo: 2; x = x_hi * 2 + x_lo), y: 4, z: 8, core: 2. Of those that a mesh axis runs over, the one named last changes fastest.
Arguments:
- activations: bfloat16 [8192, 8192], P('tensor', 'dp'), may hold values from -6 to 6
- cotangent: bfloat16 [8192, 8192], P('tensor', 'dp'), may hold values from -6 to 6
- gate_first: bfloat16 [64, 128, 448], P('tensor'), may hold values from -0.5 to 0.5
- up_first: bfloat16 [64, 128, 448], P('tensor'), may hold values from -0.5 to 0.5
- gate_second: bfloat16 [224, 128, 128], P('tensor'), may hold values from -0.5 to 0.5
- up_second: bfloat16 [224, 128, 128], P('tensor'), may hold values from -0.5 to 0.5
- down_first: bfloat16 [224, 128, 128], P('tensor'), may hold values from -0.5 to 0.5
- down_second: bfloat16 [64, 448, 128], P('tensor'), may hold values from -0.25 to 0.25
Outputs:
- input_grad: bfloat16 [8192, 8192], P('tensor', 'dp')
- gate_first_grad: float32 [64, 128, 448], P('tensor', 'dp')
- up_first_grad: float32 [64, 128, 448], P('tensor', 'dp')
- gate_second_grad: float32 [224, 128, 128], P('tensor', 'dp')
- up_second_grad: float32 [224, 128, 128], P('tensor', 'dp')
- down_first_grad: float32 [224, 128, 128], P('tensor', 'dp')
- down_second_grad: float32 [64, 448, 128], P('tensor', 'dp')
All inputs are finite; a program needn't handle non-finite values.
Results may differ from a plain program's by a relative error of at most 0.023.
Values may be sent and summed in bfloat16 or wider, within the bound.
No kernel may reach another device: no remote copies, remote signals or barrier semaphores. Data moves between devices by JAX's collectives and lax.ppermute only.
A program may use at most 64 MiB of HBM per device.

v0:
```python
import functools
import jax
import jax.numpy as jnp
from jax import lax
from jax.experimental import pallas as pl
from jax.experimental.pallas import tpu as pltpu
from jax.sharding import Mesh
from jax.sharding import PartitionSpec as P

BLOCK = 128
SUB = 2
BF = jnp.bfloat16
F32 = jnp.float32
NBD = 64
HID = 14
MINE = 28
EACH = MINE * SUB
ROWS = 64
SLOTS = 3
PER = 4
VM = pl.BlockSpec(memory_space=pltpu.VMEM)


def first_weight(held, kind, i):
    return held[(i % PER) * 4 + kind, i // PER]


def second_weight(held, kind, c):
    side, own = c // HID, c % HID
    at = own // SLOTS
    slot = own - jnp.minimum(at * SLOTS, HID - SLOTS)
    start = 16 + (side * SLOTS + slot) * 2
    return held[kind * 5 + at, pl.ds(start, 2)].reshape(BLOCK, BLOCK)


def dot(left, right):
    return lax.dot_general(left, right, (((1,), (0,)), ((), ())), preferred_element_type=F32)


def dot_first(left, right):
    return lax.dot_general(left, right, (((0,), (0,)), ((), ())), preferred_element_type=F32)


def dot_last(left, right):
    return lax.dot_general(left, right, (((1,), (1,)), ((), ())), preferred_element_type=F32)


def scatter_rows(ref, i, value):
    value = value.astype(BF).astype(F32)
    for part in range(2):
        ref[part, pl.ds(i, EACH, stride=NBD), :] = value[:, part * 128 : part * 128 + 128]


def gather_rows(ref, i):
    parts = [ref[part, pl.ds(i, EACH, stride=NBD), :] for part in range(2)]
    return jnp.concatenate(parts, axis=1)


def hidden_rows(ref, c):
    at = pl.multiple_of(c * BLOCK, BLOCK)
    return jnp.concatenate([ref[part, pl.ds(at, BLOCK), :] for part in range(2)], axis=1)


def put_hidden(ref, c, value):
    at = pl.multiple_of(c * BLOCK, BLOCK)
    value = value.astype(BF).astype(F32)
    for part in range(2):
        ref[part, pl.ds(at, BLOCK), :] = value[:, part * 128 : part * 128 + 128]


def loop(count, unroll):
    def run(body):
        def step(at, carry):
            for k in range(unroll):
                body(at * unroll + k)
            return carry

        lax.fori_loop(0, count // unroll, step, 0)

    return run


def forward_kernel(x, held, gate_in, up_in, act, gate_pre, up_pre, down_mid, mid_g, mid_u):
    @loop(NBD, 4)
    def _(i):
        block = x[i]
        scatter_rows(mid_g, i, dot(first_weight(held, 0, i), block)[:EACH])
        scatter_rows(mid_u, i, dot(first_weight(held, 1, i), block)[:EACH])

    @loop(MINE, 2)
    def _(c):
        gate, up = hidden_rows(mid_g, c).astype(BF), hidden_rows(mid_u, c).astype(BF)
        gate_in[c], up_in[c] = gate, up
        pre_g = dot_first(second_weight(held, 0, c), gate)
        pre_u = dot_first(second_weight(held, 1, c), up)
        gate_pre[c], up_pre[c] = pre_g, pre_u
        value = (pre_g * jax.nn.sigmoid(pre_g) * pre_u).astype(BF)
        act[c] = value
        put_hidden(down_mid, c, dot_first(second_weight(held, 2, c), value))


def backward_kernel(dy, held, gate_pre, up_pre, back_in, gate_back, up_back, low, parts, mid, low_g, low_u):
    @loop(NBD, 4)
    def _(i):
        scatter_rows(mid, i, dot(first_weight(held, 2, i), dy[i])[:EACH])

    @loop(MINE, 2)
    def _(c):
        back = hidden_rows(mid, c).astype(BF)
        back_in[c] = back
        grad = dot(second_weight(held, 2, c), back)
        gate, up = gate_pre[c], up_pre[c]
        sigma = jax.nn.sigmoid(gate)
        to_gate = (grad * up * sigma * (1.0 + gate * (1.0 - sigma))).astype(BF)
        to_up = (grad * gate * sigma).astype(BF)
        gate_back[c], up_back[c] = to_gate, to_up
        put_hidden(low_g, c, dot(second_weight(held, 0, c), to_gate))
        put_hidden(low_u, c, dot(second_weight(held, 1, c), to_up))

    fill = jnp.zeros((ROWS - EACH, 256), F32)

    @loop(NBD, 4)
    def _(i):
        both = jnp.concatenate([gather_rows(low_g, i), fill, gather_rows(low_u, i), fill]).astype(BF)
        low[i] = both
        weight = jnp.concatenate([first_weight(held, 0, i), first_weight(held, 1, i)])
        side, at = i // 32, i % 32
        parts[(at // PER) * 8 + side * PER + at % PER] = dot_first(weight, both).astype(BF)


def put_rows(ref, side, at, value):
    for group in range(16):
        ref[group % 2, group // 2, side, at] = value[group * 8 : group * 8 + 8].astype(BF)


def second_grads_kernel(dy, down_mid, act, back_in, gate_in, up_in, gate_back, up_back, out):
    @loop(MINE, 1)
    def _(c):
        side, own = c // HID, c % HID
        put_rows(out, side, own, dot_last(gate_in[c], gate_back[c]))
        put_rows(out, side, HID + own, dot_last(up_in[c], up_back[c]))
        put_rows(out, side, 2 * HID + own, dot_last(act[c], back_in[c]))

    fill = jnp.zeros((4, BLOCK), F32)

    @loop(NBD, 2)
    def _(i):
        side, z, p = i // 32, i % 32 // PER, i % PER
        grad = dot_last(gather_rows(down_mid, i).astype(BF), dy[i])
        for half in range(2):
            rows = jnp.concatenate([grad[half * 28 : half * 28 + 28], fill])
            for k in range(4):
                out[half, z, side, 3 * HID + p * 4 + k] = rows[k * 8 : k * 8 + 8].astype(BF)


def first_grads_kernel(x, low, out):
    @loop(NBD, 2)
    def _(i):
        put_rows(out, i // 32, i % 32, dot_last(x[i], low[i]))


def call(kernel, outs, scratch, flops, *args):
    shapes = [jax.ShapeDtypeStruct(shape, dtype) for shape, dtype in outs]
    moved = sum(a.size * a.dtype.itemsize for a in args)
    return pl.pallas_call(
        kernel,
        out_shape=shapes,
        in_specs=[VM] * len(args),
        out_specs=[VM] * len(outs),
        scratch_shapes=[pltpu.VMEM(shape, dtype) for shape, dtype in scratch],
        compiler_params=pltpu.CompilerParams(vmem_limit_bytes=52 << 20),
        cost_estimate=pl.CostEstimate(flops=flops, bytes_accessed=moved, transcendentals=0),
    )(*args)


HIDDEN = ((MINE, BLOCK, 256), BF)
WIDER = ((MINE, BLOCK, 256), F32)
SPREAD = ((2, MINE * BLOCK, 128), F32)
ONE = 2 * 448 * 4 * 128 * 512


def forward(x, held):
    return call(forward_kernel, [HIDDEN, HIDDEN, HIDDEN, WIDER, WIDER, SPREAD], [SPREAD, SPREAD], 5 * ONE, x, held)


def backward(dy, held, gate_pre, up_pre):
    return call(
        backward_kernel,
        [HIDDEN, HIDDEN, HIDDEN, ((NBD, 2 * ROWS, 256), BF), ((NBD, BLOCK, 256), BF)],
        [SPREAD] * 3,
        6 * ONE,
        dy, held, gate_pre, up_pre,
    )


def second_grads(*args):
    return call(second_grads_kernel, [((2, 8, 2, 58, 8, 128), BF)], [], 4 * ONE, *args)[0]


def first_grads(x, low):
    return call(first_grads_kernel, [((2, 8, 2, 32, 8, 128), BF)], [], 2 * ONE, x, low)[0]


GROUP = ("y", "x_lo", "core")
CHIPS = ("y", "x_lo", "x_hi")
TENSOR = ("x_hi", "z")


def size(name):
    return lax.axis_size(name)


def shift(value, step):
    count = size("z")
    return lax.ppermute(value, "z", [(i, (i + step) % count) for i in range(count)])


def swap(value):
    return lax.ppermute(value, "x_hi", [(0, 1), (1, 0)])


def halves(array, me):
    blocks = array.shape[0] // BLOCK
    half = array.shape[1] // 2
    own = lax.dynamic_slice_in_dim(array, me * half, half, 1)
    other = swap(lax.dynamic_slice_in_dim(array, (1 - me) * half, half, 1))
    return own.reshape(blocks, BLOCK, half), other.reshape(blocks, BLOCK, half)


def ring_gather(own, other, me):
    count = size("z")
    at = lax.axis_index("z")
    full = jnp.zeros((2, count) + own.shape, own.dtype)

    def put(full, value, side, step):
        where = (side, (at + step) % count) + (0,) * value.ndim
        return lax.dynamic_update_slice(full, value[None, None], where)

    full = put(full, own, me, 0)
    full = put(full, other, 1 - me, 0)
    sides = [(own, me), (other, 1 - me)]
    right, left = [own, other], [own, other]
    for step in range(1, count // 2):
        for k, (_, side) in enumerate(sides):
            right[k], left[k] = shift(right[k], 1), shift(left[k], -1)
            full = put(full, right[k], side, -step)
            full = put(full, left[k], side, step)
    full = put(full, shift(right[0], 1), me, count // 2)
    full = put(full, shift(left[1], -1), 1 - me, count // 2)
    return full.reshape((2 * count * own.shape[0],) + own.shape[1:])


def sum_groups(sent):
    pairs = lax.all_to_all(sent, "core", 0, 0, tiled=True)
    pairs = (pairs[0].astype(F32) + pairs[1].astype(F32)).astype(BF)
    pairs = pairs.reshape((-1,) + pairs.shape[2:])
    chips = lax.all_to_all(pairs, CHIPS, 0, 0, tiled=True)
    return jnp.sum(chips.astype(F32), axis=0)


def gather_weights(gate_first, up_first, gate_second, up_second, down_first, down_second):
    nh, nz = size("x_hi"), size("z")
    y, kind = lax.axis_index("y"), lax.axis_index(("x_lo", "core"))
    hid = gate_second.shape[0]
    each = hid * SUB
    take = functools.partial(lax.dynamic_index_in_dim, index=y, axis=0, keepdims=False)
    gate, up = take(gate_first).T, take(up_first).T
    first = jnp.where(kind == 0, gate, jnp.where(kind == 1, up, take(down_second)))
    first = first.reshape(nh, nz, each, BLOCK).transpose(1, 0, 2, 3).reshape(nz, nh * each, BLOCK)
    first = jnp.pad(first, ((0, 0), (0, ROWS - nh * each), (0, 0)))
    first = jnp.broadcast_to(first[None], (nh,) + first.shape).reshape(nh * nz, ROWS, BLOCK)
    first = lax.all_to_all(first, TENSOR, 0, 0, tiled=True)
    d = lax.axis_index(GROUP)
    kind, at = d // 5, jnp.minimum((d % 5) * SLOTS, hid - SLOTS)
    take = functools.partial(lax.dynamic_slice_in_dim, start_index=at, slice_size=SLOTS, axis=0)
    second = jnp.where(
        kind == 0, take(gate_second), jnp.where(kind == 1, take(up_second), take(down_first))
    )
    other = swap(second)
    me = lax.axis_index("x_hi")
    second = jnp.concatenate([jnp.where(me == 0, second, other), jnp.where(me == 0, other, second)])
    second = second.reshape(-1, ROWS, BLOCK)
    return lax.all_gather(jnp.concatenate([first, second]), GROUP, axis=0, tiled=False)


def shards(
    activations, cotangent, gate_first, up_first, gate_second, up_second, down_first, down_second
):
    tokens = activations.shape[1]
    per = gate_first.shape[0]
    wide = gate_first.shape[2]
    hid = gate_second.shape[0]
    ny, nx, nc, nh, nz = (size(a) for a in ("y", "x_lo", "core", "x_hi", "z"))
    ngroup = ny * nx * nc
    scale = (ngroup * tokens) ** (-0.5)
    me = lax.axis_index("x_hi")
    half = tokens // 2
    each = hid * SUB
    rows = BLOCK // ngroup

    held = gather_weights(gate_first, up_first, gate_second, up_second, down_first, down_second)
    x_own, x_other = halves(activations, me)
    dy_own, dy_other = halves(cotangent, me)
    x = ring_gather(x_own, x_other, me)
    dy = ring_gather(dy_own, dy_other, me)

    gate_in, up_in, act, gate_pre, up_pre, down_mid = forward(x, held)
    back_in, gate_back, up_back, low, parts = backward(dy, held, gate_pre, up_pre)

    total = lax.psum_scatter(parts, "z", scatter_dimension=0, tiled=True)
    total = total.reshape(nh, per * BLOCK, half)
    kept = lax.dynamic_index_in_dim(total, me, 0, keepdims=False)
    other = swap(lax.dynamic_index_in_dim(total, 1 - me, 0, keepdims=False))
    input_grad = jnp.concatenate(
        [jnp.where(me == 0, kept, other), jnp.where(me == 0, other, kept)], axis=1
    )

    later = second_grads(dy, down_mid, act, back_in, gate_in, up_in, gate_back, up_back)
    later = sum_groups(later) * scale
    out_gs, out_us, out_df = later[: 3 * hid].reshape(3, hid, rows, BLOCK)
    table = []
    for part in range(ngroup):
        for z in range(nz):
            to_z, side = part // nh, part % nh
            table.append((part * nz + z, (side * nz + z) * nz + to_z))
    out_ds = lax.ppermute(later[3 * hid :], GROUP + ("z",), table)
    out_ds = out_ds.reshape(per, -1, BLOCK)[:, :each]

    firsts = sum_groups(first_grads(x, low)) * scale
    firsts = firsts.reshape(nz, per * rows, 2 * ROWS)
    firsts = lax.all_to_all(firsts, "z", 0, 0, tiled=True)
    firsts = firsts.reshape(nz, per, rows, 2, ROWS)[..., : nh * each]
    firsts = firsts.reshape(nz, per, rows, 2, nh, each).transpose(3, 1, 2, 4, 0, 5)
    out_gf, out_uf = firsts.reshape(2, per, rows, wide)
    return input_grad, out_gf, out_uf, out_gs, out_us, out_df, out_ds


def solution(mesh):
    fine = Mesh(mesh.devices.reshape(4, 2, 2, 2, 8), ("y", "x_lo", "core", "x_hi", "z"))
    arrays = P(TENSOR, GROUP)
    weights = P(TENSOR, None, None)
    return jax.shard_map(
        shards,
        mesh=fine,
        in_specs=(arrays, arrays) + (weights,) * 6,
        out_specs=(arrays,) + (P(TENSOR, GROUP, None),) * 6,
        check_vma=False,
    )
```

profile of v0, /device:TPU:1, one launch (start us, length us, event | category | flops | bytes accessed | tf_op | source)
XLA Modules:
  0.0 318.6 jit_solution(10621488708439120756)
XLA Ops:
  7.2 1.1 fusion
  8.5 0.8 broadcast_in_dim.104
  9.2 11.6 %all-to-all-start = ((bf16[16,64,128]{2,1,0:T(8,128)(2,1)}), bf16[16,64,128]{2,1,0:T(8,128)(2,1)S(1)}, u32[]{:S(2)}, u32[]{:S(2)}) async-start(bf16[16,64,128]{2,1,0:T(8,128)(2,1)} %bitcast.26), calls=%async_computation | async-start | bytes 524288 | tf_op jit(solution)/shard_map/all_to_all | solution.py:272
  20.9 1.0 select_select_fusion
  21.9 3.0 collective-permute-start.15
  24.9 3.4 %collective-permute-done.15 = bf16[3,128,128]{2,1,0:T(8,128)(2,1)S(1)} collective-permute-done((bf16[3,128,128]{2,1,0:T(8,128)(2,1)S(1)}, bf16[3,128,128]{2,1,0:T(8,128)(2,1)S(1)}, u32[]{:S(2)}, u32[]{:S(2)}) %collective-permute-start.15) | collective-permute-done | bytes 98336 | tf_op jit(solution)/shard_map/ppermute | solution.py:219
  28.3 2.8 all-to-all-done
  31.0 0.8 pad_maximum_fusion.1
  32.0 2.4 collective-permute-start.18
  34.4 1.1 collective-permute-start.16
  35.5 2.3 collective-permute-start.2
  37.8 2.5 broadcast.17.clone
  40.3 0.7 constant_dynamic-update-slice_fusion.1
  41.0 2.5 broadcast.17.clone.1
  44.2 2.3 collective-permute-start
  47.2 2.7 collective-permute-start.20
  50.6 7.6 %collective-permute-done = bf16[512,256]{1,0:T(8,128)(2,1)S(1)} collective-permute-done((bf16[512,256]{1,0:T(8,128)(2,1)S(1)}, bf16[512,256]{1,0:T(8,128)(2,1)S(1)}, u32[]{:S(2)}, u32[]{:S(2)}) %collective-permute-start) | collective-permute-done | bytes 262176 | tf_op jit(solution)/shard_map/ppermute | solution.py:219
  59.5 2.1 collective-permute-start.4
  63.1 2.7 collective-permute-start.22
  67.2 2.7 collective-permute-start.6
  70.6 1.4 collective-permute-done.22
  72.0 0.8 collective-permute-start.5
  72.8 4.0 %collective-permute-done.21 = bf16[4,128,256]{2,1,0:T(8,128)(2,1)S(1)} collective-permute-done((bf16[4,128,256]{2,1,0:T(8,128)(2,1)S(1)}, bf16[4,128,256]{2,1,0:T(8,128)(2,1)S(1)}, u32[]{:S(2)}, u32[]{:S(2)}) %collective-permute-start.21) | collective-permute-done | bytes 262176 | tf_op jit(solution)/shard_map/ppermute | solution.py:215
  78.3 1.5 collective-permute-start.25
  80.4 1.2 collective-permute-start.24
  82.6 2.4 collective-permute-start.10
  86.5 6.5 %collective-permute-done.23 = bf16[4,128,256]{2,1,0:T(8,128)(2,1)S(1)} collective-permute-done((bf16[4,128,256]{2,1,0:T(8,128)(2,1)S(1)}, bf16[4,128,256]{2,1,0:T(8,128)(2,1)S(1)}, u32[]{:S(2)}, u32[]{:S(2)}) %collective-permute-start.23) | collective-permute-done | bytes 262176 | tf_op jit(solution)/shard_map/ppermute | solution.py:215
  93.7 1.1 collective-permute-start.7
  94.8 0.7 bitcast_dynamic-update-slice_fusion.6
  95.5 1.6 collective-permute-start.8
  97.8 5.5 %collective-permute-done.7 = bf16[4,128,256]{2,1,0:T(8,128)(2,1)S(1)} collective-permute-done((bf16[4,128,256]{2,1,0:T(8,128)(2,1)S(1)}, bf16[4,128,256]{2,1,0:T(8,128)(2,1)S(1)}, u32[]{:S(2)}, u32[]{:S(2)}) %collective-permute-start.7) | collective-permute-done | bytes 262176 | tf_op jit(solution)/shard_map/ppermute | solution.py:215
  104.1 2.7 collective-permute-start.28
  106.8 0.7 bitcast_dynamic-update-slice_fusion.20
  108.3 2.7 collective-permute-start.12
  111.7 0.7 bitcast_dynamic-update-slice_fusion.18
  112.4 1.6 collective-permute-done.27
  114.0 1.1 collective-permute-start.30
  115.1 2.2 collective-permute-start.14
  118.8 8.0 %collective-permute-done.11 = bf16[4,128,256]{2,1,0:T(8,128)(2,1)S(1)} collective-permute-done((bf16[4,128,256]{2,1,0:T(8,128)(2,1)S(1)}, bf16[4,128,256]{2,1,0:T(8,128)(2,1)S(1)}, u32[]{:S(2)}, u32[]{:S(2)}) %collective-permute-start.11) | collective-permute-done | bytes 262176 | tf_op jit(solution)/shard_map/ppermute | solution.py:215
  129.6 0.8 bitcast_dynamic-update-slice_fusion
  130.5 27.2 %shard_map.135 = (bf16[28,128,256]{2,1,0:T(8,128)(2,1)S(1)}, bf16[28,128,256]{2,1,0:T(8,128)(2,1)}, bf16[28,128,256]{2,1,0:T(8,128)(2,1)}, f32[28,128,256]{2,1,0...) custom-call(bf16[64,128,256]{2,1,0:T(8,128)(2,1)} %bitcast.47.x, bf16[16,28,64,128]{3,2,1,0:T(8,128)(2,1)} %bitcast.104), custom_call_target="tpu_custom_call" | custom-call | flops 1174405120 | bytes 11534336 | tf_op jit(solution)/shard_map/pallas_call | solution.py:165
  157.7 1.2 copy-done
  158.9 31.3 %shard_map.136 = (bf16[28,128,256]{2,1,0:T(8,128)(2,1)S(1)}, bf16[28,128,256]{2,1,0:T(8,128)(2,1)}, bf16[28,128,256]{2,1,0:T(8,128)(2,1)}, bf16[64,128,256]{2,1,0:T(8,128)(2,1)}, bf16[64,128,256]{2,1,0:T(8,128)(2,1)}) custom-call(bf16[64,128,256]{2,1,0:T(8,128)(2,1)} %bitcast.18.dy, bf16[16,28,64,128]{3,2,1,0:T(8,128)(2,1)} %bitcast.105, ...), custom_call_target="tpu_custom_call" | custom-call | flops 1409286144 | bytes 18874368 | tf_op jit(solution)/shard_map/pallas_call | solution.py:165
  190.2 1.3 copy-done.2
  191.4 11.1 %shard_map.137 = bf16[2,8,2,32,8,128]{5,4,3,2,1,0:T(8,128)(2,1)} custom-call(bf16[64,128,256]{2,1,0:T(8,128)(2,1)} %bitcast.47.x, bf16[64,128,256]{2,1,0:T(8,128)(2,1)} %get-tuple-element.21.low), custom_call_target="tpu_custom_call" | custom-call | flops 469762048 | bytes 8388608 | tf_op jit(solution)/shard_map/pallas_call | solution.py:165
  202.5 11.6 %all_to_all.30 = bf16[2,8,2,32,8,128]{5,4,3,2,1,0:T(8,128)(2,1)S(1)} all-to-all(bf16[2,8,2,32,8,128]{5,4,3,2,1,0:T(8,128)(2,1)} %shard_map.137), channel_id=1, replica_groups=mesh['y'=4,'x_lo'=2,'core'=2,'x_hi'=2,'z'=8] {'core'}, dimensions={0} | all-to-all | bytes 4194304 | tf_op jit(solution)/shard_map/all_to_all | solution.py:254
  214.1 1.3 add_convert_fusion.1
  215.4 7.3 %all-to-all-start.2 = ((bf16[16,32,8,128]{3,2,1,0:T(8,128)(2,1)}), bf16[16,32,8,128]{3,2,1,0:T(8,128)(2,1)S(1)}, u32[]{:S(2)}, u32[]{:S(2)}) async-start(bf16[16,32,8,128]{3,2,1,0:T(8,128)(2,1)} %bitcast.51), calls=%async_computation.3 | async-start | bytes 2097152 | tf_op jit(solution)/shard_map/all_to_all | solution.py:257
  222.7 20.1 %shard_map.138 = bf16[2,8,2,58,8,128]{5,4,3,2,1,0:T(8,128)(2,1)} custom-call(bf16[64,128,256]{2,1,0:T(8,128)(2,1)} %bitcast.18.dy, f32[2,3584,128]{2,1,0:T(8,128)} %get-tuple-element.22.down_mid, bf16[28,128,256]{2,1,0:T(8,128)(2,1)S(1)} %copy-done.1, bf16[28,128,256]{2,1,0:T(8,128)(2,1)} %copy-done.2, bf16[28,128,256]{2,1,0:T(8,128)(2,1)} %copy-done, ...), custom_call_target="tpu_custom_call" | custom-call | flops 939524096 | bytes 18874368 | tf_op jit(solution)/shard_map/pallas_call | solution.py:165
  242.8 6.1 %all-to-all-start.4 = ((bf16[2,8,2,58,8,128]{5,4,3,2,1,0:T(8,128)(2,1)}), bf16[2,8,2,58,8,128]{5,4,3,2,1,0:T(8,128)(2,1)}, u32[]{:S(2)}, u32[]{:S(2)}) async-start(bf16[2,8,2,58,8,128]{5,4,3,2,1,0:T(8,128)(2,1)} %shard_map.138), calls=%async_computation.5 | async-start | bytes 7602176 | tf_op jit(solution)/shard_map/all_to_all | solution.py:254
  249.7 3.0 all-to-all-done.4
  252.7 3.8 %all-to-all-start.3 = ((f32[8,32,128]{2,1,0:T(8,128)}), f32[8,32,128]{2,1,0:T(8,128)S(1)}, u32[]{:S(2)}, u32[]{:S(2)}) async-start(f32[8,32,128]{2,1,0:T(8,128)} %bitcast.52), calls=%async_computation.4 | async-start | bytes 262144 | tf_op jit(solution)/shard_map/all_to_all | solution.py:331
  256.5 3.9 %add_convert_fusion = bf16[1,8,2,58,8,128]{5,4,3,2,1,0:T(8,128)(2,1)} fusion(bf16[2,8,2,58,8,128]{5,4,3,2,1,0:T(8,128)(2,1)} %all-to-all-done.4), kind=kLoop, calls=%fused_computation.1 | loop fusion | flops 3801088 | bytes 5701632 | tf_op jit(solution)/shard_map/convert_element_type | solution.py:255
  260.4 4.0 %all-to-all-done.3 = f32[8,32,128]{2,1,0:T(8,128)S(1)} async-done(((f32[8,32,128]{2,1,0:T(8,128)}), f32[8,32,128]{2,1,0:T(8,128)S(1)}, u32[]{:S(2)}, u32[]{:S(2)}) %all-to-all-start.3) | async-done | bytes 131104 | tf_op jit(solution)/shard_map/all_to_all | solution.py:331
  264.4 6.9 %all-to-all-start.5 = ((bf16[16,58,8,128]{3,2,1,0:T(8,128)(2,1)}), bf16[16,58,8,128]{3,2,1,0:T(8,128)(2,1)S(1)}, u32[]{:S(2)}, u32[]{:S(2)}) async-start(bf16[16,58,8,128]{3,2,1,0:T(8,128)(2,1)} %bitcast.54), calls=%async_computation.6 | async-start | bytes 3801088 | tf_op jit(solution)/shard_map/all_to_all | solution.py:257
  272.1 0.8 unstack.27
  273.0 0.8 unstack.25
  273.8 20.7 %all-to-all-done.5 = bf16[16,58,8,128]{3,2,1,0:T(8,128)(2,1)S(1)} async-done(((bf16[16,58,8,128]{3,2,1,0:T(8,128)(2,1)}), bf16[16,58,8,128]{3,2,1,0:T(8,128)(2,1)S(1)}, u32[]{:S(2)}, u32[]{:S(2)}) %all-to-all-start.5) | async-done | bytes 1900576 | tf_op jit(solution)/shard_map/all_to_all | solution.py:257
  294.8 1.0 dynamic-slice_bitcast_fusion
  295.8 3.4 %collective-permute-start.31 = (bf16[512,256]{1,0:T(8,128)(2,1)S(1)}, bf16[512,256]{1,0:T(8,128)(2,1)S(1)}, u32[]{:S(2)}, u32[]{:S(2)}) collective-permute-start(bf16[512,256]{1,0:T(8,128)(2,1)S(1)} %dynamic-slice_bitcast_fusion), channel_id=1, source_target_pairs={{0,8},{8,0},{1,9},{9,1},{2,10},{10,2},{3,11},{11,3},{4,12},{12,4},... | collective-permute-start | bytes 786440 | tf_op jit(solution)/shard_map/ppermute | solution.py:219
  299.3 5.9 %collective-permute-start.32 = (f32[16,8,128]{2,1,0:T(8,128)S(1)}, f32[16,8,128]{2,1,0:T(8,128)S(1)}, u32[]{:S(2)}, u32[]{:S(2)}) collective-permute-start(f32[16,8,128]{2,1,0:T(8,128)S(1)} %slice.42), channel_id=1, source_target_pairs={{0,0},{1,16},{2,32},{3,48},{4,64},{5,80},{6,96},{7,112},{16,128},{... | collective-permute-start | bytes 196616 | tf_op jit(solution)/shard_map/ppermute | solution.py:326
  305.8 3.4 %collective-permute-done.32 = f32[16,8,128]{2,1,0:T(8,128)S(1)} collective-permute-done((f32[16,8,128]{2,1,0:T(8,128)S(1)}, f32[16,8,128]{2,1,0:T(8,128)S(1)}, u32[]{:S(2)}, u32[]{:S(2)}) %collective-permute-start.32) | collective-permute-done | bytes 65568 | tf_op jit(solution)/shard_map/ppermute | solution.py:326
  309.9 1.0 bitcast_select_fusion.1
  310.9 0.8 pad_maximum_fusion
  (98 shorter events, 23.2 us)
Async XLA Ops:
  7.2 24.8 %copy-start.3 = (bf16[512,512]{1,0:T(8,128)(2,1)S(1)}, bf16[512,512]{1,0:T(8,128)(2,1)}, u32[]{:S(2)}) copy-start(bf16[512,512]{1,0:T(8,128)(2,1)} %param.8) | copy-start | bytes 1572868
  7.2 28.3 %copy-start.4 = (bf16[512,512]{1,0:T(8,128)(2,1)S(1)}, bf16[512,512]{1,0:T(8,128)(2,1)}, u32[]{:S(2)}) copy-start(bf16[512,512]{1,0:T(8,128)(2,1)} %param.9) | copy-start | bytes 1572868
  9.2 21.8 %all-to-all-start = ((bf16[16,64,128]{2,1,0:T(8,128)(2,1)}), bf16[16,64,128]{2,1,0:T(8,128)(2,1)S(1)}, u32[]{:S(2)}, u32[]{:S(2)}) async-start(bf16[16,64,128]{2,1,0:T(8,128)(2,1)} %bitcast.26), calls=%async_computation | async-start | bytes 524288 | tf_op jit(solution)/shard_map/all_to_all | solution.py:272
  20.8 109.7 %all-gather.3.cloned.1.call-start = ((), (), s32[]{:S(2)}) async-start(), calls=%async_computation.8 | async-start | bytes 7798784 | tf_op jit(solution)/shard_map/all_gather | solution.py:283
  21.9 6.3 %collective-permute-start.15 = (bf16[3,128,128]{2,1,0:T(8,128)(2,1)S(1)}, bf16[3,128,128]{2,1,0:T(8,128)(2,1)S(1)}, u32[]{:S(2)}, u32[]{:S(2)}) collective-permute-start(bf16[3,128,128]{2,1,0:T(8,128)(2,1)S(1)} %select_select_fusion), channel_id=1, source_target_pairs={{0,8},{8,0},{1,9},{9,1},{2,10},{10,2},{3,11},{11,3},{4,12},{12,4},... | collective-permute-start | bytes 294920 | tf_op jit(solution)/shard_map/ppermute | solution.py:219
  31.9 263.0 %reduce-scatter.2.cloned.1.call-start = ((), (), s32[]{:S(2)}) async-start(), calls=%async_computation.7 | async-start | bytes 4718592 | tf_op jit(solution)/shard_map/reduce_scatter | solution.py:310
  32.0 30.4 %collective-permute-start.18 = (bf16[4,128,256]{2,1,0:T(8,128)(2,1)S(1)}, bf16[4,128,256]{2,1,0:T(8,128)(2,1)S(1)}, u32[]{:S(2)}, u32[]{:S(2)}) collective-permute-start(bf16[4,128,256]{2,1,0:T(8,128)(2,1)S(1)} %bitcast.107), channel_id=1, source_target_pairs={{0,7},{1,0},{2,1},{3,2},{4,3},{5,4},{6,5},{7,6},{8,15},{9,8},{10,9... | collective-permute-start | bytes 786440 | tf_op jit(solution)/shard_map/ppermute | solution.py:215
  34.3 12.8 %collective-permute-start.17 = (bf16[4,128,256]{2,1,0:T(8,128)(2,1)S(1)}, bf16[4,128,256]{2,1,0:T(8,128)(2,1)S(1)}, u32[]{:S(2)}, u32[]{:S(2)}) collective-permute-start(bf16[4,128,256]{2,1,0:T(8,128)(2,1)S(1)} %bitcast.108), channel_id=1, source_target_pairs={{0,1},{1,2},{2,3},{3,4},{4,5},{5,6},{6,7},{7,0},{8,9},{9,10},{10,1... | collective-permute-start | bytes 786440 | tf_op jit(solution)/shard_map/ppermute | solution.py:215
  34.4 9.8 %collective-permute-start.16 = (bf16[512,256]{1,0:T(8,128)(2,1)S(1)}, bf16[512,256]{1,0:T(8,128)(2,1)S(1)}, u32[]{:S(2)}, u32[]{:S(2)}) collective-permute-start(bf16[512,256]{1,0:T(8,128)(2,1)S(1)} %get-tuple-element.54), channel_id=1, source_target_pairs={{0,8},{8,0},{1,9},{9,1},{2,10},{10,2},{3,11},{11,3},{4,12},{12,4},... | collective-permute-start | bytes 786440 | tf_op jit(solution)/shard_map/ppermute | solution.py:219
  35.5 27.5 %collective-permute-start.2 = (bf16[4,128,256]{2,1,0:T(8,128)(2,1)S(1)}, bf16[4,128,256]{2,1,0:T(8,128)(2,1)S(1)}, u32[]{:S(2)}, u32[]{:S(2)}) collective-permute-start(bf16[4,128,256]{2,1,0:T(8,128)(2,1)S(1)} %bitcast.110), channel_id=1, source_target_pairs={{0,7},{1,0},{2,1},{3,2},{4,3},{5,4},{6,5},{7,6},{8,15},{9,8},{10,9... | collective-permute-start | bytes 786440 | tf_op jit(solution)/shard_map/ppermute | solution.py:215
  37.8 21.7 %collective-permute-start.1 = (bf16[4,128,256]{2,1,0:T(8,128)(2,1)S(1)}, bf16[4,128,256]{2,1,0:T(8,128)(2,1)S(1)}, u32[]{:S(2)}, u32[]{:S(2)}) collective-permute-start(bf16[4,128,256]{2,1,0:T(8,128)(2,1)S(1)} %bitcast.111), channel_id=1, source_target_pairs={{0,1},{1,2},{2,3},{3,4},{4,5},{5,6},{6,7},{7,0},{8,9},{9,10},{10,1... | collective-permute-start | bytes 786440 | tf_op jit(solution)/shard_map/ppermute | solution.py:215
  44.2 14.0 %collective-permute-start = (bf16[512,256]{1,0:T(8,128)(2,1)S(1)}, bf16[512,256]{1,0:T(8,128)(2,1)S(1)}, u32[]{:S(2)}, u32[]{:S(2)}) collective-permute-start(bf16[512,256]{1,0:T(8,128)(2,1)S(1)} %get-tuple-element.56), channel_id=1, source_target_pairs={{0,8},{8,0},{1,9},{9,1},{2,10},{10,2},{3,11},{11,3},{4,12},{12,4},... | collective-permute-start | bytes 786440 | tf_op jit(solution)/shard_map/ppermute | solution.py:219
  47.2 20.0 %collective-permute-start.20 = (bf16[4,128,256]{2,1,0:T(8,128)(2,1)S(1)}, bf16[4,128,256]{2,1,0:T(8,128)(2,1)S(1)}, u32[]{:S(2)}, u32[]{:S(2)}) collective-permute-start(bf16[4,128,256]{2,1,0:T(8,128)(2,1)S(1)} %bitcast.120), channel_id=1, source_target_pairs={{0,7},{1,0},{2,1},{3,2},{4,3},{5,4},{6,5},{7,6},{8,15},{9,8},{10,9... | collective-permute-start | bytes 786440 | tf_op jit(solution)/shard_map/ppermute | solution.py:215
  58.2 8.3 %collective-permute-start.19 = (bf16[4,128,256]{2,1,0:T(8,128)(2,1)S(1)}, bf16[4,128,256]{2,1,0:T(8,128)(2,1)S(1)}, u32[]{:S(2)}, u32[]{:S(2)}) collective-permute-start(bf16[4,128,256]{2,1,0:T(8,128)(2,1)S(1)} %bitcast.121), channel_id=1, source_target_pairs={{0,1},{1,2},{2,3},{3,4},{4,5},{5,6},{6,7},{7,0},{8,9},{9,10},{10,1... | collective-permute-start | bytes 786440 | tf_op jit(solution)/shard_map/ppermute | solution.py:215
  59.5 21.0 %collective-permute-start.4 = (bf16[4,128,256]{2,1,0:T(8,128)(2,1)S(1)}, bf16[4,128,256]{2,1,0:T(8,128)(2,1)S(1)}, u32[]{:S(2)}, u32[]{:S(2)}) collective-permute-start(bf16[4,128,256]{2,1,0:T(8,128)(2,1)S(1)} %bitcast.123), channel_id=1, source_target_pairs={{0,7},{1,0},{2,1},{3,2},{4,3},{5,4},{6,5},{7,6},{8,15},{9,8},{10,9... | collective-permute-start | bytes 786440 | tf_op jit(solution)/shard_map/ppermute | solution.py:215
  62.3 15.9 %collective-permute-start.3 = (bf16[4,128,256]{2,1,0:T(8,128)(2,1)S(1)}, bf16[4,128,256]{2,1,0:T(8,128)(2,1)S(1)}, u32[]{:S(2)}, u32[]{:S(2)}) collective-permute-start(bf16[4,128,256]{2,1,0:T(8,128)(2,1)S(1)} %bitcast.124), channel_id=1, source_target_pairs={{0,1},{1,2},{2,3},{3,4},{4,5},{5,6},{6,7},{7,0},{8,9},{9,10},{10,1... | collective-permute-start | bytes 786440 | tf_op jit(solution)/shard_map/ppermute | solution.py:215
  63.1 8.9 %collective-permute-start.22 = (bf16[4,128,256]{2,1,0:T(8,128)(2,1)S(1)}, bf16[4,128,256]{2,1,0:T(8,128)(2,1)S(1)}, u32[]{:S(2)}, u32[]{:S(2)}) collective-permute-start(bf16[4,128,256]{2,1,0:T(8,128)(2,1)S(1)} %collective-permute-done.18), channel_id=1, source_target_pairs={{0,7},{1,0},{2,1},{3,2},{4,3},{5,4},{6,5},{7,6},{8,15},{9,8},{10,9... | collective-permute-start | bytes 786440 | tf_op jit(solution)/shard_map/ppermute | solution.py:215
  66.5 10.3 %collective-permute-start.21 = (bf16[4,128,256]{2,1,0:T(8,128)(2,1)S(1)}, bf16[4,128,256]{2,1,0:T(8,128)(2,1)S(1)}, u32[]{:S(2)}, u32[]{:S(2)}) collective-permute-start(bf16[4,128,256]{2,1,0:T(8,128)(2,1)S(1)} %collective-permute-done.17), channel_id=1, source_target_pairs={{0,1},{1,2},{2,3},{3,4},{4,5},{5,6},{6,7},{7,0},{8,9},{9,10},{10,1... | collective-permute-start | bytes 786440 | tf_op jit(solution)/shard_map/ppermute | solution.py:215
  67.2 15.1 %collective-permute-start.6 = (bf16[4,128,256]{2,1,0:T(8,128)(2,1)S(1)}, bf16[4,128,256]{2,1,0:T(8,128)(2,1)S(1)}, u32[]{:S(2)}, u32[]{:S(2)}) collective-permute-start(bf16[4,128,256]{2,1,0:T(8,128)(2,1)S(1)} %collective-permute-done.2), channel_id=1, source_target_pairs={{0,7},{1,0},{2,1},{3,2},{4,3},{5,4},{6,5},{7,6},{8,15},{9,8},{10,9... | collective-permute-start | bytes 786440 | tf_op jit(solution)/shard_map/ppermute | solution.py:215
  72.0 10.7 %collective-permute-start.5 = (bf16[4,128,256]{2,1,0:T(8,128)(2,1)S(1)}, bf16[4,128,256]{2,1,0:T(8,128)(2,1)S(1)}, u32[]{:S(2)}, u32[]{:S(2)}) collective-permute-start(bf16[4,128,256]{2,1,0:T(8,128)(2,1)S(1)} %collective-permute-done.1), channel_id=1, source_target_pairs={{0,1},{1,2},{2,3},{3,4},{4,5},{5,6},{6,7},{7,0},{8,9},{9,10},{10,1... | collective-permute-start | bytes 786440 | tf_op jit(solution)/shard_map/ppermute | solution.py:215
  76.8 31.4 %collective-permute-start.26 = (bf16[4,128,256]{2,1,0:T(8,128)(2,1)S(1)}, bf16[4,128,256]{2,1,0:T(8,128)(2,1)S(1)}, u32[]{:S(2)}, u32[]{:S(2)}) collective-permute-start(bf16[4,128,256]{2,1,0:T(8,128)(2,1)S(1)} %collective-permute-done.22), channel_id=1, source_target_pairs={{0,7},{1,0},{2,1},{3,2},{4,3},{5,4},{6,5},{7,6},{8,15},{9,8},{10,9... | collective-permute-start | bytes 786440 | tf_op jit(solution)/shard_map/ppermute | solution.py:215
  78.3 17.3 %collective-permute-start.25 = (bf16[4,128,256]{2,1,0:T(8,128)(2,1)S(1)}, bf16[4,128,256]{2,1,0:T(8,128)(2,1)S(1)}, u32[]{:S(2)}, u32[]{:S(2)}) collective-permute-start(bf16[4,128,256]{2,1,0:T(8,128)(2,1)S(1)} %collective-permute-done.21), channel_id=1, source_target_pairs={{0,1},{1,2},{2,3},{3,4},{4,5},{5,6},{6,7},{7,0},{8,9},{9,10},{10,1... | collective-permute-start | bytes 786440 | tf_op jit(solution)/shard_map/ppermute | solution.py:215
  80.4 13.3 %collective-permute-start.24 = (bf16[4,128,256]{2,1,0:T(8,128)(2,1)S(1)}, bf16[4,128,256]{2,1,0:T(8,128)(2,1)S(1)}, u32[]{:S(2)}, u32[]{:S(2)}) collective-permute-start(bf16[4,128,256]{2,1,0:T(8,128)(2,1)S(1)} %collective-permute-done.20), channel_id=1, source_target_pairs={{0,7},{1,0},{2,1},{3,2},{4,3},{5,4},{6,5},{7,6},{8,15},{9,8},{10,9... | collective-permute-start | bytes 786440 | tf_op jit(solution)/shard_map/ppermute | solution.py:215
  82.4 10.7 %collective-permute-start.23 = (bf16[4,128,256]{2,1,0:T(8,128)(2,1)S(1)}, bf16[4,128,256]{2,1,0:T(8,128)(2,1)S(1)}, u32[]{:S(2)}, u32[]{:S(2)}) collective-permute-start(bf16[4,128,256]{2,1,0:T(8,128)(2,1)S(1)} %collective-permute-done.19), channel_id=1, source_target_pairs={{0,1},{1,2},{2,3},{3,4},{4,5},{5,6},{6,7},{7,0},{8,9},{9,10},{10,1... | collective-permute-start | bytes 786440 | tf_op jit(solution)/shard_map/ppermute | solution.py:215
  82.6 29.0 %collective-permute-start.10 = (bf16[4,128,256]{2,1,0:T(8,128)(2,1)S(1)}, bf16[4,128,256]{2,1,0:T(8,128)(2,1)S(1)}, u32[]{:S(2)}, u32[]{:S(2)}) collective-permute-start(bf16[4,128,256]{2,1,0:T(8,128)(2,1)S(1)} %collective-permute-done.6), channel_id=1, source_target_pairs={{0,7},{1,0},{2,1},{3,2},{4,3},{5,4},{6,5},{7,6},{8,15},{9,8},{10,9... | collective-permute-start | bytes 786440 | tf_op jit(solution)/shard_map/ppermute | solution.py:215
  93.0 14.5 %collective-permute-start.9 = (bf16[4,128,256]{2,1,0:T(8,128)(2,1)S(1)}, bf16[4,128,256]{2,1,0:T(8,128)(2,1)S(1)}, u32[]{:S(2)}, u32[]{:S(2)}) collective-permute-start(bf16[4,128,256]{2,1,0:T(8,128)(2,1)S(1)} %collective-permute-done.5), channel_id=1, source_target_pairs={{0,1},{1,2},{2,3},{3,4},{4,5},{5,6},{6,7},{7,0},{8,9},{9,10},{10,1... | collective-permute-start | bytes 786440 | tf_op jit(solution)/shard_map/ppermute | solution.py:215
  93.7 9.7 %collective-permute-start.7 = (bf16[4,128,256]{2,1,0:T(8,128)(2,1)S(1)}, bf16[4,128,256]{2,1,0:T(8,128)(2,1)S(1)}, u32[]{:S(2)}, u32[]{:S(2)}) collective-permute-start(bf16[4,128,256]{2,1,0:T(8,128)(2,1)S(1)} %collective-permute-done.3), channel_id=1, source_target_pairs={{0,1},{1,2},{2,3},{3,4},{4,5},{5,6},{6,7},{7,0},{8,9},{9,10},{10,1... | collective-permute-start | bytes 786440 | tf_op jit(solution)/shard_map/ppermute | solution.py:215
  95.5 8.6 %collective-permute-start.8 = (bf16[4,128,256]{2,1,0:T(8,128)(2,1)S(1)}, bf16[4,128,256]{2,1,0:T(8,128)(2,1)S(1)}, u32[]{:S(2)}, u32[]{:S(2)}) collective-permute-start(bf16[4,128,256]{2,1,0:T(8,128)(2,1)S(1)} %collective-permute-done.4), channel_id=1, source_target_pairs={{0,7},{1,0},{2,1},{3,2},{4,3},{5,4},{6,5},{7,6},{8,15},{9,8},{10,9... | collective-permute-start | bytes 786440 | tf_op jit(solution)/shard_map/ppermute | solution.py:215
  103.4 24.8 %collective-permute-start.29 = (bf16[4,128,256]{2,1,0:T(8,128)(2,1)S(1)}, bf16[4,128,256]{2,1,0:T(8,128)(2,1)S(1)}, u32[]{:S(2)}, u32[]{:S(2)}) collective-permute-start(bf16[4,128,256]{2,1,0:T(8,128)(2,1)S(1)} %collective-permute-done.25), channel_id=1, source_target_pairs={{0,1},{1,2},{2,3},{3,4},{4,5},{5,6},{6,7},{7,0},{8,9},{9,10},{10,1... | collective-permute-start | bytes 786440 | tf_op jit(solution)/shard_map/ppermute | solution.py:215
  104.1 8.3 %collective-permute-start.28 = (bf16[4,128,256]{2,1,0:T(8,128)(2,1)S(1)}, bf16[4,128,256]{2,1,0:T(8,128)(2,1)S(1)}, u32[]{:S(2)}, u32[]{:S(2)}) collective-permute-start(bf16[4,128,256]{2,1,0:T(8,128)(2,1)S(1)} %collective-permute-done.24), channel_id=1, source_target_pairs={{0,7},{1,0},{2,1},{3,2},{4,3},{5,4},{6,5},{7,6},{8,15},{9,8},{10,9... | collective-permute-start | bytes 786440 | tf_op jit(solution)/shard_map/ppermute | solution.py:215
  107.5 6.5 %collective-permute-start.27 = (bf16[4,128,256]{2,1,0:T(8,128)(2,1)S(1)}, bf16[4,128,256]{2,1,0:T(8,128)(2,1)S(1)}, u32[]{:S(2)}, u32[]{:S(2)}) collective-permute-start(bf16[4,128,256]{2,1,0:T(8,128)(2,1)S(1)} %collective-permute-done.23), channel_id=1, source_target_pairs={{0,1},{1,2},{2,3},{3,4},{4,5},{5,6},{6,7},{7,0},{8,9},{9,10},{10,1... | collective-permute-start | bytes 786440 | tf_op jit(solution)/shard_map/ppermute | solution.py:215
  108.3 6.9 %collective-permute-start.12 = (bf16[4,128,256]{2,1,0:T(8,128)(2,1)S(1)}, bf16[4,128,256]{2,1,0:T(8,128)(2,1)S(1)}, u32[]{:S(2)}, u32[]{:S(2)}) collective-permute-start(bf16[4,128,256]{2,1,0:T(8,128)(2,1)S(1)} %collective-permute-done.8), channel_id=1, source_target_pairs={{0,7},{1,0},{2,1},{3,2},{4,3},{5,4},{6,5},{7,6},{8,15},{9,8},{10,9... | collective-permute-start | bytes 786440 | tf_op jit(solution)/shard_map/ppermute | solution.py:215
  111.7 17.3 %collective-permute-start.13 = (bf16[4,128,256]{2,1,0:T(8,128)(2,1)S(1)}, bf16[4,128,256]{2,1,0:T(8,128)(2,1)S(1)}, u32[]{:S(2)}, u32[]{:S(2)}) collective-permute-start(bf16[4,128,256]{2,1,0:T(8,128)(2,1)S(1)} %collective-permute-done.9), channel_id=1, source_target_pairs={{0,1},{1,2},{2,3},{3,4},{4,5},{5,6},{6,7},{7,0},{8,9},{9,10},{10,1... | collective-permute-start | bytes 786440 | tf_op jit(solution)/shard_map/ppermute | solution.py:215
  112.4 14.4 %collective-permute-start.11 = (bf16[4,128,256]{2,1,0:T(8,128)(2,1)S(1)}, bf16[4,128,256]{2,1,0:T(8,128)(2,1)S(1)}, u32[]{:S(2)}, u32[]{:S(2)}) collective-permute-start(bf16[4,128,256]{2,1,0:T(8,128)(2,1)S(1)} %collective-permute-done.7), channel_id=1, source_target_pairs={{0,1},{1,2},{2,3},{3,4},{4,5},{5,6},{6,7},{7,0},{8,9},{9,10},{10,1... | collective-permute-start | bytes 786440 | tf_op jit(solution)/shard_map/ppermute | solution.py:215
  114.0 15.6 %collective-permute-start.30 = (bf16[4,128,256]{2,1,0:T(8,128)(2,1)S(1)}, bf16[4,128,256]{2,1,0:T(8,128)(2,1)S(1)}, u32[]{:S(2)}, u32[]{:S(2)}) collective-permute-start(bf16[4,128,256]{2,1,0:T(8,128)(2,1)S(1)} %collective-permute-done.28), channel_id=1, source_target_pairs={{0,7},{1,0},{2,1},{3,2},{4,3},{5,4},{6,5},{7,6},{8,15},{9,8},{10,9... | collective-permute-start | bytes 786440 | tf_op jit(solution)/shard_map/ppermute | solution.py:215
  115.1 14.5 %collective-permute-start.14 = (bf16[4,128,256]{2,1,0:T(8,128)(2,1)S(1)}, bf16[4,128,256]{2,1,0:T(8,128)(2,1)S(1)}, u32[]{:S(2)}, u32[]{:S(2)}) collective-permute-start(bf16[4,128,256]{2,1,0:T(8,128)(2,1)S(1)} %collective-permute-done.12), channel_id=1, source_target_pairs={{0,7},{1,0},{2,1},{3,2},{4,3},{5,4},{6,5},{7,6},{8,15},{9,8},{10,9... | collective-permute-start | bytes 786440 | tf_op jit(solution)/shard_map/ppermute | solution.py:215
  157.7 1.2 copy-start
  190.2 1.3 copy-start.2
  202.5 20.2 %copy-start.1 = (bf16[28,128,256]{2,1,0:T(8,128)(2,1)S(1)}, bf16[28,128,256]{2,1,0:T(8,128)(2,1)}, u32[]{:S(2)}) copy-start(bf16[28,128,256]{2,1,0:T(8,128)(2,1)} %get-tuple-element.23.act) | copy-start | bytes 5505028
  215.4 27.4 %all-to-all-start.2 = ((bf16[16,32,8,128]{3,2,1,0:T(8,128)(2,1)}), bf16[16,32,8,128]{3,2,1,0:T(8,128)(2,1)S(1)}, u32[]{:S(2)}, u32[]{:S(2)}) async-start(bf16[16,32,8,128]{3,2,1,0:T(8,128)(2,1)} %bitcast.51), calls=%async_computation.3 | async-start | bytes 2097152 | tf_op jit(solution)/shard_map/all_to_all | solution.py:257
  242.8 10.0 %all-to-all-start.4 = ((bf16[2,8,2,58,8,128]{5,4,3,2,1,0:T(8,128)(2,1)}), bf16[2,8,2,58,8,128]{5,4,3,2,1,0:T(8,128)(2,1)}, u32[]{:S(2)}, u32[]{:S(2)}) async-start(bf16[2,8,2,58,8,128]{5,4,3,2,1,0:T(8,128)(2,1)} %shard_map.138), calls=%async_computation.5 | async-start | bytes 7602176 | tf_op jit(solution)/shard_map/all_to_all | solution.py:254
  252.7 11.6 %all-to-all-start.3 = ((f32[8,32,128]{2,1,0:T(8,128)}), f32[8,32,128]{2,1,0:T(8,128)S(1)}, u32[]{:S(2)}, u32[]{:S(2)}) async-start(f32[8,32,128]{2,1,0:T(8,128)} %bitcast.52), calls=%async_computation.4 | async-start | bytes 262144 | tf_op jit(solution)/shard_map/all_to_all | solution.py:331
  264.4 30.1 %all-to-all-start.5 = ((bf16[16,58,8,128]{3,2,1,0:T(8,128)(2,1)}), bf16[16,58,8,128]{3,2,1,0:T(8,128)(2,1)S(1)}, u32[]{:S(2)}, u32[]{:S(2)}) async-start(bf16[16,58,8,128]{3,2,1,0:T(8,128)(2,1)} %bitcast.54), calls=%async_computation.6 | async-start | bytes 3801088 | tf_op jit(solution)/shard_map/all_to_all | solution.py:257
  295.8 14.1 %collective-permute-start.31 = (bf16[512,256]{1,0:T(8,128)(2,1)S(1)}, bf16[512,256]{1,0:T(8,128)(2,1)S(1)}, u32[]{:S(2)}, u32[]{:S(2)}) collective-permute-start(bf16[512,256]{1,0:T(8,128)(2,1)S(1)} %dynamic-slice_bitcast_fusion), channel_id=1, source_target_pairs={{0,8},{8,0},{1,9},{9,1},{2,10},{10,2},{3,11},{11,3},{4,12},{12,4},... | collective-permute-start | bytes 786440 | tf_op jit(solution)/shard_map/ppermute | solution.py:219
  299.3 10.0 %collective-permute-start.32 = (f32[16,8,128]{2,1,0:T(8,128)S(1)}, f32[16,8,128]{2,1,0:T(8,128)S(1)}, u32[]{:S(2)}, u32[]{:S(2)}) collective-permute-start(f32[16,8,128]{2,1,0:T(8,128)S(1)} %slice.42), channel_id=1, source_target_pairs={{0,0},{1,16},{2,32},{3,48},{4,64},{5,80},{6,96},{7,112},{16,128},{... | collective-permute-start | bytes 196616 | tf_op jit(solution)/shard_map/ppermute | solution.py:326
Sparse Core Ops, SparseCore 0:
  32.0 54.8 all-gather.2
  191.6 58.9 reduce-scatter.1
where the time goes:
time: 321 us; the launch traced here: 319 us
  Pallas kernels  89.6 us (28%)
  starting transfers between devices  84.4 us (26%)
  waiting for transfers between devices  72.1 us (22%)
  local copies, waits for them, and re-layouts  35.5 us (11%)
  between operations  14.4 us (4%)
  blocking collectives  11.6 us (4%)
  other arithmetic  11.1 us (3%)
    pallas_call x4, Pallas kernels, call(): pl.pallas_call(kernel, out_shape=shapes, in_specs=[VM] * len(args), out_s...  89.6 us
    ppermute x28, starting transfers between devices, shift(): lax.ppermute(value, 'z', [(i, (i + step) % count) for i in range(count)])  33 us
    ppermute x28, waiting for transfers between devices, shift(): lax.ppermute(value, 'z', [(i, (i + step) % count) for i in range(count)])  27.1 us
    dynamic_update_slice x31, local copies, waits for them, and re-layouts, put(): return lax.dynamic_update_slice(full, value[None, None], where)  22.4 us
    all_to_all x2, waiting for transfers between devices, sum_groups(): chips = lax.all_to_all(pairs, CHIPS, 0, 0, tiled=True)  20.7 us
    all_to_all x2, starting transfers between devices, sum_groups(): chips = lax.all_to_all(pairs, CHIPS, 0, 0, tiled=True)  14.2 us
    all_to_all x1, blocking collectives, sum_groups(): pairs = lax.all_to_all(sent, 'core', 0, 0, tiled=True)  11.6 us
    all_to_all x1, starting transfers between devices, gather_weights(): first = lax.all_to_all(first, TENSOR, 0, 0, tiled=True)  11.6 us
  transfers between devices with their start and end apart: 40, of which 13 were waited for; matrix products, arithmetic and copies ran while one was open for 12% of the time, Pallas kernels for 10%

commit v1 on v0

v1 whole, which is shorter than its diff:
```python
import functools
import jax
import jax.numpy as jnp
import numpy as np
from jax import lax
from jax.experimental import pallas as pl
from jax.experimental.pallas import tpu as pltpu
from jax.sharding import Mesh
from jax.sharding import PartitionSpec as P

BLOCK = 128
SUB = 2
BF = jnp.bfloat16
F32 = jnp.float32
NBD = 64
HID = 14
MINE = 28
EACH = MINE * SUB
ROWS = 64
SLOTS = 3
PER = 4
TOK = 256
VM = pl.BlockSpec(memory_space=pltpu.VMEM)
SM = pl.BlockSpec(memory_space=pltpu.SMEM)


def first_weight(held, kind, i):
    return held[(i % PER) * 4 + kind, i // PER]


def second_weight(held, kind, c):
    side, own = c // HID, c % HID
    at = own // SLOTS
    slot = own - jnp.minimum(at * SLOTS, HID - SLOTS)
    start = (side * SLOTS + slot) * 2
    return held[kind * 5 + at, pl.ds(start, 2)].reshape(BLOCK, BLOCK)


def dot(left, right):
    return lax.dot_general(left, right, (((1,), (0,)), ((), ())), preferred_element_type=F32)


def dot_first(left, right):
    return lax.dot_general(left, right, (((0,), (0,)), ((), ())), preferred_element_type=F32)


def dot_last(left, right):
    return lax.dot_general(left, right, (((1,), (1,)), ((), ())), preferred_element_type=F32)


def loop(count, unroll):
    def run(body):
        def step(at, carry):
            body([at * unroll + k for k in range(unroll)])
            return carry

        lax.fori_loop(0, count // unroll, step, 0)

    return run


def collect(where, shards, out):
    me, z = where[0], where[1]
    for k, shard in enumerate(shards):
        side = me if k % 2 == 0 else 1 - me
        out[pl.ds(side * 32 + lax.rem(z + k // 2, 8) * PER, PER)] = shard[...]


def turn(swap, source, target, outer):
    tiles = [source[:, k * 16 : k * 16 + 16, :].reshape(256, TOK) for k in range(4)]
    tiles = [dot(swap[...], tile).astype(BF).reshape(16, 16, TOK) for tile in tiles]
    for k, tile in enumerate(tiles):
        target[k * 16 : k * 16 + 16, pl.ds(outer, 16), :] = tile


def forward_first_kernel(where, swap, held, *refs):
    shards, (x, gate_in, up_in, mid_g, mid_u) = refs[:16], refs[16:]
    collect(where, shards, x)

    def group(at, carry):
        @loop(16, 4)
        def _(ks):
            weights = [
                jnp.concatenate([first_weight(held, 0, at * 16 + k), first_weight(held, 1, at * 16 + k)])
                for k in ks
            ]
            mids = [dot(w, x[at * 16 + k]).astype(BF) for w, k in zip(weights, ks)]
            for mid, k in zip(mids, ks):
                mid_g[k] = mid[:ROWS]
                mid_u[k] = mid[ROWS:]

        outer = pl.multiple_of(at * 16, 16)
        turn(swap, mid_g, gate_in, outer)
        turn(swap, mid_u, up_in, outer)
        return carry

    lax.fori_loop(0, 4, group, 0)


def hidden(ref, c):
    return ref[pl.ds(c * SUB, SUB)].reshape(BLOCK, TOK)


def turn_back(swap, source, target, unit):
    def group(at, carry):
        tiles = [
            source[k * 16 : k * 16 + 16, pl.ds(pl.multiple_of(at * 16, 16), 16), :].reshape(256, TOK)
            for k in range(4)
        ]
        tiles = [dot(swap[...], tile).astype(BF).reshape(16, 16, TOK) for tile in tiles]
        for k, tile in enumerate(tiles):
            target[pl.ds(at * 16, 16), unit + k * 16 : unit + k * 16 + 16, :] = tile
        return carry

    lax.fori_loop(0, 4, group, 0)


def forward_second_kernel(swap, held, gate_in, up_in, act, to_gate, to_up, down_in, down_mid):
    down_mid[EACH:] = jnp.zeros((ROWS - EACH, NBD, TOK), BF)

    @loop(MINE, 2)
    def _(cs):
        gates = [dot_first(second_weight(held, 0, c), hidden(gate_in, c)) for c in cs]
        ups = [dot_first(second_weight(held, 1, c), hidden(up_in, c)) for c in cs]
        sigmas = [jax.nn.sigmoid(g) for g in gates]
        acts = [(g * s * u).astype(BF) for g, s, u in zip(gates, sigmas, ups)]
        downs = [dot_first(second_weight(held, 2, c), a) for c, a in zip(cs, acts)]
        for c, g, s, u, a, d in zip(cs, gates, sigmas, ups, acts, downs):
            to_gate[c], to_up[c], act[c] = u * s * (1.0 + g * (1.0 - s)), g * s, a
            down_mid[pl.ds(c * SUB, SUB)] = d.astype(BF).reshape(SUB, NBD, TOK)

    turn_back(swap, down_mid, down_in, 0)


def backward_kernel(where, swap, held_first, held_second, to_gate, to_up, *refs):
    shards = refs[:16]
    dy, back_in, gate_back, up_back, low, parts, mid, low_g, low_u = refs[16:]
    collect(where, shards, dy)
    low_g[EACH:] = jnp.zeros((ROWS - EACH, NBD, TOK), BF)
    low_u[EACH:] = jnp.zeros((ROWS - EACH, NBD, TOK), BF)

    def group(at, carry):
        @loop(16, 4)
        def _(ks):
            mids = [dot(first_weight(held_first, 2, at * 16 + k), dy[at * 16 + k]).astype(BF) for k in ks]
            for value, k in zip(mids, ks):
                mid[k] = value

        turn(swap, mid, back_in, pl.multiple_of(at * 16, 16))
        return carry

    lax.fori_loop(0, 4, group, 0)

    @loop(MINE, 2)
    def _(cs):
        grads = [dot(second_weight(held_second, 2, c), hidden(back_in, c)) for c in cs]
        to_gates = [(grad * to_gate[c]).astype(BF) for c, grad in zip(cs, grads)]
        to_ups = [(grad * to_up[c]).astype(BF) for c, grad in zip(cs, grads)]
        lows_g = [dot(second_weight(held_second, 0, c), v) for c, v in zip(cs, to_gates)]
        lows_u = [dot(second_weight(held_second, 1, c), v) for c, v in zip(cs, to_ups)]
        for c, g, u, lg, lu in zip(cs, to_gates, to_ups, lows_g, lows_u):
            gate_back[c], up_back[c] = g, u
            low_g[pl.ds(c * SUB, SUB)] = lg.astype(BF).reshape(SUB, NBD, TOK)
            low_u[pl.ds(c * SUB, SUB)] = lu.astype(BF).reshape(SUB, NBD, TOK)

    turn_back(swap, low_g, low, 0)
    turn_back(swap, low_u, low, ROWS)

    @loop(NBD, 4)
    def _(blocks):
        weights = [
            jnp.concatenate([first_weight(held_first, 0, i), first_weight(held_first, 1, i)]) for i in blocks
        ]
        values = [dot_first(w, low[i]).astype(BF) for w, i in zip(weights, blocks)]
        for i, value in zip(blocks, values):
            side, at = i // 32, i % 32
            parts[(at // PER) * 8 + side * PER + at % PER] = value


def put_rows(ref, side, at, value):
    for group in range(16):
        ref[group % 2, group // 2, side, at] = value[group * 8 : group * 8 + 8].astype(BF)


def second_grads_kernel(dy, down_in, act, back_in, gate_in, up_in, gate_back, up_back, out):
    @loop(MINE, 2)
    def _(cs):
        grads = [
            (
                dot_last(hidden(gate_in, c), gate_back[c]),
                dot_last(hidden(up_in, c), up_back[c]),
                dot_last(act[c], hidden(back_in, c)),
            )
            for c in cs
        ]
        for c, grad in zip(cs, grads):
            for k in range(3):
                put_rows(out, c // HID, k * HID + c % HID, grad[k])

    fill = jnp.zeros((4, BLOCK), F32)

    @loop(NBD, 4)
    def _(blocks):
        grads = [dot_last(down_in[i], dy[i]) for i in blocks]
        for i, grad in zip(blocks, grads):
            side, z, p = i // 32, i % 32 // PER, i % PER
            for half in range(2):
                rows = jnp.concatenate([grad[half * 28 : half * 28 + 28], fill])
                for k in range(4):
                    out[half, z, side, 3 * HID + p * 4 + k] = rows[k * 8 : k * 8 + 8].astype(BF)


def first_grads_kernel(x, low, out):
    @loop(NBD, 4)
    def _(blocks):
        grads = [dot_last(x[i], low[i]) for i in blocks]
        for i, grad in zip(blocks, grads):
            put_rows(out, i // 32, i % 32, grad)


def call(kernel, outs, scratch, flops, *args):
    shapes = [jax.ShapeDtypeStruct(shape, dtype) for shape, dtype in outs]
    moved = sum(a.size * a.dtype.itemsize for a in args)
    return pl.pallas_call(
        kernel,
        out_shape=shapes,
        in_specs=[SM if a.dtype == jnp.int32 else VM for a in args],
        out_specs=[VM] * len(outs),
        scratch_shapes=[pltpu.VMEM(shape, dtype) for shape, dtype in scratch],
        compiler_params=pltpu.CompilerParams(vmem_limit_bytes=48 << 20),
        cost_estimate=pl.CostEstimate(flops=flops, bytes_accessed=moved, transcendentals=0),
    )(*args)


HIDDEN = ((MINE, BLOCK, TOK), BF)
WIDER = ((MINE, BLOCK, TOK), F32)
SPREAD = ((ROWS, NBD, TOK), BF)
MODEL = ((NBD, BLOCK, TOK), BF)
TILE = ((16, ROWS, TOK), BF)
ONE = 2 * 448 * 4 * 128 * 512


def swap_table():
    at = np.arange(256)
    table = np.zeros((256, 256), np.float32)
    table[at, at % 16 * 16 + at // 16] = 1.0
    return jnp.asarray(table, BF)


def forward_first(where, swap, held, shards):
    return call(forward_first_kernel, [MODEL, SPREAD, SPREAD], [TILE, TILE], 6 * ONE, where, swap, held, *shards)


def forward_second(swap, held, gate_in, up_in):
    outs = [HIDDEN, WIDER, WIDER, SPREAD]
    return call(forward_second_kernel, outs, [SPREAD], 5 * ONE, swap, held, gate_in, up_in)


def backward(where, swap, held_first, held_second, to_gate, to_up, shards):
    return call(
        backward_kernel,
        [MODEL, SPREAD, HIDDEN, HIDDEN, MODEL, MODEL],
        [TILE, SPREAD, SPREAD],
        12 * ONE,
        where, swap, held_first, held_second, to_gate, to_up, *shards,
    )


def second_grads(*args):
    return call(second_grads_kernel, [((2, 8, 2, 58, 8, 128), BF)], [], 4 * ONE, *args)[0]


def first_grads(x, low):
    return call(first_grads_kernel, [((2, 8, 2, 32, 8, 128), BF)], [], 2 * ONE, x, low)[0]


GROUP = ("y", "x_lo", "core")
CHIPS = ("y", "x_lo", "x_hi")
TENSOR = ("x_hi", "z")


def size(name):
    return lax.axis_size(name)


def shift(value, step):
    count = size("z")
    return lax.ppermute(value, "z", [(i, (i + step) % count) for i in range(count)])


def swap(value):
    return lax.ppermute(value, "x_hi", [(0, 1), (1, 0)])


def halves(array, me):
    blocks = array.shape[0] // BLOCK
    half = array.shape[1] // 2
    own = lax.dynamic_slice_in_dim(array, me * half, half, 1)
    other = swap(lax.dynamic_slice_in_dim(array, (1 - me) * half, half, 1))
    return own.reshape(blocks, BLOCK, half), other.reshape(blocks, BLOCK, half)


def ring_gather(own, other):
    count = size("z")
    found = [[None, None] for _ in range(count)]
    found[0] = [own, other]
    right, left = [own, other], [own, other]
    for step in range(1, count // 2):
        for k in range(2):
            right[k], left[k] = shift(right[k], 1), shift(left[k], -1)
            found[count - step][k], found[step][k] = right[k], left[k]
    found[count // 2] = [shift(right[0], 1), shift(left[1], -1)]
    return [shard for pair in found for shard in pair]


def sum_groups(sent):
    pairs = lax.all_to_all(sent, "core", 0, 0, tiled=True)
    pairs = (pairs[0].astype(F32) + pairs[1].astype(F32)).astype(BF)
    pairs = pairs.reshape((-1,) + pairs.shape[2:])
    chips = lax.all_to_all(pairs, CHIPS, 0, 0, tiled=True)
    return jnp.sum(chips.astype(F32), axis=0)


def gather_first(gate_first, up_first, down_second):
    nh, nz = size("x_hi"), size("z")
    y, kind = lax.axis_index("y"), lax.axis_index(("x_lo", "core"))
    each = gate_first.shape[2] // (nh * nz)
    take = functools.partial(lax.dynamic_index_in_dim, index=y, axis=0, keepdims=False)
    gate, up = take(gate_first).T, take(up_first).T
    first = jnp.where(kind == 0, gate, jnp.where(kind == 1, up, take(down_second)))
    first = first.reshape(nh, nz, each, BLOCK).transpose(1, 0, 2, 3).reshape(nz, nh * each, BLOCK)
    first = jnp.pad(first, ((0, 0), (0, ROWS - nh * each), (0, 0)))
    first = jnp.broadcast_to(first[None], (nh,) + first.shape).reshape(nh * nz, ROWS, BLOCK)
    first = lax.all_to_all(first, TENSOR, 0, 0, tiled=True)
    return lax.all_gather(first, GROUP, axis=0, tiled=False)


def gather_second(gate_second, up_second, down_first):
    hid = gate_second.shape[0]
    d = lax.axis_index(GROUP)
    kind, at = d // 5, jnp.minimum((d % 5) * SLOTS, hid - SLOTS)
    take = functools.partial(lax.dynamic_slice_in_dim, start_index=at, slice_size=SLOTS, axis=0)
    second = jnp.where(
        kind == 0, take(gate_second), jnp.where(kind == 1, take(up_second), take(down_first))
    )
    other = swap(second)
    me = lax.axis_index("x_hi")
    second = jnp.concatenate([jnp.where(me == 0, second, other), jnp.where(me == 0, other, second)])
    return lax.all_gather(second.reshape(-1, ROWS, BLOCK), GROUP, axis=0, tiled=False)


def shards(
    activations, cotangent, gate_first, up_first, gate_second, up_second, down_first, down_second
):
    tokens = activations.shape[1]
    per = gate_first.shape[0]
    wide = gate_first.shape[2]
    hid = gate_second.shape[0]
    ny, nx, nc, nh, nz = (size(a) for a in ("y", "x_lo", "core", "x_hi", "z"))
    ngroup = ny * nx * nc
    scale = (ngroup * tokens) ** (-0.5)
    me = lax.axis_index("x_hi")
    half = tokens // 2
    each = hid * SUB
    rows = BLOCK // ngroup

    where = jnp.stack([me, lax.axis_index("z")]).astype(jnp.int32)
    table = swap_table()
    x_own, x_other = halves(activations, me)
    held_second = gather_second(gate_second, up_second, down_first)
    xs = ring_gather(x_own, x_other)
    dy_own, dy_other = halves(cotangent, me)
    weights = (gate_first, up_first, down_second)
    weights, _ = lax.optimization_barrier((weights, (xs[2], xs[14])))
    held_first = gather_first(*weights)
    (dy_own, dy_other), _ = lax.optimization_barrier(((dy_own, dy_other), (xs[2], xs[14])))
    dys = ring_gather(dy_own, dy_other)

    x, gate_in, up_in = forward_first(where, table, held_first, xs)
    act, to_gate, to_up, down_in = forward_second(table, held_second, gate_in, up_in)
    dy, back_in, gate_back, up_back, low, parts = backward(
        where, table, held_first, held_second, to_gate, to_up, dys
    )

    total = lax.psum_scatter(parts, "z", scatter_dimension=0, tiled=True)
    total = total.reshape(nh, per * BLOCK, half)
    kept = lax.dynamic_index_in_dim(total, me, 0, keepdims=False)
    other = swap(lax.dynamic_index_in_dim(total, 1 - me, 0, keepdims=False))
    input_grad = jnp.concatenate(
        [jnp.where(me == 0, kept, other), jnp.where(me == 0, other, kept)], axis=1
    )

    later = second_grads(dy, down_in, act, back_in, gate_in, up_in, gate_back, up_back)
    later = sum_groups(later) * scale
    out_gs, out_us, out_df = later[: 3 * hid].reshape(3, hid, rows, BLOCK)
    pairs = []
    for part in range(ngroup):
        for z in range(nz):
            to_z, side = part // nh, part % nh
            pairs.append((part * nz + z, (side * nz + z) * nz + to_z))
    out_ds = lax.ppermute(later[3 * hid :], GROUP + ("z",), pairs)
    out_ds = out_ds.reshape(per, -1, BLOCK)[:, :each]

    firsts = sum_groups(first_grads(x, low)) * scale
    firsts = firsts.reshape(nz, per * rows, 2 * ROWS)
    firsts = lax.all_to_all(firsts, "z", 0, 0, tiled=True)
    firsts = firsts.reshape(nz, per, rows, 2, ROWS)[..., : nh * each]
    firsts = firsts.reshape(nz, per, rows, 2, nh, each).transpose(3, 1, 2, 4, 0, 5)
    out_gf, out_uf = firsts.reshape(2, per, rows, wide)
    return input_grad, out_gf, out_uf, out_gs, out_us, out_df, out_ds


def solution(mesh):
    fine = Mesh(mesh.devices.reshape(4, 2, 2, 2, 8), ("y", "x_lo", "core", "x_hi", "z"))
    arrays = P(TENSOR, GROUP)
    weights = P(TENSOR, None, None)
    return jax.shard_map(
        shards,
        mesh=fine,
        in_specs=(arrays, arrays) + (weights,) * 6,
        out_specs=(arrays,) + (P(TENSOR, GROUP, None),) * 6,
        check_vma=False,
    )
```

time: 321 us -> 306 us (0.953)
  blocking collectives: 11.6 us -> 37.7 us
  Pallas kernels: 89.6 us -> 72.9 us
  local copies, waits for them, and re-layouts: 35.5 us -> 21.6 us
  starting transfers between devices: 84.4 us -> 71.9 us
    dynamic_update_slice x31 -> x0, local copies, waits for them, and re-layouts: 22.4 us -> none  [put(): return lax.dynamic_update_slice(full, value[None, None], where)]
    all_to_all x0 -> x1, blocking collectives: none -> 16.7 us  [gather_first(): first = lax.all_to_all(first, TENSOR, 0, 0, tiled=True)]
    pallas_call x4 -> x5, Pallas kernels: 89.6 us -> 72.9 us  [call(): pl.pallas_call(kernel, out_shape=shapes, in_specs=[SM if a.dtype == jnp.i...]
    unnamed x12 -> x44, local copies, waits for them, and re-layouts: 3.17 us -> 16.2 us
    all_to_all x1 -> x0, starting transfers between devices: 11.6 us -> none  [gather_weights(): first = lax.all_to_all(first, TENSOR, 0, 0, tiled=True)]
    all_to_all x1, blocking collectives: 11.6 us -> 21 us  [sum_groups(): pairs = lax.all_to_all(sent, 'core', 0, 0, tiled=True)]
    another operation x2 -> x0, local copies, waits for them, and re-layouts: 4.92 us -> none
    ppermute x28, waiting for transfers between devices: 27.1 us -> 31 us  [shift(): lax.ppermute(value, 'z', [(i, (i + step) % count) for i in range(count)])]
  transfers between devices with their start and end apart: 40 -> 40, of which waited for: 13 -> 20; matrix products, arithmetic and copies ran while one was open for 12% -> 4% of each run, Pallas kernels for 10% -> 15%
where the time goes in v1:
time: 306 us; the launch traced here: 303 us
  waiting for transfers between devices  73.9 us (24%)
  Pallas kernels  72.9 us (24%)
  starting transfers between devices  71.9 us (23%)
  blocking collectives  37.7 us (12%)
  local copies, waits for them, and re-layouts  21.6 us (7%)
  between operations  14.1 us (5%)
  other arithmetic  11 us (4%)
    pallas_call x5, Pallas kernels, call(): pl.pallas_call(kernel, out_shape=shapes, in_specs=[SM if a.dtype == jnp.i...  72.9 us
    ppermute x28, starting transfers between devices, shift(): lax.ppermute(value, 'z', [(i, (i + step) % count) for i in range(count)])  34.6 us
    ppermute x28, waiting for transfers between devices, shift(): lax.ppermute(value, 'z', [(i, (i + step) % count) for i in range(count)])  31 us
    all_to_all x1, blocking collectives, sum_groups(): pairs = lax.all_to_all(sent, 'core', 0, 0, tiled=True)  21 us
    all_to_all x2, waiting for transfers between devices, sum_groups(): chips = lax.all_to_all(pairs, CHIPS, 0, 0, tiled=True)  20.6 us
    all_to_all x1, blocking collectives, gather_first(): first = lax.all_to_all(first, TENSOR, 0, 0, tiled=True)  16.7 us
    unnamed x44, local copies, waits for them, and re-layouts  16.2 us
    all_to_all x2, starting transfers between devices, sum_groups(): chips = lax.all_to_all(pairs, CHIPS, 0, 0, tiled=True)  14.1 us
  transfers between devices with their start and end apart: 40, of which 20 were waited for; matrix products, arithmetic and copies ran while one was open for 4% of the time, Pallas kernels for 15%

profile of v1, /device:TPU:1, one launch (start us, length us, event | category | flops | bytes accessed | tf_op | source)
XLA Modules:
  0.0 303.1 jit_solution(16430838248165325524)
XLA Ops:
  7.2 1.1 constant_dynamic-slice_fusion.2
  8.3 2.5 collective-permute-start.1
  10.8 4.0 %collective-permute-start = (bf16[4,128,256]{2,1,0:T(8,128)(2,1)S(1)}, bf16[4,128,256]{2,1,0:T(8,128)(2,1)S(1)}, u32[]{:S(2)}, u32[]{:S(2)}) collective-permute-start(bf16[4,128,256]{2,1,0:T(8,128)(2,1)S(1)} %bitcast.48), channel_id=1, source_target_pairs={{0,7},{1,0},{2,1},{3,2},{4,3},{5,4},{6,5},{7,6},{8,15},{9,8},{10,9... | collective-permute-start | bytes 786440 | tf_op jit(solution)/shard_map/ppermute | solution.py:288
  14.9 5.9 %collective-permute-done.1.refs_14_ = bf16[4,128,256]{2,1,0:T(8,128)(2,1)S(1)} collective-permute-done((bf16[4,128,256]{2,1,0:T(8,128)(2,1)S(1)}, bf16[4,128,256]{2,1,0:T(8,128)(2,1)S(1)}, u32[]{:S(2)}, u32[]{:S(2)}) %collective-permute-start.1) | collective-permute-done | bytes 262176 | tf_op jit(solution)/shard_map/ppermute | solution.py:288
  20.8 1.0 fusion
  22.1 16.7 %all_to_all.30 = bf16[16,64,128]{2,1,0:T(8,128)(2,1)} all-to-all(bf16[16,64,128]{2,1,0:T(8,128)(2,1)S(1)} %bitcast.59), channel_id=1, replica_groups=mesh['y'=4,'x_lo'=2,'core'=2,'x_hi'=2,'z'=8] {'x_hi','z'}, dimensions={0} | all-to-all | bytes 524288 | tf_op jit(solution)/shard_map/all_to_all | solution.py:334
  38.9 1.0 select_select_fusion
  40.7 4.2 %collective-permute-done.2 = bf16[3,128,128]{2,1,0:T(8,128)(2,1)S(1)} collective-permute-done((bf16[3,128,128]{2,1,0:T(8,128)(2,1)S(1)}, bf16[3,128,128]{2,1,0:T(8,128)(2,1)S(1)}, u32[]{:S(2)}, u32[]{:S(2)}) %collective-permute-start.2) | collective-permute-done | bytes 98336 | tf_op jit(solution)/shard_map/ppermute | solution.py:292
  46.6 2.3 collective-permute-start.16
  48.9 1.8 collective-permute-start.9
  50.7 0.9 collective-permute-start.5
  51.6 1.0 collective-permute-done.3
  52.6 1.8 collective-permute-start.13
  54.4 0.9 collective-permute-start.4
  55.2 6.5 %collective-permute-done.16 = bf16[512,256]{1,0:T(8,128)(2,1)S(1)} collective-permute-done((bf16[512,256]{1,0:T(8,128)(2,1)S(1)}, bf16[512,256]{1,0:T(8,128)(2,1)S(1)}, u32[]{:S(2)}, u32[]{:S(2)}) %collective-permute-start.16) | collective-permute-done | bytes 262176 | tf_op jit(solution)/shard_map/ppermute | solution.py:292
  61.7 3.3 %collective-permute-start.23 = (bf16[4,128,256]{2,1,0:T(8,128)(2,1)S(1)}, bf16[4,128,256]{2,1,0:T(8,128)(2,1)S(1)}, u32[]{:S(2)}, u32[]{:S(2)}) collective-permute-start(bf16[4,128,256]{2,1,0:T(8,128)(2,1)S(1)} %bitcast.44), channel_id=1, source_target_pairs={{0,1},{1,2},{2,3},{3,4},{4,5},{5,6},{6,7},{7,0},{8,9},{9,10},{10,1... | collective-permute-start | bytes 786440 | tf_op jit(solution)/shard_map/ppermute | solution.py:288
  65.0 1.5 collective-permute-start.28
  66.5 1.3 collective-permute-start.18
  68.4 2.0 collective-permute-start.7
  72.0 1.7 collective-permute-done.28.refs_15_
  75.5 1.0 collective-permute-start.24
  77.2 0.9 collective-permute-start.19
  78.2 0.9 collective-permute-done.7.refs_6_
  79.8 2.3 collective-permute-done.14.refs_13_
  82.4 1.5 collective-permute-done.6.refs_5_
  85.3 2.4 collective-permute-done.24.refs_12_
  87.7 2.1 collective-permute-start.11
  90.1 3.3 %collective-permute-done.29.refs_13_ = bf16[4,128,256]{2,1,0:T(8,128)(2,1)} collective-permute-done((bf16[4,128,256]{2,1,0:T(8,128)(2,1)S(1)}, bf16[4,128,256]{2,1,0:T(8,128)(2,1)}, u32[]{:S(2)}, u32[]{:S(2)}) %collective-permute-start.29) | collective-permute-done | bytes 262176 | tf_op jit(solution)/shard_map/ppermute | solution.py:288
  93.4 2.1 collective-permute-start.25
  96.1 4.8 %collective-permute-done.8.refs_7_ = bf16[4,128,256]{2,1,0:T(8,128)(2,1)} collective-permute-done((bf16[4,128,256]{2,1,0:T(8,128)(2,1)S(1)}, bf16[4,128,256]{2,1,0:T(8,128)(2,1)}, u32[]{:S(2)}, u32[]{:S(2)}) %collective-permute-start.8) | collective-permute-done | bytes 262176 | tf_op jit(solution)/shard_map/ppermute | solution.py:288
  101.5 3.1 %collective-permute-done.15.refs_11_ = bf16[4,128,256]{2,1,0:T(8,128)(2,1)} collective-permute-done((bf16[4,128,256]{2,1,0:T(8,128)(2,1)}, bf16[4,128,256]{2,1,0:T(8,128)(2,1)}, u32[]{:S(2)}, u32[]{:S(2)}) %collective-permute-start.15) | collective-permute-done | bytes 262176 | tf_op jit(solution)/shard_map/ppermute | solution.py:288
  104.6 2.2 collective-permute-start.30
  106.8 3.5 %collective-permute-done.25.refs_10_ = bf16[4,128,256]{2,1,0:T(8,128)(2,1)} collective-permute-done((bf16[4,128,256]{2,1,0:T(8,128)(2,1)S(1)}, bf16[4,128,256]{2,1,0:T(8,128)(2,1)}, u32[]{:S(2)}, u32[]{:S(2)}) %collective-permute-start.25) | collective-permute-done | bytes 262176 | tf_op jit(solution)/shard_map/ppermute | solution.py:288
  110.3 2.1 collective-permute-start.26
  113.0 0.9 copy-done.11
  114.0 1.0 copy-done.13
  115.0 0.9 copy-done.15
  115.9 0.9 copy-done.17
  116.9 1.0 copy-done.19
  117.8 11.0 %shard_map.144 = (bf16[64,128,256]{2,1,0:T(8,128)(2,1)}, bf16[64,64,256]{2,1,0:T(8,128)(2,1)}, bf16[64,64,256]{2,1,0:T(8,128)(2,1)}) custom-call(s32[2]{0:T(128)S(1)} %pad_add_fusion.where, bf16[256,256]{1,0:T(8,128)(2,1)S(1)} %copy-done.5, bf16[16,16,64,128]{3,2,1,0:T(8,128)(2,1)} %bitcast.56, bf16[4,128,256]{2,1,0:T(8,128)(2,1)S(1)} %bitcast.49, ...), custom_call_target="tpu_custom_call" | custom-call | flops 1409286144 | bytes 8519688 | tf_op jit(solution)/shard_map/pallas_call | solution.py:224
  128.9 1.6 copy-done
  130.5 13.2 %shard_map.145 = (bf16[28,128,256]{2,1,0:T(8,128)(2,1)S(1)}, f32[28,128,256]{2,1,0:T(8,128)}, f32[28,128,256]{2,1,0:T(8,128)}, bf16[64,64,256]{2,1,0:T(8,128)(2,1)S(1)}) custom-call(bf16[256,256]{1,0:T(8,128)(2,1)S(1)} %copy-done.5, bf16[16,12,64,128]{3,2,1,0:T(8,128)(2,1)} %all-gather.4.cloned.1.call-done.held.held_second, ...), custom_call_target="tpu_custom_call" | custom-call | flops 1174405120 | bytes 7471104 | tf_op jit(solution)/shard_map/pallas_call | solution.py:224
  143.7 1.3 copy-done.1
  145.1 27.7 %shard_map.146 = (bf16[64,128,256]{2,1,0:T(8,128)(2,1)}, bf16[64,64,256]{2,1,0:T(8,128)(2,1)}, bf16[28,128,256]{2,1,0:T(8,128)(2,1)S(1)}, bf16[28,128,256]{2,1,0...) custom-call(s32[2]{0:T(128)S(1)} %pad_add_fusion.where, bf16[256,256]{1,0:T(8,128)(2,1)S(1)} %copy-done.5, ...), custom_call_target="tpu_custom_call" | custom-call | flops 2818572288 | bytes 19005448 | tf_op jit(solution)/shard_map/pallas_call | solution.py:224
  172.8 1.3 copy-done.2
  174.1 7.2 %shard_map.147 = bf16[2,8,2,32,8,128]{5,4,3,2,1,0:T(8,128)(2,1)S(1)} custom-call(bf16[64,128,256]{2,1,0:T(8,128)(2,1)} %get-tuple-element.35.x, bf16[64,128,256]{2,1,0:T(8,128)(2,1)} %get-tuple-element.36.low), custom_call_target="tpu_custom_call" | custom-call | flops 469762048 | bytes 8388608 | tf_op jit(solution)/shard_map/pallas_call | solution.py:224
  181.3 21.0 %all_to_all.31 = bf16[2,8,2,32,8,128]{5,4,3,2,1,0:T(8,128)(2,1)S(1)} all-to-all(bf16[2,8,2,32,8,128]{5,4,3,2,1,0:T(8,128)(2,1)S(1)} %shard_map.147), channel_id=1, replica_groups=mesh['y'=4,'x_lo'=2,'core'=2,'x_hi'=2,'z'=8] {'core'}, dimensions={0} | all-to-all | bytes 4194304 | tf_op jit(solution)/shard_map/all_to_all | solution.py:317
  202.3 1.3 add_convert_fusion.1
  203.6 7.2 %all-to-all-start.2 = ((bf16[16,32,8,128]{3,2,1,0:T(8,128)(2,1)}), bf16[16,32,8,128]{3,2,1,0:T(8,128)(2,1)S(1)}, u32[]{:S(2)}, u32[]{:S(2)}) async-start(bf16[16,32,8,128]{3,2,1,0:T(8,128)(2,1)} %bitcast.19), calls=%async_computation.3 | async-start | bytes 2097152 | tf_op jit(solution)/shard_map/all_to_all | solution.py:320
  210.8 1.5 copy-done.3
  212.3 1.5 copy-done.4
  213.8 13.7 %shard_map.148 = bf16[2,8,2,58,8,128]{5,4,3,2,1,0:T(8,128)(2,1)} custom-call(bf16[64,128,256]{2,1,0:T(8,128)(2,1)} %get-tuple-element.37.dy, bf16[64,64,256]{2,1,0:T(8,128)(2,1)} %copy-done.1, bf16[28,128,256]{2,1,0:T(8,128)(2,1)S(1)} %get-tuple-element.39.act, bf16[64,64,256]{2,1,0:T(8,128)(2,1)} %get-tuple-element.40.back_in, ...), custom_call_target="tpu_custom_call" | custom-call | flops 939524096 | bytes 18087936 | tf_op jit(solution)/shard_map/pallas_call | solution.py:224
  227.6 6.2 %all-to-all-start.4 = ((bf16[2,8,2,58,8,128]{5,4,3,2,1,0:T(8,128)(2,1)}), bf16[2,8,2,58,8,128]{5,4,3,2,1,0:T(8,128)(2,1)}, u32[]{:S(2)}, u32[]{:S(2)}) async-start(bf16[2,8,2,58,8,128]{5,4,3,2,1,0:T(8,128)(2,1)} %shard_map.148), calls=%async_computation.5 | async-start | bytes 7602176 | tf_op jit(solution)/shard_map/all_to_all | solution.py:317
  234.6 3.0 %all-to-all-done.4 = bf16[2,8,2,58,8,128]{5,4,3,2,1,0:T(8,128)(2,1)} async-done(((bf16[2,8,2,58,8,128]{5,4,3,2,1,0:T(8,128)(2,1)}), bf16[2,8,2,58,8,128]{5,4,3,2,1,0:T(8,128)(2,1)}, u32[]{:S(2)}, u32[]{:S(2)}) %all-to-all-start.4) | async-done | bytes 3801120 | tf_op jit(solution)/shard_map/all_to_all | solution.py:317
  237.6 3.4 %all-to-all-start.3 = ((f32[8,32,128]{2,1,0:T(8,128)}), f32[8,32,128]{2,1,0:T(8,128)S(1)}, u32[]{:S(2)}, u32[]{:S(2)}) async-start(f32[8,32,128]{2,1,0:T(8,128)} %bitcast.20), calls=%async_computation.4 | async-start | bytes 262144 | tf_op jit(solution)/shard_map/all_to_all | solution.py:406
  241.0 3.9 %add_convert_fusion = bf16[1,8,2,58,8,128]{5,4,3,2,1,0:T(8,128)(2,1)} fusion(bf16[2,8,2,58,8,128]{5,4,3,2,1,0:T(8,128)(2,1)} %all-to-all-done.4), kind=kLoop, calls=%fused_computation.1 | loop fusion | flops 3801088 | bytes 5701632 | tf_op jit(solution)/shard_map/convert_element_type | solution.py:318
  244.9 4.4 %all-to-all-done.3 = f32[8,32,128]{2,1,0:T(8,128)S(1)} async-done(((f32[8,32,128]{2,1,0:T(8,128)}), f32[8,32,128]{2,1,0:T(8,128)S(1)}, u32[]{:S(2)}, u32[]{:S(2)}) %all-to-all-start.3) | async-done | bytes 131104 | tf_op jit(solution)/shard_map/all_to_all | solution.py:406
  249.3 6.9 %all-to-all-start.5 = ((bf16[16,58,8,128]{3,2,1,0:T(8,128)(2,1)}), bf16[16,58,8,128]{3,2,1,0:T(8,128)(2,1)S(1)}, u32[]{:S(2)}, u32[]{:S(2)}) async-start(bf16[16,58,8,128]{3,2,1,0:T(8,128)(2,1)} %bitcast.22), calls=%async_computation.6 | async-start | bytes 3801088 | tf_op jit(solution)/shard_map/all_to_all | solution.py:320
  258.7 20.6 %all-to-all-done.5 = bf16[16,58,8,128]{3,2,1,0:T(8,128)(2,1)S(1)} async-done(((bf16[16,58,8,128]{3,2,1,0:T(8,128)(2,1)}), bf16[16,58,8,128]{3,2,1,0:T(8,128)(2,1)S(1)}, u32[]{:S(2)}, u32[]{:S(2)}) %all-to-all-start.5) | async-done | bytes 1900576 | tf_op jit(solution)/shard_map/all_to_all | solution.py:320
  279.6 1.0 dynamic-slice_bitcast_fusion
  280.6 3.9 %collective-permute-start.31 = (bf16[512,256]{1,0:T(8,128)(2,1)S(1)}, bf16[512,256]{1,0:T(8,128)(2,1)S(1)}, u32[]{:S(2)}, u32[]{:S(2)}) collective-permute-start(bf16[512,256]{1,0:T(8,128)(2,1)S(1)} %dynamic-slice_bitcast_fusion), channel_id=1, source_target_pairs={{0,8},{8,0},{1,9},{9,1},{2,10},{10,2},{3,11},{11,3},{4,12},{12,4},... | collective-permute-start | bytes 786440 | tf_op jit(solution)/shard_map/ppermute | solution.py:292
  284.6 5.6 %collective-permute-start.32 = (f32[16,8,128]{2,1,0:T(8,128)S(1)}, f32[16,8,128]{2,1,0:T(8,128)S(1)}, u32[]{:S(2)}, u32[]{:S(2)}) collective-permute-start(f32[16,8,128]{2,1,0:T(8,128)S(1)} %slice.42), channel_id=1, source_target_pairs={{0,0},{1,16},{2,32},{3,48},{4,64},{5,80},{6,96},{7,112},{16,128},{... | collective-permute-start | bytes 196616 | tf_op jit(solution)/shard_map/ppermute | solution.py:401
  290.9 3.2 %collective-permute-done.32 = f32[16,8,128]{2,1,0:T(8,128)S(1)} collective-permute-done((f32[16,8,128]{2,1,0:T(8,128)S(1)}, f32[16,8,128]{2,1,0:T(8,128)S(1)}, u32[]{:S(2)}, u32[]{:S(2)}) %collective-permute-start.32) | collective-permute-done | bytes 65568 | tf_op jit(solution)/shard_map/ppermute | solution.py:401
  294.7 1.0 bitcast_select_fusion.1
  (100 shorter events, 17.7 us)
Async XLA Ops:
  7.2 105.9 %all-gather.6.cloned.1.call-start = ((), (), s32[]{:S(2)}) async-start(), calls=%async_computation.9 | async-start | bytes 4456448 | tf_op jit(solution)/shard_map/all_gather | solution.py:335
  8.3 38.3 %copy-start.20 = (bf16[512,512]{1,0:T(8,128)(2,1)S(1)}, bf16[512,512]{1,0:T(8,128)(2,1)}, u32[]{:S(2)}) copy-start(bf16[512,512]{1,0:T(8,128)(2,1)} %param.10) | copy-start | bytes 1572868
  8.3 12.5 %collective-permute-start.1 = (bf16[4,128,256]{2,1,0:T(8,128)(2,1)S(1)}, bf16[4,128,256]{2,1,0:T(8,128)(2,1)S(1)}, u32[]{:S(2)}, u32[]{:S(2)}) collective-permute-start(bf16[4,128,256]{2,1,0:T(8,128)(2,1)S(1)} %bitcast.47), channel_id=1, source_target_pairs={{0,1},{1,2},{2,3},{3,4},{4,5},{5,6},{6,7},{7,0},{8,9},{9,10},{10,1... | collective-permute-start | bytes 786440 | tf_op jit(solution)/shard_map/ppermute | solution.py:288
  10.8 10.0 %collective-permute-start = (bf16[4,128,256]{2,1,0:T(8,128)(2,1)S(1)}, bf16[4,128,256]{2,1,0:T(8,128)(2,1)S(1)}, u32[]{:S(2)}, u32[]{:S(2)}) collective-permute-start(bf16[4,128,256]{2,1,0:T(8,128)(2,1)S(1)} %bitcast.48), channel_id=1, source_target_pairs={{0,7},{1,0},{2,1},{3,2},{4,3},{5,4},{6,5},{7,6},{8,15},{9,8},{10,9... | collective-permute-start | bytes 786440 | tf_op jit(solution)/shard_map/ppermute | solution.py:288
  21.9 91.1 %copy-start.5 = (bf16[256,256]{1,0:T(8,128)(2,1)S(1)}, bf16[256,256]{1,0:T(8,128)(2,1)}, u32[]{:S(2)}) copy-start(bf16[256,256]{1,0:T(8,128)(2,1)} %constant.82.clone.swap) | copy-start | bytes 393220
  38.8 90.1 %all-gather.4.cloned.1.call-start = ((), (), s32[]{:S(2)}) async-start(), calls=%async_computation.7 | async-start | bytes 3342336 | tf_op jit(solution)/shard_map/all_gather | solution.py:349
  39.9 5.1 %collective-permute-start.2 = (bf16[3,128,128]{2,1,0:T(8,128)(2,1)S(1)}, bf16[3,128,128]{2,1,0:T(8,128)(2,1)S(1)}, u32[]{:S(2)}, u32[]{:S(2)}) collective-permute-start(bf16[3,128,128]{2,1,0:T(8,128)(2,1)S(1)} %select_select_fusion), channel_id=1, source_target_pairs={{0,8},{8,0},{1,9},{9,1},{2,10},{10,2},{3,11},{11,3},{4,12},{12,4},... | collective-permute-start | bytes 294920 | tf_op jit(solution)/shard_map/ppermute | solution.py:292
  45.7 233.9 %reduce-scatter.2.cloned.1.call-start = ((), (), s32[]{:S(2)}) async-start(), calls=%async_computation.8 | async-start | bytes 4718592 | tf_op jit(solution)/shard_map/reduce_scatter | solution.py:385
  45.7 6.8 %collective-permute-start.3 = (bf16[512,256]{1,0:T(8,128)(2,1)S(1)}, bf16[512,256]{1,0:T(8,128)(2,1)S(1)}, u32[]{:S(2)}, u32[]{:S(2)}) collective-permute-start(bf16[512,256]{1,0:T(8,128)(2,1)S(1)} %get-tuple-element.70), channel_id=1, source_target_pairs={{0,8},{8,0},{1,9},{9,1},{2,10},{10,2},{3,11},{11,3},{4,12},{12,4},... | collective-permute-start | bytes 786440 | tf_op jit(solution)/shard_map/ppermute | solution.py:292
  46.6 15.1 %collective-permute-start.16 = (bf16[512,256]{1,0:T(8,128)(2,1)S(1)}, bf16[512,256]{1,0:T(8,128)(2,1)S(1)}, u32[]{:S(2)}, u32[]{:S(2)}) collective-permute-start(bf16[512,256]{1,0:T(8,128)(2,1)S(1)} %get-tuple-element.68), channel_id=1, source_target_pairs={{0,8},{8,0},{1,9},{9,1},{2,10},{10,2},{3,11},{11,3},{4,12},{12,4},... | collective-permute-start | bytes 786440 | tf_op jit(solution)/shard_map/ppermute | solution.py:292
  48.9 16.1 %collective-permute-start.9 = (bf16[4,128,256]{2,1,0:T(8,128)(2,1)S(1)}, bf16[4,128,256]{2,1,0:T(8,128)(2,1)S(1)}, u32[]{:S(2)}, u32[]{:S(2)}) collective-permute-start(bf16[4,128,256]{2,1,0:T(8,128)(2,1)S(1)} %collective-permute-done.1.refs_14_), channel_id=1, source_target_pairs={{0,1},{1,2},{2,3},{3,4},{4,5},{5,6},{6,7},{7,0},{8,9},{9,10},{10,1... | collective-permute-start | bytes 786440 | tf_op jit(solution)/shard_map/ppermute | solution.py:288
  50.7 14.3 %collective-permute-start.5 = (bf16[4,128,256]{2,1,0:T(8,128)(2,1)S(1)}, bf16[4,128,256]{2,1,0:T(8,128)(2,1)S(1)}, u32[]{:S(2)}, u32[]{:S(2)}) collective-permute-start(bf16[4,128,256]{2,1,0:T(8,128)(2,1)S(1)} %collective-permute-done.refs_2_), channel_id=1, source_target_pairs={{0,7},{1,0},{2,1},{3,2},{4,3},{5,4},{6,5},{7,6},{8,15},{9,8},{10,9... | collective-permute-start | bytes 786440 | tf_op jit(solution)/shard_map/ppermute | solution.py:288
  52.6 13.9 %collective-permute-start.13 = (bf16[4,128,256]{2,1,0:T(8,128)(2,1)S(1)}, bf16[4,128,256]{2,1,0:T(8,128)(2,1)S(1)}, u32[]{:S(2)}, u32[]{:S(2)}) collective-permute-start(bf16[4,128,256]{2,1,0:T(8,128)(2,1)S(1)} %bitcast.53), channel_id=1, source_target_pairs={{0,1},{1,2},{2,3},{3,4},{4,5},{5,6},{6,7},{7,0},{8,9},{9,10},{10,1... | collective-permute-start | bytes 786440 | tf_op jit(solution)/shard_map/ppermute | solution.py:288
  54.4 13.4 %collective-permute-start.4 = (bf16[4,128,256]{2,1,0:T(8,128)(2,1)S(1)}, bf16[4,128,256]{2,1,0:T(8,128)(2,1)S(1)}, u32[]{:S(2)}, u32[]{:S(2)}) collective-permute-start(bf16[4,128,256]{2,1,0:T(8,128)(2,1)S(1)} %bitcast.54), channel_id=1, source_target_pairs={{0,7},{1,0},{2,1},{3,2},{4,3},{5,4},{6,5},{7,6},{8,15},{9,8},{10,9... | collective-permute-start | bytes 786440 | tf_op jit(solution)/shard_map/ppermute | solution.py:288
  61.7 6.7 %collective-permute-start.23 = (bf16[4,128,256]{2,1,0:T(8,128)(2,1)S(1)}, bf16[4,128,256]{2,1,0:T(8,128)(2,1)S(1)}, u32[]{:S(2)}, u32[]{:S(2)}) collective-permute-start(bf16[4,128,256]{2,1,0:T(8,128)(2,1)S(1)} %bitcast.44), channel_id=1, source_target_pairs={{0,1},{1,2},{2,3},{3,4},{4,5},{5,6},{6,7},{7,0},{8,9},{9,10},{10,1... | collective-permute-start | bytes 786440 | tf_op jit(solution)/shard_map/ppermute | solution.py:288
  65.0 6.2 %collective-permute-start.17 = (bf16[4,128,256]{2,1,0:T(8,128)(2,1)S(1)}, bf16[4,128,256]{2,1,0:T(8,128)(2,1)S(1)}, u32[]{:S(2)}, u32[]{:S(2)}) collective-permute-start(bf16[4,128,256]{2,1,0:T(8,128)(2,1)S(1)} %bitcast.45), channel_id=1, source_target_pairs={{0,7},{1,0},{2,1},{3,2},{4,3},{5,4},{6,5},{7,6},{8,15},{9,8},{10,9... | collective-permute-start | bytes 786440 | tf_op jit(solution)/shard_map/ppermute | solution.py:288
  65.0 8.7 %collective-permute-start.28 = (bf16[4,128,256]{2,1,0:T(8,128)(2,1)S(1)}, bf16[4,128,256]{2,1,0:T(8,128)(2,1)S(1)}, u32[]{:S(2)}, u32[]{:S(2)}) collective-permute-start(bf16[4,128,256]{2,1,0:T(8,128)(2,1)S(1)} %bitcast.50), channel_id=1, source_target_pairs={{0,1},{1,2},{2,3},{3,4},{4,5},{5,6},{6,7},{7,0},{8,9},{9,10},{10,1... | collective-permute-start | bytes 786440 | tf_op jit(solution)/shard_map/ppermute | solution.py:288
  66.5 9.0 %collective-permute-start.18 = (bf16[4,128,256]{2,1,0:T(8,128)(2,1)S(1)}, bf16[4,128,256]{2,1,0:T(8,128)(2,1)S(1)}, u32[]{:S(2)}, u32[]{:S(2)}) collective-permute-start(bf16[4,128,256]{2,1,0:T(8,128)(2,1)S(1)} %bitcast.51), channel_id=1, source_target_pairs={{0,7},{1,0},{2,1},{3,2},{4,3},{5,4},{6,5},{7,6},{8,15},{9,8},{10,9... | collective-permute-start | bytes 786440 | tf_op jit(solution)/shard_map/ppermute | solution.py:288
  67.8 9.5 %collective-permute-start.10 = (bf16[4,128,256]{2,1,0:T(8,128)(2,1)S(1)}, bf16[4,128,256]{2,1,0:T(8,128)(2,1)}, u32[]{:S(2)}, u32[]{:S(2)}) collective-permute-start(bf16[4,128,256]{2,1,0:T(8,128)(2,1)S(1)} %collective-permute-done.9.refs_12_), channel_id=1, source_target_pairs={{0,1},{1,2},{2,3},{3,4},{4,5},{5,6},{6,7},{7,0},{8,9},{9,10},{10,1... | collective-permute-start | bytes 786440 | tf_op jit(solution)/shard_map/ppermute | solution.py:288
  68.4 10.6 %collective-permute-start.7 = (bf16[4,128,256]{2,1,0:T(8,128)(2,1)S(1)}, bf16[4,128,256]{2,1,0:T(8,128)(2,1)S(1)}, u32[]{:S(2)}, u32[]{:S(2)}) collective-permute-start(bf16[4,128,256]{2,1,0:T(8,128)(2,1)S(1)} %collective-permute-done.5.refs_4_), channel_id=1, source_target_pairs={{0,7},{1,0},{2,1},{3,2},{4,3},{5,4},{6,5},{7,6},{8,15},{9,8},{10,9... | collective-permute-start | bytes 786440 | tf_op jit(solution)/shard_map/ppermute | solution.py:288
  70.5 0.7 copy-start.10
  71.2 10.9 %collective-permute-start.14 = (bf16[4,128,256]{2,1,0:T(8,128)(2,1)S(1)}, bf16[4,128,256]{2,1,0:T(8,128)(2,1)}, u32[]{:S(2)}, u32[]{:S(2)}) collective-permute-start(bf16[4,128,256]{2,1,0:T(8,128)(2,1)S(1)} %collective-permute-done.13.refs_15_), channel_id=1, source_target_pairs={{0,1},{1,2},{2,3},{3,4},{4,5},{5,6},{6,7},{7,0},{8,9},{9,10},{10,1... | collective-permute-start | bytes 786440 | tf_op jit(solution)/shard_map/ppermute | solution.py:288
  71.3 0.7 copy-start.12
  73.7 10.2 %collective-permute-start.6 = (bf16[4,128,256]{2,1,0:T(8,128)(2,1)S(1)}, bf16[4,128,256]{2,1,0:T(8,128)(2,1)S(1)}, u32[]{:S(2)}, u32[]{:S(2)}) collective-permute-start(bf16[4,128,256]{2,1,0:T(8,128)(2,1)S(1)} %collective-permute-done.4.refs_3_), channel_id=1, source_target_pairs={{0,7},{1,0},{2,1},{3,2},{4,3},{5,4},{6,5},{7,6},{8,15},{9,8},{10,9... | collective-permute-start | bytes 786440 | tf_op jit(solution)/shard_map/ppermute | solution.py:288
  74.6 0.7 copy-start.14
  75.5 12.2 %collective-permute-start.24 = (bf16[4,128,256]{2,1,0:T(8,128)(2,1)S(1)}, bf16[4,128,256]{2,1,0:T(8,128)(2,1)S(1)}, u32[]{:S(2)}, u32[]{:S(2)}) collective-permute-start(bf16[4,128,256]{2,1,0:T(8,128)(2,1)S(1)} %collective-permute-done.23.refs_14_), channel_id=1, source_target_pairs={{0,1},{1,2},{2,3},{3,4},{4,5},{5,6},{6,7},{7,0},{8,9},{9,10},{10,1... | collective-permute-start | bytes 786440 | tf_op jit(solution)/shard_map/ppermute | solution.py:288
  77.2 12.6 %collective-permute-start.19 = (bf16[4,128,256]{2,1,0:T(8,128)(2,1)S(1)}, bf16[4,128,256]{2,1,0:T(8,128)(2,1)}, u32[]{:S(2)}, u32[]{:S(2)}) collective-permute-start(bf16[4,128,256]{2,1,0:T(8,128)(2,1)S(1)} %collective-permute-done.17.refs_2_), channel_id=1, source_target_pairs={{0,7},{1,0},{2,1},{3,2},{4,3},{5,4},{6,5},{7,6},{8,15},{9,8},{10,9... | collective-permute-start | bytes 786440 | tf_op jit(solution)/shard_map/ppermute | solution.py:288
  79.1 0.7 copy-start.16
  79.8 13.7 %collective-permute-start.29 = (bf16[4,128,256]{2,1,0:T(8,128)(2,1)S(1)}, bf16[4,128,256]{2,1,0:T(8,128)(2,1)}, u32[]{:S(2)}, u32[]{:S(2)}) collective-permute-start(bf16[4,128,256]{2,1,0:T(8,128)(2,1)S(1)} %collective-permute-done.28.refs_15_), channel_id=1, source_target_pairs={{0,1},{1,2},{2,3},{3,4},{4,5},{5,6},{6,7},{7,0},{8,9},{9,10},{10,1... | collective-permute-start | bytes 786440 | tf_op jit(solution)/shard_map/ppermute | solution.py:288
  82.1 13.5 %collective-permute-start.20 = (bf16[4,128,256]{2,1,0:T(8,128)(2,1)S(1)}, bf16[4,128,256]{2,1,0:T(8,128)(2,1)S(1)}, u32[]{:S(2)}, u32[]{:S(2)}) collective-permute-start(bf16[4,128,256]{2,1,0:T(8,128)(2,1)S(1)} %collective-permute-done.18.refs_3_), channel_id=1, source_target_pairs={{0,7},{1,0},{2,1},{3,2},{4,3},{5,4},{6,5},{7,6},{8,15},{9,8},{10,9... | collective-permute-start | bytes 786440 | tf_op jit(solution)/shard_map/ppermute | solution.py:288
  83.9 17.0 %collective-permute-start.8 = (bf16[4,128,256]{2,1,0:T(8,128)(2,1)S(1)}, bf16[4,128,256]{2,1,0:T(8,128)(2,1)}, u32[]{:S(2)}, u32[]{:S(2)}) collective-permute-start(bf16[4,128,256]{2,1,0:T(8,128)(2,1)S(1)} %collective-permute-done.6.refs_5_), channel_id=1, source_target_pairs={{0,7},{1,0},{2,1},{3,2},{4,3},{5,4},{6,5},{7,6},{8,15},{9,8},{10,9... | collective-permute-start | bytes 786440 | tf_op jit(solution)/shard_map/ppermute | solution.py:288
  84.6 0.7 copy-start.18
  87.7 41.1 %copy-start.6 = (bf16[4,128,256]{2,1,0:T(8,128)(2,1)}, bf16[4,128,256]{2,1,0:T(8,128)(2,1)S(1)}, u32[]{:S(2)}) copy-start(bf16[4,128,256]{2,1,0:T(8,128)(2,1)S(1)} %collective-permute-done.24.refs_12_) | copy-start | bytes 786436
  87.7 13.7 %collective-permute-start.11 = (bf16[4,128,256]{2,1,0:T(8,128)(2,1)}, bf16[4,128,256]{2,1,0:T(8,128)(2,1)}, u32[]{:S(2)}, u32[]{:S(2)}) collective-permute-start(bf16[4,128,256]{2,1,0:T(8,128)(2,1)} %collective-permute-done.10.refs_10_), channel_id=1, source_target_pairs={{0,1},{1,2},{2,3},{3,4},{4,5},{5,6},{6,7},{7,0},{8,9},{9,10},{10,1... | collective-permute-start | bytes 786440 | tf_op jit(solution)/shard_map/ppermute | solution.py:288
  89.8 14.8 %collective-permute-start.15 = (bf16[4,128,256]{2,1,0:T(8,128)(2,1)}, bf16[4,128,256]{2,1,0:T(8,128)(2,1)}, u32[]{:S(2)}, u32[]{:S(2)}) collective-permute-start(bf16[4,128,256]{2,1,0:T(8,128)(2,1)} %collective-permute-done.14.refs_13_), channel_id=1, source_target_pairs={{0,1},{1,2},{2,3},{3,4},{4,5},{5,6},{6,7},{7,0},{8,9},{9,10},{10,1... | collective-permute-start | bytes 786440 | tf_op jit(solution)/shard_map/ppermute | solution.py:288
  93.4 16.9 %collective-permute-start.25 = (bf16[4,128,256]{2,1,0:T(8,128)(2,1)S(1)}, bf16[4,128,256]{2,1,0:T(8,128)(2,1)}, u32[]{:S(2)}, u32[]{:S(2)}) collective-permute-start(bf16[4,128,256]{2,1,0:T(8,128)(2,1)S(1)} %collective-permute-done.24.refs_12_), channel_id=1, source_target_pairs={{0,1},{1,2},{2,3},{3,4},{4,5},{5,6},{6,7},{7,0},{8,9},{9,10},{10,1... | collective-permute-start | bytes 786440 | tf_op jit(solution)/shard_map/ppermute | solution.py:288
  95.6 33.3 %copy-start.8 = (bf16[4,128,256]{2,1,0:T(8,128)(2,1)}, bf16[4,128,256]{2,1,0:T(8,128)(2,1)S(1)}, u32[]{:S(2)}) copy-start(bf16[4,128,256]{2,1,0:T(8,128)(2,1)S(1)} %collective-permute-done.20.refs_5_) | copy-start | bytes 786436
  95.6 16.9 %collective-permute-start.22 = (bf16[4,128,256]{2,1,0:T(8,128)(2,1)S(1)}, bf16[4,128,256]{2,1,0:T(8,128)(2,1)}, u32[]{:S(2)}, u32[]{:S(2)}) collective-permute-start(bf16[4,128,256]{2,1,0:T(8,128)(2,1)S(1)} %collective-permute-done.20.refs_5_), channel_id=1, source_target_pairs={{0,7},{1,0},{2,1},{3,2},{4,3},{5,4},{6,5},{7,6},{8,15},{9,8},{10,9... | collective-permute-start | bytes 786440 | tf_op jit(solution)/shard_map/ppermute | solution.py:288
  100.9 12.1 %collective-permute-start.12 = (bf16[4,128,256]{2,1,0:T(8,128)(2,1)}, bf16[4,128,256]{2,1,0:T(8,128)(2,1)}, u32[]{:S(2)}, u32[]{:S(2)}) collective-permute-start(bf16[4,128,256]{2,1,0:T(8,128)(2,1)} %collective-permute-done.8.refs_7_), channel_id=1, source_target_pairs={{0,7},{1,0},{2,1},{3,2},{4,3},{5,4},{6,5},{7,6},{8,15},{9,8},{10,9... | collective-permute-start | bytes 786440 | tf_op jit(solution)/shard_map/ppermute | solution.py:288
  101.4 43.6 %collective-permute-start.21 = (bf16[4,128,256]{2,1,0:T(8,128)(2,1)}, bf16[4,128,256]{2,1,0:T(8,128)(2,1)}, u32[]{:S(2)}, u32[]{:S(2)}) collective-permute-start(bf16[4,128,256]{2,1,0:T(8,128)(2,1)} %collective-permute-done.19.refs_4_), channel_id=1, source_target_pairs={{0,7},{1,0},{2,1},{3,2},{4,3},{5,4},{6,5},{7,6},{8,15},{9,8},{10,9... | collective-permute-start | bytes 786440 | tf_op jit(solution)/shard_map/ppermute | solution.py:288
  104.6 40.4 %collective-permute-start.30 = (bf16[4,128,256]{2,1,0:T(8,128)(2,1)}, bf16[4,128,256]{2,1,0:T(8,128)(2,1)}, u32[]{:S(2)}, u32[]{:S(2)}) collective-permute-start(bf16[4,128,256]{2,1,0:T(8,128)(2,1)} %collective-permute-done.29.refs_13_), channel_id=1, source_target_pairs={{0,1},{1,2},{2,3},{3,4},{4,5},{5,6},{6,7},{7,0},{8,9},{9,10},{10,1... | collective-permute-start | bytes 786440 | tf_op jit(solution)/shard_map/ppermute | solution.py:288
  110.3 34.8 %collective-permute-start.26 = (bf16[4,128,256]{2,1,0:T(8,128)(2,1)}, bf16[4,128,256]{2,1,0:T(8,128)(2,1)}, u32[]{:S(2)}, u32[]{:S(2)}) collective-permute-start(bf16[4,128,256]{2,1,0:T(8,128)(2,1)} %collective-permute-done.25.refs_10_), channel_id=1, source_target_pairs={{0,1},{1,2},{2,3},{3,4},{4,5},{5,6},{6,7},{7,0},{8,9},{9,10},{10,1... | collective-permute-start | bytes 786440 | tf_op jit(solution)/shard_map/ppermute | solution.py:288
  112.4 32.6 %collective-permute-start.27 = (bf16[4,128,256]{2,1,0:T(8,128)(2,1)}, bf16[4,128,256]{2,1,0:T(8,128)(2,1)}, u32[]{:S(2)}, u32[]{:S(2)}) collective-permute-start(bf16[4,128,256]{2,1,0:T(8,128)(2,1)} %collective-permute-done.22.refs_7_), channel_id=1, source_target_pairs={{0,7},{1,0},{2,1},{3,2},{4,3},{5,4},{6,5},{7,6},{8,15},{9,8},{10,9... | collective-permute-start | bytes 786440 | tf_op jit(solution)/shard_map/ppermute | solution.py:288
  113.0 1.0 copy-start.11
  114.0 1.0 copy-start.13
  115.0 0.9 copy-start.15
  115.9 0.9 copy-start.17
  116.9 1.0 copy-start.19
  128.9 1.6 copy-start
  130.5 14.6 %copy-start.7 = (bf16[4,128,256]{2,1,0:T(8,128)(2,1)S(1)}, bf16[4,128,256]{2,1,0:T(8,128)(2,1)}, u32[]{:S(2)}) copy-start(bf16[4,128,256]{2,1,0:T(8,128)(2,1)} %copy-done.6) | copy-start | bytes 786436
  130.5 14.6 %copy-start.9 = (bf16[4,128,256]{2,1,0:T(8,128)(2,1)S(1)}, bf16[4,128,256]{2,1,0:T(8,128)(2,1)}, u32[]{:S(2)}) copy-start(bf16[4,128,256]{2,1,0:T(8,128)(2,1)} %copy-done.8) | copy-start | bytes 786436
  143.7 1.3 copy-start.1
  172.8 1.3 copy-start.2
  203.6 24.0 %all-to-all-start.2 = ((bf16[16,32,8,128]{3,2,1,0:T(8,128)(2,1)}), bf16[16,32,8,128]{3,2,1,0:T(8,128)(2,1)S(1)}, u32[]{:S(2)}, u32[]{:S(2)}) async-start(bf16[16,32,8,128]{3,2,1,0:T(8,128)(2,1)} %bitcast.19), calls=%async_computation.3 | async-start | bytes 2097152 | tf_op jit(solution)/shard_map/all_to_all | solution.py:320
  210.8 1.5 copy-start.3
  212.3 1.5 copy-start.4
  227.6 10.0 %all-to-all-start.4 = ((bf16[2,8,2,58,8,128]{5,4,3,2,1,0:T(8,128)(2,1)}), bf16[2,8,2,58,8,128]{5,4,3,2,1,0:T(8,128)(2,1)}, u32[]{:S(2)}, u32[]{:S(2)}) async-start(bf16[2,8,2,58,8,128]{5,4,3,2,1,0:T(8,128)(2,1)} %shard_map.148), calls=%async_computation.5 | async-start | bytes 7602176 | tf_op jit(solution)/shard_map/all_to_all | solution.py:317
  237.6 11.7 %all-to-all-start.3 = ((f32[8,32,128]{2,1,0:T(8,128)}), f32[8,32,128]{2,1,0:T(8,128)S(1)}, u32[]{:S(2)}, u32[]{:S(2)}) async-start(f32[8,32,128]{2,1,0:T(8,128)} %bitcast.20), calls=%async_computation.4 | async-start | bytes 262144 | tf_op jit(solution)/shard_map/all_to_all | solution.py:406
  249.3 30.0 %all-to-all-start.5 = ((bf16[16,58,8,128]{3,2,1,0:T(8,128)(2,1)}), bf16[16,58,8,128]{3,2,1,0:T(8,128)(2,1)S(1)}, u32[]{:S(2)}, u32[]{:S(2)}) async-start(bf16[16,58,8,128]{3,2,1,0:T(8,128)(2,1)} %bitcast.22), calls=%async_computation.6 | async-start | bytes 3801088 | tf_op jit(solution)/shard_map/all_to_all | solution.py:320
  280.6 14.2 %collective-permute-start.31 = (bf16[512,256]{1,0:T(8,128)(2,1)S(1)}, bf16[512,256]{1,0:T(8,128)(2,1)S(1)}, u32[]{:S(2)}, u32[]{:S(2)}) collective-permute-start(bf16[512,256]{1,0:T(8,128)(2,1)S(1)} %dynamic-slice_bitcast_fusion), channel_id=1, source_target_pairs={{0,8},{8,0},{1,9},{9,1},{2,10},{10,2},{3,11},{11,3},{4,12},{12,4},... | collective-permute-start | bytes 786440 | tf_op jit(solution)/shard_map/ppermute | solution.py:292
  284.6 9.5 %collective-permute-start.32 = (f32[16,8,128]{2,1,0:T(8,128)S(1)}, f32[16,8,128]{2,1,0:T(8,128)S(1)}, u32[]{:S(2)}, u32[]{:S(2)}) collective-permute-start(f32[16,8,128]{2,1,0:T(8,128)S(1)} %slice.42), channel_id=1, source_target_pairs={{0,0},{1,16},{2,32},{3,48},{4,64},{5,80},{6,96},{7,112},{16,128},{... | collective-permute-start | bytes 196616 | tf_op jit(solution)/shard_map/ppermute | solution.py:401
Sparse Core Ops, SparseCore 0:
  38.9 44.3 all-gather.5
  85.2 36.8 all-gather.3
  174.2 68.1 reduce-scatter.1

commit v2 on v1

--- a/solution.py
+++ b/solution.py
@@ -32,8 +32,7 @@
     side, own = c // HID, c % HID
     at = own // SLOTS
     slot = own - jnp.minimum(at * SLOTS, HID - SLOTS)
-    start = (side * SLOTS + slot) * 2
-    return held[kind * 5 + at, pl.ds(start, 2)].reshape(BLOCK, BLOCK)
+    return held[(kind * 5 + at) * 2 + side, slot]
 
 
 def dot(left, right):
@@ -177,45 +176,55 @@
             parts[(at // PER) * 8 + side * PER + at % PER] = value
 
 
-def put_rows(ref, side, at, value):
-    for group in range(16):
-        ref[group % 2, group // 2, side, at] = value[group * 8 : group * 8 + 8].astype(BF)
-
-
-def second_grads_kernel(dy, down_in, act, back_in, gate_in, up_in, gate_back, up_back, out):
-    @loop(MINE, 2)
-    def _(cs):
-        grads = [
-            (
-                dot_last(hidden(gate_in, c), gate_back[c]),
-                dot_last(hidden(up_in, c), up_back[c]),
-                dot_last(act[c], hidden(back_in, c)),
+def put(keep, send, core, index, even, odd):
+    keep[index] = jnp.where(core == 0, even, odd).astype(BF)
+    send[index] = jnp.where(core == 0, odd, even).astype(BF)
+
+
+def put_rows(keep, send, core, side, at, value):
+    for pair in range(8):
+        rows = value[pair * 16 : pair * 16 + 16]
+        put(keep, send, core, (pair, side, at), rows[:8], rows[8:])
+
+
+def second_grads_kernel(
+    where, dy, down_in, act, back_in, gate_in, up_in, gate_back, up_back, keep, send
+):
+    step, core = pl.program_id(0), where[2]
+
+    @pl.when(step < MINE // 2)
+    def _():
+        grads = []
+        for k in range(2):
+            rows = slice(k * SUB, k * SUB + SUB)
+            grads.append(
+                (
+                    dot_last(gate_in[rows].reshape(BLOCK, TOK), gate_back[k]),
+                    dot_last(up_in[rows].reshape(BLOCK, TOK), up_back[k]),
+                    dot_last(act[k], back_in[rows].reshape(BLOCK, TOK)),
+                )
             )
-            for c in cs
-        ]
-        for c, grad in zip(cs, grads):
-            for k in range(3):
-                put_rows(out, c // HID, k * HID + c % HID, grad[k])
+        for k in range(2):
+            c = step * 2 + k
+            for kind in range(3):
+                put_rows(keep, send, core, c // HID, kind * HID + c % HID, grads[k][kind])
 
     fill = jnp.zeros((4, BLOCK), F32)
-
-    @loop(NBD, 4)
-    def _(blocks):
-        grads = [dot_last(down_in[i], dy[i]) for i in blocks]
-        for i, grad in zip(blocks, grads):
-            side, z, p = i // 32, i % 32 // PER, i % PER
-            for half in range(2):
-                rows = jnp.concatenate([grad[half * 28 : half * 28 + 28], fill])
-                for k in range(4):
-                    out[half, z, side, 3 * HID + p * 4 + k] = rows[k * 8 : k * 8 + 8].astype(BF)
-
-
-def first_grads_kernel(x, low, out):
-    @loop(NBD, 4)
-    def _(blocks):
-        grads = [dot_last(x[i], low[i]) for i in blocks]
-        for i, grad in zip(blocks, grads):
-            put_rows(out, i // 32, i % 32, grad)
+    grads = [dot_last(down_in[k], dy[k]) for k in range(PER)]
+    side, z = step // 8, step % 8
+    for p, grad in enumerate(grads):
+        even, odd = [jnp.concatenate([grad[g * 28 : g * 28 + 28], fill]) for g in range(2)]
+        for k in range(4):
+            rows = slice(k * 8, k * 8 + 8)
+            put(keep, send, core, (z, side, 3 * HID + p * 4 + k), even[rows], odd[rows])
+
+
+def first_grads_kernel(where, x, low, keep, send):
+    step, core = pl.program_id(0), where[2]
+    grads = [dot_last(x[k], low[k]) for k in range(8)]
+    for k, grad in enumerate(grads):
+        i = step * 8 + k
+        put_rows(keep, send, core, i // 32, i % 32, grad)
 
 
 def call(kernel, outs, scratch, flops, *args):
@@ -266,12 +275,36 @@
     )
 
 
-def second_grads(*args):
-    return call(second_grads_kernel, [((2, 8, 2, 58, 8, 128), BF)], [], 4 * ONE, *args)[0]
-
-
-def first_grads(x, low):
-    return call(first_grads_kernel, [((2, 8, 2, 32, 8, 128), BF)], [], 2 * ONE, x, low)[0]
+def blocks_of(array, count, last=None):
+    def index(step):
+        return (step if last is None else jnp.minimum(step, last),) + (0,) * (array.ndim - 1)
+
+    return pl.BlockSpec((count,) + array.shape[1:], index)
+
+
+def grads_call(kernel, steps, specs, blocks, flops, where, *args):
+    shape = (8, 2, blocks, 8, BLOCK)
+    moved = sum(a.size * a.dtype.itemsize for a in args)
+    return pl.pallas_call(
+        kernel,
+        grid=(steps,),
+        out_shape=[jax.ShapeDtypeStruct(shape, BF)] * 2,
+        in_specs=[SM] + specs,
+        out_specs=[pl.BlockSpec(shape, lambda step: (0,) * 5)] * 2,
+        compiler_params=pltpu.CompilerParams(vmem_limit_bytes=32 << 20),
+        cost_estimate=pl.CostEstimate(flops=flops, bytes_accessed=moved, transcendentals=0),
+    )(where, *args)
+
+
+def second_grads(where, *args):
+    specs = [blocks_of(a, PER) for a in args[:2]]
+    last = MINE // 2 - 1
+    specs += [blocks_of(a, 4 if a.shape[0] == NBD else 2, last) for a in args[2:]]
+    return grads_call(second_grads_kernel, NBD // PER, specs, 3 * HID + 16, 4 * ONE, where, *args)
+
+
+def first_grads(where, x, low):
+    return grads_call(first_grads_kernel, 8, [blocks_of(x, 8), blocks_of(low, 8)], 32, 2 * ONE, where, x, low)
 
 
 GROUP = ("y", "x_lo", "core")
@@ -313,17 +346,22 @@
     return [shard for pair in found for shard in pair]
 
 
-def sum_groups(sent):
-    pairs = lax.all_to_all(sent, "core", 0, 0, tiled=True)
-    pairs = (pairs[0].astype(F32) + pairs[1].astype(F32)).astype(BF)
+def sum_groups(keep, send):
+    found = lax.ppermute(send, "core", [(0, 1), (1, 0)])
+    pairs = (keep.astype(F32) + found.astype(F32)).astype(BF)
     pairs = pairs.reshape((-1,) + pairs.shape[2:])
-    chips = lax.all_to_all(pairs, CHIPS, 0, 0, tiled=True)
+    return lax.all_to_all(pairs, CHIPS, 0, 0, tiled=True)
+
+
+def total_of(chips):
     return jnp.sum(chips.astype(F32), axis=0)
 
 
-def gather_first(gate_first, up_first, down_second):
+def gather_first(gate_first, up_first, down_second, after):
     nh, nz = size("x_hi"), size("z")
     y, kind = lax.axis_index("y"), lax.axis_index(("x_lo", "core"))
+    for value in after:
+        y = y + (value[0, 0, 0].astype(F32) * 0.0).astype(jnp.int32)
     each = gate_first.shape[2] // (nh * nz)
     take = functools.partial(lax.dynamic_index_in_dim, index=y, axis=0, keepdims=False)
     gate, up = take(gate_first).T, take(up_first).T
@@ -343,10 +381,9 @@
     second = jnp.where(
         kind == 0, take(gate_second), jnp.where(kind == 1, take(up_second), take(down_first))
     )
-    other = swap(second)
-    me = lax.axis_index("x_hi")
-    second = jnp.concatenate([jnp.where(me == 0, second, other), jnp.where(me == 0, other, second)])
-    return lax.all_gather(second.reshape(-1, ROWS, BLOCK), GROUP, axis=0, tiled=False)
+    group = GROUP + ("x_hi",)
+    sent = jnp.broadcast_to(second[None], (lax.axis_size(group),) + second.shape)
+    return lax.all_to_all(sent, group, 0, 0, tiled=True)
 
 
 def shards(
@@ -364,15 +401,14 @@
     each = hid * SUB
     rows = BLOCK // ngroup
 
-    where = jnp.stack([me, lax.axis_index("z")]).astype(jnp.int32)
+    where = jnp.stack([me, lax.axis_index("z"), lax.axis_index("core")]).astype(jnp.int32)
     table = swap_table()
     x_own, x_other = halves(activations, me)
+    dy_own, dy_other = halves(cotangent, me)
     held_second = gather_second(gate_second, up_second, down_first)
     xs = ring_gather(x_own, x_other)
-    dy_own, dy_other = halves(cotangent, me)
-    weights = (gate_first, up_first, down_second)
-    weights, _ = lax.optimization_barrier((weights, (xs[2], xs[14])))
-    held_first = gather_first(*weights)
+    after = [xs[3], xs[15], dy_other]
+    held_first = gather_first(gate_first, up_first, down_second, after)
     (dy_own, dy_other), _ = lax.optimization_barrier(((dy_own, dy_other), (xs[2], xs[14])))
     dys = ring_gather(dy_own, dy_other)
 
@@ -386,12 +422,16 @@
     total = total.reshape(nh, per * BLOCK, half)
     kept = lax.dynamic_index_in_dim(total, me, 0, keepdims=False)
     other = swap(lax.dynamic_index_in_dim(total, 1 - me, 0, keepdims=False))
+
+    firsts = sum_groups(*first_grads(where, x, low))
+    later = sum_groups(
+        *second_grads(where, dy, down_in, act, back_in, gate_in, up_in, gate_back, up_back)
+    )
+    later, other = lax.optimization_barrier((later, other))
     input_grad = jnp.concatenate(
         [jnp.where(me == 0, kept, other), jnp.where(me == 0, other, kept)], axis=1
     )
-
-    later = second_grads(dy, down_in, act, back_in, gate_in, up_in, gate_back, up_back)
-    later = sum_groups(later) * scale
+    later = total_of(later) * scale
     out_gs, out_us, out_df = later[: 3 * hid].reshape(3, hid, rows, BLOCK)
     pairs = []
     for part in range(ngroup):
@@ -401,7 +441,7 @@
     out_ds = lax.ppermute(later[3 * hid :], GROUP + ("z",), pairs)
     out_ds = out_ds.reshape(per, -1, BLOCK)[:, :each]
 
-    firsts = sum_groups(first_grads(x, low)) * scale
+    firsts = total_of(firsts) * scale
     firsts = firsts.reshape(nz, per * rows, 2 * ROWS)
     firsts = lax.all_to_all(firsts, "z", 0, 0, tiled=True)
     firsts = firsts.reshape(nz, per, rows, 2, ROWS)[..., : nh * each]

time: 306 us -> 310 us (1.013)
  local copies, waits for them, and re-layouts: 21.6 us -> 36.4 us
  Pallas kernels: 72.9 us -> 64.5 us
  other arithmetic: 11 us -> 7.71 us
    pallas_call x5 -> x3, Pallas kernels: 72.9 us -> 52.1 us  [call(): pl.pallas_call(kernel, out_shape=shapes, in_specs=[SM if a.dtype == jnp.i...]
    pallas_call x0 -> x2, Pallas kernels: none -> 12.4 us  [grads_call(): pl.pallas_call(kernel, grid=(steps,), out_shape=[jax.ShapeDtypeStruct(sha...]
    unnamed x44 -> x72, local copies, waits for them, and re-layouts: 16.2 us -> 25.3 us
    ppermute x28, waiting for transfers between devices: 31 us -> 39.9 us  [shift(): lax.ppermute(value, 'z', [(i, (i + step) % count) for i in range(count)])]
    all_to_all x3 -> x2, waiting for transfers between devices: 23.7 us -> 15.1 us  [the longest x1 15.1 us: sum_groups(): return lax.all_to_all(pairs, CHIPS, 0, 0, tiled=True)]
    all_to_all x3 -> x2, starting transfers between devices: 20.2 us -> 13.3 us  [the longest x1 8.93 us: gather_second(): return lax.all_to_all(sent, group, 0, 0, tiled=True)]
    ppermute x0 -> x2, starting transfers between devices: none -> 4.15 us  [sum_groups(): found = lax.ppermute(send, 'core', [(0, 1), (1, 0)])]
    ppermute x4 -> x3, starting transfers between devices: 7.91 us -> 6.63 us  [swap(): return lax.ppermute(value, 'x_hi', [(0, 1), (1, 0)])]
  transfers between devices with their start and end apart: 40 -> 39, of which waited for: 20 -> 19; matrix products, arithmetic and copies ran while one was open for 4% -> 5% of each run, Pallas kernels for 15% -> 12%
where the time goes in v2:
time: 310 us; the launch traced here: 305 us
  starting transfers between devices  71.8 us (23%)
  waiting for transfers between devices  71 us (23%)
  Pallas kernels  64.5 us (21%)
  blocking collectives  37.6 us (12%)
  local copies, waits for them, and re-layouts  36.4 us (12%)
  between operations  16.5 us (5%)
  other arithmetic  7.71 us (2%)
    pallas_call x3, Pallas kernels, call(): pl.pallas_call(kernel, out_shape=shapes, in_specs=[SM if a.dtype == jnp.i...  52.1 us
    ppermute x28, waiting for transfers between devices, shift(): lax.ppermute(value, 'z', [(i, (i + step) % count) for i in range(count)])  39.9 us
    ppermute x28, starting transfers between devices, shift(): lax.ppermute(value, 'z', [(i, (i + step) % count) for i in range(count)])  36.9 us
    unnamed x72, local copies, waits for them, and re-layouts  25.3 us
    all_to_all x1, blocking collectives, sum_groups(): return lax.all_to_all(pairs, CHIPS, 0, 0, tiled=True)  21.4 us
    all_to_all x1, blocking collectives, gather_first(): first = lax.all_to_all(first, TENSOR, 0, 0, tiled=True)  16.2 us
    all_to_all x1, waiting for transfers between devices, sum_groups(): return lax.all_to_all(pairs, CHIPS, 0, 0, tiled=True)  15.1 us
    pallas_call x2, Pallas kernels, grads_call(): pl.pallas_call(kernel, grid=(steps,), out_shape=[jax.ShapeDtypeStruct(sha...  12.4 us
  transfers between devices with their start and end apart: 39, of which 19 were waited for; matrix products, arithmetic and copies ran while one was open for 5% of the time, Pallas kernels for 12%

profile of v2, /device:TPU:1, one launch (start us, length us, event | category | flops | bytes accessed | tf_op | source)
XLA Modules:
  0.0 305.4 jit_solution(6382348444210678800)
XLA Ops:
  7.2 1.1 constant_dynamic-slice_fusion.1
  8.3 3.7 %collective-permute-start = (bf16[512,256]{1,0:T(8,128)(2,1)S(1)}, bf16[512,256]{1,0:T(8,128)(2,1)S(1)}, u32[]{:S(2)}, u32[]{:S(2)}) collective-permute-start(bf16[512,256]{1,0:T(8,128)(2,1)S(1)} %get-tuple-element.77), channel_id=1, source_target_pairs={{0,8},{8,0},{1,9},{9,1},{2,10},{10,2},{3,11},{11,3},{4,12},{12,4},... | collective-permute-start | bytes 786440 | tf_op jit(solution)/shard_map/ppermute | solution.py:325
  12.0 1.1 constant_dynamic-slice_fusion
  13.1 3.8 %collective-permute-done = bf16[512,256]{1,0:T(8,128)(2,1)S(1)} collective-permute-done((bf16[512,256]{1,0:T(8,128)(2,1)S(1)}, bf16[512,256]{1,0:T(8,128)(2,1)S(1)}, u32[]{:S(2)}, u32[]{:S(2)}) %collective-permute-start) | collective-permute-done | bytes 262176 | tf_op jit(solution)/shard_map/ppermute | solution.py:325
  16.9 6.5 %collective-permute-start.1 = (bf16[4,128,256]{2,1,0:T(8,128)(2,1)S(1)}, bf16[4,128,256]{2,1,0:T(8,128)(2,1)S(1)}, u32[]{:S(2)}, u32[]{:S(2)}) collective-permute-start(bf16[4,128,256]{2,1,0:T(8,128)(2,1)S(1)} %bitcast.57), channel_id=1, source_target_pairs={{0,7},{1,0},{2,1},{3,2},{4,3},{5,4},{6,5},{7,6},{8,15},{9,8},{10,9... | collective-permute-start | bytes 786440 | tf_op jit(solution)/shard_map/ppermute | solution.py:321
  24.6 2.1 collective-permute-done.1.refs_3_
  27.9 1.9 collective-permute-done.2.refs_15_
  31.1 1.0 fusion
  32.3 16.2 %all_to_all.25 = bf16[16,64,128]{2,1,0:T(8,128)(2,1)} all-to-all(bf16[16,64,128]{2,1,0:T(8,128)(2,1)S(1)} %bitcast.65), channel_id=1, replica_groups=mesh['y'=4,'x_lo'=2,'core'=2,'x_hi'=2,'z'=8] {'x_hi','z'}, dimensions={0} | all-to-all | bytes 524288 | tf_op jit(solution)/shard_map/all_to_all | solution.py:372
  48.6 1.0 select_select_fusion
  49.6 2.4 broadcast_in_dim.5
  52.0 8.9 %all-to-all-start.1 = ((bf16[32,3,128,128]{3,2,1,0:T(8,128)(2,1)}), bf16[32,3,128,128]{3,2,1,0:T(8,128)(2,1)}, u32[]{:S(2)}, u32[]{:S(2)}) async-start(bf16[32,3,128,128]{3,2,1,0:T(8,128)(2,1)} %broadcast_in_dim.5), calls=%async_computation.1 | async-start | bytes 6291456 | tf_op jit(solution)/shard_map/all_to_all | solution.py:386
  61.0 1.8 collective-permute-start.9
  62.8 1.0 collective-permute-start.4
  63.8 6.2 %collective-permute-done.9.refs_14_ = bf16[4,128,256]{2,1,0:T(8,128)(2,1)S(1)} collective-permute-done((bf16[4,128,256]{2,1,0:T(8,128)(2,1)S(1)}, bf16[4,128,256]{2,1,0:T(8,128)(2,1)S(1)}, u32[]{:S(2)}, u32[]{:S(2)}) %collective-permute-start.9) | collective-permute-done | bytes 262176 | tf_op jit(solution)/shard_map/ppermute | solution.py:321
  71.2 2.2 collective-permute-start.5
  74.1 2.7 collective-permute-start.17
  76.8 1.3 collective-permute-done.10.refs_12_
  78.3 3.0 collective-permute-start.6
  81.2 2.6 collective-permute-done.22.refs_14_
  84.5 4.6 %collective-permute-done.16.refs_2_ = bf16[4,128,256]{2,1,0:T(8,128)(2,1)S(1)} collective-permute-done((bf16[4,128,256]{2,1,0:T(8,128)(2,1)S(1)}, bf16[4,128,256]{2,1,0:T(8,128)(2,1)S(1)}, u32[]{:S(2)}, u32[]{:S(2)}) %collective-permute-start.16) | collective-permute-done | bytes 262176 | tf_op jit(solution)/shard_map/ppermute | solution.py:321
  89.1 3.4 %collective-permute-start.7 = (bf16[4,128,256]{2,1,0:T(8,128)(2,1)S(1)}, bf16[4,128,256]{2,1,0:T(8,128)(2,1)S(1)}, u32[]{:S(2)}, u32[]{:S(2)}) collective-permute-start(bf16[4,128,256]{2,1,0:T(8,128)(2,1)S(1)} %collective-permute-done.5.refs_4_), channel_id=1, source_target_pairs={{0,7},{1,0},{2,1},{3,2},{4,3},{5,4},{6,5},{7,6},{8,15},{9,8},{10,9... | collective-permute-start | bytes 786440 | tf_op jit(solution)/shard_map/ppermute | solution.py:321
  93.2 1.5 collective-permute-done.6.refs_5_
  94.7 3.4 %collective-permute-start.19 = (bf16[4,128,256]{2,1,0:T(8,128)(2,1)S(1)}, bf16[4,128,256]{2,1,0:T(8,128)(2,1)S(1)}, u32[]{:S(2)}, u32[]{:S(2)}) collective-permute-start(bf16[4,128,256]{2,1,0:T(8,128)(2,1)S(1)} %collective-permute-done.17.refs_3_), channel_id=1, source_target_pairs={{0,7},{1,0},{2,1},{3,2},{4,3},{5,4},{6,5},{7,6},{8,15},{9,8},{10,9... | collective-permute-start | bytes 786440 | tf_op jit(solution)/shard_map/ppermute | solution.py:321
  98.1 2.6 collective-permute-done.14.refs_13_
  101.4 3.0 collective-permute-start.8
  105.1 1.2 collective-permute-done.23.refs_12_
  106.4 5.1 %collective-permute-done.18.refs_4_ = bf16[4,128,256]{2,1,0:T(8,128)(2,1)} collective-permute-done((bf16[4,128,256]{2,1,0:T(8,128)(2,1)S(1)}, bf16[4,128,256]{2,1,0:T(8,128)(2,1)}, u32[]{:S(2)}, u32[]{:S(2)}) %collective-permute-start.18) | collective-permute-done | bytes 262176 | tf_op jit(solution)/shard_map/ppermute | solution.py:321
  111.9 3.0 collective-permute-start.21
  114.9 2.2 collective-permute-done.8.refs_7_
  117.2 3.4 %collective-permute-start.13 = (bf16[4,128,256]{2,1,0:T(8,128)(2,1)}, bf16[4,128,256]{2,1,0:T(8,128)(2,1)}, u32[]{:S(2)}, u32[]{:S(2)}) collective-permute-start(bf16[4,128,256]{2,1,0:T(8,128)(2,1)} %collective-permute-done.8.refs_7_), channel_id=1, source_target_pairs={{0,7},{1,0},{2,1},{3,2},{4,3},{5,4},{6,5},{7,6},{8,15},{9,8},{10,9... | collective-permute-start | bytes 786440 | tf_op jit(solution)/shard_map/ppermute | solution.py:321
  120.6 2.6 collective-permute-done.15.refs_11_
  123.1 5.6 %collective-permute-done.24.refs_10_ = bf16[4,128,256]{2,1,0:T(8,128)(2,1)} collective-permute-done((bf16[4,128,256]{2,1,0:T(8,128)(2,1)S(1)}, bf16[4,128,256]{2,1,0:T(8,128)(2,1)}, u32[]{:S(2)}, u32[]{:S(2)}) %collective-permute-start.24) | collective-permute-done | bytes 262176 | tf_op jit(solution)/shard_map/ppermute | solution.py:321
  128.8 2.7 collective-permute-start.26
  132.5 0.9 copy-done.25
  133.4 0.9 copy-done.27
  134.4 0.9 copy-done.29
  135.3 0.9 copy-done.31
  136.3 0.9 copy-done.33
  137.2 11.0 %shard_map.144 = (bf16[64,128,256]{2,1,0:T(8,128)(2,1)}, bf16[64,64,256]{2,1,0:T(8,128)(2,1)}, bf16[64,64,256]{2,1,0:T(8,128)(2,1)}) custom-call(s32[3]{0:T(128)S(1)} %pad_add_fusion.where, bf16[256,256]{1,0:T(8,128)(2,1)S(1)} %copy-done.13, bf16[16,16,64,128]{3,2,1,0:T(8,128)(2,1)} %bitcast.60, bf16[4,128,256]{2,1,0:T(8,128)(2,1)S(1)} %bitcast.52, ...), custom_call_target="tpu_custom_call" | custom-call | flops 1409286144 | bytes 8519692 | tf_op jit(solution)/shard_map/pallas_call | solution.py:233
  148.3 1.6 copy-done
  149.9 13.2 %shard_map.145 = (bf16[28,128,256]{2,1,0:T(8,128)(2,1)S(1)}, f32[28,128,256]{2,1,0:T(8,128)}, f32[28,128,256]{2,1,0:T(8,128)}, bf16[64,64,256]{2,1,0:T(8,128)(2,1)S(1)}) custom-call(bf16[256,256]{1,0:T(8,128)(2,1)S(1)} %copy-done.13, bf16[32,3,128,128]{3,2,1,0:T(8,128)(2,1)} %all-to-all-done.1.held.held_second, bf16[64,64,256]{2,1,0:T(8,128)(2,1)S(1)} %copy-done, ...), custom_call_target="tpu_custom_call" | custom-call | flops 1174405120 | bytes 7471104 | tf_op jit(solution)/shard_map/pallas_call | solution.py:233
  163.2 1.2 copy-done.8
  164.5 27.8 %shard_map.146 = (bf16[64,128,256]{2,1,0:T(8,128)(2,1)}, bf16[64,64,256]{2,1,0:T(8,128)(2,1)}, bf16[28,128,256]{2,1,0:T(8,128)(2,1)S(1)}, bf16[28,128,256]{2,1,0...) custom-call(s32[3]{0:T(128)S(1)} %pad_add_fusion.where, bf16[256,256]{1,0:T(8,128)(2,1)S(1)} %copy-done.13, ...), custom_call_target="tpu_custom_call" | custom-call | flops 2818572288 | bytes 19005452 | tf_op jit(solution)/shard_map/pallas_call | solution.py:233
  192.2 1.2 copy-done.10
  193.5 2.2 copy-done.3
  195.7 2.2 copy-done.4
  197.9 3.1 %shard_map.148 = (bf16[8,2,32,8,128]{4,3,2,1,0:T(8,128)(2,1)S(1)}, bf16[8,2,32,8,128]{4,3,2,1,0:T(8,128)(2,1)S(1)}) custom-call(s32[3]{0:T(128)S(1)} %pad_add_fusion.where, bf16[64,128,256]{2,1,0:T(8,128)(2,1)S(1)} %copy-done.3, bf16[64,128,256]{2,1,0:T(8,128)(2,1)S(1)} %copy-done.4), custom_call_target="tpu_custom_call" | custom-call | flops 469762048 | bytes 8388608 | tf_op jit(solution)/shard_map/pallas_call | solution.py:288
  201.0 4.0 %collective-permute-start.32 = (bf16[8,2,32,8,128]{4,3,2,1,0:T(8,128)(2,1)S(1)}, bf16[8,2,32,8,128]{4,3,2,1,0:T(8,128)(2,1)S(1)}, u32[]{:S(2)}, u32[]{:S(2)}) collective-permute-start(bf16[8,2,32,8,128]{4,3,2,1,0:T(8,128)(2,1)S(1)} %get-tuple-element.47), channel_id=1, source_target_pairs={{0,16},{16,0},{1,17},{17,1},{2,18},{18,2},{3,19},{19,3},{4,20},{20... | collective-permute-start | bytes 3145736 | tf_op jit(solution)/shard_map/ppermute | solution.py:350
  205.0 1.7 copy-done.6
  206.7 1.5 copy-done.9
  208.2 1.5 copy-done.11
  209.7 1.5 copy-done.12
  211.2 9.3 %shard_map.147 = (bf16[8,2,58,8,128]{4,3,2,1,0:T(8,128)(2,1)S(1)}, bf16[8,2,58,8,128]{4,3,2,1,0:T(8,128)(2,1)}) custom-call(s32[3]{0:T(128)S(1)} %pad_add_fusion.where, bf16[64,128,256]{2,1,0:T(8,128)(2,1)S(1)} %copy-done.5, bf16[64,64,256]{2,1,0:T(8,128)(2,1)S(1)} %get-tuple-element.36.down_in, bf16[28,128,256]{2,1,0:T(8,128)(2,1)S(1)} %copy-done.9, ...), custom_call_target="tpu_custom_call" | custom-call | flops 939524096 | bytes 18087936 | tf_op jit(solution)/shard_map/pallas_call | solution.py:288
  221.0 21.4 %all_to_all.26 = bf16[16,32,8,128]{3,2,1,0:T(8,128)(2,1)S(1)} all-to-all(bf16[16,32,8,128]{3,2,1,0:T(8,128)(2,1)S(1)} %bitcast.63), channel_id=1, replica_groups=mesh['y'=4,'x_lo'=2,'core'=2,'x_hi'=2,'z'=8] {'y','x_lo','x_hi'}, dimensions={0} | all-to-all | bytes 2097152 | tf_op jit(solution)/shard_map/all_to_all | solution.py:353
  243.2 3.6 %all-to-all-start.4 = ((f32[8,32,128]{2,1,0:T(8,128)}), f32[8,32,128]{2,1,0:T(8,128)S(1)}, u32[]{:S(2)}, u32[]{:S(2)}) async-start(f32[8,32,128]{2,1,0:T(8,128)} %bitcast.24), calls=%async_computation.5 | async-start | bytes 262144 | tf_op jit(solution)/shard_map/all_to_all | solution.py:446
  246.8 3.3 %add_convert_fusion = bf16[8,2,58,8,128]{4,3,2,1,0:T(8,128)(2,1)} fusion(bf16[8,2,58,8,128]{4,3,2,1,0:T(8,128)(2,1)S(1)} %collective-permute-done.30, bf16[8,2,58,8,128]{4,3,2,1,0:T(8,128)(2,1)} %copy-done.7), kind=kLoop, calls=%fused_computation.1 | loop fusion | flops 3801088 | bytes 5701632 | tf_op jit(solution)/shard_map/convert_element_type | solution.py:351
  250.1 4.7 %all-to-all-done.4 = f32[8,32,128]{2,1,0:T(8,128)S(1)} async-done(((f32[8,32,128]{2,1,0:T(8,128)}), f32[8,32,128]{2,1,0:T(8,128)S(1)}, u32[]{:S(2)}, u32[]{:S(2)}) %all-to-all-start.4) | async-done | bytes 131104 | tf_op jit(solution)/shard_map/all_to_all | solution.py:446
  254.8 4.4 %all-to-all-start.2 = ((bf16[16,58,8,128]{3,2,1,0:T(8,128)(2,1)}), bf16[16,58,8,128]{3,2,1,0:T(8,128)(2,1)S(1)}, u32[]{:S(2)}, u32[]{:S(2)}) async-start(bf16[16,58,8,128]{3,2,1,0:T(8,128)(2,1)} %bitcast.62), calls=%async_computation.3 | async-start | bytes 3801088 | tf_op jit(solution)/shard_map/all_to_all | solution.py:353
  259.2 1.7 dynamic-slice_bitcast_fusion
  260.9 2.9 collective-permute-start.31
  266.2 15.1 %all-to-all-done.2 = bf16[16,58,8,128]{3,2,1,0:T(8,128)(2,1)S(1)} async-done(((bf16[16,58,8,128]{3,2,1,0:T(8,128)(2,1)}), bf16[16,58,8,128]{3,2,1,0:T(8,128)(2,1)S(1)}, u32[]{:S(2)}, u32[]{:S(2)}) %all-to-all-start.2) | async-done | bytes 1900576 | tf_op jit(solution)/shard_map/all_to_all | solution.py:353
  281.3 7.1 %collective-permute-done.31 = bf16[512,256]{1,0:T(8,128)(2,1)S(1)} collective-permute-done((bf16[512,256]{1,0:T(8,128)(2,1)}, bf16[512,256]{1,0:T(8,128)(2,1)S(1)}, u32[]{:S(2)}, u32[]{:S(2)}) %collective-permute-start.31) | collective-permute-done | bytes 262176 | tf_op jit(solution)/shard_map/ppermute | solution.py:325
  289.4 7.2 %collective-permute-start.33 = (f32[16,8,128]{2,1,0:T(8,128)S(1)}, f32[16,8,128]{2,1,0:T(8,128)S(1)}, u32[]{:S(2)}, u32[]{:S(2)}) collective-permute-start(f32[16,8,128]{2,1,0:T(8,128)S(1)} %slice.37), channel_id=1, source_target_pairs={{0,0},{1,16},{2,32},{3,48},{4,64},{5,80},{6,96},{7,112},{16,128},{... | collective-permute-start | bytes 196616 | tf_op jit(solution)/shard_map/ppermute | solution.py:441
  (127 shorter events, 15.1 us)
Async XLA Ops:
  7.2 124.4 %all-gather.3.cloned.1.call-start = ((), (), s32[]{:S(2)}) async-start(), calls=%async_computation.7 | async-start | bytes 4456448 | tf_op jit(solution)/shard_map/all_gather | solution.py:373
  8.3 8.6 %collective-permute-start = (bf16[512,256]{1,0:T(8,128)(2,1)S(1)}, bf16[512,256]{1,0:T(8,128)(2,1)S(1)}, u32[]{:S(2)}, u32[]{:S(2)}) collective-permute-start(bf16[512,256]{1,0:T(8,128)(2,1)S(1)} %get-tuple-element.77), channel_id=1, source_target_pairs={{0,8},{8,0},{1,9},{9,1},{2,10},{10,2},{3,11},{11,3},{4,12},{12,4},... | collective-permute-start | bytes 786440 | tf_op jit(solution)/shard_map/ppermute | solution.py:325
  13.0 10.5 %collective-permute-start.3 = (bf16[512,256]{1,0:T(8,128)(2,1)S(1)}, bf16[512,256]{1,0:T(8,128)(2,1)S(1)}, u32[]{:S(2)}, u32[]{:S(2)}) collective-permute-start(bf16[512,256]{1,0:T(8,128)(2,1)S(1)} %get-tuple-element.75), channel_id=1, source_target_pairs={{0,8},{8,0},{1,9},{9,1},{2,10},{10,2},{3,11},{11,3},{4,12},{12,4},... | collective-permute-start | bytes 786440 | tf_op jit(solution)/shard_map/ppermute | solution.py:325
  16.9 9.9 %collective-permute-start.1 = (bf16[4,128,256]{2,1,0:T(8,128)(2,1)S(1)}, bf16[4,128,256]{2,1,0:T(8,128)(2,1)S(1)}, u32[]{:S(2)}, u32[]{:S(2)}) collective-permute-start(bf16[4,128,256]{2,1,0:T(8,128)(2,1)S(1)} %bitcast.57), channel_id=1, source_target_pairs={{0,7},{1,0},{2,1},{3,2},{4,3},{5,4},{6,5},{7,6},{8,15},{9,8},{10,9... | collective-permute-start | bytes 786440 | tf_op jit(solution)/shard_map/ppermute | solution.py:321
  23.5 6.4 %collective-permute-start.2 = (bf16[4,128,256]{2,1,0:T(8,128)(2,1)S(1)}, bf16[4,128,256]{2,1,0:T(8,128)(2,1)S(1)}, u32[]{:S(2)}, u32[]{:S(2)}) collective-permute-start(bf16[4,128,256]{2,1,0:T(8,128)(2,1)S(1)} %bitcast.58), channel_id=1, source_target_pairs={{0,1},{1,2},{2,3},{3,4},{4,5},{5,6},{6,7},{7,0},{8,9},{9,10},{10,1... | collective-permute-start | bytes 786440 | tf_op jit(solution)/shard_map/ppermute | solution.py:321
  52.0 79.5 %copy-start.13 = (bf16[256,256]{1,0:T(8,128)(2,1)S(1)}, bf16[256,256]{1,0:T(8,128)(2,1)}, u32[]{:S(2)}) copy-start(bf16[256,256]{1,0:T(8,128)(2,1)} %constant.86.clone.swap) | copy-start | bytes 393220
  52.0 96.3 %all-to-all-start.1 = ((bf16[32,3,128,128]{3,2,1,0:T(8,128)(2,1)}), bf16[32,3,128,128]{3,2,1,0:T(8,128)(2,1)}, u32[]{:S(2)}, u32[]{:S(2)}) async-start(bf16[32,3,128,128]{3,2,1,0:T(8,128)(2,1)} %broadcast_in_dim.5), calls=%async_computation.1 | async-start | bytes 6291456 | tf_op jit(solution)/shard_map/all_to_all | solution.py:386
  61.0 198.2 %reduce-scatter.2.cloned.1.call-start = ((), (), s32[]{:S(2)}) async-start(), calls=%async_computation.6 | async-start | bytes 4718592 | tf_op jit(solution)/shard_map/reduce_scatter | solution.py:421
  61.0 9.0 %collective-permute-start.9 = (bf16[4,128,256]{2,1,0:T(8,128)(2,1)S(1)}, bf16[4,128,256]{2,1,0:T(8,128)(2,1)S(1)}, u32[]{:S(2)}, u32[]{:S(2)}) collective-permute-start(bf16[4,128,256]{2,1,0:T(8,128)(2,1)S(1)} %bitcast.50), channel_id=1, source_target_pairs={{0,1},{1,2},{2,3},{3,4},{4,5},{5,6},{6,7},{7,0},{8,9},{9,10},{10,1... | collective-permute-start | bytes 786440 | tf_op jit(solution)/shard_map/ppermute | solution.py:321
  62.8 8.4 %collective-permute-start.4 = (bf16[4,128,256]{2,1,0:T(8,128)(2,1)S(1)}, bf16[4,128,256]{2,1,0:T(8,128)(2,1)S(1)}, u32[]{:S(2)}, u32[]{:S(2)}) collective-permute-start(bf16[4,128,256]{2,1,0:T(8,128)(2,1)S(1)} %bitcast.51), channel_id=1, source_target_pairs={{0,7},{1,0},{2,1},{3,2},{4,3},{5,4},{6,5},{7,6},{8,15},{9,8},{10,9... | collective-permute-start | bytes 786440 | tf_op jit(solution)/shard_map/ppermute | solution.py:321
  70.0 8.1 %collective-permute-start.10 = (bf16[4,128,256]{2,1,0:T(8,128)(2,1)S(1)}, bf16[4,128,256]{2,1,0:T(8,128)(2,1)S(1)}, u32[]{:S(2)}, u32[]{:S(2)}) collective-permute-start(bf16[4,128,256]{2,1,0:T(8,128)(2,1)S(1)} %collective-permute-done.9.refs_14_), channel_id=1, source_target_pairs={{0,1},{1,2},{2,3},{3,4},{4,5},{5,6},{6,7},{7,0},{8,9},{9,10},{10,1... | collective-permute-start | bytes 786440 | tf_op jit(solution)/shard_map/ppermute | solution.py:321
  71.2 7.0 %collective-permute-start.5 = (bf16[4,128,256]{2,1,0:T(8,128)(2,1)S(1)}, bf16[4,128,256]{2,1,0:T(8,128)(2,1)S(1)}, u32[]{:S(2)}, u32[]{:S(2)}) collective-permute-start(bf16[4,128,256]{2,1,0:T(8,128)(2,1)S(1)} %collective-permute-done.4.refs_2_), channel_id=1, source_target_pairs={{0,7},{1,0},{2,1},{3,2},{4,3},{5,4},{6,5},{7,6},{8,15},{9,8},{10,9... | collective-permute-start | bytes 786440 | tf_op jit(solution)/shard_map/ppermute | solution.py:321
  74.1 9.7 %collective-permute-start.22 = (bf16[4,128,256]{2,1,0:T(8,128)(2,1)S(1)}, bf16[4,128,256]{2,1,0:T(8,128)(2,1)S(1)}, u32[]{:S(2)}, u32[]{:S(2)}) collective-permute-start(bf16[4,128,256]{2,1,0:T(8,128)(2,1)S(1)} %bitcast.47), channel_id=1, source_target_pairs={{0,1},{1,2},{2,3},{3,4},{4,5},{5,6},{6,7},{7,0},{8,9},{9,10},{10,1... | collective-permute-start | bytes 786440 | tf_op jit(solution)/shard_map/ppermute | solution.py:321
  74.1 10.4 %collective-permute-start.17 = (bf16[4,128,256]{2,1,0:T(8,128)(2,1)S(1)}, bf16[4,128,256]{2,1,0:T(8,128)(2,1)S(1)}, u32[]{:S(2)}, u32[]{:S(2)}) collective-permute-start(bf16[4,128,256]{2,1,0:T(8,128)(2,1)S(1)} %bitcast.54), channel_id=1, source_target_pairs={{0,7},{1,0},{2,1},{3,2},{4,3},{5,4},{6,5},{7,6},{8,15},{9,8},{10,9... | collective-permute-start | bytes 786440 | tf_op jit(solution)/shard_map/ppermute | solution.py:321
  76.8 12.3 %collective-permute-start.16 = (bf16[4,128,256]{2,1,0:T(8,128)(2,1)S(1)}, bf16[4,128,256]{2,1,0:T(8,128)(2,1)S(1)}, u32[]{:S(2)}, u32[]{:S(2)}) collective-permute-start(bf16[4,128,256]{2,1,0:T(8,128)(2,1)S(1)} %bitcast.48), channel_id=1, source_target_pairs={{0,7},{1,0},{2,1},{3,2},{4,3},{5,4},{6,5},{7,6},{8,15},{9,8},{10,9... | collective-permute-start | bytes 786440 | tf_op jit(solution)/shard_map/ppermute | solution.py:321
  78.1 15.0 %collective-permute-start.27 = (bf16[4,128,256]{2,1,0:T(8,128)(2,1)S(1)}, bf16[4,128,256]{2,1,0:T(8,128)(2,1)S(1)}, u32[]{:S(2)}, u32[]{:S(2)}) collective-permute-start(bf16[4,128,256]{2,1,0:T(8,128)(2,1)S(1)} %bitcast.55), channel_id=1, source_target_pairs={{0,1},{1,2},{2,3},{3,4},{4,5},{5,6},{6,7},{7,0},{8,9},{9,10},{10,1... | collective-permute-start | bytes 786440 | tf_op jit(solution)/shard_map/ppermute | solution.py:321
  78.3 16.4 %collective-permute-start.6 = (bf16[4,128,256]{2,1,0:T(8,128)(2,1)S(1)}, bf16[4,128,256]{2,1,0:T(8,128)(2,1)S(1)}, u32[]{:S(2)}, u32[]{:S(2)}) collective-permute-start(bf16[4,128,256]{2,1,0:T(8,128)(2,1)S(1)} %collective-permute-done.1.refs_3_), channel_id=1, source_target_pairs={{0,7},{1,0},{2,1},{3,2},{4,3},{5,4},{6,5},{7,6},{8,15},{9,8},{10,9... | collective-permute-start | bytes 786440 | tf_op jit(solution)/shard_map/ppermute | solution.py:321
  83.8 14.3 %collective-permute-start.11 = (bf16[4,128,256]{2,1,0:T(8,128)(2,1)S(1)}, bf16[4,128,256]{2,1,0:T(8,128)(2,1)}, u32[]{:S(2)}, u32[]{:S(2)}) collective-permute-start(bf16[4,128,256]{2,1,0:T(8,128)(2,1)S(1)} %collective-permute-done.10.refs_12_), channel_id=1, source_target_pairs={{0,1},{1,2},{2,3},{3,4},{4,5},{5,6},{6,7},{7,0},{8,9},{9,10},{10,1... | collective-permute-start | bytes 786440 | tf_op jit(solution)/shard_map/ppermute | solution.py:321
  84.5 16.2 %collective-permute-start.14 = (bf16[4,128,256]{2,1,0:T(8,128)(2,1)S(1)}, bf16[4,128,256]{2,1,0:T(8,128)(2,1)}, u32[]{:S(2)}, u32[]{:S(2)}) collective-permute-start(bf16[4,128,256]{2,1,0:T(8,128)(2,1)S(1)} %collective-permute-done.2.refs_15_), channel_id=1, source_target_pairs={{0,1},{1,2},{2,3},{3,4},{4,5},{5,6},{6,7},{7,0},{8,9},{9,10},{10,1... | collective-permute-start | bytes 786440 | tf_op jit(solution)/shard_map/ppermute | solution.py:321
  89.1 59.2 %copy-start.14 = (bf16[4,128,256]{2,1,0:T(8,128)(2,1)}, bf16[4,128,256]{2,1,0:T(8,128)(2,1)S(1)}, u32[]{:S(2)}) copy-start(bf16[4,128,256]{2,1,0:T(8,128)(2,1)S(1)} %collective-permute-done.16.refs_2_) | copy-start | bytes 786436
  89.1 11.6 %collective-permute-start.7 = (bf16[4,128,256]{2,1,0:T(8,128)(2,1)S(1)}, bf16[4,128,256]{2,1,0:T(8,128)(2,1)S(1)}, u32[]{:S(2)}, u32[]{:S(2)}) collective-permute-start(bf16[4,128,256]{2,1,0:T(8,128)(2,1)S(1)} %collective-permute-done.5.refs_4_), channel_id=1, source_target_pairs={{0,7},{1,0},{2,1},{3,2},{4,3},{5,4},{6,5},{7,6},{8,15},{9,8},{10,9... | collective-permute-start | bytes 786440 | tf_op jit(solution)/shard_map/ppermute | solution.py:321
  93.2 55.1 %copy-start.16 = (bf16[4,128,256]{2,1,0:T(8,128)(2,1)}, bf16[4,128,256]{2,1,0:T(8,128)(2,1)S(1)}, u32[]{:S(2)}) copy-start(bf16[4,128,256]{2,1,0:T(8,128)(2,1)S(1)} %collective-permute-done.27.refs_15_) | copy-start | bytes 786436
  93.2 13.1 %collective-permute-start.23 = (bf16[4,128,256]{2,1,0:T(8,128)(2,1)S(1)}, bf16[4,128,256]{2,1,0:T(8,128)(2,1)S(1)}, u32[]{:S(2)}, u32[]{:S(2)}) collective-permute-start(bf16[4,128,256]{2,1,0:T(8,128)(2,1)S(1)} %collective-permute-done.22.refs_14_), channel_id=1, source_target_pairs={{0,1},{1,2},{2,3},{3,4},{4,5},{5,6},{6,7},{7,0},{8,9},{9,10},{10,1... | collective-permute-start | bytes 786440 | tf_op jit(solution)/shard_map/ppermute | solution.py:321
  94.7 11.6 %collective-permute-start.19 = (bf16[4,128,256]{2,1,0:T(8,128)(2,1)S(1)}, bf16[4,128,256]{2,1,0:T(8,128)(2,1)S(1)}, u32[]{:S(2)}, u32[]{:S(2)}) collective-permute-start(bf16[4,128,256]{2,1,0:T(8,128)(2,1)S(1)} %collective-permute-done.17.refs_3_), channel_id=1, source_target_pairs={{0,7},{1,0},{2,1},{3,2},{4,3},{5,4},{6,5},{7,6},{8,15},{9,8},{10,9... | collective-permute-start | bytes 786440 | tf_op jit(solution)/shard_map/ppermute | solution.py:321
  98.1 13.5 %collective-permute-start.18 = (bf16[4,128,256]{2,1,0:T(8,128)(2,1)S(1)}, bf16[4,128,256]{2,1,0:T(8,128)(2,1)}, u32[]{:S(2)}, u32[]{:S(2)}) collective-permute-start(bf16[4,128,256]{2,1,0:T(8,128)(2,1)S(1)} %collective-permute-done.16.refs_2_), channel_id=1, source_target_pairs={{0,7},{1,0},{2,1},{3,2},{4,3},{5,4},{6,5},{7,6},{8,15},{9,8},{10,9... | collective-permute-start | bytes 786440 | tf_op jit(solution)/shard_map/ppermute | solution.py:321
  100.7 11.2 %collective-permute-start.28 = (bf16[4,128,256]{2,1,0:T(8,128)(2,1)S(1)}, bf16[4,128,256]{2,1,0:T(8,128)(2,1)}, u32[]{:S(2)}, u32[]{:S(2)}) collective-permute-start(bf16[4,128,256]{2,1,0:T(8,128)(2,1)S(1)} %collective-permute-done.27.refs_15_), channel_id=1, source_target_pairs={{0,1},{1,2},{2,3},{3,4},{4,5},{5,6},{6,7},{7,0},{8,9},{9,10},{10,1... | collective-permute-start | bytes 786440 | tf_op jit(solution)/shard_map/ppermute | solution.py:321
  101.4 15.8 %collective-permute-start.8 = (bf16[4,128,256]{2,1,0:T(8,128)(2,1)S(1)}, bf16[4,128,256]{2,1,0:T(8,128)(2,1)}, u32[]{:S(2)}, u32[]{:S(2)}) collective-permute-start(bf16[4,128,256]{2,1,0:T(8,128)(2,1)S(1)} %collective-permute-done.6.refs_5_), channel_id=1, source_target_pairs={{0,7},{1,0},{2,1},{3,2},{4,3},{5,4},{6,5},{7,6},{8,15},{9,8},{10,9... | collective-permute-start | bytes 786440 | tf_op jit(solution)/shard_map/ppermute | solution.py:321
  106.3 42.0 %copy-start.18 = (bf16[4,128,256]{2,1,0:T(8,128)(2,1)}, bf16[4,128,256]{2,1,0:T(8,128)(2,1)S(1)}, u32[]{:S(2)}) copy-start(bf16[4,128,256]{2,1,0:T(8,128)(2,1)S(1)} %collective-permute-done.23.refs_12_) | copy-start | bytes 786436
  106.3 14.3 %collective-permute-start.12 = (bf16[4,128,256]{2,1,0:T(8,128)(2,1)}, bf16[4,128,256]{2,1,0:T(8,128)(2,1)}, u32[]{:S(2)}, u32[]{:S(2)}) collective-permute-start(bf16[4,128,256]{2,1,0:T(8,128)(2,1)} %collective-permute-done.11.refs_10_), channel_id=1, source_target_pairs={{0,1},{1,2},{2,3},{3,4},{4,5},{5,6},{6,7},{7,0},{8,9},{9,10},{10,1... | collective-permute-start | bytes 786440 | tf_op jit(solution)/shard_map/ppermute | solution.py:321
  106.3 42.0 %copy-start.20 = (bf16[4,128,256]{2,1,0:T(8,128)(2,1)}, bf16[4,128,256]{2,1,0:T(8,128)(2,1)S(1)}, u32[]{:S(2)}) copy-start(bf16[4,128,256]{2,1,0:T(8,128)(2,1)S(1)} %collective-permute-done.19.refs_5_) | copy-start | bytes 786436
  106.3 16.8 %collective-permute-start.15 = (bf16[4,128,256]{2,1,0:T(8,128)(2,1)}, bf16[4,128,256]{2,1,0:T(8,128)(2,1)}, u32[]{:S(2)}, u32[]{:S(2)}) collective-permute-start(bf16[4,128,256]{2,1,0:T(8,128)(2,1)} %collective-permute-done.14.refs_13_), channel_id=1, source_target_pairs={{0,1},{1,2},{2,3},{3,4},{4,5},{5,6},{6,7},{7,0},{8,9},{9,10},{10,1... | collective-permute-start | bytes 786440 | tf_op jit(solution)/shard_map/ppermute | solution.py:321
  111.6 17.2 %collective-permute-start.24 = (bf16[4,128,256]{2,1,0:T(8,128)(2,1)S(1)}, bf16[4,128,256]{2,1,0:T(8,128)(2,1)}, u32[]{:S(2)}, u32[]{:S(2)}) collective-permute-start(bf16[4,128,256]{2,1,0:T(8,128)(2,1)S(1)} %collective-permute-done.23.refs_12_), channel_id=1, source_target_pairs={{0,1},{1,2},{2,3},{3,4},{4,5},{5,6},{6,7},{7,0},{8,9},{9,10},{10,1... | collective-permute-start | bytes 786440 | tf_op jit(solution)/shard_map/ppermute | solution.py:321
  111.9 16.9 %collective-permute-start.21 = (bf16[4,128,256]{2,1,0:T(8,128)(2,1)S(1)}, bf16[4,128,256]{2,1,0:T(8,128)(2,1)}, u32[]{:S(2)}, u32[]{:S(2)}) collective-permute-start(bf16[4,128,256]{2,1,0:T(8,128)(2,1)S(1)} %collective-permute-done.19.refs_5_), channel_id=1, source_target_pairs={{0,7},{1,0},{2,1},{3,2},{4,3},{5,4},{6,5},{7,6},{8,15},{9,8},{10,9... | collective-permute-start | bytes 786440 | tf_op jit(solution)/shard_map/ppermute | solution.py:321
  117.2 14.4 %collective-permute-start.13 = (bf16[4,128,256]{2,1,0:T(8,128)(2,1)}, bf16[4,128,256]{2,1,0:T(8,128)(2,1)}, u32[]{:S(2)}, u32[]{:S(2)}) collective-permute-start(bf16[4,128,256]{2,1,0:T(8,128)(2,1)} %collective-permute-done.8.refs_7_), channel_id=1, source_target_pairs={{0,7},{1,0},{2,1},{3,2},{4,3},{5,4},{6,5},{7,6},{8,15},{9,8},{10,9... | collective-permute-start | bytes 786440 | tf_op jit(solution)/shard_map/ppermute | solution.py:321
  120.6 43.8 %collective-permute-start.20 = (bf16[4,128,256]{2,1,0:T(8,128)(2,1)}, bf16[4,128,256]{2,1,0:T(8,128)(2,1)}, u32[]{:S(2)}, u32[]{:S(2)}) collective-permute-start(bf16[4,128,256]{2,1,0:T(8,128)(2,1)} %collective-permute-done.18.refs_4_), channel_id=1, source_target_pairs={{0,7},{1,0},{2,1},{3,2},{4,3},{5,4},{6,5},{7,6},{8,15},{9,8},{10,9... | collective-permute-start | bytes 786440 | tf_op jit(solution)/shard_map/ppermute | solution.py:321
  123.1 41.2 %collective-permute-start.29 = (bf16[4,128,256]{2,1,0:T(8,128)(2,1)}, bf16[4,128,256]{2,1,0:T(8,128)(2,1)}, u32[]{:S(2)}, u32[]{:S(2)}) collective-permute-start(bf16[4,128,256]{2,1,0:T(8,128)(2,1)} %collective-permute-done.28.refs_13_), channel_id=1, source_target_pairs={{0,1},{1,2},{2,3},{3,4},{4,5},{5,6},{6,7},{7,0},{8,9},{9,10},{10,1... | collective-permute-start | bytes 786440 | tf_op jit(solution)/shard_map/ppermute | solution.py:321
  128.8 35.6 %collective-permute-start.25 = (bf16[4,128,256]{2,1,0:T(8,128)(2,1)}, bf16[4,128,256]{2,1,0:T(8,128)(2,1)}, u32[]{:S(2)}, u32[]{:S(2)}) collective-permute-start(bf16[4,128,256]{2,1,0:T(8,128)(2,1)} %collective-permute-done.24.refs_10_), channel_id=1, source_target_pairs={{0,1},{1,2},{2,3},{3,4},{4,5},{5,6},{6,7},{7,0},{8,9},{9,10},{10,1... | collective-permute-start | bytes 786440 | tf_op jit(solution)/shard_map/ppermute | solution.py:321
  128.8 35.6 %collective-permute-start.26 = (bf16[4,128,256]{2,1,0:T(8,128)(2,1)}, bf16[4,128,256]{2,1,0:T(8,128)(2,1)}, u32[]{:S(2)}, u32[]{:S(2)}) collective-permute-start(bf16[4,128,256]{2,1,0:T(8,128)(2,1)} %collective-permute-done.21.refs_7_), channel_id=1, source_target_pairs={{0,7},{1,0},{2,1},{3,2},{4,3},{5,4},{6,5},{7,6},{8,15},{9,8},{10,9... | collective-permute-start | bytes 786440 | tf_op jit(solution)/shard_map/ppermute | solution.py:321
  131.5 1.0 copy-start.23
  132.5 0.9 copy-start.25
  148.3 1.6 copy-start
  149.9 14.5 %copy-start.15 = (bf16[4,128,256]{2,1,0:T(8,128)(2,1)S(1)}, bf16[4,128,256]{2,1,0:T(8,128)(2,1)}, u32[]{:S(2)}) copy-start(bf16[4,128,256]{2,1,0:T(8,128)(2,1)} %copy-done.14) | copy-start | bytes 786436
  149.9 14.5 %copy-start.17 = (bf16[4,128,256]{2,1,0:T(8,128)(2,1)S(1)}, bf16[4,128,256]{2,1,0:T(8,128)(2,1)}, u32[]{:S(2)}) copy-start(bf16[4,128,256]{2,1,0:T(8,128)(2,1)} %copy-done.16) | copy-start | bytes 786436
  149.9 14.5 %copy-start.19 = (bf16[4,128,256]{2,1,0:T(8,128)(2,1)S(1)}, bf16[4,128,256]{2,1,0:T(8,128)(2,1)}, u32[]{:S(2)}) copy-start(bf16[4,128,256]{2,1,0:T(8,128)(2,1)} %copy-done.18) | copy-start | bytes 786436
  149.9 14.5 %copy-start.21 = (bf16[4,128,256]{2,1,0:T(8,128)(2,1)S(1)}, bf16[4,128,256]{2,1,0:T(8,128)(2,1)}, u32[]{:S(2)}) copy-start(bf16[4,128,256]{2,1,0:T(8,128)(2,1)} %copy-done.20) | copy-start | bytes 786436
  163.1 1.2 copy-start.8
  192.2 1.2 copy-start.10
  193.5 2.2 copy-start.3
  195.7 2.2 copy-start.4
  197.9 7.1 %copy-start.1 = (bf16[64,64,256]{2,1,0:T(8,128)(2,1)S(1)}, bf16[64,64,256]{2,1,0:T(8,128)(2,1)}, u32[]{:S(2)}) copy-start(bf16[64,64,256]{2,1,0:T(8,128)(2,1)} %get-tuple-element.28.gate_in) | copy-start | bytes 6291460
  197.9 7.1 %copy-start.2 = (bf16[64,64,256]{2,1,0:T(8,128)(2,1)S(1)}, bf16[64,64,256]{2,1,0:T(8,128)(2,1)}, u32[]{:S(2)}) copy-start(bf16[64,64,256]{2,1,0:T(8,128)(2,1)} %get-tuple-element.29.up_in) | copy-start | bytes 6291460
  197.9 7.1 %copy-start.5 = (bf16[64,128,256]{2,1,0:T(8,128)(2,1)S(1)}, bf16[64,128,256]{2,1,0:T(8,128)(2,1)}, u32[]{:S(2)}) copy-start(bf16[64,128,256]{2,1,0:T(8,128)(2,1)} %get-tuple-element.35.dy) | copy-start | bytes 12582916
  201.0 19.7 %collective-permute-start.32 = (bf16[8,2,32,8,128]{4,3,2,1,0:T(8,128)(2,1)S(1)}, bf16[8,2,32,8,128]{4,3,2,1,0:T(8,128)(2,1)S(1)}, u32[]{:S(2)}, u32[]{:S(2)}) collective-permute-start(bf16[8,2,32,8,128]{4,3,2,1,0:T(8,128)(2,1)S(1)} %get-tuple-element.47), channel_id=1, source_target_pairs={{0,16},{16,0},{1,17},{17,1},{2,18},{18,2},{3,19},{19,3},{4,20},{20... | collective-permute-start | bytes 3145736 | tf_op jit(solution)/shard_map/ppermute | solution.py:350
  205.0 1.8 copy-start.6
  206.7 1.5 copy-start.9
  208.2 1.5 copy-start.11
  209.7 1.5 copy-start.12
  220.5 21.9 %copy-start.7 = (bf16[8,2,58,8,128]{4,3,2,1,0:T(8,128)(2,1)}, bf16[8,2,58,8,128]{4,3,2,1,0:T(8,128)(2,1)S(1)}, u32[]{:S(2)}) copy-start(bf16[8,2,58,8,128]{4,3,2,1,0:T(8,128)(2,1)S(1)} %get-tuple-element.41) | copy-start | bytes 5701636
  220.5 26.2 %collective-permute-start.30 = (bf16[8,2,58,8,128]{4,3,2,1,0:T(8,128)(2,1)}, bf16[8,2,58,8,128]{4,3,2,1,0:T(8,128)(2,1)S(1)}, u32[]{:S(2)}, u32[]{:S(2)}) collective-permute-start(bf16[8,2,58,8,128]{4,3,2,1,0:T(8,128)(2,1)} %get-tuple-element.42), channel_id=1, source_target_pairs={{0,16},{16,0},{1,17},{17,1},{2,18},{18,2},{3,19},{19,3},{4,20},{20... | collective-permute-start | bytes 5701640 | tf_op jit(solution)/shard_map/ppermute | solution.py:350
  243.2 11.6 %all-to-all-start.4 = ((f32[8,32,128]{2,1,0:T(8,128)}), f32[8,32,128]{2,1,0:T(8,128)S(1)}, u32[]{:S(2)}, u32[]{:S(2)}) async-start(f32[8,32,128]{2,1,0:T(8,128)} %bitcast.24), calls=%async_computation.5 | async-start | bytes 262144 | tf_op jit(solution)/shard_map/all_to_all | solution.py:446
  254.8 26.5 %all-to-all-start.2 = ((bf16[16,58,8,128]{3,2,1,0:T(8,128)(2,1)}), bf16[16,58,8,128]{3,2,1,0:T(8,128)(2,1)S(1)}, u32[]{:S(2)}, u32[]{:S(2)}) async-start(bf16[16,58,8,128]{3,2,1,0:T(8,128)(2,1)} %bitcast.62), calls=%async_computation.3 | async-start | bytes 3801088 | tf_op jit(solution)/shard_map/all_to_all | solution.py:353
  260.9 27.5 %collective-permute-start.31 = (bf16[512,256]{1,0:T(8,128)(2,1)}, bf16[512,256]{1,0:T(8,128)(2,1)S(1)}, u32[]{:S(2)}, u32[]{:S(2)}) collective-permute-start(bf16[512,256]{1,0:T(8,128)(2,1)} %dynamic-slice_bitcast_fusion), channel_id=1, source_target_pairs={{0,8},{8,0},{1,9},{9,1},{2,10},{10,2},{3,11},{11,3},{4,12},{12,4},... | collective-permute-start | bytes 786440 | tf_op jit(solution)/shard_map/ppermute | solution.py:325
  264.5 32.1 %copy-start.34 = (bf16[8,128,256]{2,1,0:T(8,128)(2,1)S(1)}, bf16[8,128,256]{2,1,0:T(8,128)(2,1)}, u32[]{:S(2)}) copy-start(bf16[8,128,256]{2,1,0:T(8,128)(2,1)} %reduce-scatter.2.cloned.1.call-done) | copy-start | bytes 1572868
  289.4 8.5 %collective-permute-start.33 = (f32[16,8,128]{2,1,0:T(8,128)S(1)}, f32[16,8,128]{2,1,0:T(8,128)S(1)}, u32[]{:S(2)}, u32[]{:S(2)}) collective-permute-start(f32[16,8,128]{2,1,0:T(8,128)S(1)} %slice.37), channel_id=1, source_target_pairs={{0,0},{1,16},{2,32},{3,48},{4,64},{5,80},{6,96},{7,112},{16,128},{... | collective-permute-start | bytes 196616 | tf_op jit(solution)/shard_map/ppermute | solution.py:441
  (10 other events, 8.0 us)
Sparse Core Ops, SparseCore 0:
  48.7 73.1 all-gather.2
  193.6 56.4 reduce-scatter.1

commit v3 on v2

--- a/solution.py
+++ b/solution.py
@@ -32,7 +32,8 @@
     side, own = c // HID, c % HID
     at = own // SLOTS
     slot = own - jnp.minimum(at * SLOTS, HID - SLOTS)
-    return held[(kind * 5 + at) * 2 + side, slot]
+    start = 16 + (side * SLOTS + slot) * 2
+    return held[kind * 5 + at, pl.ds(start, 2)].reshape(BLOCK, BLOCK)
 
 
 def dot(left, right):
@@ -131,7 +132,7 @@
     turn_back(swap, down_mid, down_in, 0)
 
 
-def backward_kernel(where, swap, held_first, held_second, to_gate, to_up, *refs):
+def backward_kernel(where, swap, held, to_gate, to_up, *refs):
     shards = refs[:16]
     dy, back_in, gate_back, up_back, low, parts, mid, low_g, low_u = refs[16:]
     collect(where, shards, dy)
@@ -141,7 +142,7 @@
     def group(at, carry):
         @loop(16, 4)
         def _(ks):
-            mids = [dot(first_weight(held_first, 2, at * 16 + k), dy[at * 16 + k]).astype(BF) for k in ks]
+            mids = [dot(first_weight(held, 2, at * 16 + k), dy[at * 16 + k]).astype(BF) for k in ks]
             for value, k in zip(mids, ks):
                 mid[k] = value
 
@@ -152,11 +153,11 @@
 
     @loop(MINE, 2)
     def _(cs):
-        grads = [dot(second_weight(held_second, 2, c), hidden(back_in, c)) for c in cs]
+        grads = [dot(second_weight(held, 2, c), hidden(back_in, c)) for c in cs]
         to_gates = [(grad * to_gate[c]).astype(BF) for c, grad in zip(cs, grads)]
         to_ups = [(grad * to_up[c]).astype(BF) for c, grad in zip(cs, grads)]
-        lows_g = [dot(second_weight(held_second, 0, c), v) for c, v in zip(cs, to_gates)]
-        lows_u = [dot(second_weight(held_second, 1, c), v) for c, v in zip(cs, to_ups)]
+        lows_g = [dot(second_weight(held, 0, c), v) for c, v in zip(cs, to_gates)]
+        lows_u = [dot(second_weight(held, 1, c), v) for c, v in zip(cs, to_ups)]
         for c, g, u, lg, lu in zip(cs, to_gates, to_ups, lows_g, lows_u):
             gate_back[c], up_back[c] = g, u
             low_g[pl.ds(c * SUB, SUB)] = lg.astype(BF).reshape(SUB, NBD, TOK)
@@ -168,7 +169,7 @@
     @loop(NBD, 4)
     def _(blocks):
         weights = [
-            jnp.concatenate([first_weight(held_first, 0, i), first_weight(held_first, 1, i)]) for i in blocks
+            jnp.concatenate([first_weight(held, 0, i), first_weight(held, 1, i)]) for i in blocks
         ]
         values = [dot_first(w, low[i]).astype(BF) for w, i in zip(weights, blocks)]
         for i, value in zip(blocks, values):
@@ -187,8 +188,8 @@
         put(keep, send, core, (pair, side, at), rows[:8], rows[8:])
 
 
-def second_grads_kernel(
-    where, dy, down_in, act, back_in, gate_in, up_in, gate_back, up_back, keep, send
+def grads_kernel(
+    where, x, low, dy, down_in, act, back_in, gate_in, up_in, gate_back, up_back, keep, send
 ):
     step, core = pl.program_id(0), where[2]
 
@@ -211,20 +212,15 @@
 
     fill = jnp.zeros((4, BLOCK), F32)
     grads = [dot_last(down_in[k], dy[k]) for k in range(PER)]
+    firsts = [dot_last(x[k], low[k]) for k in range(PER)]
     side, z = step // 8, step % 8
     for p, grad in enumerate(grads):
         even, odd = [jnp.concatenate([grad[g * 28 : g * 28 + 28], fill]) for g in range(2)]
         for k in range(4):
             rows = slice(k * 8, k * 8 + 8)
             put(keep, send, core, (z, side, 3 * HID + p * 4 + k), even[rows], odd[rows])
-
-
-def first_grads_kernel(where, x, low, keep, send):
-    step, core = pl.program_id(0), where[2]
-    grads = [dot_last(x[k], low[k]) for k in range(8)]
-    for k, grad in enumerate(grads):
-        i = step * 8 + k
-        put_rows(keep, send, core, i // 32, i % 32, grad)
+    for p, grad in enumerate(firsts):
+        put_rows(keep, send, core, side, 3 * HID + 16 + z * PER + p, grad)
 
 
 def call(kernel, outs, scratch, flops, *args):
@@ -265,13 +261,13 @@
     return call(forward_second_kernel, outs, [SPREAD], 5 * ONE, swap, held, gate_in, up_in)
 
 
-def backward(where, swap, held_first, held_second, to_gate, to_up, shards):
+def backward(where, swap, held, to_gate, to_up, shards):
     return call(
         backward_kernel,
         [MODEL, SPREAD, HIDDEN, HIDDEN, MODEL, MODEL],
         [TILE, SPREAD, SPREAD],
         12 * ONE,
-        where, swap, held_first, held_second, to_gate, to_up, *shards,
+        where, swap, held, to_gate, to_up, *shards,
     )
 
 
@@ -282,29 +278,22 @@
     return pl.BlockSpec((count,) + array.shape[1:], index)
 
 
-def grads_call(kernel, steps, specs, blocks, flops, where, *args):
-    shape = (8, 2, blocks, 8, BLOCK)
+def grads(where, x, low, dy, down_in, act, back_in, gate_in, up_in, gate_back, up_back):
+    last = MINE // 2 - 1
+    args = (x, low, dy, down_in, act, back_in, gate_in, up_in, gate_back, up_back)
+    specs = [blocks_of(a, PER) for a in args[:4]]
+    specs += [blocks_of(a, 4 if a.shape[0] == ROWS else 2, last) for a in args[4:]]
+    shape = (8, 2, 3 * HID + 16 + 32, 8, BLOCK)
     moved = sum(a.size * a.dtype.itemsize for a in args)
     return pl.pallas_call(
-        kernel,
-        grid=(steps,),
+        grads_kernel,
+        grid=(NBD // PER,),
         out_shape=[jax.ShapeDtypeStruct(shape, BF)] * 2,
         in_specs=[SM] + specs,
         out_specs=[pl.BlockSpec(shape, lambda step: (0,) * 5)] * 2,
         compiler_params=pltpu.CompilerParams(vmem_limit_bytes=32 << 20),
-        cost_estimate=pl.CostEstimate(flops=flops, bytes_accessed=moved, transcendentals=0),
+        cost_estimate=pl.CostEstimate(flops=6 * ONE, bytes_accessed=moved, transcendentals=0),
     )(where, *args)
-
-
-def second_grads(where, *args):
-    specs = [blocks_of(a, PER) for a in args[:2]]
-    last = MINE // 2 - 1
-    specs += [blocks_of(a, 4 if a.shape[0] == NBD else 2, last) for a in args[2:]]
-    return grads_call(second_grads_kernel, NBD // PER, specs, 3 * HID + 16, 4 * ONE, where, *args)
-
-
-def first_grads(where, x, low):
-    return grads_call(first_grads_kernel, 8, [blocks_of(x, 8), blocks_of(low, 8)], 32, 2 * ONE, where, x, low)
 
 
 GROUP = ("y", "x_lo", "core")
@@ -357,11 +346,9 @@
     return jnp.sum(chips.astype(F32), axis=0)
 
 
-def gather_first(gate_first, up_first, down_second, after):
+def share_first(gate_first, up_first, down_second):
     nh, nz = size("x_hi"), size("z")
     y, kind = lax.axis_index("y"), lax.axis_index(("x_lo", "core"))
-    for value in after:
-        y = y + (value[0, 0, 0].astype(F32) * 0.0).astype(jnp.int32)
     each = gate_first.shape[2] // (nh * nz)
     take = functools.partial(lax.dynamic_index_in_dim, index=y, axis=0, keepdims=False)
     gate, up = take(gate_first).T, take(up_first).T
@@ -369,11 +356,10 @@
     first = first.reshape(nh, nz, each, BLOCK).transpose(1, 0, 2, 3).reshape(nz, nh * each, BLOCK)
     first = jnp.pad(first, ((0, 0), (0, ROWS - nh * each), (0, 0)))
     first = jnp.broadcast_to(first[None], (nh,) + first.shape).reshape(nh * nz, ROWS, BLOCK)
-    first = lax.all_to_all(first, TENSOR, 0, 0, tiled=True)
-    return lax.all_gather(first, GROUP, axis=0, tiled=False)
-
-
-def gather_second(gate_second, up_second, down_first):
+    return lax.all_to_all(first, TENSOR, 0, 0, tiled=True)
+
+
+def share_second(gate_second, up_second, down_first):
     hid = gate_second.shape[0]
     d = lax.axis_index(GROUP)
     kind, at = d // 5, jnp.minimum((d % 5) * SLOTS, hid - SLOTS)
@@ -381,9 +367,10 @@
     second = jnp.where(
         kind == 0, take(gate_second), jnp.where(kind == 1, take(up_second), take(down_first))
     )
-    group = GROUP + ("x_hi",)
-    sent = jnp.broadcast_to(second[None], (lax.axis_size(group),) + second.shape)
-    return lax.all_to_all(sent, group, 0, 0, tiled=True)
+    other = swap(second)
+    me = lax.axis_index("x_hi")
+    second = jnp.concatenate([jnp.where(me == 0, second, other), jnp.where(me == 0, other, second)])
+    return second.reshape(-1, ROWS, BLOCK)
 
 
 def shards(
@@ -405,33 +392,32 @@
     table = swap_table()
     x_own, x_other = halves(activations, me)
     dy_own, dy_other = halves(cotangent, me)
-    held_second = gather_second(gate_second, up_second, down_first)
     xs = ring_gather(x_own, x_other)
-    after = [xs[3], xs[15], dy_other]
-    held_first = gather_first(gate_first, up_first, down_second, after)
-    (dy_own, dy_other), _ = lax.optimization_barrier(((dy_own, dy_other), (xs[2], xs[14])))
     dys = ring_gather(dy_own, dy_other)
-
-    x, gate_in, up_in = forward_first(where, table, held_first, xs)
-    act, to_gate, to_up, down_in = forward_second(table, held_second, gate_in, up_in)
-    dy, back_in, gate_back, up_back, low, parts = backward(
-        where, table, held_first, held_second, to_gate, to_up, dys
-    )
+    weights = (gate_first, up_first, down_second)
+    begun = (x_other, dy_other, xs[2], xs[14], dys[2], dys[14])
+    weights, _ = lax.optimization_barrier((weights, begun))
+    first = share_first(*weights)
+    second = share_second(gate_second, up_second, down_first)
+    held = lax.all_gather(jnp.concatenate([first, second]), GROUP, axis=0, tiled=False)
+
+    x, gate_in, up_in = forward_first(where, table, held, xs)
+    act, to_gate, to_up, down_in = forward_second(table, held, gate_in, up_in)
+    dy, back_in, gate_back, up_back, low, parts = backward(where, table, held, to_gate, to_up, dys)
 
     total = lax.psum_scatter(parts, "z", scatter_dimension=0, tiled=True)
     total = total.reshape(nh, per * BLOCK, half)
     kept = lax.dynamic_index_in_dim(total, me, 0, keepdims=False)
     other = swap(lax.dynamic_index_in_dim(total, 1 - me, 0, keepdims=False))
 
-    firsts = sum_groups(*first_grads(where, x, low))
-    later = sum_groups(
-        *second_grads(where, dy, down_in, act, back_in, gate_in, up_in, gate_back, up_back)
+    chips = sum_groups(
+        *grads(where, x, low, dy, down_in, act, back_in, gate_in, up_in, gate_back, up_back)
     )
-    later, other = lax.optimization_barrier((later, other))
     input_grad = jnp.concatenate(
         [jnp.where(me == 0, kept, other), jnp.where(me == 0, other, kept)], axis=1
     )
-    later = total_of(later) * scale
+    summed = total_of(chips) * scale
+    later, firsts = summed[: 3 * hid + 16], summed[3 * hid + 16 :]
     out_gs, out_us, out_df = later[: 3 * hid].reshape(3, hid, rows, BLOCK)
     pairs = []
     for part in range(ngroup):
@@ -441,7 +427,6 @@
     out_ds = lax.ppermute(later[3 * hid :], GROUP + ("z",), pairs)
     out_ds = out_ds.reshape(per, -1, BLOCK)[:, :each]
 
-    firsts = total_of(firsts) * scale
     firsts = firsts.reshape(nz, per * rows, 2 * ROWS)
     firsts = lax.all_to_all(firsts, "z", 0, 0, tiled=True)
     firsts = firsts.reshape(nz, per, rows, 2, ROWS)[..., : nh * each]

time: 310 us -> 298 us (0.961); the launches traced: 305 us -> 297 us
  blocking collectives: 37.6 us -> 0 us
  waiting for transfers between devices: 71 us -> 90.5 us
  starting transfers between devices: 71.8 us -> 79.6 us
  Pallas kernels: 64.5 us -> 68.3 us
    all_to_all x2 -> x0, blocking collectives: 37.6 us -> none  [the longest x1 21.4 us: sum_groups(): return lax.all_to_all(pairs, CHIPS, 0, 0, tiled=True)]
    all_to_all x1, waiting for transfers between devices: 15.1 us -> 37.1 us  [sum_groups(): return lax.all_to_all(pairs, CHIPS, 0, 0, tiled=True)]
    ppermute x28, waiting for transfers between devices: 39.9 us -> 29.9 us  [shift(): lax.ppermute(value, 'z', [(i, (i + step) % count) for i in range(count)])]
    ppermute x2 -> x1, starting transfers between devices: 4.15 us -> 12 us  [sum_groups(): found = lax.ppermute(send, 'core', [(0, 1), (1, 0)])]
    ppermute x2 -> x1, waiting for transfers between devices: 0.01 us -> 5 us  [sum_groups(): found = lax.ppermute(send, 'core', [(0, 1), (1, 0)])]
    unnamed x72 -> x64, local copies, waits for them, and re-layouts: 25.3 us -> 29.8 us
    ppermute x28, starting transfers between devices: 36.9 us -> 32.6 us  [shift(): lax.ppermute(value, 'z', [(i, (i + step) % count) for i in range(count)])]
    ppermute x3 -> x4, starting transfers between devices: 6.63 us -> 10.3 us  [swap(): return lax.ppermute(value, 'x_hi', [(0, 1), (1, 0)])]
  transfers between devices with their start and end apart: 39 -> 39, of which waited for: 19 -> 17; matrix products, arithmetic and copies ran while one was open for 5% -> 4% of each run, Pallas kernels for 12% -> 14%
where the time goes in v3:
time: 298 us; the launch traced here: 297 us
  waiting for transfers between devices  90.5 us (30%)
  starting transfers between devices  79.6 us (27%)
  Pallas kernels  68.3 us (23%)
  local copies, waits for them, and re-layouts  37.5 us (13%)
  between operations  14.3 us (5%)
  other arithmetic  6.6 us (2%)
    pallas_call x3, Pallas kernels, call(): pl.pallas_call(kernel, out_shape=shapes, in_specs=[SM if a.dtype == jnp.i...  53.6 us
    all_to_all x1, waiting for transfers between devices, sum_groups(): return lax.all_to_all(pairs, CHIPS, 0, 0, tiled=True)  37.1 us
    ppermute x28, starting transfers between devices, shift(): lax.ppermute(value, 'z', [(i, (i + step) % count) for i in range(count)])  32.6 us
    ppermute x28, waiting for transfers between devices, shift(): lax.ppermute(value, 'z', [(i, (i + step) % count) for i in range(count)])  29.9 us
    unnamed x64, local copies, waits for them, and re-layouts  29.8 us
    pallas_call x1, Pallas kernels, grads(): pl.pallas_call(grads_kernel, grid=(NBD // PER,), out_shape=[jax.ShapeDtyp...  14.7 us
    ppermute x1, starting transfers between devices, sum_groups(): found = lax.ppermute(send, 'core', [(0, 1), (1, 0)])  12 us
    ppermute x4, waiting for transfers between devices, swap(): return lax.ppermute(value, 'x_hi', [(0, 1), (1, 0)])  11.1 us
  transfers between devices with their start and end apart: 39, of which 17 were waited for; matrix products, arithmetic and copies ran while one was open for 4% of the time, Pallas kernels for 14%

profile of v3, /device:TPU:1, one launch (start us, length us, event | category | flops | bytes accessed | tf_op | source)
XLA Modules:
  0.0 296.8 jit_solution(10802337752407285334)
XLA Ops:
  7.2 1.1 constant_dynamic-slice_fusion.1
  8.3 2.5 collective-permute-start.3
  10.8 4.0 %collective-permute-start.2 = (bf16[4,128,256]{2,1,0:T(8,128)(2,1)S(1)}, bf16[4,128,256]{2,1,0:T(8,128)(2,1)S(1)}, u32[]{:S(2)}, u32[]{:S(2)}) collective-permute-start(bf16[4,128,256]{2,1,0:T(8,128)(2,1)S(1)} %bitcast.48), channel_id=1, source_target_pairs={{0,7},{1,0},{2,1},{3,2},{4,3},{5,4},{6,5},{7,6},{8,15},{9,8},{10,9... | collective-permute-start | bytes 786440 | tf_op jit(solution)/shard_map/ppermute | solution.py:310
  14.8 1.1 constant_dynamic-slice_fusion
  16.0 2.7 collective-permute-start.4
  18.7 2.7 collective-permute-start
  21.4 2.1 collective-permute-start.1
  23.5 2.9 collective-permute-done
  26.4 5.6 %collective-permute-done.1 = bf16[512,256]{1,0:T(8,128)(2,1)S(1)} collective-permute-done((bf16[512,256]{1,0:T(8,128)(2,1)S(1)}, bf16[512,256]{1,0:T(8,128)(2,1)S(1)}, u32[]{:S(2)}, u32[]{:S(2)}) %collective-permute-start.1) | collective-permute-done | bytes 262176 | tf_op jit(solution)/shard_map/ppermute | solution.py:314
  32.1 1.0 fusion
  34.0 7.5 %all-to-all-start = ((bf16[16,64,128]{2,1,0:T(8,128)(2,1)}), bf16[16,64,128]{2,1,0:T(8,128)(2,1)S(1)}, u32[]{:S(2)}, u32[]{:S(2)}) async-start(bf16[16,64,128]{2,1,0:T(8,128)(2,1)} %bitcast.14), calls=%async_computation | async-start | bytes 524288 | tf_op jit(solution)/shard_map/all_to_all | solution.py:359
  41.5 1.0 select_select_fusion
  42.5 3.0 collective-permute-start.6
  45.5 2.6 collective-permute-done.6
  48.2 2.6 all-to-all-done
  51.6 1.9 collective-permute-start.12
  55.0 2.1 collective-permute-start.7
  57.1 1.1 collective-permute-done.12.refs_12_
  58.1 1.6 collective-permute-start.20
  59.7 2.2 collective-permute-done.16.refs_15_
  64.2 3.5 %collective-permute-done.24.refs_12_ = bf16[4,128,256]{2,1,0:T(8,128)(2,1)S(1)} collective-permute-done((bf16[4,128,256]{2,1,0:T(8,128)(2,1)S(1)}, bf16[4,128,256]{2,1,0:T(8,128)(2,1)S(1)}, u32[]{:S(2)}, u32[]{:S(2)}) %collective-permute-start.24) | collective-permute-done | bytes 262176 | tf_op jit(solution)/shard_map/ppermute | solution.py:310
  70.7 2.5 collective-permute-done.28.refs_15_
  75.0 3.9 %collective-permute-done.13.refs_10_ = bf16[4,128,256]{2,1,0:T(8,128)(2,1)} collective-permute-done((bf16[4,128,256]{2,1,0:T(8,128)(2,1)S(1)}, bf16[4,128,256]{2,1,0:T(8,128)(2,1)}, u32[]{:S(2)}, u32[]{:S(2)}) %collective-permute-start.13) | collective-permute-done | bytes 262176 | tf_op jit(solution)/shard_map/ppermute | solution.py:310
  79.7 1.5 collective-permute-start.11
  82.0 3.1 %collective-permute-done.10.refs_6_ = bf16[4,128,256]{2,1,0:T(8,128)(2,1)S(1)} collective-permute-done((bf16[4,128,256]{2,1,0:T(8,128)(2,1)S(1)}, bf16[4,128,256]{2,1,0:T(8,128)(2,1)S(1)}, u32[]{:S(2)}, u32[]{:S(2)}) %collective-permute-start.10) | collective-permute-done | bytes 262176 | tf_op jit(solution)/shard_map/ppermute | solution.py:310
  86.8 3.4 %collective-permute-done.25.refs_10_ = bf16[4,128,256]{2,1,0:T(8,128)(2,1)S(1)} collective-permute-done((bf16[4,128,256]{2,1,0:T(8,128)(2,1)S(1)}, bf16[4,128,256]{2,1,0:T(8,128)(2,1)S(1)}, u32[]{:S(2)}, u32[]{:S(2)}) %collective-permute-start.25) | collective-permute-done | bytes 262176 | tf_op jit(solution)/shard_map/ppermute | solution.py:310
  91.0 1.9 collective-permute-start.23
  92.9 3.4 %collective-permute-done.11.refs_7_ = bf16[4,128,256]{2,1,0:T(8,128)(2,1)} collective-permute-done((bf16[4,128,256]{2,1,0:T(8,128)(2,1)S(1)}, bf16[4,128,256]{2,1,0:T(8,128)(2,1)}, u32[]{:S(2)}, u32[]{:S(2)}) %collective-permute-start.11) | collective-permute-done | bytes 262176 | tf_op jit(solution)/shard_map/ppermute | solution.py:310
  96.3 1.8 collective-permute-start.15
  98.1 2.6 collective-permute-done.14.refs_8_
  100.7 1.5 collective-permute-start.26
  102.2 4.2 %collective-permute-done.18.refs_11_ = bf16[4,128,256]{2,1,0:T(8,128)(2,1)} collective-permute-done((bf16[4,128,256]{2,1,0:T(8,128)(2,1)}, bf16[4,128,256]{2,1,0:T(8,128)(2,1)}, u32[]{:S(2)}, u32[]{:S(2)}) %collective-permute-start.18) | collective-permute-done | bytes 262176 | tf_op jit(solution)/shard_map/ppermute | solution.py:310
  106.4 1.4 collective-permute-start.30
  107.8 1.3 collective-permute-start.27
  110.2 0.9 copy-done.15
  112.1 0.9 copy-done.19
  113.0 0.9 copy-done.21
  114.9 0.9 copy-done.25
  115.9 0.9 copy-done.27
  117.8 11.8 %shard_map.144 = (bf16[64,128,256]{2,1,0:T(8,128)(2,1)}, bf16[64,64,256]{2,1,0:T(8,128)(2,1)}, bf16[64,64,256]{2,1,0:T(8,128)(2,1)}) custom-call(s32[3]{0:T(128)S(1)} %pad_add_fusion.where, bf16[256,256]{1,0:T(8,128)(2,1)S(1)} %copy-done.11, bf16[16,28,64,128]{3,2,1,0:T(8,128)(2,1)} %bitcast.56, bf16[4,128,256]{2,1,0:T(8,128)(2,1)S(1)} %bitcast.49, ...), custom_call_target="tpu_custom_call" | custom-call | flops 1409286144 | bytes 11665420 | tf_op jit(solution)/shard_map/pallas_call | solution.py:229
  129.5 1.6 copy-done
  131.1 14.4 %shard_map.145 = (bf16[28,128,256]{2,1,0:T(8,128)(2,1)S(1)}, f32[28,128,256]{2,1,0:T(8,128)}, f32[28,128,256]{2,1,0:T(8,128)}, bf16[64,64,256]{2,1,0:T(8,128)(2,1)S(1)}) custom-call(bf16[256,256]{1,0:T(8,128)(2,1)S(1)} %copy-done.11, bf16[16,28,64,128]{3,2,1,0:T(8,128)(2,1)} %bitcast.57, bf16[64,64,256]{2,1,0:T(8,128)(2,1)S(1)} %copy-done, ...), custom_call_target="tpu_custom_call" | custom-call | flops 1174405120 | bytes 11665408 | tf_op jit(solution)/shard_map/pallas_call | solution.py:229
  145.5 1.4 copy-done.3
  146.8 1.3 copy-done.6
  148.1 27.5 %shard_map.146 = (bf16[64,128,256]{2,1,0:T(8,128)(2,1)}, bf16[64,64,256]{2,1,0:T(8,128)(2,1)}, bf16[28,128,256]{2,1,0:T(8,128)(2,1)S(1)}, bf16[28,128,256]{2,1,0...) custom-call(s32[3]{0:T(128)S(1)} %pad_add_fusion.where, bf16[256,256]{1,0:T(8,128)(2,1)S(1)} %copy-done.11, ...), custom_call_target="tpu_custom_call" | custom-call | flops 2818572288 | bytes 19005452 | tf_op jit(solution)/shard_map/pallas_call | solution.py:229
  175.6 1.2 copy-done.8
  176.9 1.6 copy-done.1
  178.4 1.6 copy-done.2
  180.0 1.6 copy-done.4
  181.6 1.6 copy-done.5
  183.2 1.5 copy-done.7
  184.7 1.5 copy-done.9
  186.2 1.5 copy-done.10
  187.7 14.7 %shard_map.147 = (bf16[8,2,90,8,128]{4,3,2,1,0:T(8,128)(2,1)S(1)}, bf16[8,2,90,8,128]{4,3,2,1,0:T(8,128)(2,1)S(1)}) custom-call(s32[3]{0:T(128)S(1)} %pad_add_fusion.where, bf16[64,128,256]{2,1,0:T(8,128)(2,1)} %get-tuple-element.33.x, bf16[64,128,256]{2,1,0:T(8,128)(2,1)} %get-tuple-element.34.low, bf16[64,128,256]{2,1,0:T(8,128)(2,1)} %get-tuple-element.35.dy, ...), custom_call_target="tpu_custom_call" | custom-call | flops 1409286144 | bytes 26476544 | tf_op jit(solution)/shard_map/pallas_call | solution.py:288
  202.4 12.0 %collective-permute-start.32 = (bf16[8,2,90,8,128]{4,3,2,1,0:T(8,128)(2,1)S(1)}, bf16[8,2,90,8,128]{4,3,2,1,0:T(8,128)(2,1)S(1)}, u32[]{:S(2)}, u32[]{:S(2)}) collective-permute-start(bf16[8,2,90,8,128]{4,3,2,1,0:T(8,128)(2,1)S(1)} %get-tuple-element.42), channel_id=1, source_target_pairs={{0,16},{16,0},{1,17},{17,1},{2,18},{18,2},{3,19},{19,3},{4,20},{20... | collective-permute-start | bytes 8847368 | tf_op jit(solution)/shard_map/ppermute | solution.py:339
  214.4 5.0 %collective-permute-done.32 = bf16[8,2,90,8,128]{4,3,2,1,0:T(8,128)(2,1)S(1)} collective-permute-done((bf16[8,2,90,8,128]{4,3,2,1,0:T(8,128)(2,1)S(1)}, bf16[8,2,90,8,128]{4,3,2,1,0:T(8,128)(2,1)S(1)}, u32[]{:S(2)}, u32[]{:S(2)}) %collective-permute-start.32) | collective-permute-done | bytes 2949152 | tf_op jit(solution)/shard_map/ppermute | solution.py:339
  219.4 2.3 add_convert_fusion
  221.7 4.8 %all-to-all-start.1 = ((bf16[16,90,8,128]{3,2,1,0:T(8,128)(2,1)}), bf16[16,90,8,128]{3,2,1,0:T(8,128)(2,1)S(1)}, u32[]{:S(2)}, u32[]{:S(2)}) async-start(bf16[16,90,8,128]{3,2,1,0:T(8,128)(2,1)} %bitcast.59), calls=%async_computation.2 | async-start | bytes 5898240 | tf_op jit(solution)/shard_map/all_to_all | solution.py:342
  226.5 37.1 %all-to-all-done.1 = bf16[16,90,8,128]{3,2,1,0:T(8,128)(2,1)S(1)} async-done(((bf16[16,90,8,128]{3,2,1,0:T(8,128)(2,1)}), bf16[16,90,8,128]{3,2,1,0:T(8,128)(2,1)S(1)}, u32[]{:S(2)}, u32[]{:S(2)}) %all-to-all-start.1) | async-done | bytes 2949152 | tf_op jit(solution)/shard_map/all_to_all | solution.py:342
  264.8 6.7 %collective-permute-start.33 = (f32[16,8,128]{2,1,0:T(8,128)S(1)}, f32[16,8,128]{2,1,0:T(8,128)S(1)}, u32[]{:S(2)}, u32[]{:S(2)}) collective-permute-start(f32[16,8,128]{2,1,0:T(8,128)S(1)} %slice.30), channel_id=1, source_target_pairs={{0,0},{1,16},{2,32},{3,48},{4,64},{5,80},{6,96},{7,112},{16,128},{... | collective-permute-start | bytes 196616 | tf_op jit(solution)/shard_map/ppermute | solution.py:427
  271.5 5.6 %all-to-all-start.2 = ((f32[8,32,128]{2,1,0:T(8,128)}), f32[8,32,128]{2,1,0:T(8,128)S(1)}, u32[]{:S(2)}, u32[]{:S(2)}) async-start(f32[8,32,128]{2,1,0:T(8,128)} %bitcast.21), calls=%async_computation.3 | async-start | bytes 262144 | tf_op jit(solution)/shard_map/all_to_all | solution.py:431
  277.1 1.0 dynamic-slice_bitcast_fusion
  278.2 2.5 collective-permute-start.31
  281.9 4.7 %all-to-all-done.2 = f32[8,32,128]{2,1,0:T(8,128)S(1)} async-done(((f32[8,32,128]{2,1,0:T(8,128)}), f32[8,32,128]{2,1,0:T(8,128)S(1)}, u32[]{:S(2)}, u32[]{:S(2)}) %all-to-all-start.2) | async-done | bytes 131104 | tf_op jit(solution)/shard_map/all_to_all | solution.py:431
  (113 shorter events, 24.2 us)
Async XLA Ops:
  8.2 100.9 %copy-start.11 = (bf16[256,256]{1,0:T(8,128)(2,1)S(1)}, bf16[256,256]{1,0:T(8,128)(2,1)}, u32[]{:S(2)}) copy-start(bf16[256,256]{1,0:T(8,128)(2,1)} %constant.81.clone.swap) | copy-start | bytes 393220
  8.3 13.1 %collective-permute-start.3 = (bf16[4,128,256]{2,1,0:T(8,128)(2,1)S(1)}, bf16[4,128,256]{2,1,0:T(8,128)(2,1)S(1)}, u32[]{:S(2)}, u32[]{:S(2)}) collective-permute-start(bf16[4,128,256]{2,1,0:T(8,128)(2,1)S(1)} %bitcast.47), channel_id=1, source_target_pairs={{0,1},{1,2},{2,3},{3,4},{4,5},{5,6},{6,7},{7,0},{8,9},{9,10},{10,1... | collective-permute-start | bytes 786440 | tf_op jit(solution)/shard_map/ppermute | solution.py:310
  10.8 12.7 %collective-permute-start.2 = (bf16[4,128,256]{2,1,0:T(8,128)(2,1)S(1)}, bf16[4,128,256]{2,1,0:T(8,128)(2,1)S(1)}, u32[]{:S(2)}, u32[]{:S(2)}) collective-permute-start(bf16[4,128,256]{2,1,0:T(8,128)(2,1)S(1)} %bitcast.48), channel_id=1, source_target_pairs={{0,7},{1,0},{2,1},{3,2},{4,3},{5,4},{6,5},{7,6},{8,15},{9,8},{10,9... | collective-permute-start | bytes 786440 | tf_op jit(solution)/shard_map/ppermute | solution.py:310
  15.9 10.5 %collective-permute-start.5 = (bf16[4,128,256]{2,1,0:T(8,128)(2,1)S(1)}, bf16[4,128,256]{2,1,0:T(8,128)(2,1)S(1)}, u32[]{:S(2)}, u32[]{:S(2)}) collective-permute-start(bf16[4,128,256]{2,1,0:T(8,128)(2,1)S(1)} %bitcast.44), channel_id=1, source_target_pairs={{0,1},{1,2},{2,3},{3,4},{4,5},{5,6},{6,7},{7,0},{8,9},{9,10},{10,1... | collective-permute-start | bytes 786440 | tf_op jit(solution)/shard_map/ppermute | solution.py:310
  16.0 10.5 %collective-permute-start.4 = (bf16[4,128,256]{2,1,0:T(8,128)(2,1)S(1)}, bf16[4,128,256]{2,1,0:T(8,128)(2,1)S(1)}, u32[]{:S(2)}, u32[]{:S(2)}) collective-permute-start(bf16[4,128,256]{2,1,0:T(8,128)(2,1)S(1)} %bitcast.45), channel_id=1, source_target_pairs={{0,7},{1,0},{2,1},{3,2},{4,3},{5,4},{6,5},{7,6},{8,15},{9,8},{10,9... | collective-permute-start | bytes 786440 | tf_op jit(solution)/shard_map/ppermute | solution.py:310
  18.7 7.8 %collective-permute-start = (bf16[512,256]{1,0:T(8,128)(2,1)S(1)}, bf16[512,256]{1,0:T(8,128)(2,1)S(1)}, u32[]{:S(2)}, u32[]{:S(2)}) collective-permute-start(bf16[512,256]{1,0:T(8,128)(2,1)S(1)} %get-tuple-element.71), channel_id=1, source_target_pairs={{0,8},{8,0},{1,9},{9,1},{2,10},{10,2},{3,11},{11,3},{4,12},{12,4},... | collective-permute-start | bytes 786440 | tf_op jit(solution)/shard_map/ppermute | solution.py:314
  21.4 35.7 %copy-start.12 = (bf16[4,128,256]{2,1,0:T(8,128)(2,1)}, bf16[4,128,256]{2,1,0:T(8,128)(2,1)S(1)}, u32[]{:S(2)}) copy-start(bf16[4,128,256]{2,1,0:T(8,128)(2,1)S(1)} %collective-permute-done.3.refs_14_) | copy-start | bytes 786436
  21.4 10.7 %collective-permute-start.1 = (bf16[512,256]{1,0:T(8,128)(2,1)S(1)}, bf16[512,256]{1,0:T(8,128)(2,1)S(1)}, u32[]{:S(2)}, u32[]{:S(2)}) collective-permute-start(bf16[512,256]{1,0:T(8,128)(2,1)S(1)} %get-tuple-element.69), channel_id=1, source_target_pairs={{0,8},{8,0},{1,9},{9,1},{2,10},{10,2},{3,11},{11,3},{4,12},{12,4},... | collective-permute-start | bytes 786440 | tf_op jit(solution)/shard_map/ppermute | solution.py:314
  23.5 36.2 %copy-start.14 = (bf16[4,128,256]{2,1,0:T(8,128)(2,1)}, bf16[4,128,256]{2,1,0:T(8,128)(2,1)S(1)}, u32[]{:S(2)}) copy-start(bf16[4,128,256]{2,1,0:T(8,128)(2,1)S(1)} %collective-permute-done.2.refs_2_) | copy-start | bytes 786436
  26.4 47.7 %copy-start.16 = (bf16[512,256]{1,0:T(8,128)(2,1)}, bf16[512,256]{1,0:T(8,128)(2,1)S(1)}, u32[]{:S(2)}) copy-start(bf16[512,256]{1,0:T(8,128)(2,1)S(1)} %collective-permute-done) | copy-start | bytes 786436
  34.0 16.8 %all-to-all-start = ((bf16[16,64,128]{2,1,0:T(8,128)(2,1)}), bf16[16,64,128]{2,1,0:T(8,128)(2,1)S(1)}, u32[]{:S(2)}, u32[]{:S(2)}) async-start(bf16[16,64,128]{2,1,0:T(8,128)(2,1)} %bitcast.14), calls=%async_computation | async-start | bytes 524288 | tf_op jit(solution)/shard_map/all_to_all | solution.py:359
  41.5 67.7 %all-gather.3.cloned.1.call-start = ((), (), s32[]{:S(2)}) async-start(), calls=%async_computation.5 | async-start | bytes 7798784 | tf_op jit(solution)/shard_map/all_gather | solution.py:402
  42.5 5.6 %collective-permute-start.6 = (bf16[3,128,128]{2,1,0:T(8,128)(2,1)S(1)}, bf16[3,128,128]{2,1,0:T(8,128)(2,1)S(1)}, u32[]{:S(2)}, u32[]{:S(2)}) collective-permute-start(bf16[3,128,128]{2,1,0:T(8,128)(2,1)S(1)} %select_select_fusion), channel_id=1, source_target_pairs={{0,8},{8,0},{1,9},{9,1},{2,10},{10,2},{3,11},{11,3},{4,12},{12,4},... | collective-permute-start | bytes 294920 | tf_op jit(solution)/shard_map/ppermute | solution.py:314
  51.6 225.5 %reduce-scatter.2.cloned.1.call-start = ((), (), s32[]{:S(2)}) async-start(), calls=%async_computation.4 | async-start | bytes 4718592 | tf_op jit(solution)/shard_map/reduce_scatter | solution.py:408
  51.6 6.5 %collective-permute-start.12 = (bf16[4,128,256]{2,1,0:T(8,128)(2,1)S(1)}, bf16[4,128,256]{2,1,0:T(8,128)(2,1)S(1)}, u32[]{:S(2)}, u32[]{:S(2)}) collective-permute-start(bf16[4,128,256]{2,1,0:T(8,128)(2,1)S(1)} %collective-permute-done.3.refs_14_), channel_id=1, source_target_pairs={{0,1},{1,2},{2,3},{3,4},{4,5},{5,6},{6,7},{7,0},{8,9},{9,10},{10,1... | collective-permute-start | bytes 786440 | tf_op jit(solution)/shard_map/ppermute | solution.py:310
  53.5 6.3 %collective-permute-start.8 = (bf16[4,128,256]{2,1,0:T(8,128)(2,1)S(1)}, bf16[4,128,256]{2,1,0:T(8,128)(2,1)S(1)}, u32[]{:S(2)}, u32[]{:S(2)}) collective-permute-start(bf16[4,128,256]{2,1,0:T(8,128)(2,1)S(1)} %collective-permute-done.2.refs_2_), channel_id=1, source_target_pairs={{0,7},{1,0},{2,1},{3,2},{4,3},{5,4},{6,5},{7,6},{8,15},{9,8},{10,9... | collective-permute-start | bytes 786440 | tf_op jit(solution)/shard_map/ppermute | solution.py:310
  54.4 7.6 %collective-permute-start.16 = (bf16[4,128,256]{2,1,0:T(8,128)(2,1)S(1)}, bf16[4,128,256]{2,1,0:T(8,128)(2,1)S(1)}, u32[]{:S(2)}, u32[]{:S(2)}) collective-permute-start(bf16[4,128,256]{2,1,0:T(8,128)(2,1)S(1)} %bitcast.53), channel_id=1, source_target_pairs={{0,1},{1,2},{2,3},{3,4},{4,5},{5,6},{6,7},{7,0},{8,9},{9,10},{10,1... | collective-permute-start | bytes 786440 | tf_op jit(solution)/shard_map/ppermute | solution.py:310
  55.0 7.8 %collective-permute-start.7 = (bf16[4,128,256]{2,1,0:T(8,128)(2,1)S(1)}, bf16[4,128,256]{2,1,0:T(8,128)(2,1)S(1)}, u32[]{:S(2)}, u32[]{:S(2)}) collective-permute-start(bf16[4,128,256]{2,1,0:T(8,128)(2,1)S(1)} %bitcast.54), channel_id=1, source_target_pairs={{0,7},{1,0},{2,1},{3,2},{4,3},{5,4},{6,5},{7,6},{8,15},{9,8},{10,9... | collective-permute-start | bytes 786440 | tf_op jit(solution)/shard_map/ppermute | solution.py:310
  57.0 10.6 %collective-permute-start.24 = (bf16[4,128,256]{2,1,0:T(8,128)(2,1)S(1)}, bf16[4,128,256]{2,1,0:T(8,128)(2,1)S(1)}, u32[]{:S(2)}, u32[]{:S(2)}) collective-permute-start(bf16[4,128,256]{2,1,0:T(8,128)(2,1)S(1)} %collective-permute-done.5.refs_14_), channel_id=1, source_target_pairs={{0,1},{1,2},{2,3},{3,4},{4,5},{5,6},{6,7},{7,0},{8,9},{9,10},{10,1... | collective-permute-start | bytes 786440 | tf_op jit(solution)/shard_map/ppermute | solution.py:310
  58.1 10.9 %collective-permute-start.20 = (bf16[4,128,256]{2,1,0:T(8,128)(2,1)S(1)}, bf16[4,128,256]{2,1,0:T(8,128)(2,1)S(1)}, u32[]{:S(2)}, u32[]{:S(2)}) collective-permute-start(bf16[4,128,256]{2,1,0:T(8,128)(2,1)S(1)} %collective-permute-done.4.refs_2_), channel_id=1, source_target_pairs={{0,7},{1,0},{2,1},{3,2},{4,3},{5,4},{6,5},{7,6},{8,15},{9,8},{10,9... | collective-permute-start | bytes 786440 | tf_op jit(solution)/shard_map/ppermute | solution.py:310
  59.7 13.5 %collective-permute-start.28 = (bf16[4,128,256]{2,1,0:T(8,128)(2,1)S(1)}, bf16[4,128,256]{2,1,0:T(8,128)(2,1)S(1)}, u32[]{:S(2)}, u32[]{:S(2)}) collective-permute-start(bf16[4,128,256]{2,1,0:T(8,128)(2,1)S(1)} %bitcast.50), channel_id=1, source_target_pairs={{0,1},{1,2},{2,3},{3,4},{4,5},{5,6},{6,7},{7,0},{8,9},{9,10},{10,1... | collective-permute-start | bytes 786440 | tf_op jit(solution)/shard_map/ppermute | solution.py:310
  62.0 12.8 %collective-permute-start.19 = (bf16[4,128,256]{2,1,0:T(8,128)(2,1)S(1)}, bf16[4,128,256]{2,1,0:T(8,128)(2,1)S(1)}, u32[]{:S(2)}, u32[]{:S(2)}) collective-permute-start(bf16[4,128,256]{2,1,0:T(8,128)(2,1)S(1)} %bitcast.51), channel_id=1, source_target_pairs={{0,7},{1,0},{2,1},{3,2},{4,3},{5,4},{6,5},{7,6},{8,15},{9,8},{10,9... | collective-permute-start | bytes 786440 | tf_op jit(solution)/shard_map/ppermute | solution.py:310
  62.8 16.1 %collective-permute-start.13 = (bf16[4,128,256]{2,1,0:T(8,128)(2,1)S(1)}, bf16[4,128,256]{2,1,0:T(8,128)(2,1)}, u32[]{:S(2)}, u32[]{:S(2)}) collective-permute-start(bf16[4,128,256]{2,1,0:T(8,128)(2,1)S(1)} %collective-permute-done.12.refs_12_), channel_id=1, source_target_pairs={{0,1},{1,2},{2,3},{3,4},{4,5},{5,6},{6,7},{7,0},{8,9},{9,10},{10,1... | collective-permute-start | bytes 786440 | tf_op jit(solution)/shard_map/ppermute | solution.py:310
  67.6 12.1 %collective-permute-start.9 = (bf16[4,128,256]{2,1,0:T(8,128)(2,1)S(1)}, bf16[4,128,256]{2,1,0:T(8,128)(2,1)S(1)}, u32[]{:S(2)}, u32[]{:S(2)}) collective-permute-start(bf16[4,128,256]{2,1,0:T(8,128)(2,1)S(1)} %collective-permute-done.7.refs_3_), channel_id=1, source_target_pairs={{0,7},{1,0},{2,1},{3,2},{4,3},{5,4},{6,5},{7,6},{8,15},{9,8},{10,9... | collective-permute-start | bytes 786440 | tf_op jit(solution)/shard_map/ppermute | solution.py:310
  69.1 16.0 %collective-permute-start.10 = (bf16[4,128,256]{2,1,0:T(8,128)(2,1)S(1)}, bf16[4,128,256]{2,1,0:T(8,128)(2,1)S(1)}, u32[]{:S(2)}, u32[]{:S(2)}) collective-permute-start(bf16[4,128,256]{2,1,0:T(8,128)(2,1)S(1)} %collective-permute-done.8.refs_4_), channel_id=1, source_target_pairs={{0,7},{1,0},{2,1},{3,2},{4,3},{5,4},{6,5},{7,6},{8,15},{9,8},{10,9... | collective-permute-start | bytes 786440 | tf_op jit(solution)/shard_map/ppermute | solution.py:310
  73.2 12.8 %collective-permute-start.17 = (bf16[4,128,256]{2,1,0:T(8,128)(2,1)S(1)}, bf16[4,128,256]{2,1,0:T(8,128)(2,1)}, u32[]{:S(2)}, u32[]{:S(2)}) collective-permute-start(bf16[4,128,256]{2,1,0:T(8,128)(2,1)S(1)} %collective-permute-done.16.refs_15_), channel_id=1, source_target_pairs={{0,1},{1,2},{2,3},{3,4},{4,5},{5,6},{6,7},{7,0},{8,9},{9,10},{10,1... | collective-permute-start | bytes 786440 | tf_op jit(solution)/shard_map/ppermute | solution.py:310
  74.8 15.4 %collective-permute-start.25 = (bf16[4,128,256]{2,1,0:T(8,128)(2,1)S(1)}, bf16[4,128,256]{2,1,0:T(8,128)(2,1)S(1)}, u32[]{:S(2)}, u32[]{:S(2)}) collective-permute-start(bf16[4,128,256]{2,1,0:T(8,128)(2,1)S(1)} %collective-permute-done.24.refs_12_), channel_id=1, source_target_pairs={{0,1},{1,2},{2,3},{3,4},{4,5},{5,6},{6,7},{7,0},{8,9},{9,10},{10,1... | collective-permute-start | bytes 786440 | tf_op jit(solution)/shard_map/ppermute | solution.py:310
  78.8 12.1 %collective-permute-start.21 = (bf16[4,128,256]{2,1,0:T(8,128)(2,1)S(1)}, bf16[4,128,256]{2,1,0:T(8,128)(2,1)S(1)}, u32[]{:S(2)}, u32[]{:S(2)}) collective-permute-start(bf16[4,128,256]{2,1,0:T(8,128)(2,1)S(1)} %collective-permute-done.19.refs_3_), channel_id=1, source_target_pairs={{0,7},{1,0},{2,1},{3,2},{4,3},{5,4},{6,5},{7,6},{8,15},{9,8},{10,9... | collective-permute-start | bytes 786440 | tf_op jit(solution)/shard_map/ppermute | solution.py:310
  79.7 16.6 %collective-permute-start.11 = (bf16[4,128,256]{2,1,0:T(8,128)(2,1)S(1)}, bf16[4,128,256]{2,1,0:T(8,128)(2,1)}, u32[]{:S(2)}, u32[]{:S(2)}) collective-permute-start(bf16[4,128,256]{2,1,0:T(8,128)(2,1)S(1)} %collective-permute-done.9.refs_5_), channel_id=1, source_target_pairs={{0,7},{1,0},{2,1},{3,2},{4,3},{5,4},{6,5},{7,6},{8,15},{9,8},{10,9... | collective-permute-start | bytes 786440 | tf_op jit(solution)/shard_map/ppermute | solution.py:310
  85.8 12.3 %collective-permute-start.29 = (bf16[4,128,256]{2,1,0:T(8,128)(2,1)S(1)}, bf16[4,128,256]{2,1,0:T(8,128)(2,1)S(1)}, u32[]{:S(2)}, u32[]{:S(2)}) collective-permute-start(bf16[4,128,256]{2,1,0:T(8,128)(2,1)S(1)} %collective-permute-done.28.refs_15_), channel_id=1, source_target_pairs={{0,1},{1,2},{2,3},{3,4},{4,5},{5,6},{6,7},{7,0},{8,9},{9,10},{10,1... | collective-permute-start | bytes 786440 | tf_op jit(solution)/shard_map/ppermute | solution.py:310
  86.1 14.6 %collective-permute-start.14 = (bf16[4,128,256]{2,1,0:T(8,128)(2,1)}, bf16[4,128,256]{2,1,0:T(8,128)(2,1)}, u32[]{:S(2)}, u32[]{:S(2)}) collective-permute-start(bf16[4,128,256]{2,1,0:T(8,128)(2,1)} %collective-permute-done.13.refs_10_), channel_id=1, source_target_pairs={{0,1},{1,2},{2,3},{3,4},{4,5},{5,6},{6,7},{7,0},{8,9},{9,10},{10,1... | collective-permute-start | bytes 786440 | tf_op jit(solution)/shard_map/ppermute | solution.py:310
  90.2 16.2 %collective-permute-start.18 = (bf16[4,128,256]{2,1,0:T(8,128)(2,1)}, bf16[4,128,256]{2,1,0:T(8,128)(2,1)}, u32[]{:S(2)}, u32[]{:S(2)}) collective-permute-start(bf16[4,128,256]{2,1,0:T(8,128)(2,1)} %collective-permute-done.17.refs_13_), channel_id=1, source_target_pairs={{0,1},{1,2},{2,3},{3,4},{4,5},{5,6},{6,7},{7,0},{8,9},{9,10},{10,1... | collective-permute-start | bytes 786440 | tf_op jit(solution)/shard_map/ppermute | solution.py:310
  91.0 16.9 %collective-permute-start.23 = (bf16[4,128,256]{2,1,0:T(8,128)(2,1)S(1)}, bf16[4,128,256]{2,1,0:T(8,128)(2,1)S(1)}, u32[]{:S(2)}, u32[]{:S(2)}) collective-permute-start(bf16[4,128,256]{2,1,0:T(8,128)(2,1)S(1)} %collective-permute-done.21.refs_5_), channel_id=1, source_target_pairs={{0,7},{1,0},{2,1},{3,2},{4,3},{5,4},{6,5},{7,6},{8,15},{9,8},{10,9... | collective-permute-start | bytes 786440 | tf_op jit(solution)/shard_map/ppermute | solution.py:310
  96.3 12.9 %collective-permute-start.15 = (bf16[4,128,256]{2,1,0:T(8,128)(2,1)}, bf16[4,128,256]{2,1,0:T(8,128)(2,1)}, u32[]{:S(2)}, u32[]{:S(2)}) collective-permute-start(bf16[4,128,256]{2,1,0:T(8,128)(2,1)} %collective-permute-done.11.refs_7_), channel_id=1, source_target_pairs={{0,7},{1,0},{2,1},{3,2},{4,3},{5,4},{6,5},{7,6},{8,15},{9,8},{10,9... | collective-permute-start | bytes 786440 | tf_op jit(solution)/shard_map/ppermute | solution.py:310
  98.1 50.0 %collective-permute-start.22 = (bf16[4,128,256]{2,1,0:T(8,128)(2,1)S(1)}, bf16[4,128,256]{2,1,0:T(8,128)(2,1)}, u32[]{:S(2)}, u32[]{:S(2)}) collective-permute-start(bf16[4,128,256]{2,1,0:T(8,128)(2,1)S(1)} %collective-permute-done.20.refs_4_), channel_id=1, source_target_pairs={{0,7},{1,0},{2,1},{3,2},{4,3},{5,4},{6,5},{7,6},{8,15},{9,8},{10,9... | collective-permute-start | bytes 786440 | tf_op jit(solution)/shard_map/ppermute | solution.py:310
  100.7 47.4 %collective-permute-start.26 = (bf16[4,128,256]{2,1,0:T(8,128)(2,1)S(1)}, bf16[4,128,256]{2,1,0:T(8,128)(2,1)}, u32[]{:S(2)}, u32[]{:S(2)}) collective-permute-start(bf16[4,128,256]{2,1,0:T(8,128)(2,1)S(1)} %collective-permute-done.25.refs_10_), channel_id=1, source_target_pairs={{0,1},{1,2},{2,3},{3,4},{4,5},{5,6},{6,7},{7,0},{8,9},{9,10},{10,1... | collective-permute-start | bytes 786440 | tf_op jit(solution)/shard_map/ppermute | solution.py:310
  106.4 41.7 %collective-permute-start.30 = (bf16[4,128,256]{2,1,0:T(8,128)(2,1)S(1)}, bf16[4,128,256]{2,1,0:T(8,128)(2,1)}, u32[]{:S(2)}, u32[]{:S(2)}) collective-permute-start(bf16[4,128,256]{2,1,0:T(8,128)(2,1)S(1)} %collective-permute-done.29.refs_13_), channel_id=1, source_target_pairs={{0,1},{1,2},{2,3},{3,4},{4,5},{5,6},{6,7},{7,0},{8,9},{9,10},{10,1... | collective-permute-start | bytes 786440 | tf_op jit(solution)/shard_map/ppermute | solution.py:310
  107.8 40.3 %collective-permute-start.27 = (bf16[4,128,256]{2,1,0:T(8,128)(2,1)S(1)}, bf16[4,128,256]{2,1,0:T(8,128)(2,1)}, u32[]{:S(2)}, u32[]{:S(2)}) collective-permute-start(bf16[4,128,256]{2,1,0:T(8,128)(2,1)S(1)} %collective-permute-done.23.refs_7_), channel_id=1, source_target_pairs={{0,7},{1,0},{2,1},{3,2},{4,3},{5,4},{6,5},{7,6},{8,15},{9,8},{10,9... | collective-permute-start | bytes 786440 | tf_op jit(solution)/shard_map/ppermute | solution.py:310
  109.2 1.0 copy-start.13
  110.2 0.9 copy-start.15
  111.1 0.9 copy-start.17
  112.1 0.9 copy-start.19
  113.0 0.9 copy-start.21
  114.0 0.9 copy-start.23
  114.9 0.9 copy-start.25
  115.9 0.9 copy-start.27
  116.8 0.9 copy-start.29
  129.5 1.6 copy-start
  145.5 1.4 copy-start.3
  146.8 1.3 copy-start.6
  175.6 1.2 copy-start.8
  176.8 1.6 copy-start.1
  178.4 1.6 copy-start.2
  180.0 1.6 copy-start.4
  181.6 1.6 copy-start.5
  183.2 1.5 copy-start.7
  184.7 1.5 copy-start.9
  186.2 1.5 copy-start.10
  202.4 17.0 %collective-permute-start.32 = (bf16[8,2,90,8,128]{4,3,2,1,0:T(8,128)(2,1)S(1)}, bf16[8,2,90,8,128]{4,3,2,1,0:T(8,128)(2,1)S(1)}, u32[]{:S(2)}, u32[]{:S(2)}) collective-permute-start(bf16[8,2,90,8,128]{4,3,2,1,0:T(8,128)(2,1)S(1)} %get-tuple-element.42), channel_id=1, source_target_pairs={{0,16},{16,0},{1,17},{17,1},{2,18},{18,2},{3,19},{19,3},{4,20},{20... | collective-permute-start | bytes 8847368 | tf_op jit(solution)/shard_map/ppermute | solution.py:339
  221.7 41.9 %all-to-all-start.1 = ((bf16[16,90,8,128]{3,2,1,0:T(8,128)(2,1)}), bf16[16,90,8,128]{3,2,1,0:T(8,128)(2,1)S(1)}, u32[]{:S(2)}, u32[]{:S(2)}) async-start(bf16[16,90,8,128]{3,2,1,0:T(8,128)(2,1)} %bitcast.59), calls=%async_computation.2 | async-start | bytes 5898240 | tf_op jit(solution)/shard_map/all_to_all | solution.py:342
  264.8 16.5 %collective-permute-start.33 = (f32[16,8,128]{2,1,0:T(8,128)S(1)}, f32[16,8,128]{2,1,0:T(8,128)S(1)}, u32[]{:S(2)}, u32[]{:S(2)}) collective-permute-start(f32[16,8,128]{2,1,0:T(8,128)S(1)} %slice.30), channel_id=1, source_target_pairs={{0,0},{1,16},{2,32},{3,48},{4,64},{5,80},{6,96},{7,112},{16,128},{... | collective-permute-start | bytes 196616 | tf_op jit(solution)/shard_map/ppermute | solution.py:427
  271.5 15.1 %all-to-all-start.2 = ((f32[8,32,128]{2,1,0:T(8,128)}), f32[8,32,128]{2,1,0:T(8,128)S(1)}, u32[]{:S(2)}, u32[]{:S(2)}) async-start(f32[8,32,128]{2,1,0:T(8,128)} %bitcast.21), calls=%async_computation.3 | async-start | bytes 262144 | tf_op jit(solution)/shard_map/all_to_all | solution.py:431
  277.1 12.0 %copy-start.30 = (bf16[8,128,256]{2,1,0:T(8,128)(2,1)S(1)}, bf16[8,128,256]{2,1,0:T(8,128)(2,1)}, u32[]{:S(2)}) copy-start(bf16[8,128,256]{2,1,0:T(8,128)(2,1)} %reduce-scatter.2.cloned.1.call-done) | copy-start | bytes 1572868
  278.2 10.9 %collective-permute-start.31 = (bf16[512,256]{1,0:T(8,128)(2,1)S(1)}, bf16[512,256]{1,0:T(8,128)(2,1)S(1)}, u32[]{:S(2)}, u32[]{:S(2)}) collective-permute-start(bf16[512,256]{1,0:T(8,128)(2,1)S(1)} %dynamic-slice_bitcast_fusion), channel_id=1, source_target_pairs={{0,8},{8,0},{1,9},{9,1},{2,10},{10,2},{3,11},{11,3},{4,12},{12,4},... | collective-permute-start | bytes 786440 | tf_op jit(solution)/shard_map/ppermute | solution.py:314
  (6 other events, 4.2 us)
Sparse Core Ops, SparseCore 0:
  51.7 52.0 all-gather.2
  177.0 64.2 reduce-scatter.1

commit v4 on v3

--- a/solution.py
+++ b/solution.py
@@ -232,7 +232,7 @@
         in_specs=[SM if a.dtype == jnp.int32 else VM for a in args],
         out_specs=[VM] * len(outs),
         scratch_shapes=[pltpu.VMEM(shape, dtype) for shape, dtype in scratch],
-        compiler_params=pltpu.CompilerParams(vmem_limit_bytes=48 << 20),
+        compiler_params=pltpu.CompilerParams(vmem_limit_bytes=60 << 20),
         cost_estimate=pl.CostEstimate(flops=flops, bytes_accessed=moved, transcendentals=0),
     )(*args)
 
@@ -291,7 +291,7 @@
         out_shape=[jax.ShapeDtypeStruct(shape, BF)] * 2,
         in_specs=[SM] + specs,
         out_specs=[pl.BlockSpec(shape, lambda step: (0,) * 5)] * 2,
-        compiler_params=pltpu.CompilerParams(vmem_limit_bytes=32 << 20),
+        compiler_params=pltpu.CompilerParams(vmem_limit_bytes=60 << 20),
         cost_estimate=pl.CostEstimate(flops=6 * ONE, bytes_accessed=moved, transcendentals=0),
     )(where, *args)
 
@@ -322,17 +322,18 @@
     return own.reshape(blocks, BLOCK, half), other.reshape(blocks, BLOCK, half)
 
 
-def ring_gather(own, other):
+def ring_step(step, right, left, found):
     count = size("z")
-    found = [[None, None] for _ in range(count)]
-    found[0] = [own, other]
-    right, left = [own, other], [own, other]
-    for step in range(1, count // 2):
-        for k in range(2):
-            right[k], left[k] = shift(right[k], 1), shift(left[k], -1)
-            found[count - step][k], found[step][k] = right[k], left[k]
-    found[count // 2] = [shift(right[0], 1), shift(left[1], -1)]
-    return [shard for pair in found for shard in pair]
+    if step < count // 2:
+        right, left = [shift(v, 1) for v in right], [shift(v, -1) for v in left]
+        found[count - step], found[step] = right, left
+    else:
+        found[step] = [shift(right[0], 1), shift(left[1], -1)]
+    return right, left
+
+
+def flat(found):
+    return [shard for step in range(size("z")) for shard in found[step]]
 
 
 def sum_groups(keep, send):
@@ -392,18 +393,27 @@
     table = swap_table()
     x_own, x_other = halves(activations, me)
     dy_own, dy_other = halves(cotangent, me)
-    xs = ring_gather(x_own, x_other)
-    dys = ring_gather(dy_own, dy_other)
-    weights = (gate_first, up_first, down_second)
-    begun = (x_other, dy_other, xs[2], xs[14], dys[2], dys[14])
-    weights, _ = lax.optimization_barrier((weights, begun))
-    first = share_first(*weights)
+    first = share_first(gate_first, up_first, down_second)
     second = share_second(gate_second, up_second, down_first)
     held = lax.all_gather(jnp.concatenate([first, second]), GROUP, axis=0, tiled=False)
 
-    x, gate_in, up_in = forward_first(where, table, held, xs)
+    steps = nz // 2
+    xs, dys = {0: [x_own, x_other]}, {0: [dy_own, dy_other]}
+    state = (xs[0], xs[0])
+    for step in range(1, steps + 1):
+        state = ring_step(step, *state, xs)
+    state, _ = lax.optimization_barrier(((dys[0], dys[0]), (xs[2], xs[nz - 2])))
+    for step in range(1, steps - 1):
+        state = ring_step(step, *state, dys)
+    shards_x, _ = lax.optimization_barrier((flat(xs), state))
+    x, gate_in, up_in = forward_first(where, table, held, shards_x)
+    state = ring_step(steps - 1, *state, dys)
+    state, gate_in, up_in = lax.optimization_barrier((state, gate_in, up_in))
+    ring_step(steps, *state, dys)
     act, to_gate, to_up, down_in = forward_second(table, held, gate_in, up_in)
-    dy, back_in, gate_back, up_back, low, parts = backward(where, table, held, to_gate, to_up, dys)
+    dy, back_in, gate_back, up_back, low, parts = backward(
+        where, table, held, to_gate, to_up, flat(dys)
+    )
 
     total = lax.psum_scatter(parts, "z", scatter_dimension=0, tiled=True)
     total = total.reshape(nh, per * BLOCK, half)

time: 298 us -> 278 us (0.933)
  local copies, waits for them, and re-layouts: 37.5 us -> 7.29 us
  Pallas kernels: 68.3 us -> 76.7 us
  starting transfers between devices: 79.6 us -> 74.4 us
  waiting for transfers between devices: 90.5 us -> 95.3 us
    unnamed x64, local copies, waits for them, and re-layouts: 29.8 us -> 1.56 us
    ppermute x28, starting transfers between devices: 32.6 us -> 20.9 us  [shift(): lax.ppermute(value, 'z', [(i, (i + step) % count) for i in range(count)])]
    ppermute x28, waiting for transfers between devices: 29.9 us -> 39.5 us  [shift(): lax.ppermute(value, 'z', [(i, (i + step) % count) for i in range(count)])]
    ppermute x4, waiting for transfers between devices: 11.1 us -> 6.12 us  [swap(): return lax.ppermute(value, 'x_hi', [(0, 1), (1, 0)])]
    pallas_call x1, Pallas kernels: 14.7 us -> 19.4 us  [grads(): pl.pallas_call(grads_kernel, grid=(NBD // PER,), out_shape=[jax.ShapeDtyp...]
    all_to_all x1, starting transfers between devices: 7.48 us -> 11.6 us  [share_first(): return lax.all_to_all(first, TENSOR, 0, 0, tiled=True)]
    pallas_call x3, Pallas kernels: 53.6 us -> 57.2 us  [call(): pl.pallas_call(kernel, out_shape=shapes, in_specs=[SM if a.dtype == jnp.i...]
  transfers between devices with their start and end apart: 39 -> 39, of which waited for: 17 -> 18; matrix products, arithmetic and copies ran while one was open for 4% -> 4% of each run, Pallas kernels for 14% -> 17%
where the time goes in v4:
time: 278 us
  waiting for transfers between devices  95.3 us (34%)
  Pallas kernels  76.7 us (28%)
  starting transfers between devices  74.4 us (27%)
  between operations  14.6 us (5%)
  other arithmetic  9.31 us (3%)
  local copies, waits for them, and re-layouts  7.29 us (3%)
    pallas_call x3, Pallas kernels, call(): pl.pallas_call(kernel, out_shape=shapes, in_specs=[SM if a.dtype == jnp.i...  57.2 us
    ppermute x28, waiting for transfers between devices, shift(): lax.ppermute(value, 'z', [(i, (i + step) % count) for i in range(count)])  39.5 us
    all_to_all x1, waiting for transfers between devices, sum_groups(): return lax.all_to_all(pairs, CHIPS, 0, 0, tiled=True)  37 us
    ppermute x28, starting transfers between devices, shift(): lax.ppermute(value, 'z', [(i, (i + step) % count) for i in range(count)])  20.9 us
    pallas_call x1, Pallas kernels, grads(): pl.pallas_call(grads_kernel, grid=(NBD // PER,), out_shape=[jax.ShapeDtyp...  19.4 us
    ppermute x1, starting transfers between devices, sum_groups(): found = lax.ppermute(send, 'core', [(0, 1), (1, 0)])  13.7 us
    all_to_all x1, starting transfers between devices, share_first(): return lax.all_to_all(first, TENSOR, 0, 0, tiled=True)  11.6 us
    ppermute x4, starting transfers between devices, swap(): return lax.ppermute(value, 'x_hi', [(0, 1), (1, 0)])  10.2 us
  transfers between devices with their start and end apart: 39, of which 18 were waited for; matrix products, arithmetic and copies ran while one was open for 4% of the time, Pallas kernels for 17%

profile of v4, /device:TPU:1, one launch (start us, length us, event | category | flops | bytes accessed | tf_op | source)
XLA Modules:
  0.0 277.6 jit_solution(17795853458073364964)
XLA Ops:
  7.2 1.1 fusion
  8.5 0.8 broadcast_in_dim.2
  9.2 11.6 %all-to-all-start = ((bf16[16,64,128]{2,1,0:T(8,128)(2,1)}), bf16[16,64,128]{2,1,0:T(8,128)(2,1)S(1)}, u32[]{:S(2)}, u32[]{:S(2)}) async-start(bf16[16,64,128]{2,1,0:T(8,128)(2,1)} %bitcast.10), calls=%async_computation | async-start | bytes 524288 | tf_op jit(solution)/shard_map/all_to_all | solution.py:360
  20.9 1.0 select_select_fusion
  21.9 3.0 %collective-permute-start = (bf16[3,128,128]{2,1,0:T(8,128)(2,1)S(1)}, bf16[3,128,128]{2,1,0:T(8,128)(2,1)S(1)}, u32[]{:S(2)}, u32[]{:S(2)}) collective-permute-start(bf16[3,128,128]{2,1,0:T(8,128)(2,1)S(1)} %select_select_fusion), channel_id=1, source_target_pairs={{0,8},{8,0},{1,9},{9,1},{2,10},{10,2},{3,11},{11,3},{4,12},{12,4},... | collective-permute-start | bytes 294920 | tf_op jit(solution)/shard_map/ppermute | solution.py:314
  24.9 3.4 %collective-permute-done = bf16[3,128,128]{2,1,0:T(8,128)(2,1)S(1)} collective-permute-done((bf16[3,128,128]{2,1,0:T(8,128)(2,1)S(1)}, bf16[3,128,128]{2,1,0:T(8,128)(2,1)S(1)}, u32[]{:S(2)}, u32[]{:S(2)}) %collective-permute-start) | collective-permute-done | bytes 98336 | tf_op jit(solution)/shard_map/ppermute | solution.py:314
  28.3 2.8 all-to-all-done
  31.0 0.8 pad_maximum_fusion.1
  32.0 1.5 collective-permute-start.7
  33.5 1.9 collective-permute-start.4
  35.4 3.1 %collective-permute-done.7.refs_14_ = bf16[4,128,256]{2,1,0:T(8,128)(2,1)S(1)} collective-permute-done((bf16[4,128,256]{2,1,0:T(8,128)(2,1)S(1)}, bf16[4,128,256]{2,1,0:T(8,128)(2,1)S(1)}, u32[]{:S(2)}, u32[]{:S(2)}) %collective-permute-start.7) | collective-permute-done | bytes 262176 | tf_op jit(solution)/shard_map/ppermute | solution.py:310
  38.5 0.2 collective-permute-start.8
  38.7 1.5 collective-permute-done.4
  40.3 2.6 collective-permute-start.5
  43.0 1.9 collective-permute-done.8.refs_12_
  44.9 4.7 %collective-permute-done.9.refs_15_ = bf16[4,128,256]{2,1,0:T(8,128)(2,1)S(1)} collective-permute-done((bf16[4,128,256]{2,1,0:T(8,128)(2,1)S(1)}, bf16[4,128,256]{2,1,0:T(8,128)(2,1)S(1)}, u32[]{:S(2)}, u32[]{:S(2)}) %collective-permute-start.9) | collective-permute-done | bytes 262176 | tf_op jit(solution)/shard_map/ppermute | solution.py:310
  49.7 2.9 %collective-permute-start.1 = (bf16[512,256]{1,0:T(8,128)(2,1)S(1)}, bf16[512,256]{1,0:T(8,128)(2,1)S(1)}, u32[]{:S(2)}, u32[]{:S(2)}) collective-permute-start(bf16[512,256]{1,0:T(8,128)(2,1)S(1)} %get-tuple-element.112), channel_id=1, source_target_pairs={{0,8},{8,0},{1,9},{9,1},{2,10},{10,2},{3,11},{11,3},{4,12},{12,4},... | collective-permute-start | bytes 786440 | tf_op jit(solution)/shard_map/ppermute | solution.py:314
  52.6 1.9 collective-permute-start.6
  54.6 0.6 collective-permute-done.25.refs_10_
  55.3 0.7 collective-permute-start.26
  56.0 4.9 %collective-permute-done.10.refs_13_ = bf16[4,128,256]{2,1,0:T(8,128)(2,1)S(1)} collective-permute-done((bf16[4,128,256]{2,1,0:T(8,128)(2,1)S(1)}, bf16[4,128,256]{2,1,0:T(8,128)(2,1)S(1)}, u32[]{:S(2)}, u32[]{:S(2)}) %collective-permute-start.10) | collective-permute-done | bytes 262176 | tf_op jit(solution)/shard_map/ppermute | solution.py:310
  60.9 1.2 collective-permute-done.1
  62.1 1.1 collective-permute-start.11
  63.2 2.4 collective-permute-start.14
  65.6 0.3 collective-permute-start.17
  65.9 0.6 collective-permute-done.26.refs_8_
  66.5 0.8 collective-permute-start.20
  67.2 4.9 %collective-permute-done.28.refs_11_ = bf16[4,128,256]{2,1,0:T(8,128)(2,1)S(1)} collective-permute-done((bf16[4,128,256]{2,1,0:T(8,128)(2,1)S(1)}, bf16[4,128,256]{2,1,0:T(8,128)(2,1)S(1)}, u32[]{:S(2)}, u32[]{:S(2)}) %collective-permute-start.28) | collective-permute-done | bytes 262176 | tf_op jit(solution)/shard_map/ppermute | solution.py:310
  72.1 0.8 collective-permute-start.24
  72.9 4.9 %collective-permute-done.11.refs_14_ = bf16[4,128,256]{2,1,0:T(8,128)(2,1)S(1)} collective-permute-done((bf16[4,128,256]{2,1,0:T(8,128)(2,1)S(1)}, bf16[4,128,256]{2,1,0:T(8,128)(2,1)S(1)}, u32[]{:S(2)}, u32[]{:S(2)}) %collective-permute-start.11) | collective-permute-done | bytes 262176 | tf_op jit(solution)/shard_map/ppermute | solution.py:310
  77.7 5.6 %collective-permute-done.14.refs_15_ = bf16[4,128,256]{2,1,0:T(8,128)(2,1)S(1)} collective-permute-done((bf16[4,128,256]{2,1,0:T(8,128)(2,1)S(1)}, bf16[4,128,256]{2,1,0:T(8,128)(2,1)S(1)}, u32[]{:S(2)}, u32[]{:S(2)}) %collective-permute-start.14) | collective-permute-done | bytes 262176 | tf_op jit(solution)/shard_map/ppermute | solution.py:310
  83.4 2.7 collective-permute-start.18
  86.2 2.7 collective-permute-done.12.refs_12_
  89.0 5.6 %collective-permute-done.15.refs_13_ = bf16[4,128,256]{2,1,0:T(8,128)(2,1)S(1)} collective-permute-done((bf16[4,128,256]{2,1,0:T(8,128)(2,1)S(1)}, bf16[4,128,256]{2,1,0:T(8,128)(2,1)S(1)}, u32[]{:S(2)}, u32[]{:S(2)}) %collective-permute-start.15) | collective-permute-done | bytes 262176 | tf_op jit(solution)/shard_map/ppermute | solution.py:310
  94.6 2.7 collective-permute-start.19
  97.5 0.6 pad_add_fusion.where
  98.1 12.5 %shard_map.144 = (bf16[64,128,256]{2,1,0:T(8,128)(2,1)}, bf16[64,64,256]{2,1,0:T(8,128)(2,1)}, bf16[64,64,256]{2,1,0:T(8,128)(2,1)}) custom-call(s32[3]{0:T(128)} %pad_add_fusion.where, bf16[256,256]{1,0:T(8,128)(2,1)} %constant.81.clone.swap, bf16[16,28,64,128]{3,2,1,0:T(8,128)(2,1)} %bitcast.44, bf16[4,128,256]{2,1,0:T(8,128)(2,1)} %bitcast.54, ...), custom_call_target="tpu_custom_call" | custom-call | flops 1409286144 | bytes 11665420 | tf_op jit(solution)/shard_map/pallas_call | solution.py:229
  110.7 1.5 collective-permute-start.29
  112.2 1.2 collective-permute-start.30
  113.5 16.1 %shard_map.145 = (bf16[28,128,256]{2,1,0:T(8,128)(2,1)}, f32[28,128,256]{2,1,0:T(8,128)}, f32[28,128,256]{2,1,0:T(8,128)}, bf16[64,64,256]{2,1,0:T(8,128)(2,1)}) custom-call(bf16[256,256]{1,0:T(8,128)(2,1)} %constant.81.clone.swap, bf16[16,28,64,128]{3,2,1,0:T(8,128)(2,1)} %bitcast.45, bf16[64,64,256]{2,1,0:T(8,128)(2,1)} %get-tuple-element.68.gate_in, ...), custom_call_target="tpu_custom_call" | custom-call | flops 1174405120 | bytes 11665408 | tf_op jit(solution)/shard_map/pallas_call | solution.py:229
  129.6 0.7 copy-done.16
  130.4 28.6 %shard_map.146 = (bf16[64,128,256]{2,1,0:T(8,128)(2,1)}, bf16[64,64,256]{2,1,0:T(8,128)(2,1)}, bf16[28,128,256]{2,1,0:T(8,128)(2,1)}, bf16[28,128,256]{2,1,0:T(8...) custom-call(s32[3]{0:T(128)} %pad_add_fusion.where, bf16[256,256]{1,0:T(8,128)(2,1)} %constant.81.clone.swap, ...), custom_call_target="tpu_custom_call" | custom-call | flops 2818572288 | bytes 19005452 | tf_op jit(solution)/shard_map/pallas_call | solution.py:229
  159.1 19.4 %shard_map.147 = (bf16[8,2,90,8,128]{4,3,2,1,0:T(8,128)(2,1)}, bf16[8,2,90,8,128]{4,3,2,1,0:T(8,128)(2,1)}) custom-call(s32[3]{0:T(128)} %pad_add_fusion.where, bf16[64,128,256]{2,1,0:T(8,128)(2,1)} %get-tuple-element.75.x, bf16[64,128,256]{2,1,0:T(8,128)(2,1)} %get-tuple-element.76.low, bf16[64,128,256]{2,1,0:T(8,128)(2,1)} %get-tuple-element.77.dy, ...), custom_call_target="tpu_custom_call" | custom-call | flops 1409286144 | bytes 26476544 | tf_op jit(solution)/shard_map/pallas_call | solution.py:288
  178.5 13.7 %collective-permute-start.32 = (bf16[8,2,90,8,128]{4,3,2,1,0:T(8,128)(2,1)}, bf16[8,2,90,8,128]{4,3,2,1,0:T(8,128)(2,1)S(1)}, u32[]{:S(2)}, u32[]{:S(2)}) collective-permute-start(bf16[8,2,90,8,128]{4,3,2,1,0:T(8,128)(2,1)} %get-tuple-element.84), channel_id=1, source_target_pairs={{0,16},{16,0},{1,17},{17,1},{2,18},{18,2},{3,19},{19,3},{4,20},{20... | collective-permute-start | bytes 8847368 | tf_op jit(solution)/shard_map/ppermute | solution.py:340
  192.2 5.2 %collective-permute-done.32 = bf16[8,2,90,8,128]{4,3,2,1,0:T(8,128)(2,1)S(1)} collective-permute-done((bf16[8,2,90,8,128]{4,3,2,1,0:T(8,128)(2,1)}, bf16[8,2,90,8,128]{4,3,2,1,0:T(8,128)(2,1)S(1)}, u32[]{:S(2)}, u32[]{:S(2)}) %collective-permute-start.32) | collective-permute-done | bytes 2949152 | tf_op jit(solution)/shard_map/ppermute | solution.py:340
  197.4 4.4 %add_convert_fusion = bf16[8,2,90,8,128]{4,3,2,1,0:T(8,128)(2,1)} fusion(bf16[8,2,90,8,128]{4,3,2,1,0:T(8,128)(2,1)S(1)} %collective-permute-done.32, bf16[8,2,90,8,128]{4,3,2,1,0:T(8,128)(2,1)} %get-tuple-element.83), kind=kLoop, calls=%fused_computation.1 | loop fusion | flops 5898240 | bytes 8847360 | tf_op jit(solution)/shard_map/convert_element_type | solution.py:341
  201.8 5.5 %all-to-all-start.1 = ((bf16[16,90,8,128]{3,2,1,0:T(8,128)(2,1)}), bf16[16,90,8,128]{3,2,1,0:T(8,128)(2,1)S(1)}, u32[]{:S(2)}, u32[]{:S(2)}) async-start(bf16[16,90,8,128]{3,2,1,0:T(8,128)(2,1)} %bitcast.47), calls=%async_computation.2 | async-start | bytes 5898240 | tf_op jit(solution)/shard_map/all_to_all | solution.py:343
  207.4 37.0 %all-to-all-done.1 = bf16[16,90,8,128]{3,2,1,0:T(8,128)(2,1)S(1)} async-done(((bf16[16,90,8,128]{3,2,1,0:T(8,128)(2,1)}), bf16[16,90,8,128]{3,2,1,0:T(8,128)(2,1)S(1)}, u32[]{:S(2)}, u32[]{:S(2)}) %all-to-all-start.1) | async-done | bytes 2949152 | tf_op jit(solution)/shard_map/all_to_all | solution.py:343
  244.4 0.4 convert_reduce_fusion
  244.9 0.7 slice.28
  245.5 6.7 %collective-permute-start.33 = (f32[16,8,128]{2,1,0:T(8,128)S(1)}, f32[16,8,128]{2,1,0:T(8,128)S(1)}, u32[]{:S(2)}, u32[]{:S(2)}) collective-permute-start(f32[16,8,128]{2,1,0:T(8,128)S(1)} %slice.30), channel_id=1, source_target_pairs={{0,0},{1,16},{2,32},{3,48},{4,64},{5,80},{6,96},{7,112},{16,128},{... | collective-permute-start | bytes 196616 | tf_op jit(solution)/shard_map/ppermute | solution.py:437
  252.3 5.6 %all-to-all-start.2 = ((f32[8,32,128]{2,1,0:T(8,128)}), f32[8,32,128]{2,1,0:T(8,128)S(1)}, u32[]{:S(2)}, u32[]{:S(2)}) async-start(f32[8,32,128]{2,1,0:T(8,128)} %bitcast.21), calls=%async_computation.3 | async-start | bytes 262144 | tf_op jit(solution)/shard_map/all_to_all | solution.py:441
  257.9 1.0 dynamic-slice_bitcast_fusion
  259.0 2.5 collective-permute-start.31
  261.4 0.7 fusion.2
  262.1 0.7 copy.30
  262.8 4.7 %all-to-all-done.2 = f32[8,32,128]{2,1,0:T(8,128)S(1)} async-done(((f32[8,32,128]{2,1,0:T(8,128)}), f32[8,32,128]{2,1,0:T(8,128)S(1)}, u32[]{:S(2)}, u32[]{:S(2)}) %all-to-all-start.2) | async-done | bytes 131104 | tf_op jit(solution)/shard_map/all_to_all | solution.py:441
  267.4 0.2 reshape.80
  267.6 0.3 reshape.81
  268.0 0.2 copy.29
  268.2 0.8 unstack.27
  269.0 0.2 copy.28
  269.1 0.8 unstack.25
  269.9 0.8 pad_maximum_fusion
  (113 shorter events, 1.3 us)
Async XLA Ops:
  7.2 24.8 %copy-start.3 = (bf16[512,512]{1,0:T(8,128)(2,1)S(1)}, bf16[512,512]{1,0:T(8,128)(2,1)}, u32[]{:S(2)}) copy-start(bf16[512,512]{1,0:T(8,128)(2,1)} %param.9) | copy-start | bytes 1572868
  7.2 42.4 %copy-start.4 = (bf16[512,512]{1,0:T(8,128)(2,1)S(1)}, bf16[512,512]{1,0:T(8,128)(2,1)}, u32[]{:S(2)}) copy-start(bf16[512,512]{1,0:T(8,128)(2,1)} %param.10) | copy-start | bytes 1572868
  9.2 21.8 %all-to-all-start = ((bf16[16,64,128]{2,1,0:T(8,128)(2,1)}), bf16[16,64,128]{2,1,0:T(8,128)(2,1)S(1)}, u32[]{:S(2)}, u32[]{:S(2)}) async-start(bf16[16,64,128]{2,1,0:T(8,128)(2,1)} %bitcast.10), calls=%async_computation | async-start | bytes 524288 | tf_op jit(solution)/shard_map/all_to_all | solution.py:360
  20.8 77.3 %all-gather.3.cloned.1.call-start = ((), (), s32[]{:S(2)}) async-start(), calls=%async_computation.5 | async-start | bytes 7798784 | tf_op jit(solution)/shard_map/all_gather | solution.py:398
  21.9 6.3 %collective-permute-start = (bf16[3,128,128]{2,1,0:T(8,128)(2,1)S(1)}, bf16[3,128,128]{2,1,0:T(8,128)(2,1)S(1)}, u32[]{:S(2)}, u32[]{:S(2)}) collective-permute-start(bf16[3,128,128]{2,1,0:T(8,128)(2,1)S(1)} %select_select_fusion), channel_id=1, source_target_pairs={{0,8},{8,0},{1,9},{9,1},{2,10},{10,2},{3,11},{11,3},{4,12},{12,4},... | collective-permute-start | bytes 294920 | tf_op jit(solution)/shard_map/ppermute | solution.py:314
  31.9 226.1 %reduce-scatter.2.cloned.1.call-start = ((), (), s32[]{:S(2)}) async-start(), calls=%async_computation.4 | async-start | bytes 4718592 | tf_op jit(solution)/shard_map/reduce_scatter | solution.py:418
  32.0 66.1 %copy-start.1 = (bf16[512,256]{1,0:T(8,128)(2,1)}, bf16[512,256]{1,0:T(8,128)(2,1)S(1)}, u32[]{:S(2)}) copy-start(bf16[512,256]{1,0:T(8,128)(2,1)S(1)} %get-tuple-element.111) | copy-start | bytes 786436
  32.0 6.5 %collective-permute-start.7 = (bf16[4,128,256]{2,1,0:T(8,128)(2,1)S(1)}, bf16[4,128,256]{2,1,0:T(8,128)(2,1)S(1)}, u32[]{:S(2)}, u32[]{:S(2)}) collective-permute-start(bf16[4,128,256]{2,1,0:T(8,128)(2,1)S(1)} %bitcast.52), channel_id=1, source_target_pairs={{0,1},{1,2},{2,3},{3,4},{4,5},{5,6},{6,7},{7,0},{8,9},{9,10},{10,1... | collective-permute-start | bytes 786440 | tf_op jit(solution)/shard_map/ppermute | solution.py:310
  33.5 6.7 %collective-permute-start.4 = (bf16[512,256]{1,0:T(8,128)(2,1)S(1)}, bf16[512,256]{1,0:T(8,128)(2,1)S(1)}, u32[]{:S(2)}, u32[]{:S(2)}) collective-permute-start(bf16[512,256]{1,0:T(8,128)(2,1)S(1)} %get-tuple-element.110), channel_id=1, source_target_pairs={{0,8},{8,0},{1,9},{9,1},{2,10},{10,2},{3,11},{11,3},{4,12},{12,4},... | collective-permute-start | bytes 786440 | tf_op jit(solution)/shard_map/ppermute | solution.py:314
  35.4 7.5 %collective-permute-start.2 = (bf16[4,128,256]{2,1,0:T(8,128)(2,1)S(1)}, bf16[4,128,256]{2,1,0:T(8,128)(2,1)S(1)}, u32[]{:S(2)}, u32[]{:S(2)}) collective-permute-start(bf16[4,128,256]{2,1,0:T(8,128)(2,1)S(1)} %bitcast.53), channel_id=1, source_target_pairs={{0,7},{1,0},{2,1},{3,2},{4,3},{5,4},{6,5},{7,6},{8,15},{9,8},{10,9... | collective-permute-start | bytes 786440 | tf_op jit(solution)/shard_map/ppermute | solution.py:310
  38.5 6.4 %collective-permute-start.8 = (bf16[4,128,256]{2,1,0:T(8,128)(2,1)S(1)}, bf16[4,128,256]{2,1,0:T(8,128)(2,1)S(1)}, u32[]{:S(2)}, u32[]{:S(2)}) collective-permute-start(bf16[4,128,256]{2,1,0:T(8,128)(2,1)S(1)} %collective-permute-done.7.refs_14_), channel_id=1, source_target_pairs={{0,1},{1,2},{2,3},{3,4},{4,5},{5,6},{6,7},{7,0},{8,9},{9,10},{10,1... | collective-permute-start | bytes 786440 | tf_op jit(solution)/shard_map/ppermute | solution.py:310
  40.2 21.9 %copy-start.19 = (bf16[512,256]{1,0:T(8,128)(2,1)}, bf16[512,256]{1,0:T(8,128)(2,1)S(1)}, u32[]{:S(2)}) copy-start(bf16[512,256]{1,0:T(8,128)(2,1)S(1)} %collective-permute-done.4) | copy-start | bytes 786436
  40.2 9.4 %collective-permute-start.9 = (bf16[4,128,256]{2,1,0:T(8,128)(2,1)S(1)}, bf16[4,128,256]{2,1,0:T(8,128)(2,1)S(1)}, u32[]{:S(2)}, u32[]{:S(2)}) collective-permute-start(bf16[4,128,256]{2,1,0:T(8,128)(2,1)S(1)} %bitcast.64), channel_id=1, source_target_pairs={{0,1},{1,2},{2,3},{3,4},{4,5},{5,6},{6,7},{7,0},{8,9},{9,10},{10,1... | collective-permute-start | bytes 786440 | tf_op jit(solution)/shard_map/ppermute | solution.py:310
  40.3 12.3 %collective-permute-start.5 = (bf16[4,128,256]{2,1,0:T(8,128)(2,1)S(1)}, bf16[4,128,256]{2,1,0:T(8,128)(2,1)S(1)}, u32[]{:S(2)}, u32[]{:S(2)}) collective-permute-start(bf16[4,128,256]{2,1,0:T(8,128)(2,1)S(1)} %bitcast.65), channel_id=1, source_target_pairs={{0,7},{1,0},{2,1},{3,2},{4,3},{5,4},{6,5},{7,6},{8,15},{9,8},{10,9... | collective-permute-start | bytes 786440 | tf_op jit(solution)/shard_map/ppermute | solution.py:310
  42.9 54.3 %copy-start.20 = (bf16[4,128,256]{2,1,0:T(8,128)(2,1)}, bf16[4,128,256]{2,1,0:T(8,128)(2,1)S(1)}, u32[]{:S(2)}) copy-start(bf16[4,128,256]{2,1,0:T(8,128)(2,1)S(1)} %collective-permute-done.2.refs_2_) | copy-start | bytes 786436
  42.9 11.6 %collective-permute-start.3 = (bf16[4,128,256]{2,1,0:T(8,128)(2,1)S(1)}, bf16[4,128,256]{2,1,0:T(8,128)(2,1)S(1)}, u32[]{:S(2)}, u32[]{:S(2)}) collective-permute-start(bf16[4,128,256]{2,1,0:T(8,128)(2,1)S(1)} %collective-permute-done.2.refs_2_), channel_id=1, source_target_pairs={{0,7},{1,0},{2,1},{3,2},{4,3},{5,4},{6,5},{7,6},{8,15},{9,8},{10,9... | collective-permute-start | bytes 786440 | tf_op jit(solution)/shard_map/ppermute | solution.py:310
  44.9 52.3 %copy-start.21 = (bf16[4,128,256]{2,1,0:T(8,128)(2,1)}, bf16[4,128,256]{2,1,0:T(8,128)(2,1)S(1)}, u32[]{:S(2)}) copy-start(bf16[4,128,256]{2,1,0:T(8,128)(2,1)S(1)} %collective-permute-done.8.refs_12_) | copy-start | bytes 786436
  44.9 10.3 %collective-permute-start.25 = (bf16[4,128,256]{2,1,0:T(8,128)(2,1)S(1)}, bf16[4,128,256]{2,1,0:T(8,128)(2,1)S(1)}, u32[]{:S(2)}, u32[]{:S(2)}) collective-permute-start(bf16[4,128,256]{2,1,0:T(8,128)(2,1)S(1)} %collective-permute-done.8.refs_12_), channel_id=1, source_target_pairs={{0,1},{1,2},{2,3},{3,4},{4,5},{5,6},{6,7},{7,0},{8,9},{9,10},{10,1... | collective-permute-start | bytes 786440 | tf_op jit(solution)/shard_map/ppermute | solution.py:310
  49.6 47.6 %copy-start.22 = (bf16[4,128,256]{2,1,0:T(8,128)(2,1)}, bf16[4,128,256]{2,1,0:T(8,128)(2,1)S(1)}, u32[]{:S(2)}) copy-start(bf16[4,128,256]{2,1,0:T(8,128)(2,1)S(1)} %collective-permute-done.9.refs_15_) | copy-start | bytes 786436
  49.6 11.2 %collective-permute-start.10 = (bf16[4,128,256]{2,1,0:T(8,128)(2,1)S(1)}, bf16[4,128,256]{2,1,0:T(8,128)(2,1)S(1)}, u32[]{:S(2)}, u32[]{:S(2)}) collective-permute-start(bf16[4,128,256]{2,1,0:T(8,128)(2,1)S(1)} %collective-permute-done.9.refs_15_), channel_id=1, source_target_pairs={{0,1},{1,2},{2,3},{3,4},{4,5},{5,6},{6,7},{7,0},{8,9},{9,10},{10,1... | collective-permute-start | bytes 786440 | tf_op jit(solution)/shard_map/ppermute | solution.py:310
  49.7 60.9 %copy-start = (bf16[512,256]{1,0:T(8,128)(2,1)}, bf16[512,256]{1,0:T(8,128)(2,1)S(1)}, u32[]{:S(2)}) copy-start(bf16[512,256]{1,0:T(8,128)(2,1)S(1)} %get-tuple-element.113) | copy-start | bytes 786436
  49.7 12.4 %collective-permute-start.1 = (bf16[512,256]{1,0:T(8,128)(2,1)S(1)}, bf16[512,256]{1,0:T(8,128)(2,1)S(1)}, u32[]{:S(2)}, u32[]{:S(2)}) collective-permute-start(bf16[512,256]{1,0:T(8,128)(2,1)S(1)} %get-tuple-element.112), channel_id=1, source_target_pairs={{0,8},{8,0},{1,9},{9,1},{2,10},{10,2},{3,11},{11,3},{4,12},{12,4},... | collective-permute-start | bytes 786440 | tf_op jit(solution)/shard_map/ppermute | solution.py:314
  52.6 44.6 %copy-start.23 = (bf16[4,128,256]{2,1,0:T(8,128)(2,1)}, bf16[4,128,256]{2,1,0:T(8,128)(2,1)S(1)}, u32[]{:S(2)}) copy-start(bf16[4,128,256]{2,1,0:T(8,128)(2,1)S(1)} %collective-permute-done.5.refs_3_) | copy-start | bytes 786436
  52.6 9.5 %collective-permute-start.6 = (bf16[4,128,256]{2,1,0:T(8,128)(2,1)S(1)}, bf16[4,128,256]{2,1,0:T(8,128)(2,1)S(1)}, u32[]{:S(2)}, u32[]{:S(2)}) collective-permute-start(bf16[4,128,256]{2,1,0:T(8,128)(2,1)S(1)} %collective-permute-done.5.refs_3_), channel_id=1, source_target_pairs={{0,7},{1,0},{2,1},{3,2},{4,3},{5,4},{6,5},{7,6},{8,15},{9,8},{10,9... | collective-permute-start | bytes 786440 | tf_op jit(solution)/shard_map/ppermute | solution.py:310
  54.5 42.8 %copy-start.24 = (bf16[4,128,256]{2,1,0:T(8,128)(2,1)}, bf16[4,128,256]{2,1,0:T(8,128)(2,1)S(1)}, u32[]{:S(2)}) copy-start(bf16[4,128,256]{2,1,0:T(8,128)(2,1)S(1)} %collective-permute-done.3.refs_4_) | copy-start | bytes 786436
  54.5 11.1 %collective-permute-start.23 = (bf16[4,128,256]{2,1,0:T(8,128)(2,1)S(1)}, bf16[4,128,256]{2,1,0:T(8,128)(2,1)S(1)}, u32[]{:S(2)}, u32[]{:S(2)}) collective-permute-start(bf16[4,128,256]{2,1,0:T(8,128)(2,1)S(1)} %collective-permute-done.3.refs_4_), channel_id=1, source_target_pairs={{0,7},{1,0},{2,1},{3,2},{4,3},{5,4},{6,5},{7,6},{8,15},{9,8},{10,9... | collective-permute-start | bytes 786440 | tf_op jit(solution)/shard_map/ppermute | solution.py:310
  55.2 42.1 %copy-start.25 = (bf16[4,128,256]{2,1,0:T(8,128)(2,1)}, bf16[4,128,256]{2,1,0:T(8,128)(2,1)S(1)}, u32[]{:S(2)}) copy-start(bf16[4,128,256]{2,1,0:T(8,128)(2,1)S(1)} %collective-permute-done.25.refs_10_) | copy-start | bytes 786436
  55.3 11.2 %collective-permute-start.26 = (bf16[4,128,256]{2,1,0:T(8,128)(2,1)S(1)}, bf16[4,128,256]{2,1,0:T(8,128)(2,1)S(1)}, u32[]{:S(2)}, u32[]{:S(2)}) collective-permute-start(bf16[4,128,256]{2,1,0:T(8,128)(2,1)S(1)} %collective-permute-done.25.refs_10_), channel_id=1, source_target_pairs={{0,1},{1,2},{2,3},{3,4},{4,5},{5,6},{6,7},{7,0},{8,9},{9,10},{10,1... | collective-permute-start | bytes 786440 | tf_op jit(solution)/shard_map/ppermute | solution.py:310
  60.9 36.4 %copy-start.26 = (bf16[4,128,256]{2,1,0:T(8,128)(2,1)}, bf16[4,128,256]{2,1,0:T(8,128)(2,1)S(1)}, u32[]{:S(2)}) copy-start(bf16[4,128,256]{2,1,0:T(8,128)(2,1)S(1)} %collective-permute-done.10.refs_13_) | copy-start | bytes 786436
  60.9 11.2 %collective-permute-start.28 = (bf16[4,128,256]{2,1,0:T(8,128)(2,1)S(1)}, bf16[4,128,256]{2,1,0:T(8,128)(2,1)S(1)}, u32[]{:S(2)}, u32[]{:S(2)}) collective-permute-start(bf16[4,128,256]{2,1,0:T(8,128)(2,1)S(1)} %collective-permute-done.10.refs_13_), channel_id=1, source_target_pairs={{0,1},{1,2},{2,3},{3,4},{4,5},{5,6},{6,7},{7,0},{8,9},{9,10},{10,1... | collective-permute-start | bytes 786440 | tf_op jit(solution)/shard_map/ppermute | solution.py:310
  62.1 48.5 %copy-start.5 = (bf16[512,256]{1,0:T(8,128)(2,1)}, bf16[512,256]{1,0:T(8,128)(2,1)S(1)}, u32[]{:S(2)}) copy-start(bf16[512,256]{1,0:T(8,128)(2,1)S(1)} %collective-permute-done.1) | copy-start | bytes 786436
  62.1 35.2 %copy-start.27 = (bf16[4,128,256]{2,1,0:T(8,128)(2,1)}, bf16[4,128,256]{2,1,0:T(8,128)(2,1)S(1)}, u32[]{:S(2)}) copy-start(bf16[4,128,256]{2,1,0:T(8,128)(2,1)S(1)} %collective-permute-done.6.refs_5_) | copy-start | bytes 786436
  62.1 15.6 %collective-permute-start.11 = (bf16[4,128,256]{2,1,0:T(8,128)(2,1)S(1)}, bf16[4,128,256]{2,1,0:T(8,128)(2,1)S(1)}, u32[]{:S(2)}, u32[]{:S(2)}) collective-permute-start(bf16[4,128,256]{2,1,0:T(8,128)(2,1)S(1)} %bitcast.49), channel_id=1, source_target_pairs={{0,1},{1,2},{2,3},{3,4},{4,5},{5,6},{6,7},{7,0},{8,9},{9,10},{10,1... | collective-permute-start | bytes 786440 | tf_op jit(solution)/shard_map/ppermute | solution.py:310
  63.2 20.1 %collective-permute-start.14 = (bf16[4,128,256]{2,1,0:T(8,128)(2,1)S(1)}, bf16[4,128,256]{2,1,0:T(8,128)(2,1)S(1)}, u32[]{:S(2)}, u32[]{:S(2)}) collective-permute-start(bf16[4,128,256]{2,1,0:T(8,128)(2,1)S(1)} %bitcast.61), channel_id=1, source_target_pairs={{0,1},{1,2},{2,3},{3,4},{4,5},{5,6},{6,7},{7,0},{8,9},{9,10},{10,1... | collective-permute-start | bytes 786440 | tf_op jit(solution)/shard_map/ppermute | solution.py:310
  65.6 31.7 %copy-start.28 = (bf16[4,128,256]{2,1,0:T(8,128)(2,1)}, bf16[4,128,256]{2,1,0:T(8,128)(2,1)S(1)}, u32[]{:S(2)}) copy-start(bf16[4,128,256]{2,1,0:T(8,128)(2,1)S(1)} %collective-permute-done.23.refs_6_) | copy-start | bytes 786436
  65.6 17.8 %collective-permute-start.17 = (bf16[4,128,256]{2,1,0:T(8,128)(2,1)S(1)}, bf16[4,128,256]{2,1,0:T(8,128)(2,1)S(1)}, u32[]{:S(2)}, u32[]{:S(2)}) collective-permute-start(bf16[4,128,256]{2,1,0:T(8,128)(2,1)S(1)} %bitcast.50), channel_id=1, source_target_pairs={{0,7},{1,0},{2,1},{3,2},{4,3},{5,4},{6,5},{7,6},{8,15},{9,8},{10,9... | collective-permute-start | bytes 786440 | tf_op jit(solution)/shard_map/ppermute | solution.py:310
  66.5 30.9 %copy-start.29 = (bf16[4,128,256]{2,1,0:T(8,128)(2,1)}, bf16[4,128,256]{2,1,0:T(8,128)(2,1)S(1)}, u32[]{:S(2)}) copy-start(bf16[4,128,256]{2,1,0:T(8,128)(2,1)S(1)} %collective-permute-done.26.refs_8_) | copy-start | bytes 786436
  66.5 19.5 %collective-permute-start.20 = (bf16[4,128,256]{2,1,0:T(8,128)(2,1)S(1)}, bf16[4,128,256]{2,1,0:T(8,128)(2,1)S(1)}, u32[]{:S(2)}, u32[]{:S(2)}) collective-permute-start(bf16[4,128,256]{2,1,0:T(8,128)(2,1)S(1)} %bitcast.62), channel_id=1, source_target_pairs={{0,7},{1,0},{2,1},{3,2},{4,3},{5,4},{6,5},{7,6},{8,15},{9,8},{10,9... | collective-permute-start | bytes 786440 | tf_op jit(solution)/shard_map/ppermute | solution.py:310
  72.1 25.2 %copy-start.30 = (bf16[4,128,256]{2,1,0:T(8,128)(2,1)}, bf16[4,128,256]{2,1,0:T(8,128)(2,1)S(1)}, u32[]{:S(2)}) copy-start(bf16[4,128,256]{2,1,0:T(8,128)(2,1)S(1)} %collective-permute-done.28.refs_11_) | copy-start | bytes 786436
  72.1 14.0 %collective-permute-start.24 = (bf16[4,128,256]{2,1,0:T(8,128)(2,1)S(1)}, bf16[4,128,256]{2,1,0:T(8,128)(2,1)}, u32[]{:S(2)}, u32[]{:S(2)}) collective-permute-start(bf16[4,128,256]{2,1,0:T(8,128)(2,1)S(1)} %collective-permute-done.6.refs_5_), channel_id=1, source_target_pairs={{0,7},{1,0},{2,1},{3,2},{4,3},{5,4},{6,5},{7,6},{8,15},{9,8},{10,9... | collective-permute-start | bytes 786440 | tf_op jit(solution)/shard_map/ppermute | solution.py:310
  77.7 32.9 %copy-start.6 = (bf16[4,128,256]{2,1,0:T(8,128)(2,1)}, bf16[4,128,256]{2,1,0:T(8,128)(2,1)S(1)}, u32[]{:S(2)}) copy-start(bf16[4,128,256]{2,1,0:T(8,128)(2,1)S(1)} %collective-permute-done.11.refs_14_) | copy-start | bytes 786436
  77.7 11.2 %collective-permute-start.12 = (bf16[4,128,256]{2,1,0:T(8,128)(2,1)S(1)}, bf16[4,128,256]{2,1,0:T(8,128)(2,1)S(1)}, u32[]{:S(2)}, u32[]{:S(2)}) collective-permute-start(bf16[4,128,256]{2,1,0:T(8,128)(2,1)S(1)} %collective-permute-done.11.refs_14_), channel_id=1, source_target_pairs={{0,1},{1,2},{2,3},{3,4},{4,5},{5,6},{6,7},{7,0},{8,9},{9,10},{10,1... | collective-permute-start | bytes 786440 | tf_op jit(solution)/shard_map/ppermute | solution.py:310
  83.3 27.3 %copy-start.7 = (bf16[4,128,256]{2,1,0:T(8,128)(2,1)}, bf16[4,128,256]{2,1,0:T(8,128)(2,1)S(1)}, u32[]{:S(2)}) copy-start(bf16[4,128,256]{2,1,0:T(8,128)(2,1)S(1)} %collective-permute-done.14.refs_15_) | copy-start | bytes 786436
  83.3 11.2 %collective-permute-start.15 = (bf16[4,128,256]{2,1,0:T(8,128)(2,1)S(1)}, bf16[4,128,256]{2,1,0:T(8,128)(2,1)S(1)}, u32[]{:S(2)}, u32[]{:S(2)}) collective-permute-start(bf16[4,128,256]{2,1,0:T(8,128)(2,1)S(1)} %collective-permute-done.14.refs_15_), channel_id=1, source_target_pairs={{0,1},{1,2},{2,3},{3,4},{4,5},{5,6},{6,7},{7,0},{8,9},{9,10},{10,1... | collective-permute-start | bytes 786440 | tf_op jit(solution)/shard_map/ppermute | solution.py:310
  83.3 27.3 %copy-start.8 = (bf16[4,128,256]{2,1,0:T(8,128)(2,1)}, bf16[4,128,256]{2,1,0:T(8,128)(2,1)S(1)}, u32[]{:S(2)}) copy-start(bf16[4,128,256]{2,1,0:T(8,128)(2,1)S(1)} %collective-permute-done.17.refs_2_) | copy-start | bytes 786436
  83.4 11.2 %collective-permute-start.18 = (bf16[4,128,256]{2,1,0:T(8,128)(2,1)S(1)}, bf16[4,128,256]{2,1,0:T(8,128)(2,1)S(1)}, u32[]{:S(2)}, u32[]{:S(2)}) collective-permute-start(bf16[4,128,256]{2,1,0:T(8,128)(2,1)S(1)} %collective-permute-done.17.refs_2_), channel_id=1, source_target_pairs={{0,7},{1,0},{2,1},{3,2},{4,3},{5,4},{6,5},{7,6},{8,15},{9,8},{10,9... | collective-permute-start | bytes 786440 | tf_op jit(solution)/shard_map/ppermute | solution.py:310
  86.0 24.6 %copy-start.9 = (bf16[4,128,256]{2,1,0:T(8,128)(2,1)}, bf16[4,128,256]{2,1,0:T(8,128)(2,1)S(1)}, u32[]{:S(2)}) copy-start(bf16[4,128,256]{2,1,0:T(8,128)(2,1)S(1)} %collective-permute-done.20.refs_3_) | copy-start | bytes 786436
  86.0 11.2 %collective-permute-start.21 = (bf16[4,128,256]{2,1,0:T(8,128)(2,1)S(1)}, bf16[4,128,256]{2,1,0:T(8,128)(2,1)S(1)}, u32[]{:S(2)}, u32[]{:S(2)}) collective-permute-start(bf16[4,128,256]{2,1,0:T(8,128)(2,1)S(1)} %collective-permute-done.20.refs_3_), channel_id=1, source_target_pairs={{0,7},{1,0},{2,1},{3,2},{4,3},{5,4},{6,5},{7,6},{8,15},{9,8},{10,9... | collective-permute-start | bytes 786440 | tf_op jit(solution)/shard_map/ppermute | solution.py:310
  86.1 11.9 %collective-permute-start.27 = (bf16[4,128,256]{2,1,0:T(8,128)(2,1)}, bf16[4,128,256]{2,1,0:T(8,128)(2,1)}, u32[]{:S(2)}, u32[]{:S(2)}) collective-permute-start(bf16[4,128,256]{2,1,0:T(8,128)(2,1)} %collective-permute-done.24.refs_7_), channel_id=1, source_target_pairs={{0,7},{1,0},{2,1},{3,2},{4,3},{5,4},{6,5},{7,6},{8,15},{9,8},{10,9... | collective-permute-start | bytes 786440 | tf_op jit(solution)/shard_map/ppermute | solution.py:310
  89.0 21.7 %copy-start.10 = (bf16[4,128,256]{2,1,0:T(8,128)(2,1)}, bf16[4,128,256]{2,1,0:T(8,128)(2,1)S(1)}, u32[]{:S(2)}) copy-start(bf16[4,128,256]{2,1,0:T(8,128)(2,1)S(1)} %collective-permute-done.12.refs_12_) | copy-start | bytes 786436
  89.0 21.7 %collective-permute-start.13 = (bf16[4,128,256]{2,1,0:T(8,128)(2,1)S(1)}, bf16[4,128,256]{2,1,0:T(8,128)(2,1)S(1)}, u32[]{:S(2)}, u32[]{:S(2)}) collective-permute-start(bf16[4,128,256]{2,1,0:T(8,128)(2,1)S(1)} %collective-permute-done.12.refs_12_), channel_id=1, source_target_pairs={{0,1},{1,2},{2,3},{3,4},{4,5},{5,6},{6,7},{7,0},{8,9},{9,10},{10,1... | collective-permute-start | bytes 786440 | tf_op jit(solution)/shard_map/ppermute | solution.py:310
  94.6 16.1 %copy-start.11 = (bf16[4,128,256]{2,1,0:T(8,128)(2,1)}, bf16[4,128,256]{2,1,0:T(8,128)(2,1)S(1)}, u32[]{:S(2)}) copy-start(bf16[4,128,256]{2,1,0:T(8,128)(2,1)S(1)} %collective-permute-done.15.refs_13_) | copy-start | bytes 786436
  94.6 16.1 %collective-permute-start.16 = (bf16[4,128,256]{2,1,0:T(8,128)(2,1)S(1)}, bf16[4,128,256]{2,1,0:T(8,128)(2,1)S(1)}, u32[]{:S(2)}, u32[]{:S(2)}) collective-permute-start(bf16[4,128,256]{2,1,0:T(8,128)(2,1)S(1)} %collective-permute-done.15.refs_13_), channel_id=1, source_target_pairs={{0,1},{1,2},{2,3},{3,4},{4,5},{5,6},{6,7},{7,0},{8,9},{9,10},{10,1... | collective-permute-start | bytes 786440 | tf_op jit(solution)/shard_map/ppermute | solution.py:310
  94.6 16.1 %collective-permute-start.19 = (bf16[4,128,256]{2,1,0:T(8,128)(2,1)S(1)}, bf16[4,128,256]{2,1,0:T(8,128)(2,1)}, u32[]{:S(2)}, u32[]{:S(2)}) collective-permute-start(bf16[4,128,256]{2,1,0:T(8,128)(2,1)S(1)} %collective-permute-done.18.refs_4_), channel_id=1, source_target_pairs={{0,7},{1,0},{2,1},{3,2},{4,3},{5,4},{6,5},{7,6},{8,15},{9,8},{10,9... | collective-permute-start | bytes 786440 | tf_op jit(solution)/shard_map/ppermute | solution.py:310
  97.4 13.4 %collective-permute-start.22 = (bf16[4,128,256]{2,1,0:T(8,128)(2,1)S(1)}, bf16[4,128,256]{2,1,0:T(8,128)(2,1)}, u32[]{:S(2)}, u32[]{:S(2)}) collective-permute-start(bf16[4,128,256]{2,1,0:T(8,128)(2,1)S(1)} %collective-permute-done.21.refs_5_), channel_id=1, source_target_pairs={{0,7},{1,0},{2,1},{3,2},{4,3},{5,4},{6,5},{7,6},{8,15},{9,8},{10,9... | collective-permute-start | bytes 786440 | tf_op jit(solution)/shard_map/ppermute | solution.py:310
  110.7 18.9 %copy-start.14 = (bf16[4,128,256]{2,1,0:T(8,128)(2,1)}, bf16[4,128,256]{2,1,0:T(8,128)(2,1)S(1)}, u32[]{:S(2)}) copy-start(bf16[4,128,256]{2,1,0:T(8,128)(2,1)S(1)} %collective-permute-done.13.refs_10_) | copy-start | bytes 786436
  110.7 18.9 %copy-start.15 = (bf16[4,128,256]{2,1,0:T(8,128)(2,1)}, bf16[4,128,256]{2,1,0:T(8,128)(2,1)S(1)}, u32[]{:S(2)}) copy-start(bf16[4,128,256]{2,1,0:T(8,128)(2,1)S(1)} %collective-permute-done.16.refs_11_) | copy-start | bytes 786436
  110.7 18.9 %collective-permute-start.29 = (bf16[4,128,256]{2,1,0:T(8,128)(2,1)S(1)}, bf16[4,128,256]{2,1,0:T(8,128)(2,1)S(1)}, u32[]{:S(2)}, u32[]{:S(2)}) collective-permute-start(bf16[4,128,256]{2,1,0:T(8,128)(2,1)S(1)} %collective-permute-done.13.refs_10_), channel_id=1, source_target_pairs={{0,1},{1,2},{2,3},{3,4},{4,5},{5,6},{6,7},{7,0},{8,9},{9,10},{10,1... | collective-permute-start | bytes 786440 | tf_op jit(solution)/shard_map/ppermute | solution.py:310
  112.2 17.4 %collective-permute-start.30 = (bf16[4,128,256]{2,1,0:T(8,128)(2,1)}, bf16[4,128,256]{2,1,0:T(8,128)(2,1)S(1)}, u32[]{:S(2)}, u32[]{:S(2)}) collective-permute-start(bf16[4,128,256]{2,1,0:T(8,128)(2,1)} %collective-permute-done.22.refs_7_), channel_id=1, source_target_pairs={{0,7},{1,0},{2,1},{3,2},{4,3},{5,4},{6,5},{7,6},{8,15},{9,8},{10,9... | collective-permute-start | bytes 786440 | tf_op jit(solution)/shard_map/ppermute | solution.py:310
  178.5 18.9 %collective-permute-start.32 = (bf16[8,2,90,8,128]{4,3,2,1,0:T(8,128)(2,1)}, bf16[8,2,90,8,128]{4,3,2,1,0:T(8,128)(2,1)S(1)}, u32[]{:S(2)}, u32[]{:S(2)}) collective-permute-start(bf16[8,2,90,8,128]{4,3,2,1,0:T(8,128)(2,1)} %get-tuple-element.84), channel_id=1, source_target_pairs={{0,16},{16,0},{1,17},{17,1},{2,18},{18,2},{3,19},{19,3},{4,20},{20... | collective-permute-start | bytes 8847368 | tf_op jit(solution)/shard_map/ppermute | solution.py:340
  201.8 42.6 %all-to-all-start.1 = ((bf16[16,90,8,128]{3,2,1,0:T(8,128)(2,1)}), bf16[16,90,8,128]{3,2,1,0:T(8,128)(2,1)S(1)}, u32[]{:S(2)}, u32[]{:S(2)}) async-start(bf16[16,90,8,128]{3,2,1,0:T(8,128)(2,1)} %bitcast.47), calls=%async_computation.2 | async-start | bytes 5898240 | tf_op jit(solution)/shard_map/all_to_all | solution.py:343
  245.5 16.6 %collective-permute-start.33 = (f32[16,8,128]{2,1,0:T(8,128)S(1)}, f32[16,8,128]{2,1,0:T(8,128)S(1)}, u32[]{:S(2)}, u32[]{:S(2)}) collective-permute-start(f32[16,8,128]{2,1,0:T(8,128)S(1)} %slice.30), channel_id=1, source_target_pairs={{0,0},{1,16},{2,32},{3,48},{4,64},{5,80},{6,96},{7,112},{16,128},{... | collective-permute-start | bytes 196616 | tf_op jit(solution)/shard_map/ppermute | solution.py:437
  252.3 15.2 %all-to-all-start.2 = ((f32[8,32,128]{2,1,0:T(8,128)}), f32[8,32,128]{2,1,0:T(8,128)S(1)}, u32[]{:S(2)}, u32[]{:S(2)}) async-start(f32[8,32,128]{2,1,0:T(8,128)} %bitcast.21), calls=%async_computation.3 | async-start | bytes 262144 | tf_op jit(solution)/shard_map/all_to_all | solution.py:441
  259.0 10.9 %collective-permute-start.31 = (bf16[512,256]{1,0:T(8,128)(2,1)S(1)}, bf16[512,256]{1,0:T(8,128)(2,1)S(1)}, u32[]{:S(2)}, u32[]{:S(2)}) collective-permute-start(bf16[512,256]{1,0:T(8,128)(2,1)S(1)} %dynamic-slice_bitcast_fusion), channel_id=1, source_target_pairs={{0,8},{8,0},{1,9},{9,1},{2,10},{10,2},{3,11},{11,3},{4,12},{12,4},... | collective-permute-start | bytes 786440 | tf_op jit(solution)/shard_map/ppermute | solution.py:314
  (6 other events, 54.0 us)
Sparse Core Ops, SparseCore 0:
  32.0 54.8 all-gather.2
  159.2 68.2 reduce-scatter.1

commit v5 on v4

--- a/solution.py
+++ b/solution.py
@@ -188,39 +188,49 @@
         put(keep, send, core, (pair, side, at), rows[:8], rows[8:])
 
 
-def grads_kernel(
-    where, x, low, dy, down_in, act, back_in, gate_in, up_in, gate_back, up_back, keep, send
+def second_grads_kernel(
+    where, dy, down_in, act, back_in, gate_in, up_in, gate_back, up_back, keep, send
 ):
     step, core = pl.program_id(0), where[2]
 
-    @pl.when(step < MINE // 2)
+    @pl.when(step < MINE // 4)
     def _():
-        grads = []
-        for k in range(2):
+        for k in range(4):
             rows = slice(k * SUB, k * SUB + SUB)
-            grads.append(
-                (
-                    dot_last(gate_in[rows].reshape(BLOCK, TOK), gate_back[k]),
-                    dot_last(up_in[rows].reshape(BLOCK, TOK), up_back[k]),
-                    dot_last(act[k], back_in[rows].reshape(BLOCK, TOK)),
-                )
+            c = step * 4 + k
+            three = (
+                dot_last(gate_in[rows].reshape(BLOCK, TOK), gate_back[k]),
+                dot_last(up_in[rows].reshape(BLOCK, TOK), up_back[k]),
+                dot_last(act[k], back_in[rows].reshape(BLOCK, TOK)),
             )
-        for k in range(2):
-            c = step * 2 + k
             for kind in range(3):
-                put_rows(keep, send, core, c // HID, kind * HID + c % HID, grads[k][kind])
+                put_rows(keep, send, core, c // HID, kind * HID + c % HID, three[kind])
 
     fill = jnp.zeros((4, BLOCK), F32)
-    grads = [dot_last(down_in[k], dy[k]) for k in range(PER)]
-    firsts = [dot_last(x[k], low[k]) for k in range(PER)]
-    side, z = step // 8, step % 8
-    for p, grad in enumerate(grads):
+    grads = [dot_last(down_in[k], dy[k]) for k in range(8)]
+    for n, grad in enumerate(grads):
+        side, z, p = step // 4, step % 4 * 2 + n // PER, n % PER
         even, odd = [jnp.concatenate([grad[g * 28 : g * 28 + 28], fill]) for g in range(2)]
         for k in range(4):
             rows = slice(k * 8, k * 8 + 8)
             put(keep, send, core, (z, side, 3 * HID + p * 4 + k), even[rows], odd[rows])
-    for p, grad in enumerate(firsts):
-        put_rows(keep, send, core, side, 3 * HID + 16 + z * PER + p, grad)
+
+
+def first_grads_kernel(where, x, low, keep, send):
+    step, core = pl.program_id(0), where[2]
+    grads = [dot_last(x[k], low[k]) for k in range(8)]
+    for k, grad in enumerate(grads):
+        i = step * 8 + k
+        put_rows(keep, send, core, i // 32, i % 32, grad)
+
+
+def join_kernel(pieces, gate, up):
+    for z in range(8):
+        value = pieces[z]
+        for side in range(2):
+            at = side * 224 + z * 28
+            gate[:, at : at + 28] = value[:, side * 28 : side * 28 + 28]
+            up[:, at : at + 28] = value[:, ROWS + side * 28 : ROWS + side * 28 + 28]
 
 
 def call(kernel, outs, scratch, flops, *args):
@@ -278,22 +288,33 @@
     return pl.BlockSpec((count,) + array.shape[1:], index)
 
 
-def grads(where, x, low, dy, down_in, act, back_in, gate_in, up_in, gate_back, up_back):
-    last = MINE // 2 - 1
-    args = (x, low, dy, down_in, act, back_in, gate_in, up_in, gate_back, up_back)
-    specs = [blocks_of(a, PER) for a in args[:4]]
-    specs += [blocks_of(a, 4 if a.shape[0] == ROWS else 2, last) for a in args[4:]]
-    shape = (8, 2, 3 * HID + 16 + 32, 8, BLOCK)
+def grads_call(kernel, specs, blocks, flops, where, *args):
+    shape = (8, 2, blocks, 8, BLOCK)
     moved = sum(a.size * a.dtype.itemsize for a in args)
     return pl.pallas_call(
-        grads_kernel,
-        grid=(NBD // PER,),
+        kernel,
+        grid=(8,),
         out_shape=[jax.ShapeDtypeStruct(shape, BF)] * 2,
         in_specs=[SM] + specs,
         out_specs=[pl.BlockSpec(shape, lambda step: (0,) * 5)] * 2,
         compiler_params=pltpu.CompilerParams(vmem_limit_bytes=60 << 20),
-        cost_estimate=pl.CostEstimate(flops=6 * ONE, bytes_accessed=moved, transcendentals=0),
+        cost_estimate=pl.CostEstimate(flops=flops, bytes_accessed=moved, transcendentals=0),
     )(where, *args)
+
+
+def second_grads(where, *args):
+    specs = [blocks_of(a, 8) for a in args[:2]]
+    specs += [blocks_of(a, 8 if a.shape[0] == ROWS else 4, MINE // 4 - 1) for a in args[2:]]
+    return grads_call(second_grads_kernel, specs, 3 * HID + 16, 4 * ONE, where, *args)
+
+
+def first_grads(where, x, low):
+    return grads_call(first_grads_kernel, [blocks_of(x, 8), blocks_of(low, 8)], 32, 2 * ONE, where, x, low)
+
+
+def join(pieces):
+    outs = [((pieces.shape[1], 448), F32)] * 2
+    return call(join_kernel, outs, [], ONE // 64, pieces)
 
 
 GROUP = ("y", "x_lo", "core")
@@ -336,10 +357,13 @@
     return [shard for step in range(size("z")) for shard in found[step]]
 
 
-def sum_groups(keep, send):
+def sum_cores(keep, send):
     found = lax.ppermute(send, "core", [(0, 1), (1, 0)])
     pairs = (keep.astype(F32) + found.astype(F32)).astype(BF)
-    pairs = pairs.reshape((-1,) + pairs.shape[2:])
+    return pairs.reshape((-1,) + pairs.shape[2:])
+
+
+def to_chips(pairs):
     return lax.all_to_all(pairs, CHIPS, 0, 0, tiled=True)
 
 
@@ -402,7 +426,7 @@
     state = (xs[0], xs[0])
     for step in range(1, steps + 1):
         state = ring_step(step, *state, xs)
-    state, _ = lax.optimization_barrier(((dys[0], dys[0]), (xs[2], xs[nz - 2])))
+    state, _ = lax.optimization_barrier(((dys[0], dys[0]), (xs[1][0], xs[nz - 1][0])))
     for step in range(1, steps - 1):
         state = ring_step(step, *state, dys)
     shards_x, _ = lax.optimization_barrier((flat(xs), state))
@@ -420,14 +444,18 @@
     kept = lax.dynamic_index_in_dim(total, me, 0, keepdims=False)
     other = swap(lax.dynamic_index_in_dim(total, 1 - me, 0, keepdims=False))
 
-    chips = sum_groups(
-        *grads(where, x, low, dy, down_in, act, back_in, gate_in, up_in, gate_back, up_back)
-    )
+    later = second_grads(where, dy, down_in, act, back_in, gate_in, up_in, gate_back, up_back)
+    x, later = lax.optimization_barrier((x, later))
+    firsts = sum_cores(*first_grads(where, x, low))
+    later = to_chips(sum_cores(*later))
+    firsts, later = lax.optimization_barrier((firsts, later))
+    firsts = to_chips(firsts)
+    firsts, other = lax.optimization_barrier((firsts, other))
     input_grad = jnp.concatenate(
         [jnp.where(me == 0, kept, other), jnp.where(me == 0, other, kept)], axis=1
     )
-    summed = total_of(chips) * scale
-    later, firsts = summed[: 3 * hid + 16], summed[3 * hid + 16 :]
+    later = total_of(later) * scale
+    firsts = total_of(firsts) * scale
     out_gs, out_us, out_df = later[: 3 * hid].reshape(3, hid, rows, BLOCK)
     pairs = []
     for part in range(ngroup):
@@ -439,9 +467,7 @@
 
     firsts = firsts.reshape(nz, per * rows, 2 * ROWS)
     firsts = lax.all_to_all(firsts, "z", 0, 0, tiled=True)
-    firsts = firsts.reshape(nz, per, rows, 2, ROWS)[..., : nh * each]
-    firsts = firsts.reshape(nz, per, rows, 2, nh, each).transpose(3, 1, 2, 4, 0, 5)
-    out_gf, out_uf = firsts.reshape(2, per, rows, wide)
+    out_gf, out_uf = [value.reshape(per, rows, wide) for value in join(firsts)]
     return input_grad, out_gf, out_uf, out_gs, out_us, out_df, out_ds
 
 

time: 278 us -> 274 us (0.986)
  waiting for transfers between devices: 95.3 us -> 70.7 us
  starting transfers between devices: 74.4 us -> 91.3 us
    all_to_all x1 -> x2, waiting for transfers between devices: 37 us -> 10.9 us  [to_chips(): return lax.all_to_all(pairs, CHIPS, 0, 0, tiled=True)]
    ppermute x28, waiting for transfers between devices: 39.5 us -> 24.6 us  [shift(): lax.ppermute(value, 'z', [(i, (i + step) % count) for i in range(count)])]
    ppermute x28, starting transfers between devices: 20.9 us -> 34.6 us  [shift(): lax.ppermute(value, 'z', [(i, (i + step) % count) for i in range(count)])]
    ppermute x4, waiting for transfers between devices: 6.12 us -> 17.3 us  [swap(): return lax.ppermute(value, 'x_hi', [(0, 1), (1, 0)])]
    all_to_all x1 -> x2, starting transfers between devices: 5.52 us -> 12.9 us  [to_chips(): return lax.all_to_all(pairs, CHIPS, 0, 0, tiled=True)]
    pallas_call x3 -> x4, Pallas kernels: 57.2 us -> 59 us  [call(): pl.pallas_call(kernel, out_shape=shapes, in_specs=[SM if a.dtype == jnp.i...]
    convert_element_type x1 -> x2, other arithmetic: 4.43 us -> 5.85 us  [sum_cores(): pairs = (keep.astype(F32) + found.astype(F32)).astype(BF)]
    ppermute x1 -> x2, waiting for transfers between devices: 5.22 us -> 6.21 us  [sum_cores(): found = lax.ppermute(send, 'core', [(0, 1), (1, 0)])]
  transfers between devices with their start and end apart: 39 -> 41, of which waited for: 18 -> 21; matrix products, arithmetic and copies ran while one was open for 4% -> 4% of each run, Pallas kernels for 17% -> 18%
where the time goes in v5:
time: 274 us; the launch traced here: 272 us
  starting transfers between devices  91.3 us (33%)
  Pallas kernels  78.5 us (29%)
  waiting for transfers between devices  70.7 us (26%)
  between operations  14.6 us (5%)
  other arithmetic  11.3 us (4%)
  local copies, waits for them, and re-layouts  5.51 us (2%)
    pallas_call x4, Pallas kernels, call(): pl.pallas_call(kernel, out_shape=shapes, in_specs=[SM if a.dtype == jnp.i...  59 us
    ppermute x28, starting transfers between devices, shift(): lax.ppermute(value, 'z', [(i, (i + step) % count) for i in range(count)])  34.6 us
    ppermute x28, waiting for transfers between devices, shift(): lax.ppermute(value, 'z', [(i, (i + step) % count) for i in range(count)])  24.6 us
    pallas_call x2, Pallas kernels, grads_call(): pl.pallas_call(kernel, grid=(8,), out_shape=[jax.ShapeDtypeStruct(shape,...  19.5 us
    ppermute x4, waiting for transfers between devices, swap(): return lax.ppermute(value, 'x_hi', [(0, 1), (1, 0)])  17.3 us
    all_to_all x2, starting transfers between devices, to_chips(): return lax.all_to_all(pairs, CHIPS, 0, 0, tiled=True)  12.9 us
    ppermute x2, starting transfers between devices, sum_cores(): found = lax.ppermute(send, 'core', [(0, 1), (1, 0)])  12.9 us
    all_to_all x1, starting transfers between devices, share_first(): return lax.all_to_all(first, TENSOR, 0, 0, tiled=True)  11.7 us
  transfers between devices with their start and end apart: 41, of which 21 were waited for; matrix products, arithmetic and copies ran while one was open for 4% of the time, Pallas kernels for 18%

profile of v5, /device:TPU:1, one launch (start us, length us, event | category | flops | bytes accessed | tf_op | source)
XLA Modules:
  0.0 271.9 jit_solution(1287311721468637744)
XLA Ops:
  7.2 1.0 fusion
  8.4 0.8 broadcast_in_dim.2
  9.1 11.7 %all-to-all-start = ((bf16[16,64,128]{2,1,0:T(8,128)(2,1)}), bf16[16,64,128]{2,1,0:T(8,128)(2,1)S(1)}, u32[]{:S(2)}, u32[]{:S(2)}) async-start(bf16[16,64,128]{2,1,0:T(8,128)(2,1)} %bitcast.10), calls=%async_computation | async-start | bytes 524288 | tf_op jit(solution)/shard_map/all_to_all | solution.py:384
  20.9 1.0 select_select_fusion
  21.9 3.0 %collective-permute-start = (bf16[3,128,128]{2,1,0:T(8,128)(2,1)S(1)}, bf16[3,128,128]{2,1,0:T(8,128)(2,1)S(1)}, u32[]{:S(2)}, u32[]{:S(2)}) collective-permute-start(bf16[3,128,128]{2,1,0:T(8,128)(2,1)S(1)} %select_select_fusion), channel_id=1, source_target_pairs={{0,8},{8,0},{1,9},{9,1},{2,10},{10,2},{3,11},{11,3},{4,12},{12,4},... | collective-permute-start | bytes 294920 | tf_op jit(solution)/shard_map/ppermute | solution.py:335
  24.9 3.4 %collective-permute-done = bf16[3,128,128]{2,1,0:T(8,128)(2,1)S(1)} collective-permute-done((bf16[3,128,128]{2,1,0:T(8,128)(2,1)S(1)}, bf16[3,128,128]{2,1,0:T(8,128)(2,1)S(1)}, u32[]{:S(2)}, u32[]{:S(2)}) %collective-permute-start) | collective-permute-done | bytes 98336 | tf_op jit(solution)/shard_map/ppermute | solution.py:335
  28.3 2.8 %all-to-all-done = bf16[16,64,128]{2,1,0:T(8,128)(2,1)S(1)} async-done(((bf16[16,64,128]{2,1,0:T(8,128)(2,1)}), bf16[16,64,128]{2,1,0:T(8,128)(2,1)S(1)}, u32[]{:S(2)}, u32[]{:S(2)}) %all-to-all-start) | async-done | bytes 262176 | tf_op jit(solution)/shard_map/all_to_all | solution.py:384
  31.1 0.8 pad_maximum_fusion.1
  32.0 1.5 collective-permute-start.3
  33.5 1.2 collective-permute-start.2
  34.8 0.7 collective-permute-start.16
  35.5 2.4 collective-permute-start.1
  39.1 2.2 collective-permute-start.18
  41.7 2.4 collective-permute-start.17
  44.2 2.6 collective-permute-done.1
  47.3 2.6 collective-permute-start.10
  50.1 0.9 collective-permute-start.13
  51.5 2.6 collective-permute-done.4.refs_14_
  54.2 1.8 collective-permute-start.19
  55.9 3.3 %collective-permute-done.7.refs_15_ = bf16[4,128,256]{2,1,0:T(8,128)(2,1)S(1)} collective-permute-done((bf16[4,128,256]{2,1,0:T(8,128)(2,1)S(1)}, bf16[4,128,256]{2,1,0:T(8,128)(2,1)S(1)}, u32[]{:S(2)}, u32[]{:S(2)}) %collective-permute-start.7) | collective-permute-done | bytes 262176 | tf_op jit(solution)/shard_map/ppermute | solution.py:331
  59.2 1.9 collective-permute-start.20
  61.2 1.4 collective-permute-done.23.refs_10_
  62.6 1.0 collective-permute-start.8
  63.6 3.3 %collective-permute-start.21 = (bf16[4,128,256]{2,1,0:T(8,128)(2,1)S(1)}, bf16[4,128,256]{2,1,0:T(8,128)(2,1)}, u32[]{:S(2)}, u32[]{:S(2)}) collective-permute-start(bf16[4,128,256]{2,1,0:T(8,128)(2,1)S(1)} %collective-permute-done.19.refs_5_), channel_id=1, source_target_pairs={{0,7},{1,0},{2,1},{3,2},{4,3},{5,4},{6,5},{7,6},{8,15},{9,8},{10,9... | collective-permute-start | bytes 786440 | tf_op jit(solution)/shard_map/ppermute | solution.py:331
  66.8 1.8 collective-permute-done.20.refs_6_
  68.6 2.1 collective-permute-start.11
  70.7 1.6 collective-permute-start.14
  72.3 4.0 %collective-permute-done.5.refs_12_ = bf16[4,128,256]{2,1,0:T(8,128)(2,1)S(1)} collective-permute-done((bf16[4,128,256]{2,1,0:T(8,128)(2,1)S(1)}, bf16[4,128,256]{2,1,0:T(8,128)(2,1)S(1)}, u32[]{:S(2)}, u32[]{:S(2)}) %collective-permute-start.5) | collective-permute-done | bytes 262176 | tf_op jit(solution)/shard_map/ppermute | solution.py:331
  76.3 5.6 %collective-permute-done.8.refs_13_ = bf16[4,128,256]{2,1,0:T(8,128)(2,1)S(1)} collective-permute-done((bf16[4,128,256]{2,1,0:T(8,128)(2,1)S(1)}, bf16[4,128,256]{2,1,0:T(8,128)(2,1)S(1)}, u32[]{:S(2)}, u32[]{:S(2)}) %collective-permute-start.8) | collective-permute-done | bytes 262176 | tf_op jit(solution)/shard_map/ppermute | solution.py:331
  81.9 2.7 collective-permute-start.25
  84.6 0.9 collective-permute-done.14.refs_5_
  85.5 2.4 collective-permute-start.9
  87.9 1.3 collective-permute-start.12
  89.2 4.0 %collective-permute-done.28.refs_11_ = bf16[4,128,256]{2,1,0:T(8,128)(2,1)S(1)} collective-permute-done((bf16[4,128,256]{2,1,0:T(8,128)(2,1)S(1)}, bf16[4,128,256]{2,1,0:T(8,128)(2,1)S(1)}, u32[]{:S(2)}, u32[]{:S(2)}) %collective-permute-start.28) | collective-permute-done | bytes 262176 | tf_op jit(solution)/shard_map/ppermute | solution.py:331
  93.3 0.7 copy-done.31
  94.0 1.5 collective-permute-start.15
  96.1 12.5 %shard_map.144 = (bf16[64,128,256]{2,1,0:T(8,128)(2,1)}, bf16[64,64,256]{2,1,0:T(8,128)(2,1)}, bf16[64,64,256]{2,1,0:T(8,128)(2,1)}) custom-call(s32[3]{0:T(128)} %pad_add_fusion.where, bf16[256,256]{1,0:T(8,128)(2,1)} %constant.82.clone.swap, bf16[16,28,64,128]{3,2,1,0:T(8,128)(2,1)} %bitcast.37, bf16[4,128,256]{2,1,0:T(8,128)(2,1)} %bitcast.46, ...), custom_call_target="tpu_custom_call" | custom-call | flops 1409286144 | bytes 11665420 | tf_op jit(solution)/shard_map/pallas_call | solution.py:239
  108.8 2.7 collective-permute-start.30
  111.5 16.1 %shard_map.145 = (bf16[28,128,256]{2,1,0:T(8,128)(2,1)}, f32[28,128,256]{2,1,0:T(8,128)}, f32[28,128,256]{2,1,0:T(8,128)}, bf16[64,64,256]{2,1,0:T(8,128)(2,1)}) custom-call(bf16[256,256]{1,0:T(8,128)(2,1)} %constant.82.clone.swap, bf16[16,28,64,128]{3,2,1,0:T(8,128)(2,1)} %bitcast.38, bf16[64,64,256]{2,1,0:T(8,128)(2,1)} %get-tuple-element.79.gate_in, ...), custom_call_target="tpu_custom_call" | custom-call | flops 1174405120 | bytes 11665408 | tf_op jit(solution)/shard_map/pallas_call | solution.py:239
  127.6 0.7 copy-done.17
  128.4 28.6 %shard_map.146 = (bf16[64,128,256]{2,1,0:T(8,128)(2,1)}, bf16[64,64,256]{2,1,0:T(8,128)(2,1)}, bf16[28,128,256]{2,1,0:T(8,128)(2,1)}, bf16[28,128,256]{2,1,0:T(8...) custom-call(s32[3]{0:T(128)} %pad_add_fusion.where, bf16[256,256]{1,0:T(8,128)(2,1)} %constant.82.clone.swap, ...), custom_call_target="tpu_custom_call" | custom-call | flops 2818572288 | bytes 19005452 | tf_op jit(solution)/shard_map/pallas_call | solution.py:239
  157.0 11.5 %shard_map.147 = (bf16[8,2,58,8,128]{4,3,2,1,0:T(8,128)(2,1)}, bf16[8,2,58,8,128]{4,3,2,1,0:T(8,128)(2,1)}) custom-call(s32[3]{0:T(128)} %pad_add_fusion.where, bf16[64,128,256]{2,1,0:T(8,128)(2,1)} %get-tuple-element.87.dy, bf16[64,64,256]{2,1,0:T(8,128)(2,1)} %get-tuple-element.88.down_in, bf16[28,128,256]{2,1,0:T(8,128)(2,1)} %get-tuple-element.89.act, ...), custom_call_target="tpu_custom_call" | custom-call | flops 939524096 | bytes 18087936 | tf_op jit(solution)/shard_map/pallas_call | solution.py:294
  168.5 12.2 %collective-permute-start.32 = (bf16[8,2,58,8,128]{4,3,2,1,0:T(8,128)(2,1)}, bf16[8,2,58,8,128]{4,3,2,1,0:T(8,128)(2,1)S(1)}, u32[]{:S(2)}, u32[]{:S(2)}) collective-permute-start(bf16[8,2,58,8,128]{4,3,2,1,0:T(8,128)(2,1)} %get-tuple-element.100), channel_id=1, source_target_pairs={{0,16},{16,0},{1,17},{17,1},{2,18},{18,2},{3,19},{19,3},{4,20},{20... | collective-permute-start | bytes 5701640 | tf_op jit(solution)/shard_map/ppermute | solution.py:361
  180.7 3.7 %collective-permute-done.32 = bf16[8,2,58,8,128]{4,3,2,1,0:T(8,128)(2,1)S(1)} collective-permute-done((bf16[8,2,58,8,128]{4,3,2,1,0:T(8,128)(2,1)}, bf16[8,2,58,8,128]{4,3,2,1,0:T(8,128)(2,1)S(1)}, u32[]{:S(2)}, u32[]{:S(2)}) %collective-permute-start.32) | collective-permute-done | bytes 1900576 | tf_op jit(solution)/shard_map/ppermute | solution.py:361
  184.4 3.3 %add_convert_fusion = bf16[8,2,58,8,128]{4,3,2,1,0:T(8,128)(2,1)} fusion(bf16[8,2,58,8,128]{4,3,2,1,0:T(8,128)(2,1)S(1)} %collective-permute-done.32, bf16[8,2,58,8,128]{4,3,2,1,0:T(8,128)(2,1)} %get-tuple-element.99), kind=kLoop, calls=%fused_computation.1 | loop fusion | flops 3801088 | bytes 5701632 | tf_op jit(solution)/shard_map/convert_element_type | solution.py:362
  187.7 7.2 %all-to-all-start.1 = ((bf16[16,58,8,128]{3,2,1,0:T(8,128)(2,1)}), bf16[16,58,8,128]{3,2,1,0:T(8,128)(2,1)S(1)}, u32[]{:S(2)}, u32[]{:S(2)}) async-start(bf16[16,58,8,128]{3,2,1,0:T(8,128)(2,1)} %bitcast.40), calls=%async_computation.2 | async-start | bytes 3801088 | tf_op jit(solution)/shard_map/all_to_all | solution.py:367
  194.9 8.0 %shard_map.148 = (bf16[8,2,32,8,128]{4,3,2,1,0:T(8,128)(2,1)}, bf16[8,2,32,8,128]{4,3,2,1,0:T(8,128)(2,1)}) custom-call(s32[3]{0:T(128)} %pad_add_fusion.where, bf16[64,128,256]{2,1,0:T(8,128)(2,1)} %get-tuple-element.95.x, bf16[64,128,256]{2,1,0:T(8,128)(2,1)} %get-tuple-element.96.low), custom_call_target="tpu_custom_call" | custom-call | flops 469762048 | bytes 8388608 | tf_op jit(solution)/shard_map/pallas_call | solution.py:294
  202.9 0.7 collective-permute-start.31
  203.6 2.5 collective-permute-done.31
  206.1 2.5 add_convert_fusion.1
  208.7 10.9 %all-to-all-done.1 = bf16[16,58,8,128]{3,2,1,0:T(8,128)(2,1)S(1)} async-done(((bf16[16,58,8,128]{3,2,1,0:T(8,128)(2,1)}), bf16[16,58,8,128]{3,2,1,0:T(8,128)(2,1)S(1)}, u32[]{:S(2)}, u32[]{:S(2)}) %all-to-all-start.1) | async-done | bytes 1900576 | tf_op jit(solution)/shard_map/all_to_all | solution.py:367
  219.5 5.7 %all-to-all-start.2 = ((bf16[16,32,8,128]{3,2,1,0:T(8,128)(2,1)}), bf16[16,32,8,128]{3,2,1,0:T(8,128)(2,1)S(1)}, u32[]{:S(2)}, u32[]{:S(2)}) async-start(bf16[16,32,8,128]{3,2,1,0:T(8,128)(2,1)} %bitcast.19), calls=%async_computation.3 | async-start | bytes 2097152 | tf_op jit(solution)/shard_map/all_to_all | solution.py:367
  225.5 1.0 dynamic-slice_bitcast_fusion
  226.6 3.0 %collective-permute-start.33 = (bf16[512,256]{1,0:T(8,128)(2,1)S(1)}, bf16[512,256]{1,0:T(8,128)(2,1)S(1)}, u32[]{:S(2)}, u32[]{:S(2)}) collective-permute-start(bf16[512,256]{1,0:T(8,128)(2,1)S(1)} %dynamic-slice_bitcast_fusion), channel_id=1, source_target_pairs={{0,8},{8,0},{1,9},{9,1},{2,10},{10,2},{3,11},{11,3},{4,12},{12,4},... | collective-permute-start | bytes 786440 | tf_op jit(solution)/shard_map/ppermute | solution.py:335
  229.6 6.7 %collective-permute-start.34 = (f32[16,8,128]{2,1,0:T(8,128)S(1)}, f32[16,8,128]{2,1,0:T(8,128)S(1)}, u32[]{:S(2)}, u32[]{:S(2)}) collective-permute-start(f32[16,8,128]{2,1,0:T(8,128)S(1)} %slice.15), channel_id=1, source_target_pairs={{0,0},{1,16},{2,32},{3,48},{4,64},{5,80},{6,96},{7,112},{16,128},{... | collective-permute-start | bytes 196616 | tf_op jit(solution)/shard_map/ppermute | solution.py:465
  236.3 0.7 fusion.1
  237.0 1.8 collective-permute-done.34
  238.8 0.7 copy.21
  239.5 11.0 %collective-permute-done.33 = bf16[512,256]{1,0:T(8,128)(2,1)S(1)} collective-permute-done((bf16[512,256]{1,0:T(8,128)(2,1)S(1)}, bf16[512,256]{1,0:T(8,128)(2,1)S(1)}, u32[]{:S(2)}, u32[]{:S(2)}) %collective-permute-start.33) | collective-permute-done | bytes 262176 | tf_op jit(solution)/shard_map/ppermute | solution.py:335
  250.6 0.7 broadcast_multiply_fusion.1
  251.3 3.4 %all-to-all-start.3 = ((f32[8,32,128]{2,1,0:T(8,128)}), f32[8,32,128]{2,1,0:T(8,128)S(1)}, u32[]{:S(2)}, u32[]{:S(2)}) async-start(f32[8,32,128]{2,1,0:T(8,128)} %bitcast.22), calls=%async_computation.4 | async-start | bytes 262144 | tf_op jit(solution)/shard_map/all_to_all | solution.py:469
  254.8 0.8 pad_maximum_fusion
  255.6 7.0 %all-to-all-done.3.pieces = f32[8,32,128]{2,1,0:T(8,128)S(1)} async-done(((f32[8,32,128]{2,1,0:T(8,128)}), f32[8,32,128]{2,1,0:T(8,128)S(1)}, u32[]{:S(2)}, u32[]{:S(2)}) %all-to-all-start.3) | async-done | bytes 131104 | tf_op jit(solution)/shard_map/all_to_all | solution.py:469
  263.3 1.7 shard_map.149
  (115 shorter events, 5.3 us)
Async XLA Ops:
  8.3 23.7 %copy-start.3 = (bf16[512,512]{1,0:T(8,128)(2,1)S(1)}, bf16[512,512]{1,0:T(8,128)(2,1)}, u32[]{:S(2)}) copy-start(bf16[512,512]{1,0:T(8,128)(2,1)} %param.9) | copy-start | bytes 1572868
  9.1 26.3 %copy-start.4 = (bf16[512,512]{1,0:T(8,128)(2,1)S(1)}, bf16[512,512]{1,0:T(8,128)(2,1)}, u32[]{:S(2)}) copy-start(bf16[512,512]{1,0:T(8,128)(2,1)} %param.10) | copy-start | bytes 1572868
  9.1 22.0 %all-to-all-start = ((bf16[16,64,128]{2,1,0:T(8,128)(2,1)}), bf16[16,64,128]{2,1,0:T(8,128)(2,1)S(1)}, u32[]{:S(2)}, u32[]{:S(2)}) async-start(bf16[16,64,128]{2,1,0:T(8,128)(2,1)} %bitcast.10), calls=%async_computation | async-start | bytes 524288 | tf_op jit(solution)/shard_map/all_to_all | solution.py:384
  20.8 75.2 %all-gather.3.cloned.1.call-start = ((), (), s32[]{:S(2)}) async-start(), calls=%async_computation.6 | async-start | bytes 7798784 | tf_op jit(solution)/shard_map/all_gather | solution.py:422
  21.9 6.3 %collective-permute-start = (bf16[3,128,128]{2,1,0:T(8,128)(2,1)S(1)}, bf16[3,128,128]{2,1,0:T(8,128)(2,1)S(1)}, u32[]{:S(2)}, u32[]{:S(2)}) collective-permute-start(bf16[3,128,128]{2,1,0:T(8,128)(2,1)S(1)} %select_select_fusion), channel_id=1, source_target_pairs={{0,8},{8,0},{1,9},{9,1},{2,10},{10,2},{3,11},{11,3},{4,12},{12,4},... | collective-permute-start | bytes 294920 | tf_op jit(solution)/shard_map/ppermute | solution.py:335
  31.9 193.6 %reduce-scatter.2.cloned.1.call-start = ((), (), s32[]{:S(2)}) async-start(), calls=%async_computation.5 | async-start | bytes 4718592 | tf_op jit(solution)/shard_map/reduce_scatter | solution.py:442
  32.0 64.0 %copy-start.1 = (bf16[512,256]{1,0:T(8,128)(2,1)}, bf16[512,256]{1,0:T(8,128)(2,1)S(1)}, u32[]{:S(2)}) copy-start(bf16[512,256]{1,0:T(8,128)(2,1)S(1)} %get-tuple-element.126) | copy-start | bytes 786436
  32.0 6.5 %collective-permute-start.3 = (bf16[4,128,256]{2,1,0:T(8,128)(2,1)S(1)}, bf16[4,128,256]{2,1,0:T(8,128)(2,1)S(1)}, u32[]{:S(2)}, u32[]{:S(2)}) collective-permute-start(bf16[4,128,256]{2,1,0:T(8,128)(2,1)S(1)} %bitcast.44), channel_id=1, source_target_pairs={{0,1},{1,2},{2,3},{3,4},{4,5},{5,6},{6,7},{7,0},{8,9},{9,10},{10,1... | collective-permute-start | bytes 786440 | tf_op jit(solution)/shard_map/ppermute | solution.py:331
  33.5 5.5 %collective-permute-start.2 = (bf16[4,128,256]{2,1,0:T(8,128)(2,1)S(1)}, bf16[4,128,256]{2,1,0:T(8,128)(2,1)S(1)}, u32[]{:S(2)}, u32[]{:S(2)}) collective-permute-start(bf16[4,128,256]{2,1,0:T(8,128)(2,1)S(1)} %bitcast.45), channel_id=1, source_target_pairs={{0,7},{1,0},{2,1},{3,2},{4,3},{5,4},{6,5},{7,6},{8,15},{9,8},{10,9... | collective-permute-start | bytes 786440 | tf_op jit(solution)/shard_map/ppermute | solution.py:331
  34.8 6.7 %collective-permute-start.16 = (bf16[512,256]{1,0:T(8,128)(2,1)S(1)}, bf16[512,256]{1,0:T(8,128)(2,1)S(1)}, u32[]{:S(2)}, u32[]{:S(2)}) collective-permute-start(bf16[512,256]{1,0:T(8,128)(2,1)S(1)} %get-tuple-element.125), channel_id=1, source_target_pairs={{0,8},{8,0},{1,9},{9,1},{2,10},{10,2},{3,11},{11,3},{4,12},{12,4},... | collective-permute-start | bytes 786440 | tf_op jit(solution)/shard_map/ppermute | solution.py:335
  35.5 73.1 %copy-start = (bf16[512,256]{1,0:T(8,128)(2,1)}, bf16[512,256]{1,0:T(8,128)(2,1)S(1)}, u32[]{:S(2)}) copy-start(bf16[512,256]{1,0:T(8,128)(2,1)S(1)} %get-tuple-element.124) | copy-start | bytes 786436
  35.5 11.3 %collective-permute-start.1 = (bf16[512,256]{1,0:T(8,128)(2,1)S(1)}, bf16[512,256]{1,0:T(8,128)(2,1)S(1)}, u32[]{:S(2)}, u32[]{:S(2)}) collective-permute-start(bf16[512,256]{1,0:T(8,128)(2,1)S(1)} %get-tuple-element.123), channel_id=1, source_target_pairs={{0,8},{8,0},{1,9},{9,1},{2,10},{10,2},{3,11},{11,3},{4,12},{12,4},... | collective-permute-start | bytes 786440 | tf_op jit(solution)/shard_map/ppermute | solution.py:335
  38.5 50.6 %copy-start.19 = (bf16[4,128,256]{2,1,0:T(8,128)(2,1)}, bf16[4,128,256]{2,1,0:T(8,128)(2,1)S(1)}, u32[]{:S(2)}) copy-start(bf16[4,128,256]{2,1,0:T(8,128)(2,1)S(1)} %collective-permute-done.3.refs_14_) | copy-start | bytes 786436
  38.5 8.7 %collective-permute-start.22 = (bf16[4,128,256]{2,1,0:T(8,128)(2,1)S(1)}, bf16[4,128,256]{2,1,0:T(8,128)(2,1)S(1)}, u32[]{:S(2)}, u32[]{:S(2)}) collective-permute-start(bf16[4,128,256]{2,1,0:T(8,128)(2,1)S(1)} %collective-permute-done.3.refs_14_), channel_id=1, source_target_pairs={{0,1},{1,2},{2,3},{3,4},{4,5},{5,6},{6,7},{7,0},{8,9},{9,10},{10,1... | collective-permute-start | bytes 786440 | tf_op jit(solution)/shard_map/ppermute | solution.py:331
  39.1 54.1 %copy-start.20 = (bf16[4,128,256]{2,1,0:T(8,128)(2,1)}, bf16[4,128,256]{2,1,0:T(8,128)(2,1)S(1)}, u32[]{:S(2)}) copy-start(bf16[4,128,256]{2,1,0:T(8,128)(2,1)S(1)} %collective-permute-done.2.refs_2_) | copy-start | bytes 786436
  39.1 8.3 %collective-permute-start.18 = (bf16[4,128,256]{2,1,0:T(8,128)(2,1)S(1)}, bf16[4,128,256]{2,1,0:T(8,128)(2,1)S(1)}, u32[]{:S(2)}, u32[]{:S(2)}) collective-permute-start(bf16[4,128,256]{2,1,0:T(8,128)(2,1)S(1)} %collective-permute-done.2.refs_2_), channel_id=1, source_target_pairs={{0,7},{1,0},{2,1},{3,2},{4,3},{5,4},{6,5},{7,6},{8,15},{9,8},{10,9... | collective-permute-start | bytes 786440 | tf_op jit(solution)/shard_map/ppermute | solution.py:331
  41.5 51.7 %copy-start.21 = (bf16[512,256]{1,0:T(8,128)(2,1)}, bf16[512,256]{1,0:T(8,128)(2,1)S(1)}, u32[]{:S(2)}) copy-start(bf16[512,256]{1,0:T(8,128)(2,1)S(1)} %collective-permute-done.16) | copy-start | bytes 786436
  41.5 8.6 %collective-permute-start.26 = (bf16[4,128,256]{2,1,0:T(8,128)(2,1)S(1)}, bf16[4,128,256]{2,1,0:T(8,128)(2,1)S(1)}, u32[]{:S(2)}, u32[]{:S(2)}) collective-permute-start(bf16[4,128,256]{2,1,0:T(8,128)(2,1)S(1)} %bitcast.55), channel_id=1, source_target_pairs={{0,1},{1,2},{2,3},{3,4},{4,5},{5,6},{6,7},{7,0},{8,9},{9,10},{10,1... | collective-permute-start | bytes 786440 | tf_op jit(solution)/shard_map/ppermute | solution.py:331
  41.7 9.3 %collective-permute-start.17 = (bf16[4,128,256]{2,1,0:T(8,128)(2,1)S(1)}, bf16[4,128,256]{2,1,0:T(8,128)(2,1)S(1)}, u32[]{:S(2)}, u32[]{:S(2)}) collective-permute-start(bf16[4,128,256]{2,1,0:T(8,128)(2,1)S(1)} %bitcast.56), channel_id=1, source_target_pairs={{0,7},{1,0},{2,1},{3,2},{4,3},{5,4},{6,5},{7,6},{8,15},{9,8},{10,9... | collective-permute-start | bytes 786440 | tf_op jit(solution)/shard_map/ppermute | solution.py:331
  46.8 61.8 %copy-start.6 = (bf16[512,256]{1,0:T(8,128)(2,1)}, bf16[512,256]{1,0:T(8,128)(2,1)S(1)}, u32[]{:S(2)}) copy-start(bf16[512,256]{1,0:T(8,128)(2,1)S(1)} %collective-permute-done.1) | copy-start | bytes 786436
  46.8 7.3 %collective-permute-start.4 = (bf16[4,128,256]{2,1,0:T(8,128)(2,1)S(1)}, bf16[4,128,256]{2,1,0:T(8,128)(2,1)S(1)}, u32[]{:S(2)}, u32[]{:S(2)}) collective-permute-start(bf16[4,128,256]{2,1,0:T(8,128)(2,1)S(1)} %bitcast.41), channel_id=1, source_target_pairs={{0,1},{1,2},{2,3},{3,4},{4,5},{5,6},{6,7},{7,0},{8,9},{9,10},{10,1... | collective-permute-start | bytes 786440 | tf_op jit(solution)/shard_map/ppermute | solution.py:331
  47.2 45.9 %copy-start.22 = (bf16[4,128,256]{2,1,0:T(8,128)(2,1)}, bf16[4,128,256]{2,1,0:T(8,128)(2,1)S(1)}, u32[]{:S(2)}) copy-start(bf16[4,128,256]{2,1,0:T(8,128)(2,1)S(1)} %collective-permute-done.22.refs_12_) | copy-start | bytes 786436
  47.2 11.9 %collective-permute-start.7 = (bf16[4,128,256]{2,1,0:T(8,128)(2,1)S(1)}, bf16[4,128,256]{2,1,0:T(8,128)(2,1)S(1)}, u32[]{:S(2)}, u32[]{:S(2)}) collective-permute-start(bf16[4,128,256]{2,1,0:T(8,128)(2,1)S(1)} %bitcast.52), channel_id=1, source_target_pairs={{0,1},{1,2},{2,3},{3,4},{4,5},{5,6},{6,7},{7,0},{8,9},{9,10},{10,1... | collective-permute-start | bytes 786440 | tf_op jit(solution)/shard_map/ppermute | solution.py:331
  47.3 45.9 %copy-start.23 = (bf16[4,128,256]{2,1,0:T(8,128)(2,1)}, bf16[4,128,256]{2,1,0:T(8,128)(2,1)S(1)}, u32[]{:S(2)}) copy-start(bf16[4,128,256]{2,1,0:T(8,128)(2,1)S(1)} %collective-permute-done.18.refs_4_) | copy-start | bytes 786436
  47.3 13.8 %collective-permute-start.10 = (bf16[4,128,256]{2,1,0:T(8,128)(2,1)S(1)}, bf16[4,128,256]{2,1,0:T(8,128)(2,1)S(1)}, u32[]{:S(2)}, u32[]{:S(2)}) collective-permute-start(bf16[4,128,256]{2,1,0:T(8,128)(2,1)S(1)} %bitcast.42), channel_id=1, source_target_pairs={{0,7},{1,0},{2,1},{3,2},{4,3},{5,4},{6,5},{7,6},{8,15},{9,8},{10,9... | collective-permute-start | bytes 786440 | tf_op jit(solution)/shard_map/ppermute | solution.py:331
  50.1 43.1 %copy-start.24 = (bf16[4,128,256]{2,1,0:T(8,128)(2,1)}, bf16[4,128,256]{2,1,0:T(8,128)(2,1)S(1)}, u32[]{:S(2)}) copy-start(bf16[4,128,256]{2,1,0:T(8,128)(2,1)S(1)} %collective-permute-done.26.refs_15_) | copy-start | bytes 786436
  50.1 11.0 %collective-permute-start.13 = (bf16[4,128,256]{2,1,0:T(8,128)(2,1)S(1)}, bf16[4,128,256]{2,1,0:T(8,128)(2,1)S(1)}, u32[]{:S(2)}, u32[]{:S(2)}) collective-permute-start(bf16[4,128,256]{2,1,0:T(8,128)(2,1)S(1)} %bitcast.53), channel_id=1, source_target_pairs={{0,7},{1,0},{2,1},{3,2},{4,3},{5,4},{6,5},{7,6},{8,15},{9,8},{10,9... | collective-permute-start | bytes 786440 | tf_op jit(solution)/shard_map/ppermute | solution.py:331
  51.0 42.2 %copy-start.25 = (bf16[4,128,256]{2,1,0:T(8,128)(2,1)}, bf16[4,128,256]{2,1,0:T(8,128)(2,1)S(1)}, u32[]{:S(2)}) copy-start(bf16[4,128,256]{2,1,0:T(8,128)(2,1)S(1)} %collective-permute-done.17.refs_3_) | copy-start | bytes 786436
  51.0 11.6 %collective-permute-start.23 = (bf16[4,128,256]{2,1,0:T(8,128)(2,1)S(1)}, bf16[4,128,256]{2,1,0:T(8,128)(2,1)S(1)}, u32[]{:S(2)}, u32[]{:S(2)}) collective-permute-start(bf16[4,128,256]{2,1,0:T(8,128)(2,1)S(1)} %collective-permute-done.22.refs_12_), channel_id=1, source_target_pairs={{0,1},{1,2},{2,3},{3,4},{4,5},{5,6},{6,7},{7,0},{8,9},{9,10},{10,1... | collective-permute-start | bytes 786440 | tf_op jit(solution)/shard_map/ppermute | solution.py:331
  54.1 54.5 %copy-start.7 = (bf16[4,128,256]{2,1,0:T(8,128)(2,1)}, bf16[4,128,256]{2,1,0:T(8,128)(2,1)S(1)}, u32[]{:S(2)}) copy-start(bf16[4,128,256]{2,1,0:T(8,128)(2,1)S(1)} %collective-permute-done.4.refs_14_) | copy-start | bytes 786436
  54.2 9.4 %collective-permute-start.19 = (bf16[4,128,256]{2,1,0:T(8,128)(2,1)S(1)}, bf16[4,128,256]{2,1,0:T(8,128)(2,1)S(1)}, u32[]{:S(2)}, u32[]{:S(2)}) collective-permute-start(bf16[4,128,256]{2,1,0:T(8,128)(2,1)S(1)} %collective-permute-done.17.refs_3_), channel_id=1, source_target_pairs={{0,7},{1,0},{2,1},{3,2},{4,3},{5,4},{6,5},{7,6},{8,15},{9,8},{10,9... | collective-permute-start | bytes 786440 | tf_op jit(solution)/shard_map/ppermute | solution.py:331
  59.2 49.4 %copy-start.8 = (bf16[4,128,256]{2,1,0:T(8,128)(2,1)}, bf16[4,128,256]{2,1,0:T(8,128)(2,1)S(1)}, u32[]{:S(2)}) copy-start(bf16[4,128,256]{2,1,0:T(8,128)(2,1)S(1)} %collective-permute-done.7.refs_15_) | copy-start | bytes 786436
  59.2 9.4 %collective-permute-start.20 = (bf16[4,128,256]{2,1,0:T(8,128)(2,1)S(1)}, bf16[4,128,256]{2,1,0:T(8,128)(2,1)S(1)}, u32[]{:S(2)}, u32[]{:S(2)}) collective-permute-start(bf16[4,128,256]{2,1,0:T(8,128)(2,1)S(1)} %collective-permute-done.18.refs_4_), channel_id=1, source_target_pairs={{0,7},{1,0},{2,1},{3,2},{4,3},{5,4},{6,5},{7,6},{8,15},{9,8},{10,9... | collective-permute-start | bytes 786440 | tf_op jit(solution)/shard_map/ppermute | solution.py:331
  61.1 47.5 %copy-start.9 = (bf16[4,128,256]{2,1,0:T(8,128)(2,1)}, bf16[4,128,256]{2,1,0:T(8,128)(2,1)S(1)}, u32[]{:S(2)}) copy-start(bf16[4,128,256]{2,1,0:T(8,128)(2,1)S(1)} %collective-permute-done.10.refs_2_) | copy-start | bytes 786436
  61.1 9.6 %collective-permute-start.27 = (bf16[4,128,256]{2,1,0:T(8,128)(2,1)S(1)}, bf16[4,128,256]{2,1,0:T(8,128)(2,1)S(1)}, u32[]{:S(2)}, u32[]{:S(2)}) collective-permute-start(bf16[4,128,256]{2,1,0:T(8,128)(2,1)S(1)} %collective-permute-done.26.refs_15_), channel_id=1, source_target_pairs={{0,1},{1,2},{2,3},{3,4},{4,5},{5,6},{6,7},{7,0},{8,9},{9,10},{10,1... | collective-permute-start | bytes 786440 | tf_op jit(solution)/shard_map/ppermute | solution.py:331
  61.1 47.5 %copy-start.10 = (bf16[4,128,256]{2,1,0:T(8,128)(2,1)}, bf16[4,128,256]{2,1,0:T(8,128)(2,1)S(1)}, u32[]{:S(2)}) copy-start(bf16[4,128,256]{2,1,0:T(8,128)(2,1)S(1)} %collective-permute-done.13.refs_3_) | copy-start | bytes 786436
  61.1 15.2 %collective-permute-start.5 = (bf16[4,128,256]{2,1,0:T(8,128)(2,1)S(1)}, bf16[4,128,256]{2,1,0:T(8,128)(2,1)S(1)}, u32[]{:S(2)}, u32[]{:S(2)}) collective-permute-start(bf16[4,128,256]{2,1,0:T(8,128)(2,1)S(1)} %collective-permute-done.4.refs_14_), channel_id=1, source_target_pairs={{0,1},{1,2},{2,3},{3,4},{4,5},{5,6},{6,7},{7,0},{8,9},{9,10},{10,1... | collective-permute-start | bytes 786440 | tf_op jit(solution)/shard_map/ppermute | solution.py:331
  62.6 30.6 %copy-start.26 = (bf16[4,128,256]{2,1,0:T(8,128)(2,1)}, bf16[4,128,256]{2,1,0:T(8,128)(2,1)S(1)}, u32[]{:S(2)}) copy-start(bf16[4,128,256]{2,1,0:T(8,128)(2,1)S(1)} %collective-permute-done.23.refs_10_) | copy-start | bytes 786436
  62.6 19.4 %collective-permute-start.8 = (bf16[4,128,256]{2,1,0:T(8,128)(2,1)S(1)}, bf16[4,128,256]{2,1,0:T(8,128)(2,1)S(1)}, u32[]{:S(2)}, u32[]{:S(2)}) collective-permute-start(bf16[4,128,256]{2,1,0:T(8,128)(2,1)S(1)} %collective-permute-done.7.refs_15_), channel_id=1, source_target_pairs={{0,1},{1,2},{2,3},{3,4},{4,5},{5,6},{6,7},{7,0},{8,9},{9,10},{10,1... | collective-permute-start | bytes 786440 | tf_op jit(solution)/shard_map/ppermute | solution.py:331
  63.6 29.7 %copy-start.27 = (bf16[4,128,256]{2,1,0:T(8,128)(2,1)}, bf16[4,128,256]{2,1,0:T(8,128)(2,1)S(1)}, u32[]{:S(2)}) copy-start(bf16[4,128,256]{2,1,0:T(8,128)(2,1)S(1)} %collective-permute-done.19.refs_5_) | copy-start | bytes 786436
  63.6 18.4 %collective-permute-start.21 = (bf16[4,128,256]{2,1,0:T(8,128)(2,1)S(1)}, bf16[4,128,256]{2,1,0:T(8,128)(2,1)}, u32[]{:S(2)}, u32[]{:S(2)}) collective-permute-start(bf16[4,128,256]{2,1,0:T(8,128)(2,1)S(1)} %collective-permute-done.19.refs_5_), channel_id=1, source_target_pairs={{0,7},{1,0},{2,1},{3,2},{4,3},{5,4},{6,5},{7,6},{8,15},{9,8},{10,9... | collective-permute-start | bytes 786440 | tf_op jit(solution)/shard_map/ppermute | solution.py:331
  68.6 24.6 %copy-start.28 = (bf16[4,128,256]{2,1,0:T(8,128)(2,1)}, bf16[4,128,256]{2,1,0:T(8,128)(2,1)S(1)}, u32[]{:S(2)}) copy-start(bf16[4,128,256]{2,1,0:T(8,128)(2,1)S(1)} %collective-permute-done.20.refs_6_) | copy-start | bytes 786436
  68.6 16.0 %collective-permute-start.11 = (bf16[4,128,256]{2,1,0:T(8,128)(2,1)S(1)}, bf16[4,128,256]{2,1,0:T(8,128)(2,1)S(1)}, u32[]{:S(2)}, u32[]{:S(2)}) collective-permute-start(bf16[4,128,256]{2,1,0:T(8,128)(2,1)S(1)} %collective-permute-done.10.refs_2_), channel_id=1, source_target_pairs={{0,7},{1,0},{2,1},{3,2},{4,3},{5,4},{6,5},{7,6},{8,15},{9,8},{10,9... | collective-permute-start | bytes 786440 | tf_op jit(solution)/shard_map/ppermute | solution.py:331
  70.7 14.8 %collective-permute-start.14 = (bf16[4,128,256]{2,1,0:T(8,128)(2,1)S(1)}, bf16[4,128,256]{2,1,0:T(8,128)(2,1)S(1)}, u32[]{:S(2)}, u32[]{:S(2)}) collective-permute-start(bf16[4,128,256]{2,1,0:T(8,128)(2,1)S(1)} %collective-permute-done.13.refs_3_), channel_id=1, source_target_pairs={{0,7},{1,0},{2,1},{3,2},{4,3},{5,4},{6,5},{7,6},{8,15},{9,8},{10,9... | collective-permute-start | bytes 786440 | tf_op jit(solution)/shard_map/ppermute | solution.py:331
  76.3 32.3 %copy-start.11 = (bf16[4,128,256]{2,1,0:T(8,128)(2,1)}, bf16[4,128,256]{2,1,0:T(8,128)(2,1)S(1)}, u32[]{:S(2)}) copy-start(bf16[4,128,256]{2,1,0:T(8,128)(2,1)S(1)} %collective-permute-done.5.refs_12_) | copy-start | bytes 786436
  76.3 11.5 %collective-permute-start.24 = (bf16[4,128,256]{2,1,0:T(8,128)(2,1)S(1)}, bf16[4,128,256]{2,1,0:T(8,128)(2,1)S(1)}, u32[]{:S(2)}, u32[]{:S(2)}) collective-permute-start(bf16[4,128,256]{2,1,0:T(8,128)(2,1)S(1)} %collective-permute-done.23.refs_10_), channel_id=1, source_target_pairs={{0,1},{1,2},{2,3},{3,4},{4,5},{5,6},{6,7},{7,0},{8,9},{9,10},{10,1... | collective-permute-start | bytes 786440 | tf_op jit(solution)/shard_map/ppermute | solution.py:331
  81.9 26.7 %copy-start.12 = (bf16[4,128,256]{2,1,0:T(8,128)(2,1)}, bf16[4,128,256]{2,1,0:T(8,128)(2,1)S(1)}, u32[]{:S(2)}) copy-start(bf16[4,128,256]{2,1,0:T(8,128)(2,1)S(1)} %collective-permute-done.8.refs_13_) | copy-start | bytes 786436
  81.9 11.2 %collective-permute-start.28 = (bf16[4,128,256]{2,1,0:T(8,128)(2,1)S(1)}, bf16[4,128,256]{2,1,0:T(8,128)(2,1)S(1)}, u32[]{:S(2)}, u32[]{:S(2)}) collective-permute-start(bf16[4,128,256]{2,1,0:T(8,128)(2,1)S(1)} %collective-permute-done.27.refs_13_), channel_id=1, source_target_pairs={{0,1},{1,2},{2,3},{3,4},{4,5},{5,6},{6,7},{7,0},{8,9},{9,10},{10,1... | collective-permute-start | bytes 786440 | tf_op jit(solution)/shard_map/ppermute | solution.py:331
  81.9 14.1 %collective-permute-start.25 = (bf16[4,128,256]{2,1,0:T(8,128)(2,1)}, bf16[4,128,256]{2,1,0:T(8,128)(2,1)}, u32[]{:S(2)}, u32[]{:S(2)}) collective-permute-start(bf16[4,128,256]{2,1,0:T(8,128)(2,1)} %collective-permute-done.21.refs_7_), channel_id=1, source_target_pairs={{0,7},{1,0},{2,1},{3,2},{4,3},{5,4},{6,5},{7,6},{8,15},{9,8},{10,9... | collective-permute-start | bytes 786440 | tf_op jit(solution)/shard_map/ppermute | solution.py:331
  84.6 24.0 %copy-start.13 = (bf16[4,128,256]{2,1,0:T(8,128)(2,1)}, bf16[4,128,256]{2,1,0:T(8,128)(2,1)S(1)}, u32[]{:S(2)}) copy-start(bf16[4,128,256]{2,1,0:T(8,128)(2,1)S(1)} %collective-permute-done.11.refs_4_) | copy-start | bytes 786436
  84.6 24.1 %collective-permute-start.6 = (bf16[4,128,256]{2,1,0:T(8,128)(2,1)S(1)}, bf16[4,128,256]{2,1,0:T(8,128)(2,1)S(1)}, u32[]{:S(2)}, u32[]{:S(2)}) collective-permute-start(bf16[4,128,256]{2,1,0:T(8,128)(2,1)S(1)} %collective-permute-done.5.refs_12_), channel_id=1, source_target_pairs={{0,1},{1,2},{2,3},{3,4},{4,5},{5,6},{6,7},{7,0},{8,9},{9,10},{10,1... | collective-permute-start | bytes 786440 | tf_op jit(solution)/shard_map/ppermute | solution.py:331
  85.5 23.2 %collective-permute-start.9 = (bf16[4,128,256]{2,1,0:T(8,128)(2,1)S(1)}, bf16[4,128,256]{2,1,0:T(8,128)(2,1)S(1)}, u32[]{:S(2)}, u32[]{:S(2)}) collective-permute-start(bf16[4,128,256]{2,1,0:T(8,128)(2,1)S(1)} %collective-permute-done.8.refs_13_), channel_id=1, source_target_pairs={{0,1},{1,2},{2,3},{3,4},{4,5},{5,6},{6,7},{7,0},{8,9},{9,10},{10,1... | collective-permute-start | bytes 786440 | tf_op jit(solution)/shard_map/ppermute | solution.py:331
  87.9 20.9 %collective-permute-start.12 = (bf16[4,128,256]{2,1,0:T(8,128)(2,1)S(1)}, bf16[4,128,256]{2,1,0:T(8,128)(2,1)}, u32[]{:S(2)}, u32[]{:S(2)}) collective-permute-start(bf16[4,128,256]{2,1,0:T(8,128)(2,1)S(1)} %collective-permute-done.11.refs_4_), channel_id=1, source_target_pairs={{0,7},{1,0},{2,1},{3,2},{4,3},{5,4},{6,5},{7,6},{8,15},{9,8},{10,9... | collective-permute-start | bytes 786440 | tf_op jit(solution)/shard_map/ppermute | solution.py:331
  94.0 14.8 %collective-permute-start.15 = (bf16[4,128,256]{2,1,0:T(8,128)(2,1)S(1)}, bf16[4,128,256]{2,1,0:T(8,128)(2,1)}, u32[]{:S(2)}, u32[]{:S(2)}) collective-permute-start(bf16[4,128,256]{2,1,0:T(8,128)(2,1)S(1)} %collective-permute-done.14.refs_5_), channel_id=1, source_target_pairs={{0,7},{1,0},{2,1},{3,2},{4,3},{5,4},{6,5},{7,6},{8,15},{9,8},{10,9... | collective-permute-start | bytes 786440 | tf_op jit(solution)/shard_map/ppermute | solution.py:331
  108.7 18.8 %collective-permute-start.29 = (bf16[4,128,256]{2,1,0:T(8,128)(2,1)S(1)}, bf16[4,128,256]{2,1,0:T(8,128)(2,1)S(1)}, u32[]{:S(2)}, u32[]{:S(2)}) collective-permute-start(bf16[4,128,256]{2,1,0:T(8,128)(2,1)S(1)} %collective-permute-done.6.refs_10_), channel_id=1, source_target_pairs={{0,1},{1,2},{2,3},{3,4},{4,5},{5,6},{6,7},{7,0},{8,9},{9,10},{10,1... | collective-permute-start | bytes 786440 | tf_op jit(solution)/shard_map/ppermute | solution.py:331
  108.8 18.8 %collective-permute-start.30 = (bf16[4,128,256]{2,1,0:T(8,128)(2,1)}, bf16[4,128,256]{2,1,0:T(8,128)(2,1)S(1)}, u32[]{:S(2)}, u32[]{:S(2)}) collective-permute-start(bf16[4,128,256]{2,1,0:T(8,128)(2,1)} %collective-permute-done.15.refs_7_), channel_id=1, source_target_pairs={{0,7},{1,0},{2,1},{3,2},{4,3},{5,4},{6,5},{7,6},{8,15},{9,8},{10,9... | collective-permute-start | bytes 786440 | tf_op jit(solution)/shard_map/ppermute | solution.py:331
  168.5 15.9 %collective-permute-start.32 = (bf16[8,2,58,8,128]{4,3,2,1,0:T(8,128)(2,1)}, bf16[8,2,58,8,128]{4,3,2,1,0:T(8,128)(2,1)S(1)}, u32[]{:S(2)}, u32[]{:S(2)}) collective-permute-start(bf16[8,2,58,8,128]{4,3,2,1,0:T(8,128)(2,1)} %get-tuple-element.100), channel_id=1, source_target_pairs={{0,16},{16,0},{1,17},{17,1},{2,18},{18,2},{3,19},{19,3},{4,20},{20... | collective-permute-start | bytes 5701640 | tf_op jit(solution)/shard_map/ppermute | solution.py:361
  187.7 31.8 %all-to-all-start.1 = ((bf16[16,58,8,128]{3,2,1,0:T(8,128)(2,1)}), bf16[16,58,8,128]{3,2,1,0:T(8,128)(2,1)S(1)}, u32[]{:S(2)}, u32[]{:S(2)}) async-start(bf16[16,58,8,128]{3,2,1,0:T(8,128)(2,1)} %bitcast.40), calls=%async_computation.2 | async-start | bytes 3801088 | tf_op jit(solution)/shard_map/all_to_all | solution.py:367
  202.9 3.2 %collective-permute-start.31 = (bf16[8,2,32,8,128]{4,3,2,1,0:T(8,128)(2,1)}, bf16[8,2,32,8,128]{4,3,2,1,0:T(8,128)(2,1)S(1)}, u32[]{:S(2)}, u32[]{:S(2)}) collective-permute-start(bf16[8,2,32,8,128]{4,3,2,1,0:T(8,128)(2,1)} %get-tuple-element.98), channel_id=1, source_target_pairs={{0,16},{16,0},{1,17},{17,1},{2,18},{18,2},{3,19},{19,3},{4,20},{20... | collective-permute-start | bytes 3145736 | tf_op jit(solution)/shard_map/ppermute | solution.py:361
  219.5 19.9 %all-to-all-start.2 = ((bf16[16,32,8,128]{3,2,1,0:T(8,128)(2,1)}), bf16[16,32,8,128]{3,2,1,0:T(8,128)(2,1)S(1)}, u32[]{:S(2)}, u32[]{:S(2)}) async-start(bf16[16,32,8,128]{3,2,1,0:T(8,128)(2,1)} %bitcast.19), calls=%async_computation.3 | async-start | bytes 2097152 | tf_op jit(solution)/shard_map/all_to_all | solution.py:367
  225.5 29.2 %copy-start.2 = (bf16[8,128,256]{2,1,0:T(8,128)(2,1)S(1)}, bf16[8,128,256]{2,1,0:T(8,128)(2,1)}, u32[]{:S(2)}) copy-start(bf16[8,128,256]{2,1,0:T(8,128)(2,1)} %reduce-scatter.2.cloned.1.call-done) | copy-start | bytes 1572868
  226.6 23.9 %collective-permute-start.33 = (bf16[512,256]{1,0:T(8,128)(2,1)S(1)}, bf16[512,256]{1,0:T(8,128)(2,1)S(1)}, u32[]{:S(2)}, u32[]{:S(2)}) collective-permute-start(bf16[512,256]{1,0:T(8,128)(2,1)S(1)} %dynamic-slice_bitcast_fusion), channel_id=1, source_target_pairs={{0,8},{8,0},{1,9},{9,1},{2,10},{10,2},{3,11},{11,3},{4,12},{12,4},... | collective-permute-start | bytes 786440 | tf_op jit(solution)/shard_map/ppermute | solution.py:335
  229.6 9.2 %collective-permute-start.34 = (f32[16,8,128]{2,1,0:T(8,128)S(1)}, f32[16,8,128]{2,1,0:T(8,128)S(1)}, u32[]{:S(2)}, u32[]{:S(2)}) collective-permute-start(f32[16,8,128]{2,1,0:T(8,128)S(1)} %slice.15), channel_id=1, source_target_pairs={{0,0},{1,16},{2,32},{3,48},{4,64},{5,80},{6,96},{7,112},{16,128},{... | collective-permute-start | bytes 196616 | tf_op jit(solution)/shard_map/ppermute | solution.py:465
  251.3 11.3 %all-to-all-start.3 = ((f32[8,32,128]{2,1,0:T(8,128)}), f32[8,32,128]{2,1,0:T(8,128)S(1)}, u32[]{:S(2)}, u32[]{:S(2)}) async-start(f32[8,32,128]{2,1,0:T(8,128)} %bitcast.22), calls=%async_computation.4 | async-start | bytes 262144 | tf_op jit(solution)/shard_map/all_to_all | solution.py:469
  (9 other events, 91.7 us)
Sparse Core Ops, SparseCore 0:
  32.0 52.3 all-gather.2
  157.2 64.7 reduce-scatter.1

commit v6 on v5

--- a/solution.py
+++ b/solution.py
@@ -32,7 +32,7 @@
     side, own = c // HID, c % HID
     at = own // SLOTS
     slot = own - jnp.minimum(at * SLOTS, HID - SLOTS)
-    start = 16 + (side * SLOTS + slot) * 2
+    start = (side * SLOTS + slot) * 2
     return held[kind * 5 + at, pl.ds(start, 2)].reshape(BLOCK, BLOCK)
 
 
@@ -59,11 +59,23 @@
     return run
 
 
-def collect(where, shards, out):
+def copy(pairs, sems, first=0):
+    copies = [pltpu.make_async_copy(a, b, sems.at[first + k]) for k, (a, b) in enumerate(pairs)]
+    for one in copies:
+        one.start()
+    return copies
+
+
+def wait(copies):
+    for one in copies:
+        one.wait()
+
+
+def placed(where, shards, out):
     me, z = where[0], where[1]
     for k, shard in enumerate(shards):
         side = me if k % 2 == 0 else 1 - me
-        out[pl.ds(side * 32 + lax.rem(z + k // 2, 8) * PER, PER)] = shard[...]
+        yield shard, out.at[pl.ds(side * 32 + lax.rem(z + k // 2, 8) * PER, PER)]
 
 
 def turn(swap, source, target, outer):
@@ -73,13 +85,16 @@
         target[k * 16 : k * 16 + 16, pl.ds(outer, 16), :] = tile
 
 
-def forward_first_kernel(where, swap, held, *refs):
-    shards, (x, gate_in, up_in, mid_g, mid_u) = refs[:16], refs[16:]
-    collect(where, shards, x)
-
-    def group(at, carry):
+def forward_first_kernel(where, swap, held_all, *refs):
+    shards, (x_out, gate_out, up_out) = refs[:16], refs[16:19]
+    x, held, gate_in, up_in, mid_g, mid_u, ins, outs = refs[19:]
+    arrive = copy(list(placed(where, shards, x)) + [(held_all.at[:, pl.ds(0, 16)], held)], ins)
+    wait(arrive)
+    leave = copy([(x, x_out)], outs)
+    for at in range(4):
+
         @loop(16, 4)
-        def _(ks):
+        def _(ks, at=at):
             weights = [
                 jnp.concatenate([first_weight(held, 0, at * 16 + k), first_weight(held, 1, at * 16 + k)])
                 for k in ks
@@ -89,12 +104,12 @@
                 mid_g[k] = mid[:ROWS]
                 mid_u[k] = mid[ROWS:]
 
-        outer = pl.multiple_of(at * 16, 16)
-        turn(swap, mid_g, gate_in, outer)
-        turn(swap, mid_u, up_in, outer)
-        return carry
-
-    lax.fori_loop(0, 4, group, 0)
+        turn(swap, mid_g, gate_in, at * 16)
+        turn(swap, mid_u, up_in, at * 16)
+        part = pl.ds(at * 16, 16)
+        pairs = [(gate_in.at[:, part], gate_out.at[:, part]), (up_in.at[:, part], up_out.at[:, part])]
+        leave += copy(pairs, outs, 1 + 2 * at)
+    wait(leave)
 
 
 def hidden(ref, c):
@@ -115,29 +130,44 @@
     lax.fori_loop(0, 4, group, 0)
 
 
-def forward_second_kernel(swap, held, gate_in, up_in, act, to_gate, to_up, down_in, down_mid):
+def forward_second_kernel(swap, held_all, gate_from, up_from, *refs):
+    act_out, to_gate_out, to_up_out, down_out = refs[:4]
+    held, gate_in, up_in, act, to_gate, to_up, down_in, down_mid, ins, outs = refs[4:]
+    wait(copy([(held_all.at[:, pl.ds(16, 12)], held), (gate_from, gate_in), (up_from, up_in)], ins))
     down_mid[EACH:] = jnp.zeros((ROWS - EACH, NBD, TOK), BF)
-
-    @loop(MINE, 2)
-    def _(cs):
-        gates = [dot_first(second_weight(held, 0, c), hidden(gate_in, c)) for c in cs]
-        ups = [dot_first(second_weight(held, 1, c), hidden(up_in, c)) for c in cs]
-        sigmas = [jax.nn.sigmoid(g) for g in gates]
-        acts = [(g * s * u).astype(BF) for g, s, u in zip(gates, sigmas, ups)]
-        downs = [dot_first(second_weight(held, 2, c), a) for c, a in zip(cs, acts)]
-        for c, g, s, u, a, d in zip(cs, gates, sigmas, ups, acts, downs):
-            to_gate[c], to_up[c], act[c] = u * s * (1.0 + g * (1.0 - s)), g * s, a
-            down_mid[pl.ds(c * SUB, SUB)] = d.astype(BF).reshape(SUB, NBD, TOK)
-
+    leave = []
+    for part in range(2):
+
+        @loop(HID, 2)
+        def _(owns, part=part):
+            cs = [part * HID + own for own in owns]
+            gates = [dot_first(second_weight(held, 0, c), hidden(gate_in, c)) for c in cs]
+            ups = [dot_first(second_weight(held, 1, c), hidden(up_in, c)) for c in cs]
+            sigmas = [jax.nn.sigmoid(g) for g in gates]
+            acts = [(g * s * u).astype(BF) for g, s, u in zip(gates, sigmas, ups)]
+            downs = [dot_first(second_weight(held, 2, c), a) for c, a in zip(cs, acts)]
+            for c, g, s, u, a, d in zip(cs, gates, sigmas, ups, acts, downs):
+                to_gate[c], to_up[c], act[c] = u * s * (1.0 + g * (1.0 - s)), g * s, a
+                down_mid[pl.ds(c * SUB, SUB)] = d.astype(BF).reshape(SUB, NBD, TOK)
+
+        rows = pl.ds(part * HID, HID)
+        pairs = [(to_gate, to_gate_out), (to_up, to_up_out), (act, act_out)]
+        leave += copy([(a.at[rows], b.at[rows]) for a, b in pairs], outs, 3 * part)
     turn_back(swap, down_mid, down_in, 0)
-
-
-def backward_kernel(where, swap, held, to_gate, to_up, *refs):
-    shards = refs[:16]
-    dy, back_in, gate_back, up_back, low, parts, mid, low_g, low_u = refs[16:]
-    collect(where, shards, dy)
+    wait(leave + copy([(down_in, down_out)], outs, 6))
+
+
+def backward_kernel(where, swap, held_all, to_gate_from, to_up_from, *refs):
+    shards, out = refs[:16], refs[16:22]
+    dy, held, held_second, to_gate, to_up, back_in, gate_back, up_back = refs[22:30]
+    low, parts, mid, low_g, low_u, ins, outs = refs[30:]
+    arrive = copy(list(placed(where, shards, dy)) + [(held_all.at[:, pl.ds(0, 16)], held)], ins)
+    pairs = [(held_all.at[:, pl.ds(16, 12)], held_second), (to_gate_from, to_gate), (to_up_from, to_up)]
+    later = copy(pairs, ins, 17)
     low_g[EACH:] = jnp.zeros((ROWS - EACH, NBD, TOK), BF)
     low_u[EACH:] = jnp.zeros((ROWS - EACH, NBD, TOK), BF)
+    wait(arrive)
+    leave = copy([(dy, out[0])], outs)
 
     def group(at, carry):
         @loop(16, 4)
@@ -150,31 +180,41 @@
         return carry
 
     lax.fori_loop(0, 4, group, 0)
+    leave += copy([(back_in, out[1])], outs, 1)
+    wait(later)
 
     @loop(MINE, 2)
     def _(cs):
-        grads = [dot(second_weight(held, 2, c), hidden(back_in, c)) for c in cs]
+        grads = [dot(second_weight(held_second, 2, c), hidden(back_in, c)) for c in cs]
         to_gates = [(grad * to_gate[c]).astype(BF) for c, grad in zip(cs, grads)]
         to_ups = [(grad * to_up[c]).astype(BF) for c, grad in zip(cs, grads)]
-        lows_g = [dot(second_weight(held, 0, c), v) for c, v in zip(cs, to_gates)]
-        lows_u = [dot(second_weight(held, 1, c), v) for c, v in zip(cs, to_ups)]
+        lows_g = [dot(second_weight(held_second, 0, c), v) for c, v in zip(cs, to_gates)]
+        lows_u = [dot(second_weight(held_second, 1, c), v) for c, v in zip(cs, to_ups)]
         for c, g, u, lg, lu in zip(cs, to_gates, to_ups, lows_g, lows_u):
             gate_back[c], up_back[c] = g, u
             low_g[pl.ds(c * SUB, SUB)] = lg.astype(BF).reshape(SUB, NBD, TOK)
             low_u[pl.ds(c * SUB, SUB)] = lu.astype(BF).reshape(SUB, NBD, TOK)
 
+    leave += copy([(gate_back, out[2]), (up_back, out[3])], outs, 2)
     turn_back(swap, low_g, low, 0)
     turn_back(swap, low_u, low, ROWS)
-
-    @loop(NBD, 4)
-    def _(blocks):
-        weights = [
-            jnp.concatenate([first_weight(held, 0, i), first_weight(held, 1, i)]) for i in blocks
-        ]
-        values = [dot_first(w, low[i]).astype(BF) for w, i in zip(weights, blocks)]
-        for i, value in zip(blocks, values):
-            side, at = i // 32, i % 32
-            parts[(at // PER) * 8 + side * PER + at % PER] = value
+    leave += copy([(low, out[4])], outs, 4)
+    for part in range(4):
+
+        @loop(16, 4)
+        def _(ks, part=part):
+            at = [part * 16 + k for k in ks]
+            blocks = [k % 8 // PER * 32 + k // 8 * PER + k % PER for k in at]
+            weights = [
+                jnp.concatenate([first_weight(held, 0, i), first_weight(held, 1, i)]) for i in blocks
+            ]
+            values = [dot_first(w, low[i]).astype(BF) for w, i in zip(weights, blocks)]
+            for k, value in zip(at, values):
+                parts[k] = value
+
+        rows = pl.ds(part * 16, 16)
+        leave += copy([(parts.at[rows], out[5].at[rows])], outs, 5 + part)
+    wait(leave)
 
 
 def put(keep, send, core, index, even, odd):
@@ -247,11 +287,14 @@
     )(*args)
 
 
+ANY = pl.BlockSpec(memory_space=pl.ANY)
 HIDDEN = ((MINE, BLOCK, TOK), BF)
 WIDER = ((MINE, BLOCK, TOK), F32)
 SPREAD = ((ROWS, NBD, TOK), BF)
 MODEL = ((NBD, BLOCK, TOK), BF)
 TILE = ((16, ROWS, TOK), BF)
+FIRST = ((16, 16, ROWS, BLOCK), BF)
+SECOND = ((16, 12, ROWS, BLOCK), BF)
 ONE = 2 * 448 * 4 * 128 * 512
 
 
@@ -262,22 +305,39 @@
     return jnp.asarray(table, BF)
 
 
+def copying(kernel, outs, scratch, arrivals, flops, near, *args):
+    moved = sum(a.size * a.dtype.itemsize for a in args)
+    specs = [SM if a.dtype == jnp.int32 else VM for a in args[:near]] + [ANY] * (len(args) - near)
+    return pl.pallas_call(
+        kernel,
+        out_shape=[jax.ShapeDtypeStruct(shape, dtype) for shape, dtype in outs],
+        in_specs=specs,
+        out_specs=[ANY] * len(outs),
+        scratch_shapes=[pltpu.VMEM(shape, dtype) for shape, dtype in scratch]
+        + [pltpu.SemaphoreType.DMA((arrivals,)), pltpu.SemaphoreType.DMA((9,))],
+        compiler_params=pltpu.CompilerParams(vmem_limit_bytes=60 << 20),
+        cost_estimate=pl.CostEstimate(flops=flops, bytes_accessed=moved, transcendentals=0),
+    )(*args)
+
+
 def forward_first(where, swap, held, shards):
-    return call(forward_first_kernel, [MODEL, SPREAD, SPREAD], [TILE, TILE], 6 * ONE, where, swap, held, *shards)
+    outs = [MODEL, SPREAD, SPREAD]
+    scratch = [MODEL, FIRST, SPREAD, SPREAD, TILE, TILE]
+    return copying(forward_first_kernel, outs, scratch, 17, 6 * ONE, 2, where, swap, held, *shards)
 
 
 def forward_second(swap, held, gate_in, up_in):
     outs = [HIDDEN, WIDER, WIDER, SPREAD]
-    return call(forward_second_kernel, outs, [SPREAD], 5 * ONE, swap, held, gate_in, up_in)
+    scratch = [SECOND, SPREAD, SPREAD, HIDDEN, WIDER, WIDER, SPREAD, SPREAD]
+    return copying(forward_second_kernel, outs, scratch, 3, 5 * ONE, 1, swap, held, gate_in, up_in)
 
 
 def backward(where, swap, held, to_gate, to_up, shards):
-    return call(
-        backward_kernel,
-        [MODEL, SPREAD, HIDDEN, HIDDEN, MODEL, MODEL],
-        [TILE, SPREAD, SPREAD],
-        12 * ONE,
-        where, swap, held, to_gate, to_up, *shards,
+    outs = [MODEL, SPREAD, HIDDEN, HIDDEN, MODEL, MODEL]
+    scratch = [MODEL, FIRST, SECOND, WIDER, WIDER, SPREAD, HIDDEN, HIDDEN, MODEL, MODEL]
+    scratch += [TILE, SPREAD, SPREAD]
+    return copying(
+        backward_kernel, outs, scratch, 20, 12 * ONE, 2, where, swap, held, to_gate, to_up, *shards
     )
 
 
@@ -450,7 +510,6 @@
     later = to_chips(sum_cores(*later))
     firsts, later = lax.optimization_barrier((firsts, later))
     firsts = to_chips(firsts)
-    firsts, other = lax.optimization_barrier((firsts, other))
     input_grad = jnp.concatenate(
         [jnp.where(me == 0, kept, other), jnp.where(me == 0, other, kept)], axis=1
     )

time: 274 us -> 262 us (0.956)
  Pallas kernels: 78.5 us -> 68.1 us
    pallas_call x4 -> x1, Pallas kernels: 59 us -> 1.75 us  [call(): pl.pallas_call(kernel, out_shape=shapes, in_specs=[SM if a.dtype == jnp.i...]
    pallas_call x0 -> x3, Pallas kernels: none -> 46.9 us  [copying(): pl.pallas_call(kernel, out_shape=[jax.ShapeDtypeStruct(shape, dtype) for...]
    ppermute x4, waiting for transfers between devices: 17.3 us -> 6.3 us  [swap(): return lax.ppermute(value, 'x_hi', [(0, 1), (1, 0)])]
    all_to_all x2, waiting for transfers between devices: 10.9 us -> 21.8 us  [to_chips(): return lax.all_to_all(pairs, CHIPS, 0, 0, tiled=True)]
  transfers between devices with their start and end apart: 41 -> 41, of which waited for: 21 -> 20; matrix products, arithmetic and copies ran while one was open for 4% -> 4% of each run, Pallas kernels for 18% -> 18%
where the time goes in v6:
time: 262 us; the launch traced here: 259 us
  starting transfers between devices  90.5 us (35%)
  waiting for transfers between devices  68.5 us (26%)
  Pallas kernels  68.1 us (26%)
  between operations  14.6 us (6%)
  other arithmetic  12.2 us (5%)
  local copies, waits for them, and re-layouts  5.47 us (2%)
    pallas_call x3, Pallas kernels, copying(): pl.pallas_call(kernel, out_shape=[jax.ShapeDtypeStruct(shape, dtype) for...  46.9 us
    ppermute x28, starting transfers between devices, shift(): lax.ppermute(value, 'z', [(i, (i + step) % count) for i in range(count)])  34.6 us
    ppermute x28, waiting for transfers between devices, shift(): lax.ppermute(value, 'z', [(i, (i + step) % count) for i in range(count)])  24.6 us
    all_to_all x2, waiting for transfers between devices, to_chips(): return lax.all_to_all(pairs, CHIPS, 0, 0, tiled=True)  21.8 us
    pallas_call x2, Pallas kernels, grads_call(): pl.pallas_call(kernel, grid=(8,), out_shape=[jax.ShapeDtypeStruct(shape,...  19.5 us
    all_to_all x2, starting transfers between devices, to_chips(): return lax.all_to_all(pairs, CHIPS, 0, 0, tiled=True)  12.9 us
    ppermute x2, starting transfers between devices, sum_cores(): found = lax.ppermute(send, 'core', [(0, 1), (1, 0)])  12.9 us
    all_to_all x1, starting transfers between devices, share_first(): return lax.all_to_all(first, TENSOR, 0, 0, tiled=True)  11.7 us
  transfers between devices with their start and end apart: 41, of which 20 were waited for; matrix products, arithmetic and copies ran while one was open for 4% of the time, Pallas kernels for 18%

profile of v6, /device:TPU:1, one launch (start us, length us, event | category | flops | bytes accessed | tf_op | source)
XLA Modules:
  0.0 259.4 jit_solution(887081654773741297)
XLA Ops:
  7.2 1.0 fusion
  8.4 0.8 broadcast_in_dim.2
  9.1 11.7 %all-to-all-start = ((bf16[16,64,128]{2,1,0:T(8,128)(2,1)}), bf16[16,64,128]{2,1,0:T(8,128)(2,1)S(1)}, u32[]{:S(2)}, u32[]{:S(2)}) async-start(bf16[16,64,128]{2,1,0:T(8,128)(2,1)} %bitcast.10), calls=%async_computation | async-start | bytes 524288 | tf_op jit(solution)/shard_map/all_to_all | solution.py:444
  20.9 1.0 select_select_fusion
  21.9 3.0 %collective-permute-start = (bf16[3,128,128]{2,1,0:T(8,128)(2,1)S(1)}, bf16[3,128,128]{2,1,0:T(8,128)(2,1)S(1)}, u32[]{:S(2)}, u32[]{:S(2)}) collective-permute-start(bf16[3,128,128]{2,1,0:T(8,128)(2,1)S(1)} %select_select_fusion), channel_id=1, source_target_pairs={{0,8},{8,0},{1,9},{9,1},{2,10},{10,2},{3,11},{11,3},{4,12},{12,4},... | collective-permute-start | bytes 294920 | tf_op jit(solution)/shard_map/ppermute | solution.py:395
  24.9 3.4 %collective-permute-done = bf16[3,128,128]{2,1,0:T(8,128)(2,1)S(1)} collective-permute-done((bf16[3,128,128]{2,1,0:T(8,128)(2,1)S(1)}, bf16[3,128,128]{2,1,0:T(8,128)(2,1)S(1)}, u32[]{:S(2)}, u32[]{:S(2)}) %collective-permute-start) | collective-permute-done | bytes 98336 | tf_op jit(solution)/shard_map/ppermute | solution.py:395
  28.3 2.8 %all-to-all-done = bf16[16,64,128]{2,1,0:T(8,128)(2,1)S(1)} async-done(((bf16[16,64,128]{2,1,0:T(8,128)(2,1)}), bf16[16,64,128]{2,1,0:T(8,128)(2,1)S(1)}, u32[]{:S(2)}, u32[]{:S(2)}) %all-to-all-start) | async-done | bytes 262176 | tf_op jit(solution)/shard_map/all_to_all | solution.py:444
  31.1 0.8 pad_maximum_fusion.1
  32.0 1.5 collective-permute-start.3
  33.5 1.2 collective-permute-start.2
  34.8 0.7 collective-permute-start.16
  35.5 2.4 collective-permute-start.1
  39.1 2.2 collective-permute-start.18
  41.7 2.4 collective-permute-start.17
  44.2 2.6 %collective-permute-done.1 = bf16[512,256]{1,0:T(8,128)(2,1)S(1)} collective-permute-done((bf16[512,256]{1,0:T(8,128)(2,1)S(1)}, bf16[512,256]{1,0:T(8,128)(2,1)S(1)}, u32[]{:S(2)}, u32[]{:S(2)}) %collective-permute-start.1) | collective-permute-done | bytes 262176 | tf_op jit(solution)/shard_map/ppermute | solution.py:395
  47.3 2.6 collective-permute-start.10
  50.1 0.9 collective-permute-start.13
  51.5 2.6 %collective-permute-done.4.refs_14_ = bf16[4,128,256]{2,1,0:T(8,128)(2,1)S(1)} collective-permute-done((bf16[4,128,256]{2,1,0:T(8,128)(2,1)S(1)}, bf16[4,128,256]{2,1,0:T(8,128)(2,1)S(1)}, u32[]{:S(2)}, u32[]{:S(2)}) %collective-permute-start.4) | collective-permute-done | bytes 262176 | tf_op jit(solution)/shard_map/ppermute | solution.py:391
  54.2 1.8 collective-permute-start.19
  55.9 3.3 %collective-permute-done.7.refs_15_ = bf16[4,128,256]{2,1,0:T(8,128)(2,1)S(1)} collective-permute-done((bf16[4,128,256]{2,1,0:T(8,128)(2,1)S(1)}, bf16[4,128,256]{2,1,0:T(8,128)(2,1)S(1)}, u32[]{:S(2)}, u32[]{:S(2)}) %collective-permute-start.7) | collective-permute-done | bytes 262176 | tf_op jit(solution)/shard_map/ppermute | solution.py:391
  59.2 1.9 collective-permute-start.20
  61.2 1.4 collective-permute-done.23.refs_10_
  62.6 1.0 collective-permute-start.8
  63.6 3.3 %collective-permute-start.21 = (bf16[4,128,256]{2,1,0:T(8,128)(2,1)S(1)}, bf16[4,128,256]{2,1,0:T(8,128)(2,1)}, u32[]{:S(2)}, u32[]{:S(2)}) collective-permute-start(bf16[4,128,256]{2,1,0:T(8,128)(2,1)S(1)} %collective-permute-done.19.refs_5_), channel_id=1, source_target_pairs={{0,7},{1,0},{2,1},{3,2},{4,3},{5,4},{6,5},{7,6},{8,15},{9,8},{10,9... | collective-permute-start | bytes 786440 | tf_op jit(solution)/shard_map/ppermute | solution.py:391
  66.8 1.8 collective-permute-done.20.refs_6_
  68.6 2.1 collective-permute-start.11
  70.7 1.6 collective-permute-start.14
  72.3 4.0 %collective-permute-done.5.refs_12_ = bf16[4,128,256]{2,1,0:T(8,128)(2,1)S(1)} collective-permute-done((bf16[4,128,256]{2,1,0:T(8,128)(2,1)S(1)}, bf16[4,128,256]{2,1,0:T(8,128)(2,1)S(1)}, u32[]{:S(2)}, u32[]{:S(2)}) %collective-permute-start.5) | collective-permute-done | bytes 262176 | tf_op jit(solution)/shard_map/ppermute | solution.py:391
  76.3 5.6 %collective-permute-done.8.refs_13_ = bf16[4,128,256]{2,1,0:T(8,128)(2,1)S(1)} collective-permute-done((bf16[4,128,256]{2,1,0:T(8,128)(2,1)S(1)}, bf16[4,128,256]{2,1,0:T(8,128)(2,1)S(1)}, u32[]{:S(2)}, u32[]{:S(2)}) %collective-permute-start.8) | collective-permute-done | bytes 262176 | tf_op jit(solution)/shard_map/ppermute | solution.py:391
  81.9 2.7 %collective-permute-start.25 = (bf16[4,128,256]{2,1,0:T(8,128)(2,1)}, bf16[4,128,256]{2,1,0:T(8,128)(2,1)}, u32[]{:S(2)}, u32[]{:S(2)}) collective-permute-start(bf16[4,128,256]{2,1,0:T(8,128)(2,1)} %collective-permute-done.21.refs_7_), channel_id=1, source_target_pairs={{0,7},{1,0},{2,1},{3,2},{4,3},{5,4},{6,5},{7,6},{8,15},{9,8},{10,9... | collective-permute-start | bytes 786440 | tf_op jit(solution)/shard_map/ppermute | solution.py:391
  84.6 0.9 collective-permute-done.14.refs_5_
  85.5 2.4 collective-permute-start.9
  87.9 1.3 collective-permute-start.12
  89.2 4.0 %collective-permute-done.28.refs_11_ = bf16[4,128,256]{2,1,0:T(8,128)(2,1)S(1)} collective-permute-done((bf16[4,128,256]{2,1,0:T(8,128)(2,1)S(1)}, bf16[4,128,256]{2,1,0:T(8,128)(2,1)S(1)}, u32[]{:S(2)}, u32[]{:S(2)}) %collective-permute-start.28) | collective-permute-done | bytes 262176 | tf_op jit(solution)/shard_map/ppermute | solution.py:391
  93.3 0.7 copy-done.30
  94.0 1.5 collective-permute-start.15
  96.1 10.7 %shard_map.144 = (bf16[64,128,256]{2,1,0:T(8,128)(2,1)}, bf16[64,64,256]{2,1,0:T(8,128)(2,1)}, bf16[64,64,256]{2,1,0:T(8,128)(2,1)}) custom-call(s32[3]{0:T(128)} %pad_add_fusion.where, bf16[256,256]{1,0:T(8,128)(2,1)} %constant.82.clone.swap, bf16[16,28,64,128]{3,2,1,0:T(8,128)(2,1)} %bitcast.37, bf16[4,128,256]{2,1,0:T(8,128)(2,1)} %bitcast.46, ...), custom_call_target="tpu_custom_call" | custom-call | flops 1409286144 | bytes 11665420 | tf_op jit(solution)/shard_map/pallas_call | solution.py:311
  107.1 2.7 %collective-permute-start.30 = (bf16[4,128,256]{2,1,0:T(8,128)(2,1)}, bf16[4,128,256]{2,1,0:T(8,128)(2,1)S(1)}, u32[]{:S(2)}, u32[]{:S(2)}) collective-permute-start(bf16[4,128,256]{2,1,0:T(8,128)(2,1)} %collective-permute-done.15.refs_7_), channel_id=1, source_target_pairs={{0,7},{1,0},{2,1},{3,2},{4,3},{5,4},{6,5},{7,6},{8,15},{9,8},{10,9... | collective-permute-start | bytes 786440 | tf_op jit(solution)/shard_map/ppermute | solution.py:391
  109.7 13.5 %shard_map.145 = (bf16[28,128,256]{2,1,0:T(8,128)(2,1)}, f32[28,128,256]{2,1,0:T(8,128)}, f32[28,128,256]{2,1,0:T(8,128)}, bf16[64,64,256]{2,1,0:T(8,128)(2,1)}) custom-call(bf16[256,256]{1,0:T(8,128)(2,1)} %constant.82.clone.swap, bf16[16,28,64,128]{3,2,1,0:T(8,128)(2,1)} %bitcast.38, bf16[64,64,256]{2,1,0:T(8,128)(2,1)} %get-tuple-element.77.gate_from.gate_in, ...), custom_call_target="tpu_custom_call" | custom-call | flops 1174405120 | bytes 11665408 | tf_op jit(solution)/shard_map/pallas_call | solution.py:311
  123.3 0.7 copy-done.16
  124.1 22.6 %shard_map.146 = (bf16[64,128,256]{2,1,0:T(8,128)(2,1)}, bf16[64,64,256]{2,1,0:T(8,128)(2,1)}, bf16[28,128,256]{2,1,0:T(8,128)(2,1)}, bf16[28,128,256]{2,1,0:T(8...) custom-call(s32[3]{0:T(128)} %pad_add_fusion.where, bf16[256,256]{1,0:T(8,128)(2,1)} %constant.82.clone.swap, ...), custom_call_target="tpu_custom_call" | custom-call | flops 2818572288 | bytes 19005452 | tf_op jit(solution)/shard_map/pallas_call | solution.py:311
  146.7 11.5 %shard_map.147 = (bf16[8,2,58,8,128]{4,3,2,1,0:T(8,128)(2,1)}, bf16[8,2,58,8,128]{4,3,2,1,0:T(8,128)(2,1)}) custom-call(s32[3]{0:T(128)} %pad_add_fusion.where, bf16[64,128,256]{2,1,0:T(8,128)(2,1)} %get-tuple-element.85.dy, bf16[64,64,256]{2,1,0:T(8,128)(2,1)} %get-tuple-element.86.down_in, bf16[28,128,256]{2,1,0:T(8,128)(2,1)} %get-tuple-element.87.act, ...), custom_call_target="tpu_custom_call" | custom-call | flops 939524096 | bytes 18087936 | tf_op jit(solution)/shard_map/pallas_call | solution.py:354
  158.2 12.2 %collective-permute-start.33 = (bf16[8,2,58,8,128]{4,3,2,1,0:T(8,128)(2,1)}, bf16[8,2,58,8,128]{4,3,2,1,0:T(8,128)(2,1)S(1)}, u32[]{:S(2)}, u32[]{:S(2)}) collective-permute-start(bf16[8,2,58,8,128]{4,3,2,1,0:T(8,128)(2,1)} %get-tuple-element.98), channel_id=1, source_target_pairs={{0,16},{16,0},{1,17},{17,1},{2,18},{18,2},{3,19},{19,3},{4,20},{20... | collective-permute-start | bytes 5701640 | tf_op jit(solution)/shard_map/ppermute | solution.py:421
  170.4 3.7 %collective-permute-done.33 = bf16[8,2,58,8,128]{4,3,2,1,0:T(8,128)(2,1)S(1)} collective-permute-done((bf16[8,2,58,8,128]{4,3,2,1,0:T(8,128)(2,1)}, bf16[8,2,58,8,128]{4,3,2,1,0:T(8,128)(2,1)S(1)}, u32[]{:S(2)}, u32[]{:S(2)}) %collective-permute-start.33) | collective-permute-done | bytes 1900576 | tf_op jit(solution)/shard_map/ppermute | solution.py:421
  174.1 3.3 %add_convert_fusion = bf16[8,2,58,8,128]{4,3,2,1,0:T(8,128)(2,1)} fusion(bf16[8,2,58,8,128]{4,3,2,1,0:T(8,128)(2,1)S(1)} %collective-permute-done.33, bf16[8,2,58,8,128]{4,3,2,1,0:T(8,128)(2,1)} %get-tuple-element.97), kind=kLoop, calls=%fused_computation.1 | loop fusion | flops 3801088 | bytes 5701632 | tf_op jit(solution)/shard_map/convert_element_type | solution.py:422
  177.4 7.2 %all-to-all-start.1 = ((bf16[16,58,8,128]{3,2,1,0:T(8,128)(2,1)}), bf16[16,58,8,128]{3,2,1,0:T(8,128)(2,1)S(1)}, u32[]{:S(2)}, u32[]{:S(2)}) async-start(bf16[16,58,8,128]{3,2,1,0:T(8,128)(2,1)} %bitcast.40), calls=%async_computation.2 | async-start | bytes 3801088 | tf_op jit(solution)/shard_map/all_to_all | solution.py:427
  184.6 8.0 %shard_map.148 = (bf16[8,2,32,8,128]{4,3,2,1,0:T(8,128)(2,1)}, bf16[8,2,32,8,128]{4,3,2,1,0:T(8,128)(2,1)}) custom-call(s32[3]{0:T(128)} %pad_add_fusion.where, bf16[64,128,256]{2,1,0:T(8,128)(2,1)} %get-tuple-element.93.x, bf16[64,128,256]{2,1,0:T(8,128)(2,1)} %get-tuple-element.94.low), custom_call_target="tpu_custom_call" | custom-call | flops 469762048 | bytes 8388608 | tf_op jit(solution)/shard_map/pallas_call | solution.py:354
  192.7 0.7 collective-permute-start.32
  193.3 2.5 collective-permute-done.32
  195.8 2.5 add_convert_fusion.1
  198.3 10.9 %all-to-all-done.1 = bf16[16,58,8,128]{3,2,1,0:T(8,128)(2,1)S(1)} async-done(((bf16[16,58,8,128]{3,2,1,0:T(8,128)(2,1)}), bf16[16,58,8,128]{3,2,1,0:T(8,128)(2,1)S(1)}, u32[]{:S(2)}, u32[]{:S(2)}) %all-to-all-start.1) | async-done | bytes 1900576 | tf_op jit(solution)/shard_map/all_to_all | solution.py:427
  209.2 5.7 %all-to-all-start.2 = ((bf16[16,32,8,128]{3,2,1,0:T(8,128)(2,1)}), bf16[16,32,8,128]{3,2,1,0:T(8,128)(2,1)S(1)}, u32[]{:S(2)}, u32[]{:S(2)}) async-start(bf16[16,32,8,128]{3,2,1,0:T(8,128)(2,1)} %bitcast.20), calls=%async_computation.3 | async-start | bytes 2097152 | tf_op jit(solution)/shard_map/all_to_all | solution.py:427
  215.2 6.6 %collective-permute-start.34 = (f32[16,8,128]{2,1,0:T(8,128)S(1)}, f32[16,8,128]{2,1,0:T(8,128)S(1)}, u32[]{:S(2)}, u32[]{:S(2)}) collective-permute-start(f32[16,8,128]{2,1,0:T(8,128)S(1)} %slice.15), channel_id=1, source_target_pairs={{0,0},{1,16},{2,32},{3,48},{4,64},{5,80},{6,96},{7,112},{16,128},{... | collective-permute-start | bytes 196616 | tf_op jit(solution)/shard_map/ppermute | solution.py:524
  221.9 11.0 %all-to-all-done.2 = bf16[16,32,8,128]{3,2,1,0:T(8,128)(2,1)S(1)} async-done(((bf16[16,32,8,128]{3,2,1,0:T(8,128)(2,1)}), bf16[16,32,8,128]{3,2,1,0:T(8,128)(2,1)S(1)}, u32[]{:S(2)}, u32[]{:S(2)}) %all-to-all-start.2) | async-done | bytes 1048608 | tf_op jit(solution)/shard_map/all_to_all | solution.py:427
  233.0 1.0 dynamic-slice_bitcast_fusion
  234.0 1.2 collective-permute-start.31
  235.1 0.7 broadcast_multiply_fusion.1
  235.8 4.5 %all-to-all-start.3 = ((f32[8,32,128]{2,1,0:T(8,128)}), f32[8,32,128]{2,1,0:T(8,128)S(1)}, u32[]{:S(2)}, u32[]{:S(2)}) async-start(f32[8,32,128]{2,1,0:T(8,128)} %bitcast.22), calls=%async_computation.4 | async-start | bytes 262144 | tf_op jit(solution)/shard_map/all_to_all | solution.py:528
  240.3 0.7 fusion.1
  241.0 0.7 copy.21
  241.7 6.7 %all-to-all-done.3.pieces = f32[8,32,128]{2,1,0:T(8,128)S(1)} async-done(((f32[8,32,128]{2,1,0:T(8,128)}), f32[8,32,128]{2,1,0:T(8,128)S(1)}, u32[]{:S(2)}, u32[]{:S(2)}) %all-to-all-start.3) | async-done | bytes 131104 | tf_op jit(solution)/shard_map/all_to_all | solution.py:528
  249.0 1.7 shard_map.149
  250.8 1.0 bitcast_select_fusion.1
  251.8 0.8 pad_maximum_fusion
  (113 shorter events, 5.3 us)
Async XLA Ops:
  8.3 23.7 %copy-start.2 = (bf16[512,512]{1,0:T(8,128)(2,1)S(1)}, bf16[512,512]{1,0:T(8,128)(2,1)}, u32[]{:S(2)}) copy-start(bf16[512,512]{1,0:T(8,128)(2,1)} %param.9) | copy-start | bytes 1572868
  9.1 26.3 %copy-start.3 = (bf16[512,512]{1,0:T(8,128)(2,1)S(1)}, bf16[512,512]{1,0:T(8,128)(2,1)}, u32[]{:S(2)}) copy-start(bf16[512,512]{1,0:T(8,128)(2,1)} %param.10) | copy-start | bytes 1572868
  9.1 22.0 %all-to-all-start = ((bf16[16,64,128]{2,1,0:T(8,128)(2,1)}), bf16[16,64,128]{2,1,0:T(8,128)(2,1)S(1)}, u32[]{:S(2)}, u32[]{:S(2)}) async-start(bf16[16,64,128]{2,1,0:T(8,128)(2,1)} %bitcast.10), calls=%async_computation | async-start | bytes 524288 | tf_op jit(solution)/shard_map/all_to_all | solution.py:444
  20.8 75.2 %all-gather.3.cloned.1.call-start = ((), (), s32[]{:S(2)}) async-start(), calls=%async_computation.6 | async-start | bytes 7798784 | tf_op jit(solution)/shard_map/all_gather | solution.py:482
  21.9 6.3 %collective-permute-start = (bf16[3,128,128]{2,1,0:T(8,128)(2,1)S(1)}, bf16[3,128,128]{2,1,0:T(8,128)(2,1)S(1)}, u32[]{:S(2)}, u32[]{:S(2)}) collective-permute-start(bf16[3,128,128]{2,1,0:T(8,128)(2,1)S(1)} %select_select_fusion), channel_id=1, source_target_pairs={{0,8},{8,0},{1,9},{9,1},{2,10},{10,2},{3,11},{11,3},{4,12},{12,4},... | collective-permute-start | bytes 294920 | tf_op jit(solution)/shard_map/ppermute | solution.py:395
  31.9 201.1 %reduce-scatter.2.cloned.1.call-start = ((), (), s32[]{:S(2)}) async-start(), calls=%async_computation.5 | async-start | bytes 4718592 | tf_op jit(solution)/shard_map/reduce_scatter | solution.py:502
  32.0 64.1 %copy-start.1 = (bf16[512,256]{1,0:T(8,128)(2,1)}, bf16[512,256]{1,0:T(8,128)(2,1)S(1)}, u32[]{:S(2)}) copy-start(bf16[512,256]{1,0:T(8,128)(2,1)S(1)} %get-tuple-element.120) | copy-start | bytes 786436
  32.0 6.5 %collective-permute-start.3 = (bf16[4,128,256]{2,1,0:T(8,128)(2,1)S(1)}, bf16[4,128,256]{2,1,0:T(8,128)(2,1)S(1)}, u32[]{:S(2)}, u32[]{:S(2)}) collective-permute-start(bf16[4,128,256]{2,1,0:T(8,128)(2,1)S(1)} %bitcast.44), channel_id=1, source_target_pairs={{0,1},{1,2},{2,3},{3,4},{4,5},{5,6},{6,7},{7,0},{8,9},{9,10},{10,1... | collective-permute-start | bytes 786440 | tf_op jit(solution)/shard_map/ppermute | solution.py:391
  33.5 5.5 %collective-permute-start.2 = (bf16[4,128,256]{2,1,0:T(8,128)(2,1)S(1)}, bf16[4,128,256]{2,1,0:T(8,128)(2,1)S(1)}, u32[]{:S(2)}, u32[]{:S(2)}) collective-permute-start(bf16[4,128,256]{2,1,0:T(8,128)(2,1)S(1)} %bitcast.45), channel_id=1, source_target_pairs={{0,7},{1,0},{2,1},{3,2},{4,3},{5,4},{6,5},{7,6},{8,15},{9,8},{10,9... | collective-permute-start | bytes 786440 | tf_op jit(solution)/shard_map/ppermute | solution.py:391
  34.8 6.7 %collective-permute-start.16 = (bf16[512,256]{1,0:T(8,128)(2,1)S(1)}, bf16[512,256]{1,0:T(8,128)(2,1)S(1)}, u32[]{:S(2)}, u32[]{:S(2)}) collective-permute-start(bf16[512,256]{1,0:T(8,128)(2,1)S(1)} %get-tuple-element.119), channel_id=1, source_target_pairs={{0,8},{8,0},{1,9},{9,1},{2,10},{10,2},{3,11},{11,3},{4,12},{12,4},... | collective-permute-start | bytes 786440 | tf_op jit(solution)/shard_map/ppermute | solution.py:395
  35.5 71.3 %copy-start = (bf16[512,256]{1,0:T(8,128)(2,1)}, bf16[512,256]{1,0:T(8,128)(2,1)S(1)}, u32[]{:S(2)}) copy-start(bf16[512,256]{1,0:T(8,128)(2,1)S(1)} %get-tuple-element.122) | copy-start | bytes 786436
  35.5 11.3 %collective-permute-start.1 = (bf16[512,256]{1,0:T(8,128)(2,1)S(1)}, bf16[512,256]{1,0:T(8,128)(2,1)S(1)}, u32[]{:S(2)}, u32[]{:S(2)}) collective-permute-start(bf16[512,256]{1,0:T(8,128)(2,1)S(1)} %get-tuple-element.121), channel_id=1, source_target_pairs={{0,8},{8,0},{1,9},{9,1},{2,10},{10,2},{3,11},{11,3},{4,12},{12,4},... | collective-permute-start | bytes 786440 | tf_op jit(solution)/shard_map/ppermute | solution.py:395
  38.5 50.6 %copy-start.18 = (bf16[4,128,256]{2,1,0:T(8,128)(2,1)}, bf16[4,128,256]{2,1,0:T(8,128)(2,1)S(1)}, u32[]{:S(2)}) copy-start(bf16[4,128,256]{2,1,0:T(8,128)(2,1)S(1)} %collective-permute-done.3.refs_14_) | copy-start | bytes 786436
  38.5 8.7 %collective-permute-start.22 = (bf16[4,128,256]{2,1,0:T(8,128)(2,1)S(1)}, bf16[4,128,256]{2,1,0:T(8,128)(2,1)S(1)}, u32[]{:S(2)}, u32[]{:S(2)}) collective-permute-start(bf16[4,128,256]{2,1,0:T(8,128)(2,1)S(1)} %collective-permute-done.3.refs_14_), channel_id=1, source_target_pairs={{0,1},{1,2},{2,3},{3,4},{4,5},{5,6},{6,7},{7,0},{8,9},{9,10},{10,1... | collective-permute-start | bytes 786440 | tf_op jit(solution)/shard_map/ppermute | solution.py:391
  39.1 54.1 %copy-start.19 = (bf16[4,128,256]{2,1,0:T(8,128)(2,1)}, bf16[4,128,256]{2,1,0:T(8,128)(2,1)S(1)}, u32[]{:S(2)}) copy-start(bf16[4,128,256]{2,1,0:T(8,128)(2,1)S(1)} %collective-permute-done.2.refs_2_) | copy-start | bytes 786436
  39.1 8.3 %collective-permute-start.18 = (bf16[4,128,256]{2,1,0:T(8,128)(2,1)S(1)}, bf16[4,128,256]{2,1,0:T(8,128)(2,1)S(1)}, u32[]{:S(2)}, u32[]{:S(2)}) collective-permute-start(bf16[4,128,256]{2,1,0:T(8,128)(2,1)S(1)} %collective-permute-done.2.refs_2_), channel_id=1, source_target_pairs={{0,7},{1,0},{2,1},{3,2},{4,3},{5,4},{6,5},{7,6},{8,15},{9,8},{10,9... | collective-permute-start | bytes 786440 | tf_op jit(solution)/shard_map/ppermute | solution.py:391
  41.5 51.7 %copy-start.20 = (bf16[512,256]{1,0:T(8,128)(2,1)}, bf16[512,256]{1,0:T(8,128)(2,1)S(1)}, u32[]{:S(2)}) copy-start(bf16[512,256]{1,0:T(8,128)(2,1)S(1)} %collective-permute-done.16) | copy-start | bytes 786436
  41.5 8.6 %collective-permute-start.26 = (bf16[4,128,256]{2,1,0:T(8,128)(2,1)S(1)}, bf16[4,128,256]{2,1,0:T(8,128)(2,1)S(1)}, u32[]{:S(2)}, u32[]{:S(2)}) collective-permute-start(bf16[4,128,256]{2,1,0:T(8,128)(2,1)S(1)} %bitcast.55), channel_id=1, source_target_pairs={{0,1},{1,2},{2,3},{3,4},{4,5},{5,6},{6,7},{7,0},{8,9},{9,10},{10,1... | collective-permute-start | bytes 786440 | tf_op jit(solution)/shard_map/ppermute | solution.py:391
  41.7 9.3 %collective-permute-start.17 = (bf16[4,128,256]{2,1,0:T(8,128)(2,1)S(1)}, bf16[4,128,256]{2,1,0:T(8,128)(2,1)S(1)}, u32[]{:S(2)}, u32[]{:S(2)}) collective-permute-start(bf16[4,128,256]{2,1,0:T(8,128)(2,1)S(1)} %bitcast.56), channel_id=1, source_target_pairs={{0,7},{1,0},{2,1},{3,2},{4,3},{5,4},{6,5},{7,6},{8,15},{9,8},{10,9... | collective-permute-start | bytes 786440 | tf_op jit(solution)/shard_map/ppermute | solution.py:391
  46.8 60.0 %copy-start.5 = (bf16[512,256]{1,0:T(8,128)(2,1)}, bf16[512,256]{1,0:T(8,128)(2,1)S(1)}, u32[]{:S(2)}) copy-start(bf16[512,256]{1,0:T(8,128)(2,1)S(1)} %collective-permute-done.1) | copy-start | bytes 786436
  46.8 7.3 %collective-permute-start.4 = (bf16[4,128,256]{2,1,0:T(8,128)(2,1)S(1)}, bf16[4,128,256]{2,1,0:T(8,128)(2,1)S(1)}, u32[]{:S(2)}, u32[]{:S(2)}) collective-permute-start(bf16[4,128,256]{2,1,0:T(8,128)(2,1)S(1)} %bitcast.41), channel_id=1, source_target_pairs={{0,1},{1,2},{2,3},{3,4},{4,5},{5,6},{6,7},{7,0},{8,9},{9,10},{10,1... | collective-permute-start | bytes 786440 | tf_op jit(solution)/shard_map/ppermute | solution.py:391
  47.2 45.9 %copy-start.21 = (bf16[4,128,256]{2,1,0:T(8,128)(2,1)}, bf16[4,128,256]{2,1,0:T(8,128)(2,1)S(1)}, u32[]{:S(2)}) copy-start(bf16[4,128,256]{2,1,0:T(8,128)(2,1)S(1)} %collective-permute-done.22.refs_12_) | copy-start | bytes 786436
  47.2 11.9 %collective-permute-start.7 = (bf16[4,128,256]{2,1,0:T(8,128)(2,1)S(1)}, bf16[4,128,256]{2,1,0:T(8,128)(2,1)S(1)}, u32[]{:S(2)}, u32[]{:S(2)}) collective-permute-start(bf16[4,128,256]{2,1,0:T(8,128)(2,1)S(1)} %bitcast.52), channel_id=1, source_target_pairs={{0,1},{1,2},{2,3},{3,4},{4,5},{5,6},{6,7},{7,0},{8,9},{9,10},{10,1... | collective-permute-start | bytes 786440 | tf_op jit(solution)/shard_map/ppermute | solution.py:391
  47.3 45.9 %copy-start.22 = (bf16[4,128,256]{2,1,0:T(8,128)(2,1)}, bf16[4,128,256]{2,1,0:T(8,128)(2,1)S(1)}, u32[]{:S(2)}) copy-start(bf16[4,128,256]{2,1,0:T(8,128)(2,1)S(1)} %collective-permute-done.18.refs_4_) | copy-start | bytes 786436
  47.3 13.8 %collective-permute-start.10 = (bf16[4,128,256]{2,1,0:T(8,128)(2,1)S(1)}, bf16[4,128,256]{2,1,0:T(8,128)(2,1)S(1)}, u32[]{:S(2)}, u32[]{:S(2)}) collective-permute-start(bf16[4,128,256]{2,1,0:T(8,128)(2,1)S(1)} %bitcast.42), channel_id=1, source_target_pairs={{0,7},{1,0},{2,1},{3,2},{4,3},{5,4},{6,5},{7,6},{8,15},{9,8},{10,9... | collective-permute-start | bytes 786440 | tf_op jit(solution)/shard_map/ppermute | solution.py:391
  50.1 43.1 %copy-start.23 = (bf16[4,128,256]{2,1,0:T(8,128)(2,1)}, bf16[4,128,256]{2,1,0:T(8,128)(2,1)S(1)}, u32[]{:S(2)}) copy-start(bf16[4,128,256]{2,1,0:T(8,128)(2,1)S(1)} %collective-permute-done.26.refs_15_) | copy-start | bytes 786436
  50.1 11.0 %collective-permute-start.13 = (bf16[4,128,256]{2,1,0:T(8,128)(2,1)S(1)}, bf16[4,128,256]{2,1,0:T(8,128)(2,1)S(1)}, u32[]{:S(2)}, u32[]{:S(2)}) collective-permute-start(bf16[4,128,256]{2,1,0:T(8,128)(2,1)S(1)} %bitcast.53), channel_id=1, source_target_pairs={{0,7},{1,0},{2,1},{3,2},{4,3},{5,4},{6,5},{7,6},{8,15},{9,8},{10,9... | collective-permute-start | bytes 786440 | tf_op jit(solution)/shard_map/ppermute | solution.py:391
  51.0 42.2 %copy-start.24 = (bf16[4,128,256]{2,1,0:T(8,128)(2,1)}, bf16[4,128,256]{2,1,0:T(8,128)(2,1)S(1)}, u32[]{:S(2)}) copy-start(bf16[4,128,256]{2,1,0:T(8,128)(2,1)S(1)} %collective-permute-done.17.refs_3_) | copy-start | bytes 786436
  51.0 11.6 %collective-permute-start.23 = (bf16[4,128,256]{2,1,0:T(8,128)(2,1)S(1)}, bf16[4,128,256]{2,1,0:T(8,128)(2,1)S(1)}, u32[]{:S(2)}, u32[]{:S(2)}) collective-permute-start(bf16[4,128,256]{2,1,0:T(8,128)(2,1)S(1)} %collective-permute-done.22.refs_12_), channel_id=1, source_target_pairs={{0,1},{1,2},{2,3},{3,4},{4,5},{5,6},{6,7},{7,0},{8,9},{9,10},{10,1... | collective-permute-start | bytes 786440 | tf_op jit(solution)/shard_map/ppermute | solution.py:391
  54.1 52.7 %copy-start.6 = (bf16[4,128,256]{2,1,0:T(8,128)(2,1)}, bf16[4,128,256]{2,1,0:T(8,128)(2,1)S(1)}, u32[]{:S(2)}) copy-start(bf16[4,128,256]{2,1,0:T(8,128)(2,1)S(1)} %collective-permute-done.4.refs_14_) | copy-start | bytes 786436
  54.2 9.4 %collective-permute-start.19 = (bf16[4,128,256]{2,1,0:T(8,128)(2,1)S(1)}, bf16[4,128,256]{2,1,0:T(8,128)(2,1)S(1)}, u32[]{:S(2)}, u32[]{:S(2)}) collective-permute-start(bf16[4,128,256]{2,1,0:T(8,128)(2,1)S(1)} %collective-permute-done.17.refs_3_), channel_id=1, source_target_pairs={{0,7},{1,0},{2,1},{3,2},{4,3},{5,4},{6,5},{7,6},{8,15},{9,8},{10,9... | collective-permute-start | bytes 786440 | tf_op jit(solution)/shard_map/ppermute | solution.py:391
  59.2 47.7 %copy-start.7 = (bf16[4,128,256]{2,1,0:T(8,128)(2,1)}, bf16[4,128,256]{2,1,0:T(8,128)(2,1)S(1)}, u32[]{:S(2)}) copy-start(bf16[4,128,256]{2,1,0:T(8,128)(2,1)S(1)} %collective-permute-done.7.refs_15_) | copy-start | bytes 786436
  59.2 9.4 %collective-permute-start.20 = (bf16[4,128,256]{2,1,0:T(8,128)(2,1)S(1)}, bf16[4,128,256]{2,1,0:T(8,128)(2,1)S(1)}, u32[]{:S(2)}, u32[]{:S(2)}) collective-permute-start(bf16[4,128,256]{2,1,0:T(8,128)(2,1)S(1)} %collective-permute-done.18.refs_4_), channel_id=1, source_target_pairs={{0,7},{1,0},{2,1},{3,2},{4,3},{5,4},{6,5},{7,6},{8,15},{9,8},{10,9... | collective-permute-start | bytes 786440 | tf_op jit(solution)/shard_map/ppermute | solution.py:391
  61.1 45.8 %copy-start.8 = (bf16[4,128,256]{2,1,0:T(8,128)(2,1)}, bf16[4,128,256]{2,1,0:T(8,128)(2,1)S(1)}, u32[]{:S(2)}) copy-start(bf16[4,128,256]{2,1,0:T(8,128)(2,1)S(1)} %collective-permute-done.10.refs_2_) | copy-start | bytes 786436
  61.1 9.6 %collective-permute-start.27 = (bf16[4,128,256]{2,1,0:T(8,128)(2,1)S(1)}, bf16[4,128,256]{2,1,0:T(8,128)(2,1)S(1)}, u32[]{:S(2)}, u32[]{:S(2)}) collective-permute-start(bf16[4,128,256]{2,1,0:T(8,128)(2,1)S(1)} %collective-permute-done.26.refs_15_), channel_id=1, source_target_pairs={{0,1},{1,2},{2,3},{3,4},{4,5},{5,6},{6,7},{7,0},{8,9},{9,10},{10,1... | collective-permute-start | bytes 786440 | tf_op jit(solution)/shard_map/ppermute | solution.py:391
  61.1 45.7 %copy-start.9 = (bf16[4,128,256]{2,1,0:T(8,128)(2,1)}, bf16[4,128,256]{2,1,0:T(8,128)(2,1)S(1)}, u32[]{:S(2)}) copy-start(bf16[4,128,256]{2,1,0:T(8,128)(2,1)S(1)} %collective-permute-done.13.refs_3_) | copy-start | bytes 786436
  61.1 15.2 %collective-permute-start.5 = (bf16[4,128,256]{2,1,0:T(8,128)(2,1)S(1)}, bf16[4,128,256]{2,1,0:T(8,128)(2,1)S(1)}, u32[]{:S(2)}, u32[]{:S(2)}) collective-permute-start(bf16[4,128,256]{2,1,0:T(8,128)(2,1)S(1)} %collective-permute-done.4.refs_14_), channel_id=1, source_target_pairs={{0,1},{1,2},{2,3},{3,4},{4,5},{5,6},{6,7},{7,0},{8,9},{9,10},{10,1... | collective-permute-start | bytes 786440 | tf_op jit(solution)/shard_map/ppermute | solution.py:391
  62.6 30.6 %copy-start.25 = (bf16[4,128,256]{2,1,0:T(8,128)(2,1)}, bf16[4,128,256]{2,1,0:T(8,128)(2,1)S(1)}, u32[]{:S(2)}) copy-start(bf16[4,128,256]{2,1,0:T(8,128)(2,1)S(1)} %collective-permute-done.23.refs_10_) | copy-start | bytes 786436
  62.6 19.4 %collective-permute-start.8 = (bf16[4,128,256]{2,1,0:T(8,128)(2,1)S(1)}, bf16[4,128,256]{2,1,0:T(8,128)(2,1)S(1)}, u32[]{:S(2)}, u32[]{:S(2)}) collective-permute-start(bf16[4,128,256]{2,1,0:T(8,128)(2,1)S(1)} %collective-permute-done.7.refs_15_), channel_id=1, source_target_pairs={{0,1},{1,2},{2,3},{3,4},{4,5},{5,6},{6,7},{7,0},{8,9},{9,10},{10,1... | collective-permute-start | bytes 786440 | tf_op jit(solution)/shard_map/ppermute | solution.py:391
  63.6 29.7 %copy-start.26 = (bf16[4,128,256]{2,1,0:T(8,128)(2,1)}, bf16[4,128,256]{2,1,0:T(8,128)(2,1)S(1)}, u32[]{:S(2)}) copy-start(bf16[4,128,256]{2,1,0:T(8,128)(2,1)S(1)} %collective-permute-done.19.refs_5_) | copy-start | bytes 786436
  63.6 18.4 %collective-permute-start.21 = (bf16[4,128,256]{2,1,0:T(8,128)(2,1)S(1)}, bf16[4,128,256]{2,1,0:T(8,128)(2,1)}, u32[]{:S(2)}, u32[]{:S(2)}) collective-permute-start(bf16[4,128,256]{2,1,0:T(8,128)(2,1)S(1)} %collective-permute-done.19.refs_5_), channel_id=1, source_target_pairs={{0,7},{1,0},{2,1},{3,2},{4,3},{5,4},{6,5},{7,6},{8,15},{9,8},{10,9... | collective-permute-start | bytes 786440 | tf_op jit(solution)/shard_map/ppermute | solution.py:391
  68.6 24.6 %copy-start.27 = (bf16[4,128,256]{2,1,0:T(8,128)(2,1)}, bf16[4,128,256]{2,1,0:T(8,128)(2,1)S(1)}, u32[]{:S(2)}) copy-start(bf16[4,128,256]{2,1,0:T(8,128)(2,1)S(1)} %collective-permute-done.20.refs_6_) | copy-start | bytes 786436
  68.6 16.0 %collective-permute-start.11 = (bf16[4,128,256]{2,1,0:T(8,128)(2,1)S(1)}, bf16[4,128,256]{2,1,0:T(8,128)(2,1)S(1)}, u32[]{:S(2)}, u32[]{:S(2)}) collective-permute-start(bf16[4,128,256]{2,1,0:T(8,128)(2,1)S(1)} %collective-permute-done.10.refs_2_), channel_id=1, source_target_pairs={{0,7},{1,0},{2,1},{3,2},{4,3},{5,4},{6,5},{7,6},{8,15},{9,8},{10,9... | collective-permute-start | bytes 786440 | tf_op jit(solution)/shard_map/ppermute | solution.py:391
  70.7 22.5 %copy-start.28 = (bf16[4,128,256]{2,1,0:T(8,128)(2,1)}, bf16[4,128,256]{2,1,0:T(8,128)(2,1)S(1)}, u32[]{:S(2)}) copy-start(bf16[4,128,256]{2,1,0:T(8,128)(2,1)S(1)} %collective-permute-done.27.refs_13_) | copy-start | bytes 786436
  70.7 14.8 %collective-permute-start.14 = (bf16[4,128,256]{2,1,0:T(8,128)(2,1)S(1)}, bf16[4,128,256]{2,1,0:T(8,128)(2,1)S(1)}, u32[]{:S(2)}, u32[]{:S(2)}) collective-permute-start(bf16[4,128,256]{2,1,0:T(8,128)(2,1)S(1)} %collective-permute-done.13.refs_3_), channel_id=1, source_target_pairs={{0,7},{1,0},{2,1},{3,2},{4,3},{5,4},{6,5},{7,6},{8,15},{9,8},{10,9... | collective-permute-start | bytes 786440 | tf_op jit(solution)/shard_map/ppermute | solution.py:391
  76.3 30.6 %copy-start.10 = (bf16[4,128,256]{2,1,0:T(8,128)(2,1)}, bf16[4,128,256]{2,1,0:T(8,128)(2,1)S(1)}, u32[]{:S(2)}) copy-start(bf16[4,128,256]{2,1,0:T(8,128)(2,1)S(1)} %collective-permute-done.5.refs_12_) | copy-start | bytes 786436
  76.3 11.5 %collective-permute-start.24 = (bf16[4,128,256]{2,1,0:T(8,128)(2,1)S(1)}, bf16[4,128,256]{2,1,0:T(8,128)(2,1)S(1)}, u32[]{:S(2)}, u32[]{:S(2)}) collective-permute-start(bf16[4,128,256]{2,1,0:T(8,128)(2,1)S(1)} %collective-permute-done.23.refs_10_), channel_id=1, source_target_pairs={{0,1},{1,2},{2,3},{3,4},{4,5},{5,6},{6,7},{7,0},{8,9},{9,10},{10,1... | collective-permute-start | bytes 786440 | tf_op jit(solution)/shard_map/ppermute | solution.py:391
  81.9 25.0 %copy-start.11 = (bf16[4,128,256]{2,1,0:T(8,128)(2,1)}, bf16[4,128,256]{2,1,0:T(8,128)(2,1)S(1)}, u32[]{:S(2)}) copy-start(bf16[4,128,256]{2,1,0:T(8,128)(2,1)S(1)} %collective-permute-done.8.refs_13_) | copy-start | bytes 786436
  81.9 11.2 %collective-permute-start.28 = (bf16[4,128,256]{2,1,0:T(8,128)(2,1)S(1)}, bf16[4,128,256]{2,1,0:T(8,128)(2,1)S(1)}, u32[]{:S(2)}, u32[]{:S(2)}) collective-permute-start(bf16[4,128,256]{2,1,0:T(8,128)(2,1)S(1)} %collective-permute-done.27.refs_13_), channel_id=1, source_target_pairs={{0,1},{1,2},{2,3},{3,4},{4,5},{5,6},{6,7},{7,0},{8,9},{9,10},{10,1... | collective-permute-start | bytes 786440 | tf_op jit(solution)/shard_map/ppermute | solution.py:391
  81.9 14.1 %collective-permute-start.25 = (bf16[4,128,256]{2,1,0:T(8,128)(2,1)}, bf16[4,128,256]{2,1,0:T(8,128)(2,1)}, u32[]{:S(2)}, u32[]{:S(2)}) collective-permute-start(bf16[4,128,256]{2,1,0:T(8,128)(2,1)} %collective-permute-done.21.refs_7_), channel_id=1, source_target_pairs={{0,7},{1,0},{2,1},{3,2},{4,3},{5,4},{6,5},{7,6},{8,15},{9,8},{10,9... | collective-permute-start | bytes 786440 | tf_op jit(solution)/shard_map/ppermute | solution.py:391
  84.6 22.3 %copy-start.12 = (bf16[4,128,256]{2,1,0:T(8,128)(2,1)}, bf16[4,128,256]{2,1,0:T(8,128)(2,1)S(1)}, u32[]{:S(2)}) copy-start(bf16[4,128,256]{2,1,0:T(8,128)(2,1)S(1)} %collective-permute-done.11.refs_4_) | copy-start | bytes 786436
  84.6 22.3 %collective-permute-start.6 = (bf16[4,128,256]{2,1,0:T(8,128)(2,1)S(1)}, bf16[4,128,256]{2,1,0:T(8,128)(2,1)S(1)}, u32[]{:S(2)}, u32[]{:S(2)}) collective-permute-start(bf16[4,128,256]{2,1,0:T(8,128)(2,1)S(1)} %collective-permute-done.5.refs_12_), channel_id=1, source_target_pairs={{0,1},{1,2},{2,3},{3,4},{4,5},{5,6},{6,7},{7,0},{8,9},{9,10},{10,1... | collective-permute-start | bytes 786440 | tf_op jit(solution)/shard_map/ppermute | solution.py:391
  85.5 21.4 %collective-permute-start.9 = (bf16[4,128,256]{2,1,0:T(8,128)(2,1)S(1)}, bf16[4,128,256]{2,1,0:T(8,128)(2,1)S(1)}, u32[]{:S(2)}, u32[]{:S(2)}) collective-permute-start(bf16[4,128,256]{2,1,0:T(8,128)(2,1)S(1)} %collective-permute-done.8.refs_13_), channel_id=1, source_target_pairs={{0,1},{1,2},{2,3},{3,4},{4,5},{5,6},{6,7},{7,0},{8,9},{9,10},{10,1... | collective-permute-start | bytes 786440 | tf_op jit(solution)/shard_map/ppermute | solution.py:391
  87.9 19.1 %collective-permute-start.12 = (bf16[4,128,256]{2,1,0:T(8,128)(2,1)S(1)}, bf16[4,128,256]{2,1,0:T(8,128)(2,1)}, u32[]{:S(2)}, u32[]{:S(2)}) collective-permute-start(bf16[4,128,256]{2,1,0:T(8,128)(2,1)S(1)} %collective-permute-done.11.refs_4_), channel_id=1, source_target_pairs={{0,7},{1,0},{2,1},{3,2},{4,3},{5,4},{6,5},{7,6},{8,15},{9,8},{10,9... | collective-permute-start | bytes 786440 | tf_op jit(solution)/shard_map/ppermute | solution.py:391
  94.0 13.0 %collective-permute-start.15 = (bf16[4,128,256]{2,1,0:T(8,128)(2,1)S(1)}, bf16[4,128,256]{2,1,0:T(8,128)(2,1)}, u32[]{:S(2)}, u32[]{:S(2)}) collective-permute-start(bf16[4,128,256]{2,1,0:T(8,128)(2,1)S(1)} %collective-permute-done.14.refs_5_), channel_id=1, source_target_pairs={{0,7},{1,0},{2,1},{3,2},{4,3},{5,4},{6,5},{7,6},{8,15},{9,8},{10,9... | collective-permute-start | bytes 786440 | tf_op jit(solution)/shard_map/ppermute | solution.py:391
  107.0 16.3 %collective-permute-start.29 = (bf16[4,128,256]{2,1,0:T(8,128)(2,1)S(1)}, bf16[4,128,256]{2,1,0:T(8,128)(2,1)S(1)}, u32[]{:S(2)}, u32[]{:S(2)}) collective-permute-start(bf16[4,128,256]{2,1,0:T(8,128)(2,1)S(1)} %collective-permute-done.6.refs_10_), channel_id=1, source_target_pairs={{0,1},{1,2},{2,3},{3,4},{4,5},{5,6},{6,7},{7,0},{8,9},{9,10},{10,1... | collective-permute-start | bytes 786440 | tf_op jit(solution)/shard_map/ppermute | solution.py:391
  107.1 16.3 %collective-permute-start.30 = (bf16[4,128,256]{2,1,0:T(8,128)(2,1)}, bf16[4,128,256]{2,1,0:T(8,128)(2,1)S(1)}, u32[]{:S(2)}, u32[]{:S(2)}) collective-permute-start(bf16[4,128,256]{2,1,0:T(8,128)(2,1)} %collective-permute-done.15.refs_7_), channel_id=1, source_target_pairs={{0,7},{1,0},{2,1},{3,2},{4,3},{5,4},{6,5},{7,6},{8,15},{9,8},{10,9... | collective-permute-start | bytes 786440 | tf_op jit(solution)/shard_map/ppermute | solution.py:391
  158.2 15.9 %collective-permute-start.33 = (bf16[8,2,58,8,128]{4,3,2,1,0:T(8,128)(2,1)}, bf16[8,2,58,8,128]{4,3,2,1,0:T(8,128)(2,1)S(1)}, u32[]{:S(2)}, u32[]{:S(2)}) collective-permute-start(bf16[8,2,58,8,128]{4,3,2,1,0:T(8,128)(2,1)} %get-tuple-element.98), channel_id=1, source_target_pairs={{0,16},{16,0},{1,17},{17,1},{2,18},{18,2},{3,19},{19,3},{4,20},{20... | collective-permute-start | bytes 5701640 | tf_op jit(solution)/shard_map/ppermute | solution.py:421
  177.4 31.8 %all-to-all-start.1 = ((bf16[16,58,8,128]{3,2,1,0:T(8,128)(2,1)}), bf16[16,58,8,128]{3,2,1,0:T(8,128)(2,1)S(1)}, u32[]{:S(2)}, u32[]{:S(2)}) async-start(bf16[16,58,8,128]{3,2,1,0:T(8,128)(2,1)} %bitcast.40), calls=%async_computation.2 | async-start | bytes 3801088 | tf_op jit(solution)/shard_map/all_to_all | solution.py:427
  192.7 3.2 %collective-permute-start.32 = (bf16[8,2,32,8,128]{4,3,2,1,0:T(8,128)(2,1)}, bf16[8,2,32,8,128]{4,3,2,1,0:T(8,128)(2,1)S(1)}, u32[]{:S(2)}, u32[]{:S(2)}) collective-permute-start(bf16[8,2,32,8,128]{4,3,2,1,0:T(8,128)(2,1)} %get-tuple-element.96), channel_id=1, source_target_pairs={{0,16},{16,0},{1,17},{17,1},{2,18},{18,2},{3,19},{19,3},{4,20},{20... | collective-permute-start | bytes 3145736 | tf_op jit(solution)/shard_map/ppermute | solution.py:421
  209.2 23.6 %all-to-all-start.2 = ((bf16[16,32,8,128]{3,2,1,0:T(8,128)(2,1)}), bf16[16,32,8,128]{3,2,1,0:T(8,128)(2,1)S(1)}, u32[]{:S(2)}, u32[]{:S(2)}) async-start(bf16[16,32,8,128]{3,2,1,0:T(8,128)(2,1)} %bitcast.20), calls=%async_computation.3 | async-start | bytes 2097152 | tf_op jit(solution)/shard_map/all_to_all | solution.py:427
  215.2 25.8 %collective-permute-start.34 = (f32[16,8,128]{2,1,0:T(8,128)S(1)}, f32[16,8,128]{2,1,0:T(8,128)S(1)}, u32[]{:S(2)}, u32[]{:S(2)}) collective-permute-start(f32[16,8,128]{2,1,0:T(8,128)S(1)} %slice.15), channel_id=1, source_target_pairs={{0,0},{1,16},{2,32},{3,48},{4,64},{5,80},{6,96},{7,112},{16,128},{... | collective-permute-start | bytes 196616 | tf_op jit(solution)/shard_map/ppermute | solution.py:524
  234.0 16.8 %collective-permute-start.31 = (bf16[512,256]{1,0:T(8,128)(2,1)S(1)}, bf16[512,256]{1,0:T(8,128)(2,1)S(1)}, u32[]{:S(2)}, u32[]{:S(2)}) collective-permute-start(bf16[512,256]{1,0:T(8,128)(2,1)S(1)} %dynamic-slice_bitcast_fusion), channel_id=1, source_target_pairs={{0,8},{8,0},{1,9},{9,1},{2,10},{10,2},{3,11},{11,3},{4,12},{12,4},... | collective-permute-start | bytes 786440 | tf_op jit(solution)/shard_map/ppermute | solution.py:395
  235.8 12.5 %all-to-all-start.3 = ((f32[8,32,128]{2,1,0:T(8,128)}), f32[8,32,128]{2,1,0:T(8,128)S(1)}, u32[]{:S(2)}, u32[]{:S(2)}) async-start(f32[8,32,128]{2,1,0:T(8,128)} %bitcast.22), calls=%async_computation.4 | async-start | bytes 262144 | tf_op jit(solution)/shard_map/all_to_all | solution.py:528
  (8 other events, 62.4 us)
Sparse Core Ops, SparseCore 0:
  32.0 52.3 all-gather.2
  146.9 64.7 reduce-scatter.1

commit v7 on v6

--- a/solution.py
+++ b/solution.py
@@ -487,14 +487,16 @@
     for step in range(1, steps + 1):
         state = ring_step(step, *state, xs)
     state, _ = lax.optimization_barrier(((dys[0], dys[0]), (xs[1][0], xs[nz - 1][0])))
-    for step in range(1, steps - 1):
-        state = ring_step(step, *state, dys)
+    state = ring_step(1, *state, dys)
     shards_x, _ = lax.optimization_barrier((flat(xs), state))
     x, gate_in, up_in = forward_first(where, table, held, shards_x)
+    for step in range(2, steps - 1):
+        state = ring_step(step, *state, dys)
+    state, gate_in, up_in = lax.optimization_barrier((state, gate_in, up_in))
     state = ring_step(steps - 1, *state, dys)
-    state, gate_in, up_in = lax.optimization_barrier((state, gate_in, up_in))
+    act, to_gate, to_up, down_in = forward_second(table, held, gate_in, up_in)
+    state, to_gate, to_up = lax.optimization_barrier((state, to_gate, to_up))
     ring_step(steps, *state, dys)
-    act, to_gate, to_up, down_in = forward_second(table, held, gate_in, up_in)
     dy, back_in, gate_back, up_back, low, parts = backward(
         where, table, held, to_gate, to_up, flat(dys)
     )
@@ -507,14 +509,11 @@
     later = second_grads(where, dy, down_in, act, back_in, gate_in, up_in, gate_back, up_back)
     x, later = lax.optimization_barrier((x, later))
     firsts = sum_cores(*first_grads(where, x, low))
-    later = to_chips(sum_cores(*later))
-    firsts, later = lax.optimization_barrier((firsts, later))
-    firsts = to_chips(firsts)
+    summed = total_of(to_chips(jnp.concatenate([sum_cores(*later), firsts], axis=1))) * scale
+    later, firsts = summed[: 3 * hid + 16], summed[3 * hid + 16 :]
     input_grad = jnp.concatenate(
         [jnp.where(me == 0, kept, other), jnp.where(me == 0, other, kept)], axis=1
     )
-    later = total_of(later) * scale
-    firsts = total_of(firsts) * scale
     out_gs, out_us, out_df = later[: 3 * hid].reshape(3, hid, rows, BLOCK)
     pairs = []
     for part in range(ngroup):

time: 262 us -> 265 us (1.011)
  waiting for transfers between devices: 68.5 us -> 87.7 us
  starting transfers between devices: 90.5 us -> 78.6 us
  other arithmetic: 12.2 us -> 8.67 us
    all_to_all x2 -> x1, waiting for transfers between devices: 21.8 us -> 38.6 us  [to_chips(): return lax.all_to_all(pairs, CHIPS, 0, 0, tiled=True)]
    all_to_all x2 -> x1, starting transfers between devices: 12.9 us -> 4.67 us  [to_chips(): return lax.all_to_all(pairs, CHIPS, 0, 0, tiled=True)]
    ppermute x28, waiting for transfers between devices: 24.6 us -> 30.4 us  [shift(): lax.ppermute(value, 'z', [(i, (i + step) % count) for i in range(count)])]
    ppermute x28, starting transfers between devices: 34.6 us -> 29.2 us  [shift(): lax.ppermute(value, 'z', [(i, (i + step) % count) for i in range(count)])]
    convert_element_type x2, other arithmetic: 5.85 us -> 2.03 us  [sum_cores(): pairs = (keep.astype(F32) + found.astype(F32)).astype(BF)]
    ppermute x2, waiting for transfers between devices: 6.21 us -> 2.82 us  [sum_cores(): found = lax.ppermute(send, 'core', [(0, 1), (1, 0)])]
  transfers between devices with their start and end apart: 41 -> 40, of which waited for: 20 -> 19; matrix products, arithmetic and copies ran while one was open for 4% -> 3% of each run, Pallas kernels for 18% -> 17%
where the time goes in v7:
time: 265 us; the launch traced here: 264 us
  waiting for transfers between devices  87.7 us (33%)
  starting transfers between devices  78.6 us (30%)
  Pallas kernels  68.1 us (26%)
  between operations  14.6 us (6%)
  other arithmetic  8.67 us (3%)
  local copies, waits for them, and re-layouts  6.13 us (2%)
    pallas_call x3, Pallas kernels, copying(): pl.pallas_call(kernel, out_shape=[jax.ShapeDtypeStruct(shape, dtype) for...  46.8 us
    all_to_all x1, waiting for transfers between devices, to_chips(): return lax.all_to_all(pairs, CHIPS, 0, 0, tiled=True)  38.6 us
    ppermute x28, waiting for transfers between devices, shift(): lax.ppermute(value, 'z', [(i, (i + step) % count) for i in range(count)])  30.4 us
    ppermute x28, starting transfers between devices, shift(): lax.ppermute(value, 'z', [(i, (i + step) % count) for i in range(count)])  29.2 us
    pallas_call x2, Pallas kernels, grads_call(): pl.pallas_call(kernel, grid=(8,), out_shape=[jax.ShapeDtypeStruct(shape,...  19.5 us
    ppermute x2, starting transfers between devices, sum_cores(): found = lax.ppermute(send, 'core', [(0, 1), (1, 0)])  13.4 us
    all_to_all x1, starting transfers between devices, share_first(): return lax.all_to_all(first, TENSOR, 0, 0, tiled=True)  11.7 us
    ppermute x4, starting transfers between devices, swap(): return lax.ppermute(value, 'x_hi', [(0, 1), (1, 0)])  8.38 us
  transfers between devices with their start and end apart: 40, of which 19 were waited for; matrix products, arithmetic and copies ran while one was open for 3% of the time, Pallas kernels for 17%

profile of v7, /device:TPU:1, one launch (start us, length us, event | category | flops | bytes accessed | tf_op | source)
XLA Modules:
  0.0 263.8 jit_solution(13144178160609441292)
XLA Ops:
  7.2 1.0 fusion
  8.4 0.8 broadcast_in_dim.2
  9.1 11.7 %all-to-all-start = ((bf16[16,64,128]{2,1,0:T(8,128)(2,1)}), bf16[16,64,128]{2,1,0:T(8,128)(2,1)S(1)}, u32[]{:S(2)}, u32[]{:S(2)}) async-start(bf16[16,64,128]{2,1,0:T(8,128)(2,1)} %bitcast.10), calls=%async_computation | async-start | bytes 524288 | tf_op jit(solution)/shard_map/all_to_all | solution.py:444
  20.9 1.0 select_select_fusion
  21.9 3.0 %collective-permute-start = (bf16[3,128,128]{2,1,0:T(8,128)(2,1)S(1)}, bf16[3,128,128]{2,1,0:T(8,128)(2,1)S(1)}, u32[]{:S(2)}, u32[]{:S(2)}) collective-permute-start(bf16[3,128,128]{2,1,0:T(8,128)(2,1)S(1)} %select_select_fusion), channel_id=1, source_target_pairs={{0,8},{8,0},{1,9},{9,1},{2,10},{10,2},{3,11},{11,3},{4,12},{12,4},... | collective-permute-start | bytes 294920 | tf_op jit(solution)/shard_map/ppermute | solution.py:395
  24.9 3.4 %collective-permute-done = bf16[3,128,128]{2,1,0:T(8,128)(2,1)S(1)} collective-permute-done((bf16[3,128,128]{2,1,0:T(8,128)(2,1)S(1)}, bf16[3,128,128]{2,1,0:T(8,128)(2,1)S(1)}, u32[]{:S(2)}, u32[]{:S(2)}) %collective-permute-start) | collective-permute-done | bytes 98336 | tf_op jit(solution)/shard_map/ppermute | solution.py:395
  28.3 2.8 %all-to-all-done = bf16[16,64,128]{2,1,0:T(8,128)(2,1)S(1)} async-done(((bf16[16,64,128]{2,1,0:T(8,128)(2,1)}), bf16[16,64,128]{2,1,0:T(8,128)(2,1)S(1)}, u32[]{:S(2)}, u32[]{:S(2)}) %all-to-all-start) | async-done | bytes 262176 | tf_op jit(solution)/shard_map/all_to_all | solution.py:444
  31.1 0.8 pad_maximum_fusion.2
  32.0 0.7 collective-permute-start.12
  32.8 2.7 %collective-permute-start.3 = (bf16[4,128,256]{2,1,0:T(8,128)(2,1)S(1)}, bf16[4,128,256]{2,1,0:T(8,128)(2,1)S(1)}, u32[]{:S(2)}, u32[]{:S(2)}) collective-permute-start(bf16[4,128,256]{2,1,0:T(8,128)(2,1)S(1)} %bitcast.45), channel_id=1, source_target_pairs={{0,1},{1,2},{2,3},{3,4},{4,5},{5,6},{6,7},{7,0},{8,9},{9,10},{10,1... | collective-permute-start | bytes 786440 | tf_op jit(solution)/shard_map/ppermute | solution.py:391
  35.5 2.4 collective-permute-start.1
  37.9 0.9 collective-permute-done.12
  38.8 2.6 %collective-permute-start.13 = (bf16[4,128,256]{2,1,0:T(8,128)(2,1)S(1)}, bf16[4,128,256]{2,1,0:T(8,128)(2,1)S(1)}, u32[]{:S(2)}, u32[]{:S(2)}) collective-permute-start(bf16[4,128,256]{2,1,0:T(8,128)(2,1)S(1)} %bitcast.56), channel_id=1, source_target_pairs={{0,7},{1,0},{2,1},{3,2},{4,3},{5,4},{6,5},{7,6},{8,15},{9,8},{10,9... | collective-permute-start | bytes 786440 | tf_op jit(solution)/shard_map/ppermute | solution.py:391
  41.8 2.5 collective-permute-start.14
  44.3 1.1 collective-permute-done.1
  45.4 1.4 collective-permute-start.4
  46.8 1.8 collective-permute-start.15
  48.7 2.1 collective-permute-done.18.refs_12_
  51.1 2.3 collective-permute-start.8
  53.4 2.1 collective-permute-done.4.refs_14_
  55.6 1.2 collective-permute-done.15.refs_5_
  56.7 1.5 collective-permute-start.17
  58.3 2.9 %collective-permute-done.6.refs_15_ = bf16[4,128,256]{2,1,0:T(8,128)(2,1)S(1)} collective-permute-done((bf16[4,128,256]{2,1,0:T(8,128)(2,1)S(1)}, bf16[4,128,256]{2,1,0:T(8,128)(2,1)S(1)}, u32[]{:S(2)}, u32[]{:S(2)}) %collective-permute-start.6) | collective-permute-done | bytes 262176 | tf_op jit(solution)/shard_map/ppermute | solution.py:391
  61.2 1.2 collective-permute-done.8.refs_2_
  62.4 1.4 collective-permute-start.16
  63.8 3.0 %collective-permute-done.19.refs_10_ = bf16[4,128,256]{2,1,0:T(8,128)(2,1)S(1)} collective-permute-done((bf16[4,128,256]{2,1,0:T(8,128)(2,1)S(1)}, bf16[4,128,256]{2,1,0:T(8,128)(2,1)S(1)}, u32[]{:S(2)}, u32[]{:S(2)}) %collective-permute-start.19) | collective-permute-done | bytes 262176 | tf_op jit(solution)/shard_map/ppermute | solution.py:391
  66.8 5.6 %collective-permute-done.23.refs_13_ = bf16[4,128,256]{2,1,0:T(8,128)(2,1)S(1)} collective-permute-done((bf16[4,128,256]{2,1,0:T(8,128)(2,1)S(1)}, bf16[4,128,256]{2,1,0:T(8,128)(2,1)S(1)}, u32[]{:S(2)}, u32[]{:S(2)}) %collective-permute-start.23) | collective-permute-done | bytes 262176 | tf_op jit(solution)/shard_map/ppermute | solution.py:391
  72.4 2.7 %collective-permute-start.21 = (bf16[4,128,256]{2,1,0:T(8,128)(2,1)}, bf16[4,128,256]{2,1,0:T(8,128)(2,1)}, u32[]{:S(2)}, u32[]{:S(2)}) collective-permute-start(bf16[4,128,256]{2,1,0:T(8,128)(2,1)} %collective-permute-done.17.refs_7_), channel_id=1, source_target_pairs={{0,7},{1,0},{2,1},{3,2},{4,3},{5,4},{6,5},{7,6},{8,15},{9,8},{10,9... | collective-permute-start | bytes 786440 | tf_op jit(solution)/shard_map/ppermute | solution.py:391
  75.2 1.4 collective-permute-done.16.refs_6_
  76.6 1.5 collective-permute-start.7
  78.1 1.2 collective-permute-start.9
  79.4 4.3 %collective-permute-done.24.refs_11_ = bf16[4,128,256]{2,1,0:T(8,128)(2,1)S(1)} collective-permute-done((bf16[4,128,256]{2,1,0:T(8,128)(2,1)S(1)}, bf16[4,128,256]{2,1,0:T(8,128)(2,1)S(1)}, u32[]{:S(2)}, u32[]{:S(2)}) %collective-permute-start.24) | collective-permute-done | bytes 262176 | tf_op jit(solution)/shard_map/ppermute | solution.py:391
  83.7 0.7 copy-done.34
  84.4 0.6 pad_add_fusion.where
  85.0 10.8 %shard_map.144 = (bf16[64,128,256]{2,1,0:T(8,128)(2,1)}, bf16[64,64,256]{2,1,0:T(8,128)(2,1)}, bf16[64,64,256]{2,1,0:T(8,128)(2,1)}) custom-call(s32[3]{0:T(128)} %pad_add_fusion.where, bf16[256,256]{1,0:T(8,128)(2,1)} %constant.81.clone.swap, bf16[16,28,64,128]{3,2,1,0:T(8,128)(2,1)} %bitcast.37, bf16[4,128,256]{2,1,0:T(8,128)(2,1)} %bitcast.47, ...), custom_call_target="tpu_custom_call" | custom-call | flops 1409286144 | bytes 11665420 | tf_op jit(solution)/shard_map/pallas_call | solution.py:311
  95.9 1.5 collective-permute-start.25
  97.6 2.6 collective-permute-start.27
  100.2 13.5 %shard_map.145 = (bf16[28,128,256]{2,1,0:T(8,128)(2,1)}, f32[28,128,256]{2,1,0:T(8,128)}, f32[28,128,256]{2,1,0:T(8,128)}, bf16[64,64,256]{2,1,0:T(8,128)(2,1)}) custom-call(bf16[256,256]{1,0:T(8,128)(2,1)} %constant.81.clone.swap, bf16[16,28,64,128]{3,2,1,0:T(8,128)(2,1)} %bitcast.38, bf16[64,64,256]{2,1,0:T(8,128)(2,1)} %get-tuple-element.85.gate_from.gate_in, ...), custom_call_target="tpu_custom_call" | custom-call | flops 1174405120 | bytes 11665408 | tf_op jit(solution)/shard_map/pallas_call | solution.py:311
  113.8 1.5 collective-permute-start.29
  115.3 1.2 collective-permute-start.30
  116.6 4.6 %collective-permute-done.29.refs_8_ = bf16[4,128,256]{2,1,0:T(8,128)(2,1)S(1)} collective-permute-done((bf16[4,128,256]{2,1,0:T(8,128)(2,1)S(1)}, bf16[4,128,256]{2,1,0:T(8,128)(2,1)S(1)}, u32[]{:S(2)}, u32[]{:S(2)}) %collective-permute-start.29) | collective-permute-done | bytes 262176 | tf_op jit(solution)/shard_map/ppermute | solution.py:391
  121.2 1.6 collective-permute-done.30.refs_9_
  122.8 0.7 copy-done.21
  123.5 22.6 %shard_map.146 = (bf16[64,128,256]{2,1,0:T(8,128)(2,1)}, bf16[64,64,256]{2,1,0:T(8,128)(2,1)}, bf16[28,128,256]{2,1,0:T(8,128)(2,1)}, bf16[28,128,256]{2,1,0:T(8...) custom-call(s32[3]{0:T(128)} %pad_add_fusion.where, bf16[256,256]{1,0:T(8,128)(2,1)} %constant.81.clone.swap, ...), custom_call_target="tpu_custom_call" | custom-call | flops 2818572288 | bytes 19005452 | tf_op jit(solution)/shard_map/pallas_call | solution.py:311
  146.1 11.5 %shard_map.147 = (bf16[8,2,58,8,128]{4,3,2,1,0:T(8,128)(2,1)}, bf16[8,2,58,8,128]{4,3,2,1,0:T(8,128)(2,1)}) custom-call(s32[3]{0:T(128)} %pad_add_fusion.where, bf16[64,128,256]{2,1,0:T(8,128)(2,1)} %get-tuple-element.95.dy, bf16[64,64,256]{2,1,0:T(8,128)(2,1)} %get-tuple-element.96.down_in, bf16[28,128,256]{2,1,0:T(8,128)(2,1)} %get-tuple-element.97.act, ...), custom_call_target="tpu_custom_call" | custom-call | flops 939524096 | bytes 18087936 | tf_op jit(solution)/shard_map/pallas_call | solution.py:354
  157.6 13.4 %collective-permute-start.32 = (bf16[8,2,58,8,128]{4,3,2,1,0:T(8,128)(2,1)}, bf16[8,2,58,8,128]{4,3,2,1,0:T(8,128)(2,1)S(1)}, u32[]{:S(2)}, u32[]{:S(2)}) collective-permute-start(bf16[8,2,58,8,128]{4,3,2,1,0:T(8,128)(2,1)} %get-tuple-element.104), channel_id=1, source_target_pairs={{0,16},{16,0},{1,17},{17,1},{2,18},{18,2},{3,19},{19,3},{4,20},{20... | collective-permute-start | bytes 5701640 | tf_op jit(solution)/shard_map/ppermute | solution.py:421
  170.9 8.0 %shard_map.148 = (bf16[8,2,32,8,128]{4,3,2,1,0:T(8,128)(2,1)}, bf16[8,2,32,8,128]{4,3,2,1,0:T(8,128)(2,1)}) custom-call(s32[3]{0:T(128)} %pad_add_fusion.where, bf16[64,128,256]{2,1,0:T(8,128)(2,1)} %get-tuple-element.105.x, bf16[64,128,256]{2,1,0:T(8,128)(2,1)} %get-tuple-element.106.low), custom_call_target="tpu_custom_call" | custom-call | flops 469762048 | bytes 8388608 | tf_op jit(solution)/shard_map/pallas_call | solution.py:354
  179.0 2.8 %collective-permute-done.33 = bf16[8,2,32,8,128]{4,3,2,1,0:T(8,128)(2,1)S(1)} collective-permute-done((bf16[8,2,32,8,128]{4,3,2,1,0:T(8,128)(2,1)}, bf16[8,2,32,8,128]{4,3,2,1,0:T(8,128)(2,1)S(1)}, u32[]{:S(2)}, u32[]{:S(2)}) %collective-permute-start.33) | collective-permute-done | bytes 1048608 | tf_op jit(solution)/shard_map/ppermute | solution.py:421
  181.8 1.5 add_convert_fusion.1
  183.4 0.5 add_convert_fusion
  183.9 1.8 pad_maximum_fusion
  185.7 4.7 %all-to-all-start.1 = ((bf16[16,90,8,128]{3,2,1,0:T(8,128)(2,1)}), bf16[16,90,8,128]{3,2,1,0:T(8,128)(2,1)S(1)}, u32[]{:S(2)}, u32[]{:S(2)}) async-start(bf16[16,90,8,128]{3,2,1,0:T(8,128)(2,1)} %pad_maximum_fusion), calls=%async_computation.2 | async-start | bytes 5898240 | tf_op jit(solution)/shard_map/all_to_all | solution.py:427
  190.4 38.6 %all-to-all-done.1 = bf16[16,90,8,128]{3,2,1,0:T(8,128)(2,1)S(1)} async-done(((bf16[16,90,8,128]{3,2,1,0:T(8,128)(2,1)}), bf16[16,90,8,128]{3,2,1,0:T(8,128)(2,1)S(1)}, u32[]{:S(2)}, u32[]{:S(2)}) %all-to-all-start.1) | async-done | bytes 2949152 | tf_op jit(solution)/shard_map/all_to_all | solution.py:427
  229.5 1.0 dynamic-slice_bitcast_fusion
  230.5 2.3 collective-permute-start.31
  232.8 0.7 slice.22
  233.5 5.2 %collective-permute-start.34 = (f32[16,8,128]{2,1,0:T(8,128)S(1)}, f32[16,8,128]{2,1,0:T(8,128)S(1)}, u32[]{:S(2)}, u32[]{:S(2)}) collective-permute-start(f32[16,8,128]{2,1,0:T(8,128)S(1)} %slice.23), channel_id=1, source_target_pairs={{0,0},{1,16},{2,32},{3,48},{4,64},{5,80},{6,96},{7,112},{16,128},{... | collective-permute-start | bytes 196616 | tf_op jit(solution)/shard_map/ppermute | solution.py:523
  238.7 6.0 %all-to-all-start.2 = ((f32[8,32,128]{2,1,0:T(8,128)}), f32[8,32,128]{2,1,0:T(8,128)S(1)}, u32[]{:S(2)}, u32[]{:S(2)}) async-start(f32[8,32,128]{2,1,0:T(8,128)} %bitcast.22), calls=%async_computation.3 | async-start | bytes 262144 | tf_op jit(solution)/shard_map/all_to_all | solution.py:527
  244.7 0.7 fusion.1
  245.4 0.7 copy.21
  246.0 7.7 %all-to-all-done.2.pieces = f32[8,32,128]{2,1,0:T(8,128)S(1)} async-done(((f32[8,32,128]{2,1,0:T(8,128)}), f32[8,32,128]{2,1,0:T(8,128)S(1)}, u32[]{:S(2)}, u32[]{:S(2)}) %all-to-all-start.2) | async-done | bytes 131104 | tf_op jit(solution)/shard_map/all_to_all | solution.py:527
  253.7 0.7 copy-done.6
  254.3 1.7 shard_map.149
  256.1 0.8 pad_maximum_fusion.1
  (119 shorter events, 1.9 us)
Async XLA Ops:
  8.3 23.7 %copy-start.4 = (bf16[512,512]{1,0:T(8,128)(2,1)S(1)}, bf16[512,512]{1,0:T(8,128)(2,1)}, u32[]{:S(2)}) copy-start(bf16[512,512]{1,0:T(8,128)(2,1)} %param.9) | copy-start | bytes 1572868
  9.1 26.3 %copy-start.5 = (bf16[512,512]{1,0:T(8,128)(2,1)S(1)}, bf16[512,512]{1,0:T(8,128)(2,1)}, u32[]{:S(2)}) copy-start(bf16[512,512]{1,0:T(8,128)(2,1)} %param.10) | copy-start | bytes 1572868
  9.1 22.0 %all-to-all-start = ((bf16[16,64,128]{2,1,0:T(8,128)(2,1)}), bf16[16,64,128]{2,1,0:T(8,128)(2,1)S(1)}, u32[]{:S(2)}, u32[]{:S(2)}) async-start(bf16[16,64,128]{2,1,0:T(8,128)(2,1)} %bitcast.10), calls=%async_computation | async-start | bytes 524288 | tf_op jit(solution)/shard_map/all_to_all | solution.py:444
  20.8 64.2 %all-gather.3.cloned.1.call-start = ((), (), s32[]{:S(2)}) async-start(), calls=%async_computation.5 | async-start | bytes 7798784 | tf_op jit(solution)/shard_map/all_gather | solution.py:482
  21.9 6.3 %collective-permute-start = (bf16[3,128,128]{2,1,0:T(8,128)(2,1)S(1)}, bf16[3,128,128]{2,1,0:T(8,128)(2,1)S(1)}, u32[]{:S(2)}, u32[]{:S(2)}) collective-permute-start(bf16[3,128,128]{2,1,0:T(8,128)(2,1)S(1)} %select_select_fusion), channel_id=1, source_target_pairs={{0,8},{8,0},{1,9},{9,1},{2,10},{10,2},{3,11},{11,3},{4,12},{12,4},... | collective-permute-start | bytes 294920 | tf_op jit(solution)/shard_map/ppermute | solution.py:395
  31.9 197.5 %reduce-scatter.2.cloned.1.call-start = ((), (), s32[]{:S(2)}) async-start(), calls=%async_computation.4 | async-start | bytes 4718592 | tf_op jit(solution)/shard_map/reduce_scatter | solution.py:504
  32.0 53.0 %copy-start.2 = (bf16[512,256]{1,0:T(8,128)(2,1)}, bf16[512,256]{1,0:T(8,128)(2,1)S(1)}, u32[]{:S(2)}) copy-start(bf16[512,256]{1,0:T(8,128)(2,1)S(1)} %get-tuple-element.128) | copy-start | bytes 786436
  32.0 6.8 %collective-permute-start.12 = (bf16[512,256]{1,0:T(8,128)(2,1)S(1)}, bf16[512,256]{1,0:T(8,128)(2,1)S(1)}, u32[]{:S(2)}, u32[]{:S(2)}) collective-permute-start(bf16[512,256]{1,0:T(8,128)(2,1)S(1)} %get-tuple-element.127), channel_id=1, source_target_pairs={{0,8},{8,0},{1,9},{9,1},{2,10},{10,2},{3,11},{11,3},{4,12},{12,4},... | collective-permute-start | bytes 786440 | tf_op jit(solution)/shard_map/ppermute | solution.py:395
  32.8 8.7 %collective-permute-start.3 = (bf16[4,128,256]{2,1,0:T(8,128)(2,1)S(1)}, bf16[4,128,256]{2,1,0:T(8,128)(2,1)S(1)}, u32[]{:S(2)}, u32[]{:S(2)}) collective-permute-start(bf16[4,128,256]{2,1,0:T(8,128)(2,1)S(1)} %bitcast.45), channel_id=1, source_target_pairs={{0,1},{1,2},{2,3},{3,4},{4,5},{5,6},{6,7},{7,0},{8,9},{9,10},{10,1... | collective-permute-start | bytes 786440 | tf_op jit(solution)/shard_map/ppermute | solution.py:391
  35.5 6.3 %collective-permute-start.2 = (bf16[4,128,256]{2,1,0:T(8,128)(2,1)S(1)}, bf16[4,128,256]{2,1,0:T(8,128)(2,1)S(1)}, u32[]{:S(2)}, u32[]{:S(2)}) collective-permute-start(bf16[4,128,256]{2,1,0:T(8,128)(2,1)S(1)} %bitcast.46), channel_id=1, source_target_pairs={{0,7},{1,0},{2,1},{3,2},{4,3},{5,4},{6,5},{7,6},{8,15},{9,8},{10,9... | collective-permute-start | bytes 786440 | tf_op jit(solution)/shard_map/ppermute | solution.py:391
  35.5 60.3 %copy-start.1 = (bf16[512,256]{1,0:T(8,128)(2,1)}, bf16[512,256]{1,0:T(8,128)(2,1)S(1)}, u32[]{:S(2)}) copy-start(bf16[512,256]{1,0:T(8,128)(2,1)S(1)} %get-tuple-element.130) | copy-start | bytes 786436
  35.5 9.9 %collective-permute-start.1 = (bf16[512,256]{1,0:T(8,128)(2,1)S(1)}, bf16[512,256]{1,0:T(8,128)(2,1)S(1)}, u32[]{:S(2)}, u32[]{:S(2)}) collective-permute-start(bf16[512,256]{1,0:T(8,128)(2,1)S(1)} %get-tuple-element.129), channel_id=1, source_target_pairs={{0,8},{8,0},{1,9},{9,1},{2,10},{10,2},{3,11},{11,3},{4,12},{12,4},... | collective-permute-start | bytes 786440 | tf_op jit(solution)/shard_map/ppermute | solution.py:395
  38.8 46.2 %copy-start.22 = (bf16[512,256]{1,0:T(8,128)(2,1)}, bf16[512,256]{1,0:T(8,128)(2,1)S(1)}, u32[]{:S(2)}) copy-start(bf16[512,256]{1,0:T(8,128)(2,1)S(1)} %collective-permute-done.12) | copy-start | bytes 786436
  38.8 8.0 %collective-permute-start.13 = (bf16[4,128,256]{2,1,0:T(8,128)(2,1)S(1)}, bf16[4,128,256]{2,1,0:T(8,128)(2,1)S(1)}, u32[]{:S(2)}, u32[]{:S(2)}) collective-permute-start(bf16[4,128,256]{2,1,0:T(8,128)(2,1)S(1)} %bitcast.56), channel_id=1, source_target_pairs={{0,7},{1,0},{2,1},{3,2},{4,3},{5,4},{6,5},{7,6},{8,15},{9,8},{10,9... | collective-permute-start | bytes 786440 | tf_op jit(solution)/shard_map/ppermute | solution.py:391
  41.5 11.9 %collective-permute-start.22 = (bf16[4,128,256]{2,1,0:T(8,128)(2,1)S(1)}, bf16[4,128,256]{2,1,0:T(8,128)(2,1)S(1)}, u32[]{:S(2)}, u32[]{:S(2)}) collective-permute-start(bf16[4,128,256]{2,1,0:T(8,128)(2,1)S(1)} %bitcast.57), channel_id=1, source_target_pairs={{0,1},{1,2},{2,3},{3,4},{4,5},{5,6},{6,7},{7,0},{8,9},{9,10},{10,1... | collective-permute-start | bytes 786440 | tf_op jit(solution)/shard_map/ppermute | solution.py:391
  41.5 43.5 %copy-start.23 = (bf16[4,128,256]{2,1,0:T(8,128)(2,1)}, bf16[4,128,256]{2,1,0:T(8,128)(2,1)S(1)}, u32[]{:S(2)}) copy-start(bf16[4,128,256]{2,1,0:T(8,128)(2,1)S(1)} %collective-permute-done.3.refs_14_) | copy-start | bytes 786436
  41.5 9.2 %collective-permute-start.18 = (bf16[4,128,256]{2,1,0:T(8,128)(2,1)S(1)}, bf16[4,128,256]{2,1,0:T(8,128)(2,1)S(1)}, u32[]{:S(2)}, u32[]{:S(2)}) collective-permute-start(bf16[4,128,256]{2,1,0:T(8,128)(2,1)S(1)} %collective-permute-done.3.refs_14_), channel_id=1, source_target_pairs={{0,1},{1,2},{2,3},{3,4},{4,5},{5,6},{6,7},{7,0},{8,9},{9,10},{10,1... | collective-permute-start | bytes 786440 | tf_op jit(solution)/shard_map/ppermute | solution.py:391
  41.8 16.5 %copy-start.24 = (bf16[4,128,256]{2,1,0:T(8,128)(2,1)}, bf16[4,128,256]{2,1,0:T(8,128)(2,1)S(1)}, u32[]{:S(2)}) copy-start(bf16[4,128,256]{2,1,0:T(8,128)(2,1)S(1)} %collective-permute-done.2.refs_2_) | copy-start | bytes 786436
  41.8 9.4 %collective-permute-start.14 = (bf16[4,128,256]{2,1,0:T(8,128)(2,1)S(1)}, bf16[4,128,256]{2,1,0:T(8,128)(2,1)S(1)}, u32[]{:S(2)}, u32[]{:S(2)}) collective-permute-start(bf16[4,128,256]{2,1,0:T(8,128)(2,1)S(1)} %collective-permute-done.2.refs_2_), channel_id=1, source_target_pairs={{0,7},{1,0},{2,1},{3,2},{4,3},{5,4},{6,5},{7,6},{8,15},{9,8},{10,9... | collective-permute-start | bytes 786440 | tf_op jit(solution)/shard_map/ppermute | solution.py:391
  45.4 50.4 %copy-start.7 = (bf16[512,256]{1,0:T(8,128)(2,1)}, bf16[512,256]{1,0:T(8,128)(2,1)S(1)}, u32[]{:S(2)}) copy-start(bf16[512,256]{1,0:T(8,128)(2,1)S(1)} %collective-permute-done.1) | copy-start | bytes 786436
  45.4 10.2 %collective-permute-start.4 = (bf16[4,128,256]{2,1,0:T(8,128)(2,1)S(1)}, bf16[4,128,256]{2,1,0:T(8,128)(2,1)S(1)}, u32[]{:S(2)}, u32[]{:S(2)}) collective-permute-start(bf16[4,128,256]{2,1,0:T(8,128)(2,1)S(1)} %bitcast.42), channel_id=1, source_target_pairs={{0,1},{1,2},{2,3},{3,4},{4,5},{5,6},{6,7},{7,0},{8,9},{9,10},{10,1... | collective-permute-start | bytes 786440 | tf_op jit(solution)/shard_map/ppermute | solution.py:391
  46.8 28.3 %copy-start.25 = (bf16[4,128,256]{2,1,0:T(8,128)(2,1)}, bf16[4,128,256]{2,1,0:T(8,128)(2,1)S(1)}, u32[]{:S(2)}) copy-start(bf16[4,128,256]{2,1,0:T(8,128)(2,1)S(1)} %collective-permute-done.13.refs_3_) | copy-start | bytes 786436
  46.8 9.9 %collective-permute-start.15 = (bf16[4,128,256]{2,1,0:T(8,128)(2,1)S(1)}, bf16[4,128,256]{2,1,0:T(8,128)(2,1)S(1)}, u32[]{:S(2)}, u32[]{:S(2)}) collective-permute-start(bf16[4,128,256]{2,1,0:T(8,128)(2,1)S(1)} %collective-permute-done.13.refs_3_), channel_id=1, source_target_pairs={{0,7},{1,0},{2,1},{3,2},{4,3},{5,4},{6,5},{7,6},{8,15},{9,8},{10,9... | collective-permute-start | bytes 786440 | tf_op jit(solution)/shard_map/ppermute | solution.py:391
  50.7 27.4 %copy-start.27 = (bf16[4,128,256]{2,1,0:T(8,128)(2,1)}, bf16[4,128,256]{2,1,0:T(8,128)(2,1)S(1)}, u32[]{:S(2)}) copy-start(bf16[4,128,256]{2,1,0:T(8,128)(2,1)S(1)} %collective-permute-done.18.refs_12_) | copy-start | bytes 786436
  50.7 10.5 %collective-permute-start.6 = (bf16[4,128,256]{2,1,0:T(8,128)(2,1)S(1)}, bf16[4,128,256]{2,1,0:T(8,128)(2,1)S(1)}, u32[]{:S(2)}, u32[]{:S(2)}) collective-permute-start(bf16[4,128,256]{2,1,0:T(8,128)(2,1)S(1)} %bitcast.53), channel_id=1, source_target_pairs={{0,1},{1,2},{2,3},{3,4},{4,5},{5,6},{6,7},{7,0},{8,9},{9,10},{10,1... | collective-permute-start | bytes 786440 | tf_op jit(solution)/shard_map/ppermute | solution.py:391
  51.1 28.2 %copy-start.28 = (bf16[4,128,256]{2,1,0:T(8,128)(2,1)}, bf16[4,128,256]{2,1,0:T(8,128)(2,1)S(1)}, u32[]{:S(2)}) copy-start(bf16[4,128,256]{2,1,0:T(8,128)(2,1)S(1)} %collective-permute-done.14.refs_4_) | copy-start | bytes 786436
  51.1 11.2 %collective-permute-start.8 = (bf16[4,128,256]{2,1,0:T(8,128)(2,1)S(1)}, bf16[4,128,256]{2,1,0:T(8,128)(2,1)S(1)}, u32[]{:S(2)}, u32[]{:S(2)}) collective-permute-start(bf16[4,128,256]{2,1,0:T(8,128)(2,1)S(1)} %bitcast.43), channel_id=1, source_target_pairs={{0,7},{1,0},{2,1},{3,2},{4,3},{5,4},{6,5},{7,6},{8,15},{9,8},{10,9... | collective-permute-start | bytes 786440 | tf_op jit(solution)/shard_map/ppermute | solution.py:391
  53.4 21.8 %copy-start.26 = (bf16[4,128,256]{2,1,0:T(8,128)(2,1)}, bf16[4,128,256]{2,1,0:T(8,128)(2,1)S(1)}, u32[]{:S(2)}) copy-start(bf16[4,128,256]{2,1,0:T(8,128)(2,1)S(1)} %collective-permute-done.22.refs_15_) | copy-start | bytes 786436
  53.4 13.4 %collective-permute-start.19 = (bf16[4,128,256]{2,1,0:T(8,128)(2,1)S(1)}, bf16[4,128,256]{2,1,0:T(8,128)(2,1)S(1)}, u32[]{:S(2)}, u32[]{:S(2)}) collective-permute-start(bf16[4,128,256]{2,1,0:T(8,128)(2,1)S(1)} %collective-permute-done.18.refs_12_), channel_id=1, source_target_pairs={{0,1},{1,2},{2,3},{3,4},{4,5},{5,6},{6,7},{7,0},{8,9},{9,10},{10,1... | collective-permute-start | bytes 786440 | tf_op jit(solution)/shard_map/ppermute | solution.py:391
  55.6 40.2 %copy-start.8 = (bf16[4,128,256]{2,1,0:T(8,128)(2,1)}, bf16[4,128,256]{2,1,0:T(8,128)(2,1)S(1)}, u32[]{:S(2)}) copy-start(bf16[4,128,256]{2,1,0:T(8,128)(2,1)S(1)} %collective-permute-done.4.refs_14_) | copy-start | bytes 786436
  55.6 16.9 %collective-permute-start.23 = (bf16[4,128,256]{2,1,0:T(8,128)(2,1)S(1)}, bf16[4,128,256]{2,1,0:T(8,128)(2,1)S(1)}, u32[]{:S(2)}, u32[]{:S(2)}) collective-permute-start(bf16[4,128,256]{2,1,0:T(8,128)(2,1)S(1)} %collective-permute-done.22.refs_15_), channel_id=1, source_target_pairs={{0,1},{1,2},{2,3},{3,4},{4,5},{5,6},{6,7},{7,0},{8,9},{9,10},{10,1... | collective-permute-start | bytes 786440 | tf_op jit(solution)/shard_map/ppermute | solution.py:391
  56.7 26.9 %copy-start.29 = (bf16[4,128,256]{2,1,0:T(8,128)(2,1)}, bf16[4,128,256]{2,1,0:T(8,128)(2,1)S(1)}, u32[]{:S(2)}) copy-start(bf16[4,128,256]{2,1,0:T(8,128)(2,1)S(1)} %collective-permute-done.15.refs_5_) | copy-start | bytes 786436
  56.7 15.7 %collective-permute-start.17 = (bf16[4,128,256]{2,1,0:T(8,128)(2,1)S(1)}, bf16[4,128,256]{2,1,0:T(8,128)(2,1)}, u32[]{:S(2)}, u32[]{:S(2)}) collective-permute-start(bf16[4,128,256]{2,1,0:T(8,128)(2,1)S(1)} %collective-permute-done.15.refs_5_), channel_id=1, source_target_pairs={{0,7},{1,0},{2,1},{3,2},{4,3},{5,4},{6,5},{7,6},{8,15},{9,8},{10,9... | collective-permute-start | bytes 786440 | tf_op jit(solution)/shard_map/ppermute | solution.py:391
  61.2 34.6 %copy-start.9 = (bf16[4,128,256]{2,1,0:T(8,128)(2,1)}, bf16[4,128,256]{2,1,0:T(8,128)(2,1)S(1)}, u32[]{:S(2)}) copy-start(bf16[4,128,256]{2,1,0:T(8,128)(2,1)S(1)} %collective-permute-done.6.refs_15_) | copy-start | bytes 786436
  61.2 13.9 %collective-permute-start.10 = (bf16[4,128,256]{2,1,0:T(8,128)(2,1)S(1)}, bf16[4,128,256]{2,1,0:T(8,128)(2,1)S(1)}, u32[]{:S(2)}, u32[]{:S(2)}) collective-permute-start(bf16[4,128,256]{2,1,0:T(8,128)(2,1)S(1)} %bitcast.54), channel_id=1, source_target_pairs={{0,7},{1,0},{2,1},{3,2},{4,3},{5,4},{6,5},{7,6},{8,15},{9,8},{10,9... | collective-permute-start | bytes 786440 | tf_op jit(solution)/shard_map/ppermute | solution.py:391
  62.4 33.5 %copy-start.10 = (bf16[4,128,256]{2,1,0:T(8,128)(2,1)}, bf16[4,128,256]{2,1,0:T(8,128)(2,1)S(1)}, u32[]{:S(2)}) copy-start(bf16[4,128,256]{2,1,0:T(8,128)(2,1)S(1)} %collective-permute-done.8.refs_2_) | copy-start | bytes 786436
  62.4 14.2 %collective-permute-start.16 = (bf16[4,128,256]{2,1,0:T(8,128)(2,1)S(1)}, bf16[4,128,256]{2,1,0:T(8,128)(2,1)S(1)}, u32[]{:S(2)}, u32[]{:S(2)}) collective-permute-start(bf16[4,128,256]{2,1,0:T(8,128)(2,1)S(1)} %collective-permute-done.14.refs_4_), channel_id=1, source_target_pairs={{0,7},{1,0},{2,1},{3,2},{4,3},{5,4},{6,5},{7,6},{8,15},{9,8},{10,9... | collective-permute-start | bytes 786440 | tf_op jit(solution)/shard_map/ppermute | solution.py:391
  66.8 16.9 %copy-start.30 = (bf16[4,128,256]{2,1,0:T(8,128)(2,1)}, bf16[4,128,256]{2,1,0:T(8,128)(2,1)S(1)}, u32[]{:S(2)}) copy-start(bf16[4,128,256]{2,1,0:T(8,128)(2,1)S(1)} %collective-permute-done.19.refs_10_) | copy-start | bytes 786436
  66.8 11.3 %collective-permute-start.20 = (bf16[4,128,256]{2,1,0:T(8,128)(2,1)S(1)}, bf16[4,128,256]{2,1,0:T(8,128)(2,1)S(1)}, u32[]{:S(2)}, u32[]{:S(2)}) collective-permute-start(bf16[4,128,256]{2,1,0:T(8,128)(2,1)S(1)} %collective-permute-done.19.refs_10_), channel_id=1, source_target_pairs={{0,1},{1,2},{2,3},{3,4},{4,5},{5,6},{6,7},{7,0},{8,9},{9,10},{10,1... | collective-permute-start | bytes 786440 | tf_op jit(solution)/shard_map/ppermute | solution.py:391
  72.4 11.2 %copy-start.31 = (bf16[4,128,256]{2,1,0:T(8,128)(2,1)}, bf16[4,128,256]{2,1,0:T(8,128)(2,1)S(1)}, u32[]{:S(2)}) copy-start(bf16[4,128,256]{2,1,0:T(8,128)(2,1)S(1)} %collective-permute-done.23.refs_13_) | copy-start | bytes 786436
  72.4 11.2 %collective-permute-start.24 = (bf16[4,128,256]{2,1,0:T(8,128)(2,1)S(1)}, bf16[4,128,256]{2,1,0:T(8,128)(2,1)S(1)}, u32[]{:S(2)}, u32[]{:S(2)}) collective-permute-start(bf16[4,128,256]{2,1,0:T(8,128)(2,1)S(1)} %collective-permute-done.23.refs_13_), channel_id=1, source_target_pairs={{0,1},{1,2},{2,3},{3,4},{4,5},{5,6},{6,7},{7,0},{8,9},{9,10},{10,1... | collective-permute-start | bytes 786440 | tf_op jit(solution)/shard_map/ppermute | solution.py:391
  72.4 12.6 %collective-permute-start.21 = (bf16[4,128,256]{2,1,0:T(8,128)(2,1)}, bf16[4,128,256]{2,1,0:T(8,128)(2,1)}, u32[]{:S(2)}, u32[]{:S(2)}) collective-permute-start(bf16[4,128,256]{2,1,0:T(8,128)(2,1)} %collective-permute-done.17.refs_7_), channel_id=1, source_target_pairs={{0,7},{1,0},{2,1},{3,2},{4,3},{5,4},{6,5},{7,6},{8,15},{9,8},{10,9... | collective-permute-start | bytes 786440 | tf_op jit(solution)/shard_map/ppermute | solution.py:391
  75.1 20.7 %copy-start.11 = (bf16[4,128,256]{2,1,0:T(8,128)(2,1)}, bf16[4,128,256]{2,1,0:T(8,128)(2,1)S(1)}, u32[]{:S(2)}) copy-start(bf16[4,128,256]{2,1,0:T(8,128)(2,1)S(1)} %collective-permute-done.10.refs_3_) | copy-start | bytes 786436
  75.1 20.7 %collective-permute-start.5 = (bf16[4,128,256]{2,1,0:T(8,128)(2,1)S(1)}, bf16[4,128,256]{2,1,0:T(8,128)(2,1)S(1)}, u32[]{:S(2)}, u32[]{:S(2)}) collective-permute-start(bf16[4,128,256]{2,1,0:T(8,128)(2,1)S(1)} %collective-permute-done.4.refs_14_), channel_id=1, source_target_pairs={{0,1},{1,2},{2,3},{3,4},{4,5},{5,6},{6,7},{7,0},{8,9},{9,10},{10,1... | collective-permute-start | bytes 786440 | tf_op jit(solution)/shard_map/ppermute | solution.py:391
  76.6 19.3 %collective-permute-start.7 = (bf16[4,128,256]{2,1,0:T(8,128)(2,1)S(1)}, bf16[4,128,256]{2,1,0:T(8,128)(2,1)S(1)}, u32[]{:S(2)}, u32[]{:S(2)}) collective-permute-start(bf16[4,128,256]{2,1,0:T(8,128)(2,1)S(1)} %collective-permute-done.6.refs_15_), channel_id=1, source_target_pairs={{0,1},{1,2},{2,3},{3,4},{4,5},{5,6},{6,7},{7,0},{8,9},{9,10},{10,1... | collective-permute-start | bytes 786440 | tf_op jit(solution)/shard_map/ppermute | solution.py:391
  78.1 17.8 %collective-permute-start.9 = (bf16[4,128,256]{2,1,0:T(8,128)(2,1)S(1)}, bf16[4,128,256]{2,1,0:T(8,128)(2,1)S(1)}, u32[]{:S(2)}, u32[]{:S(2)}) collective-permute-start(bf16[4,128,256]{2,1,0:T(8,128)(2,1)S(1)} %collective-permute-done.8.refs_2_), channel_id=1, source_target_pairs={{0,7},{1,0},{2,1},{3,2},{4,3},{5,4},{6,5},{7,6},{8,15},{9,8},{10,9... | collective-permute-start | bytes 786440 | tf_op jit(solution)/shard_map/ppermute | solution.py:391
  84.4 11.5 %collective-permute-start.11 = (bf16[4,128,256]{2,1,0:T(8,128)(2,1)S(1)}, bf16[4,128,256]{2,1,0:T(8,128)(2,1)S(1)}, u32[]{:S(2)}, u32[]{:S(2)}) collective-permute-start(bf16[4,128,256]{2,1,0:T(8,128)(2,1)S(1)} %collective-permute-done.10.refs_3_), channel_id=1, source_target_pairs={{0,7},{1,0},{2,1},{3,2},{4,3},{5,4},{6,5},{7,6},{8,15},{9,8},{10,9... | collective-permute-start | bytes 786440 | tf_op jit(solution)/shard_map/ppermute | solution.py:391
  95.9 17.9 %copy-start.12 = (bf16[4,128,256]{2,1,0:T(8,128)(2,1)}, bf16[4,128,256]{2,1,0:T(8,128)(2,1)S(1)}, u32[]{:S(2)}) copy-start(bf16[4,128,256]{2,1,0:T(8,128)(2,1)S(1)} %collective-permute-done.5.refs_12_) | copy-start | bytes 786436
  95.9 17.8 %copy-start.13 = (bf16[4,128,256]{2,1,0:T(8,128)(2,1)}, bf16[4,128,256]{2,1,0:T(8,128)(2,1)S(1)}, u32[]{:S(2)}) copy-start(bf16[4,128,256]{2,1,0:T(8,128)(2,1)S(1)} %collective-permute-done.7.refs_13_) | copy-start | bytes 786436
  95.9 17.8 %copy-start.14 = (bf16[4,128,256]{2,1,0:T(8,128)(2,1)}, bf16[4,128,256]{2,1,0:T(8,128)(2,1)S(1)}, u32[]{:S(2)}) copy-start(bf16[4,128,256]{2,1,0:T(8,128)(2,1)S(1)} %collective-permute-done.9.refs_4_) | copy-start | bytes 786436
  95.9 17.8 %copy-start.15 = (bf16[4,128,256]{2,1,0:T(8,128)(2,1)}, bf16[4,128,256]{2,1,0:T(8,128)(2,1)S(1)}, u32[]{:S(2)}) copy-start(bf16[4,128,256]{2,1,0:T(8,128)(2,1)S(1)} %collective-permute-done.11.refs_5_) | copy-start | bytes 786436
  95.9 17.8 %collective-permute-start.25 = (bf16[4,128,256]{2,1,0:T(8,128)(2,1)S(1)}, bf16[4,128,256]{2,1,0:T(8,128)(2,1)S(1)}, u32[]{:S(2)}, u32[]{:S(2)}) collective-permute-start(bf16[4,128,256]{2,1,0:T(8,128)(2,1)S(1)} %collective-permute-done.5.refs_12_), channel_id=1, source_target_pairs={{0,1},{1,2},{2,3},{3,4},{4,5},{5,6},{6,7},{7,0},{8,9},{9,10},{10,1... | collective-permute-start | bytes 786440 | tf_op jit(solution)/shard_map/ppermute | solution.py:391
  97.5 16.3 %collective-permute-start.26 = (bf16[4,128,256]{2,1,0:T(8,128)(2,1)S(1)}, bf16[4,128,256]{2,1,0:T(8,128)(2,1)S(1)}, u32[]{:S(2)}, u32[]{:S(2)}) collective-permute-start(bf16[4,128,256]{2,1,0:T(8,128)(2,1)S(1)} %collective-permute-done.7.refs_13_), channel_id=1, source_target_pairs={{0,1},{1,2},{2,3},{3,4},{4,5},{5,6},{6,7},{7,0},{8,9},{9,10},{10,1... | collective-permute-start | bytes 786440 | tf_op jit(solution)/shard_map/ppermute | solution.py:391
  97.6 16.2 %collective-permute-start.27 = (bf16[4,128,256]{2,1,0:T(8,128)(2,1)S(1)}, bf16[4,128,256]{2,1,0:T(8,128)(2,1)S(1)}, u32[]{:S(2)}, u32[]{:S(2)}) collective-permute-start(bf16[4,128,256]{2,1,0:T(8,128)(2,1)S(1)} %collective-permute-done.9.refs_4_), channel_id=1, source_target_pairs={{0,7},{1,0},{2,1},{3,2},{4,3},{5,4},{6,5},{7,6},{8,15},{9,8},{10,9... | collective-permute-start | bytes 786440 | tf_op jit(solution)/shard_map/ppermute | solution.py:391
  100.1 13.7 %collective-permute-start.28 = (bf16[4,128,256]{2,1,0:T(8,128)(2,1)S(1)}, bf16[4,128,256]{2,1,0:T(8,128)(2,1)S(1)}, u32[]{:S(2)}, u32[]{:S(2)}) collective-permute-start(bf16[4,128,256]{2,1,0:T(8,128)(2,1)S(1)} %collective-permute-done.11.refs_5_), channel_id=1, source_target_pairs={{0,7},{1,0},{2,1},{3,2},{4,3},{5,4},{6,5},{7,6},{8,15},{9,8},{10,9... | collective-permute-start | bytes 786440 | tf_op jit(solution)/shard_map/ppermute | solution.py:391
  113.8 7.4 %collective-permute-start.29 = (bf16[4,128,256]{2,1,0:T(8,128)(2,1)S(1)}, bf16[4,128,256]{2,1,0:T(8,128)(2,1)S(1)}, u32[]{:S(2)}, u32[]{:S(2)}) collective-permute-start(bf16[4,128,256]{2,1,0:T(8,128)(2,1)S(1)} %collective-permute-done.25.refs_10_), channel_id=1, source_target_pairs={{0,1},{1,2},{2,3},{3,4},{4,5},{5,6},{6,7},{7,0},{8,9},{9,10},{10,1... | collective-permute-start | bytes 786440 | tf_op jit(solution)/shard_map/ppermute | solution.py:391
  115.3 7.4 %collective-permute-start.30 = (bf16[4,128,256]{2,1,0:T(8,128)(2,1)S(1)}, bf16[4,128,256]{2,1,0:T(8,128)(2,1)S(1)}, u32[]{:S(2)}, u32[]{:S(2)}) collective-permute-start(bf16[4,128,256]{2,1,0:T(8,128)(2,1)S(1)} %collective-permute-done.28.refs_7_), channel_id=1, source_target_pairs={{0,7},{1,0},{2,1},{3,2},{4,3},{5,4},{6,5},{7,6},{8,15},{9,8},{10,9... | collective-permute-start | bytes 786440 | tf_op jit(solution)/shard_map/ppermute | solution.py:391
  157.6 25.8 %collective-permute-start.32 = (bf16[8,2,58,8,128]{4,3,2,1,0:T(8,128)(2,1)}, bf16[8,2,58,8,128]{4,3,2,1,0:T(8,128)(2,1)S(1)}, u32[]{:S(2)}, u32[]{:S(2)}) collective-permute-start(bf16[8,2,58,8,128]{4,3,2,1,0:T(8,128)(2,1)} %get-tuple-element.104), channel_id=1, source_target_pairs={{0,16},{16,0},{1,17},{17,1},{2,18},{18,2},{3,19},{19,3},{4,20},{20... | collective-permute-start | bytes 5701640 | tf_op jit(solution)/shard_map/ppermute | solution.py:421
  178.9 2.9 %collective-permute-start.33 = (bf16[8,2,32,8,128]{4,3,2,1,0:T(8,128)(2,1)}, bf16[8,2,32,8,128]{4,3,2,1,0:T(8,128)(2,1)S(1)}, u32[]{:S(2)}, u32[]{:S(2)}) collective-permute-start(bf16[8,2,32,8,128]{4,3,2,1,0:T(8,128)(2,1)} %get-tuple-element.108), channel_id=1, source_target_pairs={{0,16},{16,0},{1,17},{17,1},{2,18},{18,2},{3,19},{19,3},{4,20},{20... | collective-permute-start | bytes 3145736 | tf_op jit(solution)/shard_map/ppermute | solution.py:421
  185.7 43.3 %all-to-all-start.1 = ((bf16[16,90,8,128]{3,2,1,0:T(8,128)(2,1)}), bf16[16,90,8,128]{3,2,1,0:T(8,128)(2,1)S(1)}, u32[]{:S(2)}, u32[]{:S(2)}) async-start(bf16[16,90,8,128]{3,2,1,0:T(8,128)(2,1)} %pad_maximum_fusion), calls=%async_computation.2 | async-start | bytes 5898240 | tf_op jit(solution)/shard_map/all_to_all | solution.py:427
  229.4 26.6 %copy-start.3 = (bf16[8,128,256]{2,1,0:T(8,128)(2,1)S(1)}, bf16[8,128,256]{2,1,0:T(8,128)(2,1)}, u32[]{:S(2)}) copy-start(bf16[8,128,256]{2,1,0:T(8,128)(2,1)} %reduce-scatter.2.cloned.1.call-done) | copy-start | bytes 1572868
  230.5 25.6 %collective-permute-start.31 = (bf16[512,256]{1,0:T(8,128)(2,1)S(1)}, bf16[512,256]{1,0:T(8,128)(2,1)S(1)}, u32[]{:S(2)}, u32[]{:S(2)}) collective-permute-start(bf16[512,256]{1,0:T(8,128)(2,1)S(1)} %dynamic-slice_bitcast_fusion), channel_id=1, source_target_pairs={{0,8},{8,0},{1,9},{9,1},{2,10},{10,2},{3,11},{11,3},{4,12},{12,4},... | collective-permute-start | bytes 786440 | tf_op jit(solution)/shard_map/ppermute | solution.py:395
  233.5 11.9 %collective-permute-start.34 = (f32[16,8,128]{2,1,0:T(8,128)S(1)}, f32[16,8,128]{2,1,0:T(8,128)S(1)}, u32[]{:S(2)}, u32[]{:S(2)}) collective-permute-start(f32[16,8,128]{2,1,0:T(8,128)S(1)} %slice.23), channel_id=1, source_target_pairs={{0,0},{1,16},{2,32},{3,48},{4,64},{5,80},{6,96},{7,112},{16,128},{... | collective-permute-start | bytes 196616 | tf_op jit(solution)/shard_map/ppermute | solution.py:523
  238.7 15.0 %all-to-all-start.2 = ((f32[8,32,128]{2,1,0:T(8,128)}), f32[8,32,128]{2,1,0:T(8,128)S(1)}, u32[]{:S(2)}, u32[]{:S(2)}) async-start(f32[8,32,128]{2,1,0:T(8,128)} %bitcast.22), calls=%async_computation.3 | async-start | bytes 262144 | tf_op jit(solution)/shard_map/all_to_all | solution.py:527
  (11 other events, 56.7 us)
Sparse Core Ops, SparseCore 0:
  32.0 49.9 all-gather.2
  146.2 65.7 reduce-scatter.1

commit v8 on v7

--- a/solution.py
+++ b/solution.py
@@ -525,6 +525,7 @@
 
     firsts = firsts.reshape(nz, per * rows, 2 * ROWS)
     firsts = lax.all_to_all(firsts, "z", 0, 0, tiled=True)
+    firsts, input_grad = lax.optimization_barrier((firsts, input_grad))
     out_gf, out_uf = [value.reshape(per, rows, wide) for value in join(firsts)]
     return input_grad, out_gf, out_uf, out_gs, out_us, out_df, out_ds
 

time: 265 us -> 264 us (level)
  no operation moved by 1% of the time
where the time goes in v8:
time: 264 us
  waiting for transfers between devices  87.4 us (33%)
  starting transfers between devices  78.6 us (30%)
  Pallas kernels  68.1 us (26%)
  between operations  14.6 us (6%)
  other arithmetic  8.67 us (3%)
  local copies, waits for them, and re-layouts  6.13 us (2%)
    pallas_call x3, Pallas kernels, copying(): pl.pallas_call(kernel, out_shape=[jax.ShapeDtypeStruct(shape, dtype) for...  46.8 us
    all_to_all x1, waiting for transfers between devices, to_chips(): return lax.all_to_all(pairs, CHIPS, 0, 0, tiled=True)  38.6 us
    ppermute x28, waiting for transfers between devices, shift(): lax.ppermute(value, 'z', [(i, (i + step) % count) for i in range(count)])  30.4 us
    ppermute x28, starting transfers between devices, shift(): lax.ppermute(value, 'z', [(i, (i + step) % count) for i in range(count)])  29.2 us
    pallas_call x2, Pallas kernels, grads_call(): pl.pallas_call(kernel, grid=(8,), out_shape=[jax.ShapeDtypeStruct(shape,...  19.5 us
    ppermute x2, starting transfers between devices, sum_cores(): found = lax.ppermute(send, 'core', [(0, 1), (1, 0)])  13.4 us
    all_to_all x1, starting transfers between devices, share_first(): return lax.all_to_all(first, TENSOR, 0, 0, tiled=True)  11.7 us
    ppermute x4, starting transfers between devices, swap(): return lax.ppermute(value, 'x_hi', [(0, 1), (1, 0)])  8.38 us
  transfers between devices with their start and end apart: 40, of which 19 were waited for; matrix products, arithmetic and copies ran while one was open for 3% of the time, Pallas kernels for 17%

profile of v8, /device:TPU:1, one launch (start us, length us, event | category | flops | bytes accessed | tf_op | source)
XLA Modules:
  0.0 263.6 jit_solution(16097440472322720348)
XLA Ops:
  7.2 1.0 fusion
  8.4 0.8 broadcast_in_dim.2
  9.1 11.7 %all-to-all-start = ((bf16[16,64,128]{2,1,0:T(8,128)(2,1)}), bf16[16,64,128]{2,1,0:T(8,128)(2,1)S(1)}, u32[]{:S(2)}, u32[]{:S(2)}) async-start(bf16[16,64,128]{2,1,0:T(8,128)(2,1)} %bitcast.10), calls=%async_computation | async-start | bytes 524288 | tf_op jit(solution)/shard_map/all_to_all | solution.py:444
  20.9 1.0 select_select_fusion
  21.9 3.0 %collective-permute-start = (bf16[3,128,128]{2,1,0:T(8,128)(2,1)S(1)}, bf16[3,128,128]{2,1,0:T(8,128)(2,1)S(1)}, u32[]{:S(2)}, u32[]{:S(2)}) collective-permute-start(bf16[3,128,128]{2,1,0:T(8,128)(2,1)S(1)} %select_select_fusion), channel_id=1, source_target_pairs={{0,8},{8,0},{1,9},{9,1},{2,10},{10,2},{3,11},{11,3},{4,12},{12,4},... | collective-permute-start | bytes 294920 | tf_op jit(solution)/shard_map/ppermute | solution.py:395
  24.9 3.4 %collective-permute-done = bf16[3,128,128]{2,1,0:T(8,128)(2,1)S(1)} collective-permute-done((bf16[3,128,128]{2,1,0:T(8,128)(2,1)S(1)}, bf16[3,128,128]{2,1,0:T(8,128)(2,1)S(1)}, u32[]{:S(2)}, u32[]{:S(2)}) %collective-permute-start) | collective-permute-done | bytes 98336 | tf_op jit(solution)/shard_map/ppermute | solution.py:395
  28.3 2.8 %all-to-all-done = bf16[16,64,128]{2,1,0:T(8,128)(2,1)S(1)} async-done(((bf16[16,64,128]{2,1,0:T(8,128)(2,1)}), bf16[16,64,128]{2,1,0:T(8,128)(2,1)S(1)}, u32[]{:S(2)}, u32[]{:S(2)}) %all-to-all-start) | async-done | bytes 262176 | tf_op jit(solution)/shard_map/all_to_all | solution.py:444
  31.1 0.8 pad_maximum_fusion.2
  32.0 0.7 collective-permute-start.1
  32.8 2.7 %collective-permute-start.8 = (bf16[4,128,256]{2,1,0:T(8,128)(2,1)S(1)}, bf16[4,128,256]{2,1,0:T(8,128)(2,1)S(1)}, u32[]{:S(2)}, u32[]{:S(2)}) collective-permute-start(bf16[4,128,256]{2,1,0:T(8,128)(2,1)S(1)} %bitcast.45), channel_id=1, source_target_pairs={{0,1},{1,2},{2,3},{3,4},{4,5},{5,6},{6,7},{7,0},{8,9},{9,10},{10,1... | collective-permute-start | bytes 786440 | tf_op jit(solution)/shard_map/ppermute | solution.py:391
  35.5 2.4 collective-permute-start.16
  37.9 0.9 collective-permute-done.1
  38.8 2.6 %collective-permute-start.3 = (bf16[4,128,256]{2,1,0:T(8,128)(2,1)S(1)}, bf16[4,128,256]{2,1,0:T(8,128)(2,1)S(1)}, u32[]{:S(2)}, u32[]{:S(2)}) collective-permute-start(bf16[4,128,256]{2,1,0:T(8,128)(2,1)S(1)} %bitcast.56), channel_id=1, source_target_pairs={{0,7},{1,0},{2,1},{3,2},{4,3},{5,4},{6,5},{7,6},{8,15},{9,8},{10,9... | collective-permute-start | bytes 786440 | tf_op jit(solution)/shard_map/ppermute | solution.py:391
  41.8 2.5 collective-permute-start.4
  44.3 1.1 collective-permute-done.16
  45.4 1.4 collective-permute-start.17
  46.8 1.8 collective-permute-start.5
  48.7 2.1 collective-permute-done.9.refs_12_
  51.1 2.3 collective-permute-start.19
  53.4 2.1 collective-permute-done.17.refs_14_
  55.6 1.2 collective-permute-done.5.refs_5_
  56.7 1.5 collective-permute-start.7
  58.3 2.9 %collective-permute-done.18.refs_15_ = bf16[4,128,256]{2,1,0:T(8,128)(2,1)S(1)} collective-permute-done((bf16[4,128,256]{2,1,0:T(8,128)(2,1)S(1)}, bf16[4,128,256]{2,1,0:T(8,128)(2,1)S(1)}, u32[]{:S(2)}, u32[]{:S(2)}) %collective-permute-start.18) | collective-permute-done | bytes 262176 | tf_op jit(solution)/shard_map/ppermute | solution.py:391
  61.2 1.2 collective-permute-done.19.refs_2_
  62.4 1.4 collective-permute-start.6
  63.8 3.0 %collective-permute-done.10.refs_10_ = bf16[4,128,256]{2,1,0:T(8,128)(2,1)S(1)} collective-permute-done((bf16[4,128,256]{2,1,0:T(8,128)(2,1)S(1)}, bf16[4,128,256]{2,1,0:T(8,128)(2,1)S(1)}, u32[]{:S(2)}, u32[]{:S(2)}) %collective-permute-start.10) | collective-permute-done | bytes 262176 | tf_op jit(solution)/shard_map/ppermute | solution.py:391
  66.8 5.6 %collective-permute-done.14.refs_13_ = bf16[4,128,256]{2,1,0:T(8,128)(2,1)S(1)} collective-permute-done((bf16[4,128,256]{2,1,0:T(8,128)(2,1)S(1)}, bf16[4,128,256]{2,1,0:T(8,128)(2,1)S(1)}, u32[]{:S(2)}, u32[]{:S(2)}) %collective-permute-start.14) | collective-permute-done | bytes 262176 | tf_op jit(solution)/shard_map/ppermute | solution.py:391
  72.4 2.7 %collective-permute-start.12 = (bf16[4,128,256]{2,1,0:T(8,128)(2,1)}, bf16[4,128,256]{2,1,0:T(8,128)(2,1)}, u32[]{:S(2)}, u32[]{:S(2)}) collective-permute-start(bf16[4,128,256]{2,1,0:T(8,128)(2,1)} %collective-permute-done.7.refs_7_), channel_id=1, source_target_pairs={{0,7},{1,0},{2,1},{3,2},{4,3},{5,4},{6,5},{7,6},{8,15},{9,8},{10,9... | collective-permute-start | bytes 786440 | tf_op jit(solution)/shard_map/ppermute | solution.py:391
  75.2 1.4 collective-permute-done.6.refs_6_
  76.6 1.5 collective-permute-start.22
  78.1 1.2 collective-permute-start.23
  79.4 4.3 %collective-permute-done.15.refs_11_ = bf16[4,128,256]{2,1,0:T(8,128)(2,1)S(1)} collective-permute-done((bf16[4,128,256]{2,1,0:T(8,128)(2,1)S(1)}, bf16[4,128,256]{2,1,0:T(8,128)(2,1)S(1)}, u32[]{:S(2)}, u32[]{:S(2)}) %collective-permute-start.15) | collective-permute-done | bytes 262176 | tf_op jit(solution)/shard_map/ppermute | solution.py:391
  83.7 0.7 copy-done.34
  84.4 0.6 pad_add_fusion.where
  85.0 10.8 %shard_map.144 = (bf16[64,128,256]{2,1,0:T(8,128)(2,1)}, bf16[64,64,256]{2,1,0:T(8,128)(2,1)}, bf16[64,64,256]{2,1,0:T(8,128)(2,1)}) custom-call(s32[3]{0:T(128)} %pad_add_fusion.where, bf16[256,256]{1,0:T(8,128)(2,1)} %constant.81.clone.swap, bf16[16,28,64,128]{3,2,1,0:T(8,128)(2,1)} %bitcast.37, bf16[4,128,256]{2,1,0:T(8,128)(2,1)} %bitcast.47, ...), custom_call_target="tpu_custom_call" | custom-call | flops 1409286144 | bytes 11665420 | tf_op jit(solution)/shard_map/pallas_call | solution.py:311
  95.9 1.5 collective-permute-start.25
  97.6 2.6 collective-permute-start.27
  100.2 13.5 %shard_map.145 = (bf16[28,128,256]{2,1,0:T(8,128)(2,1)}, f32[28,128,256]{2,1,0:T(8,128)}, f32[28,128,256]{2,1,0:T(8,128)}, bf16[64,64,256]{2,1,0:T(8,128)(2,1)}) custom-call(bf16[256,256]{1,0:T(8,128)(2,1)} %constant.81.clone.swap, bf16[16,28,64,128]{3,2,1,0:T(8,128)(2,1)} %bitcast.38, bf16[64,64,256]{2,1,0:T(8,128)(2,1)} %get-tuple-element.88.gate_from.gate_in, ...), custom_call_target="tpu_custom_call" | custom-call | flops 1174405120 | bytes 11665408 | tf_op jit(solution)/shard_map/pallas_call | solution.py:311
  113.8 1.5 collective-permute-start.29
  115.3 1.2 collective-permute-start.30
  116.6 4.6 %collective-permute-done.29.refs_8_ = bf16[4,128,256]{2,1,0:T(8,128)(2,1)S(1)} collective-permute-done((bf16[4,128,256]{2,1,0:T(8,128)(2,1)S(1)}, bf16[4,128,256]{2,1,0:T(8,128)(2,1)S(1)}, u32[]{:S(2)}, u32[]{:S(2)}) %collective-permute-start.29) | collective-permute-done | bytes 262176 | tf_op jit(solution)/shard_map/ppermute | solution.py:391
  121.2 1.6 collective-permute-done.30.refs_9_
  122.8 0.7 copy-done.21
  123.5 22.6 %shard_map.146 = (bf16[64,128,256]{2,1,0:T(8,128)(2,1)}, bf16[64,64,256]{2,1,0:T(8,128)(2,1)}, bf16[28,128,256]{2,1,0:T(8,128)(2,1)}, bf16[28,128,256]{2,1,0:T(8...) custom-call(s32[3]{0:T(128)} %pad_add_fusion.where, bf16[256,256]{1,0:T(8,128)(2,1)} %constant.81.clone.swap, ...), custom_call_target="tpu_custom_call" | custom-call | flops 2818572288 | bytes 19005452 | tf_op jit(solution)/shard_map/pallas_call | solution.py:311
  146.1 11.5 %shard_map.147 = (bf16[8,2,58,8,128]{4,3,2,1,0:T(8,128)(2,1)}, bf16[8,2,58,8,128]{4,3,2,1,0:T(8,128)(2,1)}) custom-call(s32[3]{0:T(128)} %pad_add_fusion.where, bf16[64,128,256]{2,1,0:T(8,128)(2,1)} %get-tuple-element.96.dy, bf16[64,64,256]{2,1,0:T(8,128)(2,1)} %get-tuple-element.97.down_in, bf16[28,128,256]{2,1,0:T(8,128)(2,1)} %get-tuple-element.98.act, ...), custom_call_target="tpu_custom_call" | custom-call | flops 939524096 | bytes 18087936 | tf_op jit(solution)/shard_map/pallas_call | solution.py:354
  157.6 13.4 %collective-permute-start.31 = (bf16[8,2,58,8,128]{4,3,2,1,0:T(8,128)(2,1)}, bf16[8,2,58,8,128]{4,3,2,1,0:T(8,128)(2,1)S(1)}, u32[]{:S(2)}, u32[]{:S(2)}) collective-permute-start(bf16[8,2,58,8,128]{4,3,2,1,0:T(8,128)(2,1)} %get-tuple-element.105), channel_id=1, source_target_pairs={{0,16},{16,0},{1,17},{17,1},{2,18},{18,2},{3,19},{19,3},{4,20},{20... | collective-permute-start | bytes 5701640 | tf_op jit(solution)/shard_map/ppermute | solution.py:421
  170.9 8.0 %shard_map.148 = (bf16[8,2,32,8,128]{4,3,2,1,0:T(8,128)(2,1)}, bf16[8,2,32,8,128]{4,3,2,1,0:T(8,128)(2,1)}) custom-call(s32[3]{0:T(128)} %pad_add_fusion.where, bf16[64,128,256]{2,1,0:T(8,128)(2,1)} %get-tuple-element.106.x, bf16[64,128,256]{2,1,0:T(8,128)(2,1)} %get-tuple-element.107.low), custom_call_target="tpu_custom_call" | custom-call | flops 469762048 | bytes 8388608 | tf_op jit(solution)/shard_map/pallas_call | solution.py:354
  179.0 2.8 %collective-permute-done.32 = bf16[8,2,32,8,128]{4,3,2,1,0:T(8,128)(2,1)S(1)} collective-permute-done((bf16[8,2,32,8,128]{4,3,2,1,0:T(8,128)(2,1)}, bf16[8,2,32,8,128]{4,3,2,1,0:T(8,128)(2,1)S(1)}, u32[]{:S(2)}, u32[]{:S(2)}) %collective-permute-start.32) | collective-permute-done | bytes 1048608 | tf_op jit(solution)/shard_map/ppermute | solution.py:421
  181.8 1.5 add_convert_fusion.1
  183.4 0.5 add_convert_fusion
  183.9 1.8 pad_maximum_fusion
  185.7 4.7 %all-to-all-start.1 = ((bf16[16,90,8,128]{3,2,1,0:T(8,128)(2,1)}), bf16[16,90,8,128]{3,2,1,0:T(8,128)(2,1)S(1)}, u32[]{:S(2)}, u32[]{:S(2)}) async-start(bf16[16,90,8,128]{3,2,1,0:T(8,128)(2,1)} %pad_maximum_fusion), calls=%async_computation.1 | async-start | bytes 5898240 | tf_op jit(solution)/shard_map/all_to_all | solution.py:427
  190.4 38.6 %all-to-all-done.1 = bf16[16,90,8,128]{3,2,1,0:T(8,128)(2,1)S(1)} async-done(((bf16[16,90,8,128]{3,2,1,0:T(8,128)(2,1)}), bf16[16,90,8,128]{3,2,1,0:T(8,128)(2,1)S(1)}, u32[]{:S(2)}, u32[]{:S(2)}) %all-to-all-start.1) | async-done | bytes 2949152 | tf_op jit(solution)/shard_map/all_to_all | solution.py:427
  229.5 1.0 dynamic-slice_bitcast_fusion
  230.5 2.3 collective-permute-start.33
  232.8 5.2 %collective-permute-start.34 = (f32[16,8,128]{2,1,0:T(8,128)S(1)}, f32[16,8,128]{2,1,0:T(8,128)S(1)}, u32[]{:S(2)}, u32[]{:S(2)}) collective-permute-start(f32[16,8,128]{2,1,0:T(8,128)S(1)} %slice.23), channel_id=1, source_target_pairs={{0,0},{1,16},{2,32},{3,48},{4,64},{5,80},{6,96},{7,112},{16,128},{... | collective-permute-start | bytes 196616 | tf_op jit(solution)/shard_map/ppermute | solution.py:523
  238.0 0.7 fusion.1
  238.7 0.7 slice.22
  239.4 6.0 %all-to-all-start.2 = ((f32[8,32,128]{2,1,0:T(8,128)}), f32[8,32,128]{2,1,0:T(8,128)S(1)}, u32[]{:S(2)}, u32[]{:S(2)}) async-start(f32[8,32,128]{2,1,0:T(8,128)} %bitcast.19), calls=%async_computation.2 | async-start | bytes 262144 | tf_op jit(solution)/shard_map/all_to_all | solution.py:527
  245.4 0.7 copy.21
  246.1 0.8 pad_maximum_fusion.1
  246.9 7.4 %all-to-all-done.2.pieces = f32[8,32,128]{2,1,0:T(8,128)S(1)} async-done(((f32[8,32,128]{2,1,0:T(8,128)}), f32[8,32,128]{2,1,0:T(8,128)S(1)}, u32[]{:S(2)}, u32[]{:S(2)}) %all-to-all-start.2) | async-done | bytes 131104 | tf_op jit(solution)/shard_map/all_to_all | solution.py:527
  254.3 0.7 copy-done.6
  255.0 1.7 shard_map.149
  (119 shorter events, 1.9 us)
Async XLA Ops:
  8.3 23.7 %copy-start.4 = (bf16[512,512]{1,0:T(8,128)(2,1)S(1)}, bf16[512,512]{1,0:T(8,128)(2,1)}, u32[]{:S(2)}) copy-start(bf16[512,512]{1,0:T(8,128)(2,1)} %param.9) | copy-start | bytes 1572868
  9.1 26.3 %copy-start.5 = (bf16[512,512]{1,0:T(8,128)(2,1)S(1)}, bf16[512,512]{1,0:T(8,128)(2,1)}, u32[]{:S(2)}) copy-start(bf16[512,512]{1,0:T(8,128)(2,1)} %param.10) | copy-start | bytes 1572868
  9.1 22.0 %all-to-all-start = ((bf16[16,64,128]{2,1,0:T(8,128)(2,1)}), bf16[16,64,128]{2,1,0:T(8,128)(2,1)S(1)}, u32[]{:S(2)}, u32[]{:S(2)}) async-start(bf16[16,64,128]{2,1,0:T(8,128)(2,1)} %bitcast.10), calls=%async_computation | async-start | bytes 524288 | tf_op jit(solution)/shard_map/all_to_all | solution.py:444
  20.8 64.2 %all-gather.3.cloned.1.call-start = ((), (), s32[]{:S(2)}) async-start(), calls=%async_computation.5 | async-start | bytes 7798784 | tf_op jit(solution)/shard_map/all_gather | solution.py:482
  21.9 6.3 %collective-permute-start = (bf16[3,128,128]{2,1,0:T(8,128)(2,1)S(1)}, bf16[3,128,128]{2,1,0:T(8,128)(2,1)S(1)}, u32[]{:S(2)}, u32[]{:S(2)}) collective-permute-start(bf16[3,128,128]{2,1,0:T(8,128)(2,1)S(1)} %select_select_fusion), channel_id=1, source_target_pairs={{0,8},{8,0},{1,9},{9,1},{2,10},{10,2},{3,11},{11,3},{4,12},{12,4},... | collective-permute-start | bytes 294920 | tf_op jit(solution)/shard_map/ppermute | solution.py:395
  31.9 197.5 %reduce-scatter.2.cloned.1.call-start = ((), (), s32[]{:S(2)}) async-start(), calls=%async_computation.4 | async-start | bytes 4718592 | tf_op jit(solution)/shard_map/reduce_scatter | solution.py:504
  32.0 53.0 %copy-start.2 = (bf16[512,256]{1,0:T(8,128)(2,1)}, bf16[512,256]{1,0:T(8,128)(2,1)S(1)}, u32[]{:S(2)}) copy-start(bf16[512,256]{1,0:T(8,128)(2,1)S(1)} %get-tuple-element.134) | copy-start | bytes 786436
  32.0 6.8 %collective-permute-start.1 = (bf16[512,256]{1,0:T(8,128)(2,1)S(1)}, bf16[512,256]{1,0:T(8,128)(2,1)S(1)}, u32[]{:S(2)}, u32[]{:S(2)}) collective-permute-start(bf16[512,256]{1,0:T(8,128)(2,1)S(1)} %get-tuple-element.133), channel_id=1, source_target_pairs={{0,8},{8,0},{1,9},{9,1},{2,10},{10,2},{3,11},{11,3},{4,12},{12,4},... | collective-permute-start | bytes 786440 | tf_op jit(solution)/shard_map/ppermute | solution.py:395
  32.8 8.7 %collective-permute-start.8 = (bf16[4,128,256]{2,1,0:T(8,128)(2,1)S(1)}, bf16[4,128,256]{2,1,0:T(8,128)(2,1)S(1)}, u32[]{:S(2)}, u32[]{:S(2)}) collective-permute-start(bf16[4,128,256]{2,1,0:T(8,128)(2,1)S(1)} %bitcast.45), channel_id=1, source_target_pairs={{0,1},{1,2},{2,3},{3,4},{4,5},{5,6},{6,7},{7,0},{8,9},{9,10},{10,1... | collective-permute-start | bytes 786440 | tf_op jit(solution)/shard_map/ppermute | solution.py:391
  35.5 6.3 %collective-permute-start.2 = (bf16[4,128,256]{2,1,0:T(8,128)(2,1)S(1)}, bf16[4,128,256]{2,1,0:T(8,128)(2,1)S(1)}, u32[]{:S(2)}, u32[]{:S(2)}) collective-permute-start(bf16[4,128,256]{2,1,0:T(8,128)(2,1)S(1)} %bitcast.46), channel_id=1, source_target_pairs={{0,7},{1,0},{2,1},{3,2},{4,3},{5,4},{6,5},{7,6},{8,15},{9,8},{10,9... | collective-permute-start | bytes 786440 | tf_op jit(solution)/shard_map/ppermute | solution.py:391
  35.5 60.3 %copy-start.1 = (bf16[512,256]{1,0:T(8,128)(2,1)}, bf16[512,256]{1,0:T(8,128)(2,1)S(1)}, u32[]{:S(2)}) copy-start(bf16[512,256]{1,0:T(8,128)(2,1)S(1)} %get-tuple-element.132) | copy-start | bytes 786436
  35.5 9.9 %collective-permute-start.16 = (bf16[512,256]{1,0:T(8,128)(2,1)S(1)}, bf16[512,256]{1,0:T(8,128)(2,1)S(1)}, u32[]{:S(2)}, u32[]{:S(2)}) collective-permute-start(bf16[512,256]{1,0:T(8,128)(2,1)S(1)} %get-tuple-element.131), channel_id=1, source_target_pairs={{0,8},{8,0},{1,9},{9,1},{2,10},{10,2},{3,11},{11,3},{4,12},{12,4},... | collective-permute-start | bytes 786440 | tf_op jit(solution)/shard_map/ppermute | solution.py:395
  38.8 46.2 %copy-start.22 = (bf16[512,256]{1,0:T(8,128)(2,1)}, bf16[512,256]{1,0:T(8,128)(2,1)S(1)}, u32[]{:S(2)}) copy-start(bf16[512,256]{1,0:T(8,128)(2,1)S(1)} %collective-permute-done.1) | copy-start | bytes 786436
  38.8 8.0 %collective-permute-start.3 = (bf16[4,128,256]{2,1,0:T(8,128)(2,1)S(1)}, bf16[4,128,256]{2,1,0:T(8,128)(2,1)S(1)}, u32[]{:S(2)}, u32[]{:S(2)}) collective-permute-start(bf16[4,128,256]{2,1,0:T(8,128)(2,1)S(1)} %bitcast.56), channel_id=1, source_target_pairs={{0,7},{1,0},{2,1},{3,2},{4,3},{5,4},{6,5},{7,6},{8,15},{9,8},{10,9... | collective-permute-start | bytes 786440 | tf_op jit(solution)/shard_map/ppermute | solution.py:391
  41.5 11.9 %collective-permute-start.13 = (bf16[4,128,256]{2,1,0:T(8,128)(2,1)S(1)}, bf16[4,128,256]{2,1,0:T(8,128)(2,1)S(1)}, u32[]{:S(2)}, u32[]{:S(2)}) collective-permute-start(bf16[4,128,256]{2,1,0:T(8,128)(2,1)S(1)} %bitcast.57), channel_id=1, source_target_pairs={{0,1},{1,2},{2,3},{3,4},{4,5},{5,6},{6,7},{7,0},{8,9},{9,10},{10,1... | collective-permute-start | bytes 786440 | tf_op jit(solution)/shard_map/ppermute | solution.py:391
  41.5 43.5 %copy-start.23 = (bf16[4,128,256]{2,1,0:T(8,128)(2,1)}, bf16[4,128,256]{2,1,0:T(8,128)(2,1)S(1)}, u32[]{:S(2)}) copy-start(bf16[4,128,256]{2,1,0:T(8,128)(2,1)S(1)} %collective-permute-done.8.refs_14_) | copy-start | bytes 786436
  41.5 9.2 %collective-permute-start.9 = (bf16[4,128,256]{2,1,0:T(8,128)(2,1)S(1)}, bf16[4,128,256]{2,1,0:T(8,128)(2,1)S(1)}, u32[]{:S(2)}, u32[]{:S(2)}) collective-permute-start(bf16[4,128,256]{2,1,0:T(8,128)(2,1)S(1)} %collective-permute-done.8.refs_14_), channel_id=1, source_target_pairs={{0,1},{1,2},{2,3},{3,4},{4,5},{5,6},{6,7},{7,0},{8,9},{9,10},{10,1... | collective-permute-start | bytes 786440 | tf_op jit(solution)/shard_map/ppermute | solution.py:391
  41.8 16.5 %copy-start.24 = (bf16[4,128,256]{2,1,0:T(8,128)(2,1)}, bf16[4,128,256]{2,1,0:T(8,128)(2,1)S(1)}, u32[]{:S(2)}) copy-start(bf16[4,128,256]{2,1,0:T(8,128)(2,1)S(1)} %collective-permute-done.2.refs_2_) | copy-start | bytes 786436
  41.8 9.4 %collective-permute-start.4 = (bf16[4,128,256]{2,1,0:T(8,128)(2,1)S(1)}, bf16[4,128,256]{2,1,0:T(8,128)(2,1)S(1)}, u32[]{:S(2)}, u32[]{:S(2)}) collective-permute-start(bf16[4,128,256]{2,1,0:T(8,128)(2,1)S(1)} %collective-permute-done.2.refs_2_), channel_id=1, source_target_pairs={{0,7},{1,0},{2,1},{3,2},{4,3},{5,4},{6,5},{7,6},{8,15},{9,8},{10,9... | collective-permute-start | bytes 786440 | tf_op jit(solution)/shard_map/ppermute | solution.py:391
  45.4 50.4 %copy-start.7 = (bf16[512,256]{1,0:T(8,128)(2,1)}, bf16[512,256]{1,0:T(8,128)(2,1)S(1)}, u32[]{:S(2)}) copy-start(bf16[512,256]{1,0:T(8,128)(2,1)S(1)} %collective-permute-done.16) | copy-start | bytes 786436
  45.4 10.2 %collective-permute-start.17 = (bf16[4,128,256]{2,1,0:T(8,128)(2,1)S(1)}, bf16[4,128,256]{2,1,0:T(8,128)(2,1)S(1)}, u32[]{:S(2)}, u32[]{:S(2)}) collective-permute-start(bf16[4,128,256]{2,1,0:T(8,128)(2,1)S(1)} %bitcast.42), channel_id=1, source_target_pairs={{0,1},{1,2},{2,3},{3,4},{4,5},{5,6},{6,7},{7,0},{8,9},{9,10},{10,1... | collective-permute-start | bytes 786440 | tf_op jit(solution)/shard_map/ppermute | solution.py:391
  46.8 28.3 %copy-start.25 = (bf16[4,128,256]{2,1,0:T(8,128)(2,1)}, bf16[4,128,256]{2,1,0:T(8,128)(2,1)S(1)}, u32[]{:S(2)}) copy-start(bf16[4,128,256]{2,1,0:T(8,128)(2,1)S(1)} %collective-permute-done.3.refs_3_) | copy-start | bytes 786436
  46.8 9.9 %collective-permute-start.5 = (bf16[4,128,256]{2,1,0:T(8,128)(2,1)S(1)}, bf16[4,128,256]{2,1,0:T(8,128)(2,1)S(1)}, u32[]{:S(2)}, u32[]{:S(2)}) collective-permute-start(bf16[4,128,256]{2,1,0:T(8,128)(2,1)S(1)} %collective-permute-done.3.refs_3_), channel_id=1, source_target_pairs={{0,7},{1,0},{2,1},{3,2},{4,3},{5,4},{6,5},{7,6},{8,15},{9,8},{10,9... | collective-permute-start | bytes 786440 | tf_op jit(solution)/shard_map/ppermute | solution.py:391
  50.7 27.4 %copy-start.27 = (bf16[4,128,256]{2,1,0:T(8,128)(2,1)}, bf16[4,128,256]{2,1,0:T(8,128)(2,1)S(1)}, u32[]{:S(2)}) copy-start(bf16[4,128,256]{2,1,0:T(8,128)(2,1)S(1)} %collective-permute-done.9.refs_12_) | copy-start | bytes 786436
  50.7 10.5 %collective-permute-start.18 = (bf16[4,128,256]{2,1,0:T(8,128)(2,1)S(1)}, bf16[4,128,256]{2,1,0:T(8,128)(2,1)S(1)}, u32[]{:S(2)}, u32[]{:S(2)}) collective-permute-start(bf16[4,128,256]{2,1,0:T(8,128)(2,1)S(1)} %bitcast.53), channel_id=1, source_target_pairs={{0,1},{1,2},{2,3},{3,4},{4,5},{5,6},{6,7},{7,0},{8,9},{9,10},{10,1... | collective-permute-start | bytes 786440 | tf_op jit(solution)/shard_map/ppermute | solution.py:391
  51.1 28.2 %copy-start.28 = (bf16[4,128,256]{2,1,0:T(8,128)(2,1)}, bf16[4,128,256]{2,1,0:T(8,128)(2,1)S(1)}, u32[]{:S(2)}) copy-start(bf16[4,128,256]{2,1,0:T(8,128)(2,1)S(1)} %collective-permute-done.4.refs_4_) | copy-start | bytes 786436
  51.1 11.2 %collective-permute-start.19 = (bf16[4,128,256]{2,1,0:T(8,128)(2,1)S(1)}, bf16[4,128,256]{2,1,0:T(8,128)(2,1)S(1)}, u32[]{:S(2)}, u32[]{:S(2)}) collective-permute-start(bf16[4,128,256]{2,1,0:T(8,128)(2,1)S(1)} %bitcast.43), channel_id=1, source_target_pairs={{0,7},{1,0},{2,1},{3,2},{4,3},{5,4},{6,5},{7,6},{8,15},{9,8},{10,9... | collective-permute-start | bytes 786440 | tf_op jit(solution)/shard_map/ppermute | solution.py:391
  53.4 21.8 %copy-start.26 = (bf16[4,128,256]{2,1,0:T(8,128)(2,1)}, bf16[4,128,256]{2,1,0:T(8,128)(2,1)S(1)}, u32[]{:S(2)}) copy-start(bf16[4,128,256]{2,1,0:T(8,128)(2,1)S(1)} %collective-permute-done.13.refs_15_) | copy-start | bytes 786436
  53.4 13.4 %collective-permute-start.10 = (bf16[4,128,256]{2,1,0:T(8,128)(2,1)S(1)}, bf16[4,128,256]{2,1,0:T(8,128)(2,1)S(1)}, u32[]{:S(2)}, u32[]{:S(2)}) collective-permute-start(bf16[4,128,256]{2,1,0:T(8,128)(2,1)S(1)} %collective-permute-done.9.refs_12_), channel_id=1, source_target_pairs={{0,1},{1,2},{2,3},{3,4},{4,5},{5,6},{6,7},{7,0},{8,9},{9,10},{10,1... | collective-permute-start | bytes 786440 | tf_op jit(solution)/shard_map/ppermute | solution.py:391
  55.6 40.2 %copy-start.8 = (bf16[4,128,256]{2,1,0:T(8,128)(2,1)}, bf16[4,128,256]{2,1,0:T(8,128)(2,1)S(1)}, u32[]{:S(2)}) copy-start(bf16[4,128,256]{2,1,0:T(8,128)(2,1)S(1)} %collective-permute-done.17.refs_14_) | copy-start | bytes 786436
  55.6 16.9 %collective-permute-start.14 = (bf16[4,128,256]{2,1,0:T(8,128)(2,1)S(1)}, bf16[4,128,256]{2,1,0:T(8,128)(2,1)S(1)}, u32[]{:S(2)}, u32[]{:S(2)}) collective-permute-start(bf16[4,128,256]{2,1,0:T(8,128)(2,1)S(1)} %collective-permute-done.13.refs_15_), channel_id=1, source_target_pairs={{0,1},{1,2},{2,3},{3,4},{4,5},{5,6},{6,7},{7,0},{8,9},{9,10},{10,1... | collective-permute-start | bytes 786440 | tf_op jit(solution)/shard_map/ppermute | solution.py:391
  56.7 26.9 %copy-start.29 = (bf16[4,128,256]{2,1,0:T(8,128)(2,1)}, bf16[4,128,256]{2,1,0:T(8,128)(2,1)S(1)}, u32[]{:S(2)}) copy-start(bf16[4,128,256]{2,1,0:T(8,128)(2,1)S(1)} %collective-permute-done.5.refs_5_) | copy-start | bytes 786436
  56.7 15.7 %collective-permute-start.7 = (bf16[4,128,256]{2,1,0:T(8,128)(2,1)S(1)}, bf16[4,128,256]{2,1,0:T(8,128)(2,1)}, u32[]{:S(2)}, u32[]{:S(2)}) collective-permute-start(bf16[4,128,256]{2,1,0:T(8,128)(2,1)S(1)} %collective-permute-done.5.refs_5_), channel_id=1, source_target_pairs={{0,7},{1,0},{2,1},{3,2},{4,3},{5,4},{6,5},{7,6},{8,15},{9,8},{10,9... | collective-permute-start | bytes 786440 | tf_op jit(solution)/shard_map/ppermute | solution.py:391
  61.2 34.6 %copy-start.9 = (bf16[4,128,256]{2,1,0:T(8,128)(2,1)}, bf16[4,128,256]{2,1,0:T(8,128)(2,1)S(1)}, u32[]{:S(2)}) copy-start(bf16[4,128,256]{2,1,0:T(8,128)(2,1)S(1)} %collective-permute-done.18.refs_15_) | copy-start | bytes 786436
  61.2 13.9 %collective-permute-start.20 = (bf16[4,128,256]{2,1,0:T(8,128)(2,1)S(1)}, bf16[4,128,256]{2,1,0:T(8,128)(2,1)S(1)}, u32[]{:S(2)}, u32[]{:S(2)}) collective-permute-start(bf16[4,128,256]{2,1,0:T(8,128)(2,1)S(1)} %bitcast.54), channel_id=1, source_target_pairs={{0,7},{1,0},{2,1},{3,2},{4,3},{5,4},{6,5},{7,6},{8,15},{9,8},{10,9... | collective-permute-start | bytes 786440 | tf_op jit(solution)/shard_map/ppermute | solution.py:391
  62.4 33.5 %copy-start.10 = (bf16[4,128,256]{2,1,0:T(8,128)(2,1)}, bf16[4,128,256]{2,1,0:T(8,128)(2,1)S(1)}, u32[]{:S(2)}) copy-start(bf16[4,128,256]{2,1,0:T(8,128)(2,1)S(1)} %collective-permute-done.19.refs_2_) | copy-start | bytes 786436
  62.4 14.2 %collective-permute-start.6 = (bf16[4,128,256]{2,1,0:T(8,128)(2,1)S(1)}, bf16[4,128,256]{2,1,0:T(8,128)(2,1)S(1)}, u32[]{:S(2)}, u32[]{:S(2)}) collective-permute-start(bf16[4,128,256]{2,1,0:T(8,128)(2,1)S(1)} %collective-permute-done.4.refs_4_), channel_id=1, source_target_pairs={{0,7},{1,0},{2,1},{3,2},{4,3},{5,4},{6,5},{7,6},{8,15},{9,8},{10,9... | collective-permute-start | bytes 786440 | tf_op jit(solution)/shard_map/ppermute | solution.py:391
  66.8 16.9 %copy-start.30 = (bf16[4,128,256]{2,1,0:T(8,128)(2,1)}, bf16[4,128,256]{2,1,0:T(8,128)(2,1)S(1)}, u32[]{:S(2)}) copy-start(bf16[4,128,256]{2,1,0:T(8,128)(2,1)S(1)} %collective-permute-done.10.refs_10_) | copy-start | bytes 786436
  66.8 11.3 %collective-permute-start.11 = (bf16[4,128,256]{2,1,0:T(8,128)(2,1)S(1)}, bf16[4,128,256]{2,1,0:T(8,128)(2,1)S(1)}, u32[]{:S(2)}, u32[]{:S(2)}) collective-permute-start(bf16[4,128,256]{2,1,0:T(8,128)(2,1)S(1)} %collective-permute-done.10.refs_10_), channel_id=1, source_target_pairs={{0,1},{1,2},{2,3},{3,4},{4,5},{5,6},{6,7},{7,0},{8,9},{9,10},{10,1... | collective-permute-start | bytes 786440 | tf_op jit(solution)/shard_map/ppermute | solution.py:391
  72.4 11.2 %copy-start.31 = (bf16[4,128,256]{2,1,0:T(8,128)(2,1)}, bf16[4,128,256]{2,1,0:T(8,128)(2,1)S(1)}, u32[]{:S(2)}) copy-start(bf16[4,128,256]{2,1,0:T(8,128)(2,1)S(1)} %collective-permute-done.14.refs_13_) | copy-start | bytes 786436
  72.4 11.2 %collective-permute-start.15 = (bf16[4,128,256]{2,1,0:T(8,128)(2,1)S(1)}, bf16[4,128,256]{2,1,0:T(8,128)(2,1)S(1)}, u32[]{:S(2)}, u32[]{:S(2)}) collective-permute-start(bf16[4,128,256]{2,1,0:T(8,128)(2,1)S(1)} %collective-permute-done.14.refs_13_), channel_id=1, source_target_pairs={{0,1},{1,2},{2,3},{3,4},{4,5},{5,6},{6,7},{7,0},{8,9},{9,10},{10,1... | collective-permute-start | bytes 786440 | tf_op jit(solution)/shard_map/ppermute | solution.py:391
  72.4 12.6 %collective-permute-start.12 = (bf16[4,128,256]{2,1,0:T(8,128)(2,1)}, bf16[4,128,256]{2,1,0:T(8,128)(2,1)}, u32[]{:S(2)}, u32[]{:S(2)}) collective-permute-start(bf16[4,128,256]{2,1,0:T(8,128)(2,1)} %collective-permute-done.7.refs_7_), channel_id=1, source_target_pairs={{0,7},{1,0},{2,1},{3,2},{4,3},{5,4},{6,5},{7,6},{8,15},{9,8},{10,9... | collective-permute-start | bytes 786440 | tf_op jit(solution)/shard_map/ppermute | solution.py:391
  75.1 20.7 %copy-start.11 = (bf16[4,128,256]{2,1,0:T(8,128)(2,1)}, bf16[4,128,256]{2,1,0:T(8,128)(2,1)S(1)}, u32[]{:S(2)}) copy-start(bf16[4,128,256]{2,1,0:T(8,128)(2,1)S(1)} %collective-permute-done.20.refs_3_) | copy-start | bytes 786436
  75.1 20.7 %collective-permute-start.21 = (bf16[4,128,256]{2,1,0:T(8,128)(2,1)S(1)}, bf16[4,128,256]{2,1,0:T(8,128)(2,1)S(1)}, u32[]{:S(2)}, u32[]{:S(2)}) collective-permute-start(bf16[4,128,256]{2,1,0:T(8,128)(2,1)S(1)} %collective-permute-done.17.refs_14_), channel_id=1, source_target_pairs={{0,1},{1,2},{2,3},{3,4},{4,5},{5,6},{6,7},{7,0},{8,9},{9,10},{10,1... | collective-permute-start | bytes 786440 | tf_op jit(solution)/shard_map/ppermute | solution.py:391
  76.6 19.3 %collective-permute-start.22 = (bf16[4,128,256]{2,1,0:T(8,128)(2,1)S(1)}, bf16[4,128,256]{2,1,0:T(8,128)(2,1)S(1)}, u32[]{:S(2)}, u32[]{:S(2)}) collective-permute-start(bf16[4,128,256]{2,1,0:T(8,128)(2,1)S(1)} %collective-permute-done.18.refs_15_), channel_id=1, source_target_pairs={{0,1},{1,2},{2,3},{3,4},{4,5},{5,6},{6,7},{7,0},{8,9},{9,10},{10,1... | collective-permute-start | bytes 786440 | tf_op jit(solution)/shard_map/ppermute | solution.py:391
  78.1 17.8 %collective-permute-start.23 = (bf16[4,128,256]{2,1,0:T(8,128)(2,1)S(1)}, bf16[4,128,256]{2,1,0:T(8,128)(2,1)S(1)}, u32[]{:S(2)}, u32[]{:S(2)}) collective-permute-start(bf16[4,128,256]{2,1,0:T(8,128)(2,1)S(1)} %collective-permute-done.19.refs_2_), channel_id=1, source_target_pairs={{0,7},{1,0},{2,1},{3,2},{4,3},{5,4},{6,5},{7,6},{8,15},{9,8},{10,9... | collective-permute-start | bytes 786440 | tf_op jit(solution)/shard_map/ppermute | solution.py:391
  84.4 11.5 %collective-permute-start.24 = (bf16[4,128,256]{2,1,0:T(8,128)(2,1)S(1)}, bf16[4,128,256]{2,1,0:T(8,128)(2,1)S(1)}, u32[]{:S(2)}, u32[]{:S(2)}) collective-permute-start(bf16[4,128,256]{2,1,0:T(8,128)(2,1)S(1)} %collective-permute-done.20.refs_3_), channel_id=1, source_target_pairs={{0,7},{1,0},{2,1},{3,2},{4,3},{5,4},{6,5},{7,6},{8,15},{9,8},{10,9... | collective-permute-start | bytes 786440 | tf_op jit(solution)/shard_map/ppermute | solution.py:391
  95.9 17.9 %copy-start.12 = (bf16[4,128,256]{2,1,0:T(8,128)(2,1)}, bf16[4,128,256]{2,1,0:T(8,128)(2,1)S(1)}, u32[]{:S(2)}) copy-start(bf16[4,128,256]{2,1,0:T(8,128)(2,1)S(1)} %collective-permute-done.21.refs_12_) | copy-start | bytes 786436
  95.9 17.8 %copy-start.13 = (bf16[4,128,256]{2,1,0:T(8,128)(2,1)}, bf16[4,128,256]{2,1,0:T(8,128)(2,1)S(1)}, u32[]{:S(2)}) copy-start(bf16[4,128,256]{2,1,0:T(8,128)(2,1)S(1)} %collective-permute-done.22.refs_13_) | copy-start | bytes 786436
  95.9 17.8 %copy-start.14 = (bf16[4,128,256]{2,1,0:T(8,128)(2,1)}, bf16[4,128,256]{2,1,0:T(8,128)(2,1)S(1)}, u32[]{:S(2)}) copy-start(bf16[4,128,256]{2,1,0:T(8,128)(2,1)S(1)} %collective-permute-done.23.refs_4_) | copy-start | bytes 786436
  95.9 17.8 %copy-start.15 = (bf16[4,128,256]{2,1,0:T(8,128)(2,1)}, bf16[4,128,256]{2,1,0:T(8,128)(2,1)S(1)}, u32[]{:S(2)}) copy-start(bf16[4,128,256]{2,1,0:T(8,128)(2,1)S(1)} %collective-permute-done.24.refs_5_) | copy-start | bytes 786436
  95.9 17.8 %collective-permute-start.25 = (bf16[4,128,256]{2,1,0:T(8,128)(2,1)S(1)}, bf16[4,128,256]{2,1,0:T(8,128)(2,1)S(1)}, u32[]{:S(2)}, u32[]{:S(2)}) collective-permute-start(bf16[4,128,256]{2,1,0:T(8,128)(2,1)S(1)} %collective-permute-done.21.refs_12_), channel_id=1, source_target_pairs={{0,1},{1,2},{2,3},{3,4},{4,5},{5,6},{6,7},{7,0},{8,9},{9,10},{10,1... | collective-permute-start | bytes 786440 | tf_op jit(solution)/shard_map/ppermute | solution.py:391
  97.5 16.3 %collective-permute-start.26 = (bf16[4,128,256]{2,1,0:T(8,128)(2,1)S(1)}, bf16[4,128,256]{2,1,0:T(8,128)(2,1)S(1)}, u32[]{:S(2)}, u32[]{:S(2)}) collective-permute-start(bf16[4,128,256]{2,1,0:T(8,128)(2,1)S(1)} %collective-permute-done.22.refs_13_), channel_id=1, source_target_pairs={{0,1},{1,2},{2,3},{3,4},{4,5},{5,6},{6,7},{7,0},{8,9},{9,10},{10,1... | collective-permute-start | bytes 786440 | tf_op jit(solution)/shard_map/ppermute | solution.py:391
  97.6 16.2 %collective-permute-start.27 = (bf16[4,128,256]{2,1,0:T(8,128)(2,1)S(1)}, bf16[4,128,256]{2,1,0:T(8,128)(2,1)S(1)}, u32[]{:S(2)}, u32[]{:S(2)}) collective-permute-start(bf16[4,128,256]{2,1,0:T(8,128)(2,1)S(1)} %collective-permute-done.23.refs_4_), channel_id=1, source_target_pairs={{0,7},{1,0},{2,1},{3,2},{4,3},{5,4},{6,5},{7,6},{8,15},{9,8},{10,9... | collective-permute-start | bytes 786440 | tf_op jit(solution)/shard_map/ppermute | solution.py:391
  100.1 13.7 %collective-permute-start.28 = (bf16[4,128,256]{2,1,0:T(8,128)(2,1)S(1)}, bf16[4,128,256]{2,1,0:T(8,128)(2,1)S(1)}, u32[]{:S(2)}, u32[]{:S(2)}) collective-permute-start(bf16[4,128,256]{2,1,0:T(8,128)(2,1)S(1)} %collective-permute-done.24.refs_5_), channel_id=1, source_target_pairs={{0,7},{1,0},{2,1},{3,2},{4,3},{5,4},{6,5},{7,6},{8,15},{9,8},{10,9... | collective-permute-start | bytes 786440 | tf_op jit(solution)/shard_map/ppermute | solution.py:391
  113.8 7.4 %collective-permute-start.29 = (bf16[4,128,256]{2,1,0:T(8,128)(2,1)S(1)}, bf16[4,128,256]{2,1,0:T(8,128)(2,1)S(1)}, u32[]{:S(2)}, u32[]{:S(2)}) collective-permute-start(bf16[4,128,256]{2,1,0:T(8,128)(2,1)S(1)} %collective-permute-done.25.refs_10_), channel_id=1, source_target_pairs={{0,1},{1,2},{2,3},{3,4},{4,5},{5,6},{6,7},{7,0},{8,9},{9,10},{10,1... | collective-permute-start | bytes 786440 | tf_op jit(solution)/shard_map/ppermute | solution.py:391
  115.3 7.4 %collective-permute-start.30 = (bf16[4,128,256]{2,1,0:T(8,128)(2,1)S(1)}, bf16[4,128,256]{2,1,0:T(8,128)(2,1)S(1)}, u32[]{:S(2)}, u32[]{:S(2)}) collective-permute-start(bf16[4,128,256]{2,1,0:T(8,128)(2,1)S(1)} %collective-permute-done.28.refs_7_), channel_id=1, source_target_pairs={{0,7},{1,0},{2,1},{3,2},{4,3},{5,4},{6,5},{7,6},{8,15},{9,8},{10,9... | collective-permute-start | bytes 786440 | tf_op jit(solution)/shard_map/ppermute | solution.py:391
  157.6 25.8 %collective-permute-start.31 = (bf16[8,2,58,8,128]{4,3,2,1,0:T(8,128)(2,1)}, bf16[8,2,58,8,128]{4,3,2,1,0:T(8,128)(2,1)S(1)}, u32[]{:S(2)}, u32[]{:S(2)}) collective-permute-start(bf16[8,2,58,8,128]{4,3,2,1,0:T(8,128)(2,1)} %get-tuple-element.105), channel_id=1, source_target_pairs={{0,16},{16,0},{1,17},{17,1},{2,18},{18,2},{3,19},{19,3},{4,20},{20... | collective-permute-start | bytes 5701640 | tf_op jit(solution)/shard_map/ppermute | solution.py:421
  178.9 2.9 %collective-permute-start.32 = (bf16[8,2,32,8,128]{4,3,2,1,0:T(8,128)(2,1)}, bf16[8,2,32,8,128]{4,3,2,1,0:T(8,128)(2,1)S(1)}, u32[]{:S(2)}, u32[]{:S(2)}) collective-permute-start(bf16[8,2,32,8,128]{4,3,2,1,0:T(8,128)(2,1)} %get-tuple-element.109), channel_id=1, source_target_pairs={{0,16},{16,0},{1,17},{17,1},{2,18},{18,2},{3,19},{19,3},{4,20},{20... | collective-permute-start | bytes 3145736 | tf_op jit(solution)/shard_map/ppermute | solution.py:421
  185.7 43.3 %all-to-all-start.1 = ((bf16[16,90,8,128]{3,2,1,0:T(8,128)(2,1)}), bf16[16,90,8,128]{3,2,1,0:T(8,128)(2,1)S(1)}, u32[]{:S(2)}, u32[]{:S(2)}) async-start(bf16[16,90,8,128]{3,2,1,0:T(8,128)(2,1)} %pad_maximum_fusion), calls=%async_computation.1 | async-start | bytes 5898240 | tf_op jit(solution)/shard_map/all_to_all | solution.py:427
  229.4 16.6 %copy-start.3 = (bf16[8,128,256]{2,1,0:T(8,128)(2,1)S(1)}, bf16[8,128,256]{2,1,0:T(8,128)(2,1)}, u32[]{:S(2)}) copy-start(bf16[8,128,256]{2,1,0:T(8,128)(2,1)} %reduce-scatter.2.cloned.1.call-done) | copy-start | bytes 1572868
  230.5 15.5 %collective-permute-start.33 = (bf16[512,256]{1,0:T(8,128)(2,1)S(1)}, bf16[512,256]{1,0:T(8,128)(2,1)S(1)}, u32[]{:S(2)}, u32[]{:S(2)}) collective-permute-start(bf16[512,256]{1,0:T(8,128)(2,1)S(1)} %dynamic-slice_bitcast_fusion), channel_id=1, source_target_pairs={{0,8},{8,0},{1,9},{9,1},{2,10},{10,2},{3,11},{11,3},{4,12},{12,4},... | collective-permute-start | bytes 786440 | tf_op jit(solution)/shard_map/ppermute | solution.py:395
  232.8 12.5 %collective-permute-start.34 = (f32[16,8,128]{2,1,0:T(8,128)S(1)}, f32[16,8,128]{2,1,0:T(8,128)S(1)}, u32[]{:S(2)}, u32[]{:S(2)}) collective-permute-start(f32[16,8,128]{2,1,0:T(8,128)S(1)} %slice.23), channel_id=1, source_target_pairs={{0,0},{1,16},{2,32},{3,48},{4,64},{5,80},{6,96},{7,112},{16,128},{... | collective-permute-start | bytes 196616 | tf_op jit(solution)/shard_map/ppermute | solution.py:523
  239.4 15.0 %all-to-all-start.2 = ((f32[8,32,128]{2,1,0:T(8,128)}), f32[8,32,128]{2,1,0:T(8,128)S(1)}, u32[]{:S(2)}, u32[]{:S(2)}) async-start(f32[8,32,128]{2,1,0:T(8,128)} %bitcast.19), calls=%async_computation.2 | async-start | bytes 262144 | tf_op jit(solution)/shard_map/all_to_all | solution.py:527
  (11 other events, 56.7 us)
Sparse Core Ops, SparseCore 0:
  32.0 49.9 all-gather.2
  146.2 65.7 reduce-scatter.1
